TPU v7x, 32 devices: a whole 2x2x4 slice. The times are simulated.
32 devices in a mesh: rep: 8 (over y, x, core), shard: 4 (over z).
Axes of the slice: x: 2, y: 2, z: 4, core: 2. Of those that a mesh axis runs over, the one named last changes fastest.
Arguments:
- inputs: bfloat16 [8, 4, 1104, 1024], P('rep', 'shard'), may hold values from -6 to 6
- counts: int32 [8], P('rep'), may hold values from 1 to 4, as said below
- ln1_gain: bfloat16 [1024], P('shard'), may hold values from 0.5 to 1.5
- ln1_shift: bfloat16 [1024], P('shard'), may hold values from -4 to 4
- w_qkv: bfloat16 [1024, 3072], P('shard'), may hold values from -0.1875 to 0.1875
- qv_bias: bfloat16 [2048], P('shard'), may hold values from -4 to 4
- w_out: bfloat16 [1024, 1024], P('shard'), may hold values from -0.75 to 0.75
- out_bias: bfloat16 [1024], P('shard'), may hold values from -4 to 4
- ln2_gain: bfloat16 [1024], P('shard'), may hold values from 0.5 to 1.5
- ln2_shift: bfloat16 [1024], P('shard'), may hold values from -4 to 4
- w_up: bfloat16 [1024, 4096], P('shard'), may hold values from -0.1875 to 0.1875
- up_bias: bfloat16 [4096], P('shard'), may hold values from -4 to 4
- w_down: bfloat16 [4096, 1024], P('shard'), may hold values from -0.09375 to 0.09375
- down_bias: bfloat16 [1024], P('shard'), may hold values from -4 to 4
- cotangent: bfloat16 [8, 4, 1104, 1024], P('rep', 'shard'), may hold values from -6 to 6
Outputs:
- output: bfloat16 [8, 4, 1104, 1024], P('rep', 'shard')
- input_grad: float32 [8, 4, 1104, 1024], P('rep', 'shard')
- grad_ln1_gain: float32 [1024], P('shard')
- grad_ln1_shift: float32 [1024], P('shard')
- grad_w_qkv: float32 [1024, 3072], P('shard')
- grad_qv_bias: float32 [2048], P('shard')
- grad_w_out: float32 [1024, 1024], P('shard')
- grad_out_bias: float32 [1024], P('shard')
- grad_ln2_gain: float32 [1024], P('shard')
- grad_ln2_shift: float32 [1024], P('shard')
- grad_w_up: float32 [1024, 4096], P('shard')
- grad_up_bias: float32 [4096], P('shard')
- grad_w_down: float32 [4096, 1024], P('shard')
- grad_down_bias: float32 [1024], P('shard')
Inputs may be any that keep to these rules, and one draw needn't show every extreme that they name: A group's live sequences occupy its slots 0 to counts - 1; some group has exactly 4 and some exactly 1.
All inputs are finite; a program needn't handle non-finite values.
Results may differ from a plain program's by a relative error of at most 0.018.
Values may be sent and summed in bfloat16 or wider, within the bound.
No kernel may reach another device: no remote copies, remote signals or barrier semaphores. Data moves between devices by JAX's collectives and lax.ppermute only.
A program may use at most 256 MiB of HBM per device.

v0:
```python
import jax
import jax.numpy as jnp
from jax import lax
from jax.sharding import PartitionSpec as P

HEADS = 16
HDIM = 64


eps = 1e-06
head_block = 4


def layer_norm(values, gain, shift):
    centre = values - jnp.mean(values, -1, keepdims=True)
    spread = jnp.mean(centre * centre, -1, keepdims=True)
    return centre * lax.rsqrt(spread + eps) * gain + shift


def gelu_exact(values):
    return jax.nn.gelu(values, approximate=False)


def matmul(left, right):
    return jnp.dot(left, right, preferred_element_type=jnp.float32)


def left_trans(left, right):
    return lax.dot_general(
        left, right, (((0,), (0,)), ((), ())), preferred_element_type=jnp.float32
    )


def right_trans(left, right):
    return lax.dot_general(
        left, right, (((1,), (1,)), ((), ())), preferred_element_type=jnp.float32
    )


def body(
    inputs,
    counts,
    ln1_gain,
    ln1_shift,
    w_qkv,
    qv_bias,
    w_out,
    out_bias,
    ln2_gain,
    ln2_shift,
    w_up,
    up_bias,
    w_down,
    down_bias,
    cotangent,
):
    gathered = (
        lax.all_gather(ln1_gain, "shard", axis=0, tiled=True),
        lax.all_gather(ln1_shift, "shard", axis=0, tiled=True),
        lax.all_gather(w_qkv, "shard", axis=0, tiled=True),
        lax.all_gather(qv_bias, "shard", axis=0, tiled=True),
        lax.all_gather(w_out, "shard", axis=0, tiled=True),
        lax.all_gather(out_bias, "shard", axis=0, tiled=True),
        lax.all_gather(ln2_gain, "shard", axis=0, tiled=True),
        lax.all_gather(ln2_shift, "shard", axis=0, tiled=True),
        lax.all_gather(w_up, "shard", axis=0, tiled=True),
        lax.all_gather(up_bias, "shard", axis=0, tiled=True),
        lax.all_gather(w_down, "shard", axis=0, tiled=True),
        lax.all_gather(down_bias, "shard", axis=0, tiled=True),
    )
    (
        full_g1,
        full_s1,
        full_qkv,
        full_qvb,
        full_wout,
        full_bout,
        full_g2,
        full_s2,
        full_wup,
        full_bup,
        full_wdown,
        full_bdown,
    ) = gathered
    slots = inputs.shape[1]
    seq_len = inputs.shape[2]
    width = inputs.shape[3]
    n_rows = slots * seq_len
    groups = HEADS // head_block
    scale = HDIM ** (-0.5)
    first_slot = lax.axis_index("shard") * slots
    alive = (jnp.arange(slots, dtype=jnp.int32) + first_slot < counts[0]).astype(jnp.float32)
    alive_rows = jnp.broadcast_to(alive[:, None], (slots, seq_len)).reshape(n_rows, 1)
    tokens = inputs.reshape(n_rows, width).astype(jnp.float32)
    hidden_one, norm_one_back = jax.vjp(
        layer_norm, tokens, full_g1.astype(jnp.float32), full_s1.astype(jnp.float32)
    )
    hidden_one_b = hidden_one.astype(jnp.bfloat16)
    projected = matmul(hidden_one_b, full_qkv)
    bias_f = full_qvb.astype(jnp.float32)
    queries_b = (projected[:, :width] + bias_f[:width]).astype(jnp.bfloat16)
    keys_b = projected[:, width : 2 * width].astype(jnp.bfloat16)
    values_b = (projected[:, 2 * width :] + bias_f[width:]).astype(jnp.bfloat16)

    def arrange(values):
        return values.reshape(slots, seq_len, groups, head_block, HDIM).transpose(2, 0, 1, 3, 4)

    def restore(values):
        return values.transpose(1, 2, 0, 3, 4).reshape(n_rows, width)

    query_groups = arrange(queries_b)
    key_groups = arrange(keys_b)
    value_groups = arrange(values_b)

    def forward_group(operands):
        query_part, key_part, value_part = operands
        scores = (
            jnp.einsum("cqhd,ckhd->chqk", query_part, key_part, preferred_element_type=jnp.float32)
            * scale
        )
        largest = jnp.max(scores, -1, keepdims=True)
        exponent = jnp.exp(scores - largest)
        denominator = jnp.sum(exponent, -1, keepdims=True)
        probs_b = (exponent / denominator).astype(jnp.bfloat16)
        mixed = jnp.einsum(
            "chqk,ckhd->cqhd", probs_b, value_part, preferred_element_type=jnp.float32
        )
        return (mixed, (largest + jnp.log(denominator))[..., 0])

    mixed_groups, log_totals = lax.map(forward_group, (query_groups, key_groups, value_groups))
    attended_b = restore(mixed_groups).astype(jnp.bfloat16)
    middle = tokens + matmul(attended_b, full_wout) + full_bout.astype(jnp.float32)
    hidden_two, norm_two_back = jax.vjp(
        layer_norm, middle, full_g2.astype(jnp.float32), full_s2.astype(jnp.float32)
    )
    hidden_two_b = hidden_two.astype(jnp.bfloat16)
    pre_act = matmul(hidden_two_b, full_wup) + full_bup.astype(jnp.float32)
    activated, gelu_back = jax.vjp(gelu_exact, pre_act)
    activated_b = activated.astype(jnp.bfloat16)
    result = middle + matmul(activated_b, full_wdown) + full_bdown.astype(jnp.float32)
    output = (alive_rows * result).astype(jnp.bfloat16).reshape(inputs.shape)
    again = (
        lax.all_gather(ln1_gain, "shard", axis=0, tiled=True),
        lax.all_gather(ln1_shift, "shard", axis=0, tiled=True),
        lax.all_gather(w_qkv, "shard", axis=0, tiled=True),
        lax.all_gather(qv_bias, "shard", axis=0, tiled=True),
        lax.all_gather(w_out, "shard", axis=0, tiled=True),
        lax.all_gather(out_bias, "shard", axis=0, tiled=True),
        lax.all_gather(ln2_gain, "shard", axis=0, tiled=True),
        lax.all_gather(ln2_shift, "shard", axis=0, tiled=True),
        lax.all_gather(w_up, "shard", axis=0, tiled=True),
        lax.all_gather(up_bias, "shard", axis=0, tiled=True),
        lax.all_gather(w_down, "shard", axis=0, tiled=True),
        lax.all_gather(down_bias, "shard", axis=0, tiled=True),
    )
    back_qkv = again[2]
    back_wout = again[4]
    back_wup = again[8]
    back_wdown = again[10]
    d_out = alive_rows * cotangent.reshape(n_rows, width).astype(jnp.float32)
    d_out_b = d_out.astype(jnp.bfloat16)
    grad_wdown = left_trans(activated_b, d_out_b)
    grad_bdown = jnp.sum(d_out, 0)
    d_act = right_trans(d_out_b, back_wdown)
    d_pre_b = gelu_back(d_act)[0].astype(jnp.bfloat16)
    grad_wup = left_trans(hidden_two_b, d_pre_b)
    grad_bup = jnp.sum(d_pre_b.astype(jnp.float32), 0)
    d_hidden_two = right_trans(d_pre_b, back_wup)
    d_mid_norm, grad_g2, grad_s2 = norm_two_back(d_hidden_two)
    d_mid = d_out + d_mid_norm
    d_proj_b = d_mid.astype(jnp.bfloat16)
    grad_wout = left_trans(attended_b, d_proj_b)
    grad_bout = jnp.sum(d_proj_b.astype(jnp.float32), 0)
    d_att_b = right_trans(d_proj_b, back_wout).astype(jnp.bfloat16)
    d_att_groups = arrange(d_att_b)

    def backward_group(operands):
        query_part, key_part, value_part, log_total, grad_part = operands
        scores = (
            jnp.einsum("cqhd,ckhd->chqk", query_part, key_part, preferred_element_type=jnp.float32)
            * scale
        )
        attn_probs = jnp.exp(scores - log_total[..., None])
        probs_b = attn_probs.astype(jnp.bfloat16)
        d_probs = jnp.einsum(
            "cqhd,ckhd->chqk", grad_part, value_part, preferred_element_type=jnp.float32
        )
        row_inner = jnp.sum(d_probs * attn_probs, -1, keepdims=True)
        d_scores_b = (attn_probs * (d_probs - row_inner)).astype(jnp.bfloat16)
        d_query = (
            jnp.einsum("chqk,ckhd->cqhd", d_scores_b, key_part, preferred_element_type=jnp.float32)
            * scale
        )
        d_key = (
            jnp.einsum(
                "chqk,cqhd->ckhd", d_scores_b, query_part, preferred_element_type=jnp.float32
            )
            * scale
        )
        d_value = jnp.einsum(
            "chqk,cqhd->ckhd", probs_b, grad_part, preferred_element_type=jnp.float32
        )
        return (d_query, d_key, d_value)

    d_query_groups, d_key_groups, d_value_groups = lax.map(
        backward_group, (query_groups, key_groups, value_groups, log_totals, d_att_groups)
    )
    d_qkv_b = jnp.concatenate(
        [restore(d_query_groups), restore(d_key_groups), restore(d_value_groups)], 1
    ).astype(jnp.bfloat16)
    grad_qkv = left_trans(hidden_one_b, d_qkv_b)
    column_sums = jnp.sum(d_qkv_b.astype(jnp.float32), 0)
    grad_qvb = jnp.concatenate([column_sums[:width], column_sums[2 * width :]])
    d_hidden_one = right_trans(d_qkv_b, back_qkv)
    d_in_norm, grad_g1, grad_s1 = norm_one_back(d_hidden_one)
    input_grad = (d_mid + d_in_norm).reshape(inputs.shape)
    owned = (
        lax.psum_scatter(
            grad_g1.astype(jnp.bfloat16), "shard", scatter_dimension=0, tiled=True
        ).astype(jnp.float32),
        lax.psum_scatter(
            grad_s1.astype(jnp.bfloat16), "shard", scatter_dimension=0, tiled=True
        ).astype(jnp.float32),
        lax.psum_scatter(
            grad_qkv.astype(jnp.bfloat16), "shard", scatter_dimension=0, tiled=True
        ).astype(jnp.float32),
        lax.psum_scatter(
            grad_qvb.astype(jnp.bfloat16), "shard", scatter_dimension=0, tiled=True
        ).astype(jnp.float32),
        lax.psum_scatter(
            grad_wout.astype(jnp.bfloat16), "shard", scatter_dimension=0, tiled=True
        ).astype(jnp.float32),
        lax.psum_scatter(
            grad_bout.astype(jnp.bfloat16), "shard", scatter_dimension=0, tiled=True
        ).astype(jnp.float32),
        lax.psum_scatter(
            grad_g2.astype(jnp.bfloat16), "shard", scatter_dimension=0, tiled=True
        ).astype(jnp.float32),
        lax.psum_scatter(
            grad_s2.astype(jnp.bfloat16), "shard", scatter_dimension=0, tiled=True
        ).astype(jnp.float32),
        lax.psum_scatter(
            grad_wup.astype(jnp.bfloat16), "shard", scatter_dimension=0, tiled=True
        ).astype(jnp.float32),
        lax.psum_scatter(
            grad_bup.astype(jnp.bfloat16), "shard", scatter_dimension=0, tiled=True
        ).astype(jnp.float32),
        lax.psum_scatter(
            grad_wdown.astype(jnp.bfloat16), "shard", scatter_dimension=0, tiled=True
        ).astype(jnp.float32),
        lax.psum_scatter(
            grad_bdown.astype(jnp.bfloat16), "shard", scatter_dimension=0, tiled=True
        ).astype(jnp.float32),
    )
    o_g1, o_s1, o_qkv, o_qvb, o_wout, o_bout, o_g2, o_s2, o_wup, o_bup, o_wdown, o_bdown = owned
    summed = (
        lax.psum(o_g1.astype(jnp.bfloat16), "rep").astype(jnp.float32),
        lax.psum(o_s1.astype(jnp.bfloat16), "rep").astype(jnp.float32),
        lax.psum(o_qkv.astype(jnp.bfloat16), "rep").astype(jnp.float32),
        lax.psum(o_qvb.astype(jnp.bfloat16), "rep").astype(jnp.float32),
        lax.psum(o_wout.astype(jnp.bfloat16), "rep").astype(jnp.float32),
        lax.psum(o_bout.astype(jnp.bfloat16), "rep").astype(jnp.float32),
        lax.psum(o_g2.astype(jnp.bfloat16), "rep").astype(jnp.float32),
        lax.psum(o_s2.astype(jnp.bfloat16), "rep").astype(jnp.float32),
        lax.psum(o_wup.astype(jnp.bfloat16), "rep").astype(jnp.float32),
        lax.psum(o_bup.astype(jnp.bfloat16), "rep").astype(jnp.float32),
        lax.psum(o_wdown.astype(jnp.bfloat16), "rep").astype(jnp.float32),
        lax.psum(o_bdown.astype(jnp.bfloat16), "rep").astype(jnp.float32),
    )
    return (
        output,
        input_grad,
        summed[0],
        summed[1],
        summed[2],
        summed[3],
        summed[4],
        summed[5],
        summed[6],
        summed[7],
        summed[8],
        summed[9],
        summed[10],
        summed[11],
    )


def solution(mesh):
    placed = (
        P("rep", "shard", None, None),
        P("rep"),
        P("shard"),
        P("shard"),
        P("shard", None),
        P("shard"),
        P("shard", None),
        P("shard"),
        P("shard"),
        P("shard"),
        P("shard", None),
        P("shard"),
        P("shard", None),
        P("shard"),
        P("rep", "shard", None, None),
    )
    return jax.shard_map(
        body,
        mesh=mesh,
        in_specs=placed,
        out_specs=(
            P("rep", "shard", None, None),
            P("rep", "shard", None, None),
            P("shard"),
            P("shard"),
            P("shard", None),
            P("shard"),
            P("shard", None),
            P("shard"),
            P("shard"),
            P("shard"),
            P("shard", None),
            P("shard"),
            P("shard", None),
            P("shard"),
        ),
        check_vma=False,
    )
```

profile of v0, /device:TPU:1, one launch (start us, length us, event | category | flops | bytes accessed | tf_op | source)
XLA Modules:
  0.0 1329.7 jit_solution(4466956774392505986)
XLA Ops:
  10.9 10.0 all-gather.5
  52.2 11.2 all-gather.2
  63.5 13.1 all_gather.49
  78.9 48.9 %all-gather.12.cloned.1.call-done = bf16[1024,3072]{1,0:T(8,128)(2,1)} async-done(((bf16[256,3072]{1,0:T(8,128)(2,1)}), bf16[1024,3072]{1,0:T(8,128)(2,1)}) %all-gather.12.cloned.1.call-update) | async-done | bytes 6291472 | tf_op jit(solution)/shard_map/all_gather | solution.py:60
  127.8 9.7 fusion.78
  155.8 131.8 %while.26 = (s32[]{:T(128)}, bf16[4,1,1104,4,64]{2,4,3,1,0:T(8,128)(2,1)}, f32[4,1,4,1104]{3,2,1,0:T(4,128)}, bf16[4,1,1104,4,64]{2,4,3,1,0:T(8,128)(2,1)}, bf16...) while((s32[]{:T(128)}, bf16[4,1,1104,4,64]{2,4,3,1,0:T(8,128)(2,1)}, ...), condition=%wide.region_5.6_spmd, body=%wide.region_2.5_spmd.sunk | while | flops 1282190080 | bytes 62444376 | solution.py:130
  156.2 10.7 fusion.129
  176.5 12.7 fusion.131
  189.8 10.7 fusion.129
  200.6 9.7 fusion.130
  210.2 11.6 fusion.131
  222.4 10.7 fusion.129
  233.1 9.7 fusion.130
  242.8 11.5 fusion.131
  255.0 10.7 fusion.129
  275.3 11.5 fusion.131
  297.9 25.6 %all-gather.16.cloned.1.call-done = bf16[1024,4096]{1,0:T(8,128)(2,1)} async-done(((bf16[256,4096]{1,0:T(8,128)(2,1)}), bf16[1024,4096]{1,0:T(8,128)(2,1)}) %all-gather.16.cloned.1.call-update) | async-done | bytes 8388624 | tf_op jit(solution)/shard_map/all_gather | solution.py:66
  323.5 54.4 %multiply_convert_fusion.1 = (bf16[1104,4096]{1,0:T(8,128)(2,1)}, f32[1104,4096]{1,0:T(8,128)}, f32[1104,4096]{1,0:T(8,128)}) fusion(f32[4096]{0:T(1024)S(1)} %copy-done.39, bf16[1024,4096]{1,0:T(8,128)(2,1)} %all-gather.16.cloned.1.call-done, f32[1104,1024]{1,0:T(8,128)} %copy-done.8, f32[1024]{0:T(1024)S(1)} %bitcast.254, f32[1024]{0:T(1024)S(1)} %bitcast.248, ...), kind=kOutput, calls=%fused_computation.56 | convolution fusion | flops 9565126656 | bytes 58163840 | tf_op jit(solution)/shard_map/dot_general | solution.py:25
  377.9 94.9 %all-gather.18.cloned.1.call-done = bf16[4096,1024]{1,0:T(8,128)(2,1)} async-done(((bf16[1024,1024]{1,0:T(8,128)(2,1)}), bf16[4096,1024]{1,0:T(8,128)(2,1)}) %all-gather.18.cloned.1.call-update) | async-done | bytes 8388624 | tf_op jit(solution)/shard_map/all_gather | solution.py:68
  472.8 25.3 %fusion.92 = (bf16[4096]{0:T(1024)(128)(2,1)}, bf16[1104,4096]{1,0:T(8,128)(2,1)}) fusion(f32[1104,4096]{1,0:T(8,128)} %get-tuple-element.193, f32[1104,4096]{1,0:T(8,128)} %get-tuple-element.206, bf16[4096,1024]{1,0:T(8,128)(2,1)} %all-gather.18.cloned.1.call-done, bf16[1,1,1104,1024]{3,2,1,0:T(8,128)(2,1)S(1)} %copy-done.6, f32[]{:T(128)} %bitcast.22), kind=kOutput, calls=%fused_computation.137 | convolution fusion | flops 9332240384 | bytes 55877636 | tf_op jit(solution)/shard_map/dot_general | solution.py:35
  498.1 18.1 %multiply_reduce_fusion.1 = (bf16[1024]{0:T(1024)(128)(2,1)}, f32[1104]{0:T(1024)S(1)}, bf16[1024]{0:T(1024)(128)(2,1)}, f32[1104,1024]{1,0:T(8,128)S(1)}) fusion(f32[1104,1024]{1,0:T(8,128)} %copy-done.8, f32[1104]{0:T(1024)S(1)} %fusion.76, f32[1104]{0:T(1024)S(1)} %broadcast_multiply_fusion, f32[1024]{0:T(1024)S(1)} %bitcast.249, ...), kind=kOutput, calls=%fused_computation.102 | convolution fusion | flops 9270064128 | bytes 26497984 | tf_op jit(solution)/shard_map/dot_general | solution.py:35
  538.3 243.8 %while.27 = (s32[]{:T(128)}, bf16[4,1,1104,4,64]{2,4,3,1,0:T(8,128)(2,1)}, bf16[4,1,1104,4,64]{2,4,3,1,0:T(8,128)(2,1)}, bf16[4,1,1104,4,64]{2,4,3,1,0:T(8,128)(...) while((s32[]{:T(128)}, ...), condition=%wide.region_12.13_spmd, body=%wide.region_10.12_spmd.sunk | while | flops 3159731968 | bytes 219023680 | solution.py:205
  539.1 11.1 fusion.140
  550.2 10.1 fusion.143
  560.2 17.6 %multiply_reduce_fusion.5 = (f32[4,1104]{1,0:T(4,128)S(1)}, f32[4,1104,1104]{1,2,0:T(8,128)}) fusion(f32[4,1104,1104]{1,2,0:T(8,128)} %fusion.140, bf16[4,1,1104,4,64]{2,4,3,1,0:T(8,128)(2,1)} %get-tuple-element.360, s32[]{:T(128)S(6)} %copy.89, bf16[4,1,1104,4,64]{2,4,3,1,0:T(8,128)(2,1)S(1)} %copy-done.5), kind=kOutput, calls=%fused_computation.20.clone.1 | convolution fusion | flops 633779904 | bytes 41048320 | tf_op jit(solution)/shard_map/while/body/eval_jaxpr/cqhd,ckhd->chqk/dot_general | solution.py:185
  577.9 13.5 %multiply_convert_fusion.3 = bf16[4,1104,1104]{1,2,0:T(8,128)(2,1)S(1)} fusion(f32[4,1104,1104]{1,2,0:T(8,128)} %fusion.140, f32[4,1104,1104]{1,2,0:T(8,128)} %get-tuple-element.309, f32[4,1104]{1,0:T(4,128)S(1)} %get-tuple-element.310), kind=kLoop, calls=%fused_computation.19.clone.1 | loop fusion | flops 14625792 | bytes 48770304 | tf_op jit(solution)/shard_map/while/body/eval_jaxpr/convert_element_type | solution.py:189
  600.1 11.0 fusion.140
  611.2 10.0 fusion.143
  621.2 17.5 %multiply_reduce_fusion.5 = (f32[4,1104]{1,0:T(4,128)S(1)}, f32[4,1104,1104]{1,2,0:T(8,128)}) fusion(f32[4,1104,1104]{1,2,0:T(8,128)} %fusion.140, bf16[4,1,1104,4,64]{2,4,3,1,0:T(8,128)(2,1)} %get-tuple-element.360, s32[]{:T(128)S(6)} %copy.89, bf16[4,1,1104,4,64]{2,4,3,1,0:T(8,128)(2,1)S(1)} %copy-done.5), kind=kOutput, calls=%fused_computation.20.clone.1 | convolution fusion | flops 633779904 | bytes 41048320 | tf_op jit(solution)/shard_map/while/body/eval_jaxpr/cqhd,ckhd->chqk/dot_general | solution.py:185
  638.7 13.5 %multiply_convert_fusion.3 = bf16[4,1104,1104]{1,2,0:T(8,128)(2,1)S(1)} fusion(f32[4,1104,1104]{1,2,0:T(8,128)} %fusion.140, f32[4,1104,1104]{1,2,0:T(8,128)} %get-tuple-element.309, f32[4,1104]{1,0:T(4,128)S(1)} %get-tuple-element.310), kind=kLoop, calls=%fused_computation.19.clone.1 | loop fusion | flops 14625792 | bytes 48770304 | tf_op jit(solution)/shard_map/while/body/eval_jaxpr/convert_element_type | solution.py:189
  661.0 11.0 fusion.140
  672.0 10.0 fusion.143
  682.0 17.5 %multiply_reduce_fusion.5 = (f32[4,1104]{1,0:T(4,128)S(1)}, f32[4,1104,1104]{1,2,0:T(8,128)}) fusion(f32[4,1104,1104]{1,2,0:T(8,128)} %fusion.140, bf16[4,1,1104,4,64]{2,4,3,1,0:T(8,128)(2,1)} %get-tuple-element.360, s32[]{:T(128)S(6)} %copy.89, bf16[4,1,1104,4,64]{2,4,3,1,0:T(8,128)(2,1)S(1)} %copy-done.5), kind=kOutput, calls=%fused_computation.20.clone.1 | convolution fusion | flops 633779904 | bytes 41048320 | tf_op jit(solution)/shard_map/while/body/eval_jaxpr/cqhd,ckhd->chqk/dot_general | solution.py:185
  699.5 13.5 %multiply_convert_fusion.3 = bf16[4,1104,1104]{1,2,0:T(8,128)(2,1)S(1)} fusion(f32[4,1104,1104]{1,2,0:T(8,128)} %fusion.140, f32[4,1104,1104]{1,2,0:T(8,128)} %get-tuple-element.309, f32[4,1104]{1,0:T(4,128)S(1)} %get-tuple-element.310), kind=kLoop, calls=%fused_computation.19.clone.1 | loop fusion | flops 14625792 | bytes 48770304 | tf_op jit(solution)/shard_map/while/body/eval_jaxpr/convert_element_type | solution.py:189
  721.8 11.0 fusion.140
  732.9 10.0 fusion.143
  742.8 17.5 %multiply_reduce_fusion.5 = (f32[4,1104]{1,0:T(4,128)S(1)}, f32[4,1104,1104]{1,2,0:T(8,128)}) fusion(f32[4,1104,1104]{1,2,0:T(8,128)} %fusion.140, bf16[4,1,1104,4,64]{2,4,3,1,0:T(8,128)(2,1)} %get-tuple-element.360, s32[]{:T(128)S(6)} %copy.89, bf16[4,1,1104,4,64]{2,4,3,1,0:T(8,128)(2,1)S(1)} %copy-done.5), kind=kOutput, calls=%fused_computation.20.clone.1 | convolution fusion | flops 633779904 | bytes 41048320 | tf_op jit(solution)/shard_map/while/body/eval_jaxpr/cqhd,ckhd->chqk/dot_general | solution.py:185
  760.4 13.5 %multiply_convert_fusion.3 = bf16[4,1104,1104]{1,2,0:T(8,128)(2,1)S(1)} fusion(f32[4,1104,1104]{1,2,0:T(8,128)} %fusion.140, f32[4,1104,1104]{1,2,0:T(8,128)} %get-tuple-element.309, f32[4,1104]{1,0:T(4,128)S(1)} %get-tuple-element.310), kind=kLoop, calls=%fused_computation.19.clone.1 | loop fusion | flops 14625792 | bytes 48770304 | tf_op jit(solution)/shard_map/while/body/eval_jaxpr/convert_element_type | solution.py:189
  782.2 15.3 %convolution_convert_fusion.2 = bf16[1024,3072]{1,0:T(8,128)(2,1)} fusion(bf16[1,1,1104,1024]{3,2,1,0:T(8,128)(2,1)} %param.19, f32[1024]{0:T(1024)S(1)} %bitcast.257, f32[1024]{0:T(1024)S(1)} %bitcast.244, f32[1104]{0:T(1024)S(1)} %copy-done.24, f32[1104]{0:T(1024)S(1)} %copy-done.22, bf16[1104,1024]{0,1:T(8,128)(2,1)} %bitcast.232, ...), kind=kOutput, calls=%fused_computation.75 | convolution fusion | flops 6976045056 | bytes 15352448 | tf_op jit(solution)/shard_map/dot_general | solution.py:29
  798.2 18.4 %convolution_convert_fusion.1 = bf16[1024,4096]{1,0:T(8,128)(2,1)} fusion(bf16[1104,4096]{1,0:T(8,128)(2,1)} %get-tuple-element.210, f32[1104,1024]{1,0:T(8,128)} %copy-done.8, f32[1024]{0:T(1024)S(1)} %bitcast.255, f32[1024]{0:T(1024)S(1)} %bitcast.251, f32[1104]{0:T(1024)S(1)} %copy-done.36, f32[1104]{0:T(1024)S(1)} %copy-done.26), kind=kOutput, calls=%fused_computation.71 | convolution fusion | flops 9270870016 | bytes 21971584 | tf_op jit(solution)/shard_map/dot_general | solution.py:29
  818.1 17.4 %convolution_convert_fusion = bf16[4096,1024]{1,0:T(8,128)(2,1)} fusion(bf16[1104,4096]{1,0:T(8,128)(2,1)} %get-tuple-element.192, bf16[1,1,1104,1024]{3,2,1,0:T(8,128)(2,1)S(1)} %copy-done.7, f32[]{:T(128)} %bitcast.22), kind=kOutput, calls=%fused_computation.70 | convolution fusion | flops 9268609024 | bytes 19693572 | tf_op jit(solution)/shard_map/dot_general | solution.py:29
  852.4 12.8 fusion.83
  869.9 21.4 %all-reduce.10 = (bf16[1024]{0:T(1024)(128)(2,1)S(1)}, bf16[1024]{0:T(1024)(128)(2,1)S(1)}, bf16[2048]{0:T(1024)(128)(2,1)S(1)}, bf16[1024]{0:T(1024)(128)(2,1)S...) all-reduce(bf16[1024]{0:T(1024)(128)(2,1)S(1)} %get-tuple-element.1, ...), channel_id=2, replica_groups=mesh['rep'=8,'shard'=4] {'shard'}, use_global_device_ids=true, to_apply=%region_16.17.clone | all-reduce | flops 12288 | bytes 49152
  891.9 14.6 %all-reduce.8 = (bf16[256]{0:T(256)(128)(2,1)S(1)}, bf16[256]{0:T(256)(128)(2,1)S(1)}, bf16[512]{0:T(512)(128)(2,1)S(1)}, bf16[256]{0:T(256)(128)(2,1)S(1)}, bf1...) all-reduce(bf16[256]{0:T(256)(128)(2,1)S(1)} %dynamic-slice.1, ...), channel_id=1, replica_groups=mesh['rep'=8,'shard'=4] {'rep'}, use_global_device_ids=true, to_apply=%region_17.18 | all-reduce | flops 3072 | bytes 12288 | tf_op jit(solution)/shard_map/psum | solution.py:257
  911.1 143.7 %reduce-scatter.9.cloned.1.call-done = bf16[256,4096]{1,0:T(8,128)(2,1)} async-done(((bf16[1024,4096]{1,0:T(8,128)(2,1)}), bf16[256,4096]{1,0:T(8,128)(2,1)}) %reduce-scatter.9.cloned.1.call-update) | async-done | bytes 2097168 | tf_op jit(solution)/shard_map/reduce_scatter | solution.py:242
  1054.8 147.7 %reduce-scatter.11.cloned.1.call-done = bf16[1024,1024]{1,0:T(8,128)(2,1)} async-done(((bf16[4096,1024]{1,0:T(8,128)(2,1)}), bf16[1024,1024]{1,0:T(8,128)(2,1)}) %reduce-scatter.11.cloned.1.call-update) | async-done | bytes 2097168 | tf_op jit(solution)/shard_map/reduce_scatter | solution.py:248
  1209.3 17.2 %fusion.72 = bf16[1,1,1104,1024]{3,2,1,0:T(8,128)(2,1)} fusion(f32[1104,1024]{1,0:T(8,128)} %copy-done.8, bf16[1104,4096]{1,0:T(8,128)(2,1)} %get-tuple-element.192, bf16[4096,1024]{1,0:T(8,128)(2,1)} %all-gather.18.cloned.1.call-done, f32[1024]{0:T(1024)S(1)} %bitcast.258, f32[]{:T(128)} %bitcast.22), kind=kOutput, calls=%fused_computation.111 | convolution fusion | flops 9265545216 | bytes 24219652 | tf_op jit(solution)/shard_map/dot_general | solution.py:25
  1226.5 85.6 %all-reduce.13.cloned.1.call-done = (bf16[256,3072]{1,0:T(8,128)(2,1)}, bf16[256,1024]{1,0:T(8,128)(2,1)}, bf16[256,4096]{1,0:T(8,128)(2,1)}, bf16[1024,1024]{1,0:T(8,128)(2,1)}) async-done(((bf16[256,3072]{1,0:T(8,128)(2,1)}, bf16[256,1024]{1,0:T(8,128)(2,1)}, bf16[256,4096]{1,0:T(8,128)(2,1)}, bf16[1024,1024]{1,0:T(8,128)(2,1)}), (bf16[256,3072]{1,0:T(8,128)(2,1)}, bf16[256,1024]{1,0:T(8,128)(2,1)}, ...) | async-done | bytes 6291472 | tf_op jit(solution)/shard_map/psum | solution.py:259
  (271 shorter events, 187.9 us)
Async XLA Ops:
  7.2 56.2 %copy-start.47 = (bf16[1024]{0:T(1024)(128)(2,1)S(1)}, bf16[1024]{0:T(1024)(128)(2,1)}, u32[]{:S(2)}) copy-start(bf16[1024]{0:T(1024)(128)(2,1)} %param.30) | copy-start | bytes 6148
  7.3 69.9 %copy-start.3 = (bf16[1,1,1104,1024]{3,2,1,0:T(8,128)(2,1)S(1)}, bf16[1,1,1104,1024]{3,2,1,0:T(8,128)(2,1)}, u32[]{:S(2)}) copy-start(bf16[1,1,1104,1024]{3,2,1,0:T(8,128)(2,1)} %param.19) | copy-start | bytes 6782980
  7.3 120.5 %all-gather.12.cloned.1.call-start = ((), (), s32[]{:S(2)}) async-start(), calls=%async_computation.4 | async-start | bytes 7864320 | tf_op jit(solution)/shard_map/all_gather | solution.py:60
  8.0 279.7 %all-gather.14.cloned.1.call-start = ((), (), s32[]{:S(2)}) async-start(), calls=%async_computation.5 | async-start | bytes 2621440 | tf_op jit(solution)/shard_map/all_gather | solution.py:62
  8.7 314.7 %all-gather.16.cloned.1.call-start = ((), (), s32[]{:S(2)}) async-start(), calls=%async_computation.6 | async-start | bytes 10485760 | tf_op jit(solution)/shard_map/all_gather | solution.py:66
  9.5 463.3 %all-gather.18.cloned.1.call-start = ((), (), s32[]{:S(2)}) async-start(), calls=%async_computation.7 | async-start | bytes 10485760 | tf_op jit(solution)/shard_map/all_gather | solution.py:68
  10.1 901.0 %reduce-scatter.7.cloned.1.call-start = ((), (), s32[]{:S(2)}) async-start(), calls=%async_computation.9 | async-start | bytes 2621440 | tf_op jit(solution)/shard_map/reduce_scatter | solution.py:230
  43.7 93.7 %copy-start.44 = (f32[4,1,256]{2,1,0:T(1,128)}, f32[4,1,256]{2,1,0:T(1,128)S(1)}, u32[]{:S(2)}) copy-start(f32[4,1,256]{2,1,0:T(1,128)S(1)} %convert_element_type.230) | copy-start | bytes 12292
  52.2 85.2 %copy-start.33 = (f32[4,1,256]{2,1,0:T(1,128)}, f32[4,1,256]{2,1,0:T(1,128)S(1)}, u32[]{:S(2)}) copy-start(f32[4,1,256]{2,1,0:T(1,128)S(1)} %convert_element_type.229) | copy-start | bytes 12292
  77.5 59.9 %copy-start.21 = (f32[1104]{0:T(1024)}, f32[1104]{0:T(1024)S(1)}, u32[]{:S(2)}) copy-start(f32[1104]{0:T(1024)S(1)} %broadcast_multiply_fusion.1) | copy-start | bytes 13252
  78.9 58.6 %copy-start.23 = (f32[1104]{0:T(1024)}, f32[1104]{0:T(1024)S(1)}, u32[]{:S(2)}) copy-start(f32[1104]{0:T(1024)S(1)} %fusion.75) | copy-start | bytes 13252
  155.8 131.9 %copy-start.46 = (f32[4,1,256]{2,1,0:T(1,128)S(1)}, f32[4,1,256]{2,1,0:T(1,128)}, u32[]{:S(2)}) copy-start(f32[4,1,256]{2,1,0:T(1,128)} %convert_element_type.232) | copy-start | bytes 12292
  287.6 6.9 copy-start
  294.5 28.9 %copy-start.37 = (f32[4,1,256]{2,1,0:T(1,128)S(1)}, f32[4,1,256]{2,1,0:T(1,128)}, u32[]{:S(2)}) copy-start(f32[4,1,256]{2,1,0:T(1,128)} %convert_element_type.233) | copy-start | bytes 12292
  294.5 28.9 %copy-start.39 = (f32[4096]{0:T(1024)S(1)}, f32[4096]{0:T(1024)}, u32[]{:S(2)}) copy-start(f32[4096]{0:T(1024)} %convert_element_type.198) | copy-start | bytes 49156
  294.6 28.9 %copy-start.42 = (f32[4,1,256]{2,1,0:T(1,128)S(1)}, f32[4,1,256]{2,1,0:T(1,128)}, u32[]{:S(2)}) copy-start(f32[4,1,256]{2,1,0:T(1,128)} %convert_element_type.234) | copy-start | bytes 12292
  294.6 221.7 %copy-start.25 = (f32[1104]{0:T(1024)}, f32[1104]{0:T(1024)S(1)}, u32[]{:S(2)}) copy-start(f32[1104]{0:T(1024)S(1)} %broadcast_multiply_fusion) | copy-start | bytes 13252
  297.9 218.4 %copy-start.35 = (f32[1104]{0:T(1024)}, f32[1104]{0:T(1024)S(1)}, u32[]{:S(2)}) copy-start(f32[1104]{0:T(1024)S(1)} %fusion.76) | copy-start | bytes 13252
  323.5 149.3 %copy-start.6 = (bf16[1,1,1104,1024]{3,2,1,0:T(8,128)(2,1)S(1)}, bf16[1,1,1104,1024]{3,2,1,0:T(8,128)(2,1)}, u32[]{:S(2)}) copy-start(bf16[1,1,1104,1024]{3,2,1,0:T(8,128)(2,1)} %param.33) | copy-start | bytes 6782980
  498.1 18.1 %copy-start.30 = (f32[1104]{0:T(1024)S(1)}, f32[1104]{0:T(1024)}, u32[]{:S(2)}) copy-start(f32[1104]{0:T(1024)} %copy-done.29) | copy-start | bytes 13252
  498.1 18.2 %copy-start.9 = (f32[1104,1024]{1,0:T(8,128)S(1)}, f32[1104,1024]{1,0:T(8,128)}, u32[]{:S(2)}) copy-start(f32[1104,1024]{1,0:T(8,128)} %copy-done.8) | copy-start | bytes 13565956
  525.6 385.6 %reduce-scatter.5.cloned.1.call-start = ((), (), s32[]{:S(2)}) async-start(), calls=%async_computation.8 | async-start | bytes 7864320 | tf_op jit(solution)/shard_map/reduce_scatter | solution.py:224
  538.3 243.8 %copy-start.22 = (f32[1104]{0:T(1024)S(1)}, f32[1104]{0:T(1024)}, u32[]{:S(2)}) copy-start(f32[1104]{0:T(1024)} %copy-done.21) | copy-start | bytes 13252
  538.3 243.8 %copy-start.24 = (f32[1104]{0:T(1024)S(1)}, f32[1104]{0:T(1024)}, u32[]{:S(2)}) copy-start(f32[1104]{0:T(1024)} %copy-done.23) | copy-start | bytes 13252
  538.3 243.8 %copy-start.34 = (f32[4,1,256]{2,1,0:T(1,128)S(1)}, f32[4,1,256]{2,1,0:T(1,128)}, u32[]{:S(2)}) copy-start(f32[4,1,256]{2,1,0:T(1,128)} %copy-done.33) | copy-start | bytes 12292
  538.3 243.8 %copy-start.45 = (f32[4,1,256]{2,1,0:T(1,128)S(1)}, f32[4,1,256]{2,1,0:T(1,128)}, u32[]{:S(2)}) copy-start(f32[4,1,256]{2,1,0:T(1,128)} %copy-done.44) | copy-start | bytes 12292
  539.1 11.1 copy-start.5
  539.1 11.1 copy-start.11
  560.2 17.6 %copy-start.12 = (bf16[4,1,1104,4,64]{2,4,3,1,0:T(8,128)(2,1)}, bf16[4,1,1104,4,64]{2,4,3,1,0:T(8,128)(2,1)S(1)}, u32[]{:S(2)}) copy-start(bf16[4,1,1104,4,64]{2,4,3,1,0:T(8,128)(2,1)S(1)} %fusion.143) | copy-start | bytes 6782980 | tf_op jit(solution)/shard_map/while
  577.9 13.6 %copy-start.13 = (bf16[4,1,1104,4,64]{2,4,3,1,0:T(8,128)(2,1)S(1)}, bf16[4,1,1104,4,64]{2,4,3,1,0:T(8,128)(2,1)}, u32[]{:S(2)}) copy-start(bf16[4,1,1104,4,64]{2,4,3,1,0:T(8,128)(2,1)} %get-tuple-element.344) | copy-start | bytes 6782980 | tf_op jit(solution)/shard_map/while
  600.1 11.0 copy-start.5
  600.1 11.0 copy-start.11
  621.2 17.6 %copy-start.12 = (bf16[4,1,1104,4,64]{2,4,3,1,0:T(8,128)(2,1)}, bf16[4,1,1104,4,64]{2,4,3,1,0:T(8,128)(2,1)S(1)}, u32[]{:S(2)}) copy-start(bf16[4,1,1104,4,64]{2,4,3,1,0:T(8,128)(2,1)S(1)} %fusion.143) | copy-start | bytes 6782980 | tf_op jit(solution)/shard_map/while
  638.7 13.6 %copy-start.13 = (bf16[4,1,1104,4,64]{2,4,3,1,0:T(8,128)(2,1)S(1)}, bf16[4,1,1104,4,64]{2,4,3,1,0:T(8,128)(2,1)}, u32[]{:S(2)}) copy-start(bf16[4,1,1104,4,64]{2,4,3,1,0:T(8,128)(2,1)} %get-tuple-element.344) | copy-start | bytes 6782980 | tf_op jit(solution)/shard_map/while
  661.0 11.0 copy-start.5
  661.0 11.0 copy-start.11
  682.0 17.6 %copy-start.12 = (bf16[4,1,1104,4,64]{2,4,3,1,0:T(8,128)(2,1)}, bf16[4,1,1104,4,64]{2,4,3,1,0:T(8,128)(2,1)S(1)}, u32[]{:S(2)}) copy-start(bf16[4,1,1104,4,64]{2,4,3,1,0:T(8,128)(2,1)S(1)} %fusion.143) | copy-start | bytes 6782980 | tf_op jit(solution)/shard_map/while
  699.5 13.6 %copy-start.13 = (bf16[4,1,1104,4,64]{2,4,3,1,0:T(8,128)(2,1)S(1)}, bf16[4,1,1104,4,64]{2,4,3,1,0:T(8,128)(2,1)}, u32[]{:S(2)}) copy-start(bf16[4,1,1104,4,64]{2,4,3,1,0:T(8,128)(2,1)} %get-tuple-element.344) | copy-start | bytes 6782980 | tf_op jit(solution)/shard_map/while
  721.8 11.0 copy-start.5
  721.8 11.0 copy-start.11
  742.8 17.6 %copy-start.12 = (bf16[4,1,1104,4,64]{2,4,3,1,0:T(8,128)(2,1)}, bf16[4,1,1104,4,64]{2,4,3,1,0:T(8,128)(2,1)S(1)}, u32[]{:S(2)}) copy-start(bf16[4,1,1104,4,64]{2,4,3,1,0:T(8,128)(2,1)S(1)} %fusion.143) | copy-start | bytes 6782980 | tf_op jit(solution)/shard_map/while
  760.4 13.6 %copy-start.13 = (bf16[4,1,1104,4,64]{2,4,3,1,0:T(8,128)(2,1)S(1)}, bf16[4,1,1104,4,64]{2,4,3,1,0:T(8,128)(2,1)}, u32[]{:S(2)}) copy-start(bf16[4,1,1104,4,64]{2,4,3,1,0:T(8,128)(2,1)} %get-tuple-element.344) | copy-start | bytes 6782980 | tf_op jit(solution)/shard_map/while
  797.5 257.3 %reduce-scatter.9.cloned.1.call-start = ((), (), s32[]{:S(2)}) async-start(), calls=%async_computation.10 | async-start | bytes 10485760 | tf_op jit(solution)/shard_map/reduce_scatter | solution.py:242
  816.5 386.0 %reduce-scatter.11.cloned.1.call-start = ((), (), s32[]{:S(2)}) async-start(), calls=%async_computation.11 | async-start | bytes 10485760 | tf_op jit(solution)/shard_map/reduce_scatter | solution.py:248
  835.6 476.6 %all-reduce.13.cloned.1.call-start = ((), (), s32[]{:S(2)}) async-start(), calls=%async_computation.12 | async-start | bytes 12582912 | tf_op jit(solution)/shard_map/psum | solution.py:259
  845.4 7.0 copy-start.4
  852.4 12.9 copy-start.28
  869.9 332.6 %copy-start.32 = (f32[1104]{0:T(1024)S(1)}, f32[1104]{0:T(1024)}, u32[]{:S(2)}) copy-start(f32[1104]{0:T(1024)} %copy-done.31) | copy-start | bytes 13252
  (40 other events, 113.0 us)
Sparse Core Ops, SparseCore 0:
  9.7 118.0 all-gather.11
  129.3 43.9 all-gather.13
  174.9 148.5 all-gather.15
  324.9 147.8 all-gather.17
  525.7 41.7 reduce-scatter.6
  797.6 109.9 reduce-scatter.4
  910.0 144.7 reduce-scatter.8
  1057.3 145.1 reduce-scatter.10
  1206.5 105.5 all-reduce.12
where the time goes:
time: 1340 us; the launch traced here: 1330 us
  waiting for transfers between devices  549 us (41%)
  matrix products  475 us (35%)
  other arithmetic  137 us (10%)
  blocking collectives  107 us (8%)
  local copies, waits for them, and re-layouts  42.8 us (3%)
  between operations  17.3 us (1%)
    reduce_scatter x1, waiting for transfers between devices, body(): lax.psum_scatter(grad_wdown.astype(jnp.bfloat16), 'shard', scatter_dimens...  148 us
    reduce_scatter x1, waiting for transfers between devices, body(): lax.psum_scatter(grad_wup.astype(jnp.bfloat16), 'shard', scatter_dimensio...  144 us
    all_gather x1, waiting for transfers between devices, body(): lax.all_gather(w_down, 'shard', axis=0, tiled=True)  94.9 us
    dot_general x4, matrix products, matmul(): return jnp.dot(left, right, preferred_element_type=jnp.float32)  88.1 us
    psum x1, waiting for transfers between devices, body(): lax.psum(o_qkv.astype(jnp.bfloat16), 'rep').astype(jnp.float32)  85.6 us
    dot_general x4, matrix products, backward_group(): jnp.einsum('cqhd,ckhd->chqk', grad_part, value_part, preferred_element_ty...  70.2 us
    dot_general x4, matrix products, right_trans(): lax.dot_general(left, right, (((1,), (1,)), ((), ())), preferred_element_...  61 us
    dot_general x4, matrix products, left_trans(): lax.dot_general(left, right, (((0,), (0,)), ((), ())), preferred_element_...  55.2 us
  transfers between devices with their start and end apart: 9, of which 6 were waited for; matrix products, arithmetic and copies ran while one was open for 43% of the time, Pallas kernels for 0%

commit v1 on v0

v1 whole, which is shorter than its diff:
```python
import functools

import jax
import jax.numpy as jnp
from jax import lax
from jax.experimental import pallas as pl
from jax.experimental.pallas import tpu as pltpu
from jax.sharding import PartitionSpec as P

HEADS = 16
HDIM = 64

eps = 1e-06
head_block = 4
bf16 = jnp.bfloat16
f32 = jnp.float32


def layer_norm(values, gain, shift):
    centre = values - jnp.mean(values, -1, keepdims=True)
    spread = jnp.mean(centre * centre, -1, keepdims=True)
    return centre * lax.rsqrt(spread + eps) * gain + shift


def gelu_exact(values):
    return jax.nn.gelu(values, approximate=False)


def matmul(left, right):
    return jnp.dot(left, right, preferred_element_type=f32)


def left_trans(left, right):
    return lax.dot_general(left, right, (((0,), (0,)), ((), ())), preferred_element_type=f32)


def right_trans(left, right):
    return lax.dot_general(left, right, (((1,), (1,)), ((), ())), preferred_element_type=f32)


class Links:
    def __init__(self, mesh):
        self.ns = mesh.shape["shard"]
        self.nr = mesh.shape["rep"]
        self.nq = self.nr // 2

    def here(self):
        rep = lax.axis_index("rep")
        return lax.axis_index("shard"), rep // 2, rep % 2

    def along(self, values, step):
        return lax.ppermute(values, "shard", [(i, (i + step) % self.ns) for i in range(self.ns)])

    def chip(self, values, k):
        return lax.ppermute(values, "rep", [(i, i ^ (2 * k)) for i in range(self.nr)])

    def core(self, values):
        return lax.ppermute(values, "rep", [(i, i ^ 1) for i in range(self.nr)])


def piece_of(links, weight):
    rows, cols = weight.shape
    _, q, c = links.here()
    rq, half = rows // links.nq, cols // 2
    return lax.dynamic_slice(weight, (q * rq, c * half), (rq, half))


def assemble(links, weights, own, crossed, mate):
    ns, nq = links.ns, links.nq
    rows = [w.shape[0] for w in weights]
    cols = [w.shape[1] for w in weights]
    rq = [r // nq for r in rows]

    def kernel(*refs):
        n = len(weights)
        w_refs = refs[:n]
        part_refs = refs[n : n + nq]
        mate_ref = refs[n + nq]
        out_refs = refs[n + nq + 1 : n + nq + 1 + n]
        sem = refs[-1]
        z = lax.axis_index("shard")
        rep = lax.axis_index("rep")
        q, c = rep // 2, rep % 2
        copies = []

        def go(src, dst):
            copy = pltpu.make_async_copy(src, dst, sem.at[len(copies)])
            copy.start()
            copies.append(copy)

        base = 0
        for i in range(n):
            half = cols[i] // 2
            go(w_refs[i], out_refs[i].at[pl.ds(pl.multiple_of(z * rows[i], rows[i]), rows[i]), :])
            mine = pl.ds(pl.multiple_of(c * half, half), half)
            other = pl.ds(pl.multiple_of((1 - c) * half, half), half)
            for s in range(1, ns):
                zs = lax.rem(z + (ns - s), ns)
                for k in range(nq):
                    at = pl.ds(pl.multiple_of(zs * rows[i] + (q ^ k) * rq[i], rq[i]), rq[i])
                    lanes = pl.ds(base, half)
                    go(part_refs[k].at[s - 1, :, lanes], out_refs[i].at[at, mine])
                    go(mate_ref.at[k, s - 1, :, lanes], out_refs[i].at[at, other])
            base += half
        for copy in copies:
            copy.wait()

    count = len(weights) * (1 + 2 * (ns - 1) * nq)
    anywhere = pl.BlockSpec(memory_space=pl.ANY)
    return pl.pallas_call(
        kernel,
        out_shape=[jax.ShapeDtypeStruct((ns * r, n), bf16) for r, n in zip(rows, cols)],
        in_specs=[anywhere] * (len(weights) + nq + 1),
        out_specs=[anywhere] * len(weights),
        scratch_shapes=[pltpu.SemaphoreType.DMA((count,))],
        name="assemble",
    )(*weights, own, *crossed, mate)


def gather(links, weights, extra=None):
    piece = jnp.concatenate([piece_of(links, w) for w in weights], 1)
    n = piece.shape[0]
    sent = piece if extra is None else jnp.concatenate([piece, extra], 0)
    got = [links.along(sent, s) for s in range(1, links.ns)]
    own = jnp.stack([g[:n] for g in got])
    crossed = [links.chip(own, k) for k in range(1, links.nq)]
    mate = links.core(jnp.stack([own] + crossed))
    full = assemble(links, weights, own, crossed, mate)
    if extra is None:
        return full
    return full, [g[n:] for g in got]


def scatter(links, sent, kept):
    ns, nq = links.ns, links.nq
    z, q, c = links.here()
    got = [links.core(s) for s in sent]
    rq = sent[0].shape[0] // (ns * nq)

    def view(values):
        return values.reshape(ns, nq, rq, values.shape[1])

    def part(k):
        pairs = [
            lax.dynamic_index_in_dim(view(a), q ^ k, 1, False).astype(f32)
            + lax.dynamic_index_in_dim(view(b), q ^ k, 1, False).astype(f32)
            for a, b in zip(kept, got)
        ]
        return jnp.concatenate(pairs, -1) if len(pairs) > 1 else pairs[0]

    crossed = [links.chip(part(k).astype(bf16), k) for k in range(1, nq)]
    total = part(0)
    for x in crossed:
        total = total + x.astype(f32)
    total = total.astype(bf16)
    moved = [
        links.along(lax.dynamic_index_in_dim(total, (z + s) % ns, 0, False), s)
        for s in range(1, ns)
    ]
    final = lax.dynamic_index_in_dim(total, z, 0, False).astype(f32)
    for x in moved:
        final = final + x.astype(f32)
    final = final.astype(bf16)
    mine = jnp.stack([final] + [links.chip(final, k) for k in range(1, nq)])
    mate = links.core(mine)
    first = jnp.where(c == 0, mine, mate)
    second = jnp.where(c == 0, mate, mine)
    outs = []
    base = 0
    for s in sent:
        half = s.shape[1]
        both = jnp.concatenate(
            [first[:, :, base : base + half], second[:, :, base : base + half]], -1
        )
        ordered = [lax.dynamic_index_in_dim(both, q ^ j, 0, False) for j in range(nq)]
        outs.append(jnp.concatenate(ordered).astype(f32))
        base += half
    return outs


def halves(links, left, right):
    _, _, c = links.here()
    half = right.shape[1] // 2
    away = lax.dynamic_slice_in_dim(right, (1 - c) * half, half, 1)
    home = lax.dynamic_slice_in_dim(right, c * half, half, 1)
    return left_trans(left, away).astype(bf16), left_trans(left, home).astype(bf16)


def body(
    links,
    inputs,
    counts,
    ln1_gain,
    ln1_shift,
    w_qkv,
    qv_bias,
    w_out,
    out_bias,
    ln2_gain,
    ln2_shift,
    w_up,
    up_bias,
    w_down,
    down_bias,
    cotangent,
):
    ns = links.ns
    slots = inputs.shape[1]
    seq_len = inputs.shape[2]
    width = inputs.shape[3]
    n_rows = slots * seq_len
    groups = HEADS // head_block
    scale = HDIM ** (-0.5)
    z = lax.axis_index("shard")

    small = (ln1_gain, ln1_shift, qv_bias, out_bias, ln2_gain, ln2_shift, up_bias, down_bias)
    sizes = [v.shape[0] for v in small]
    line = w_qkv.shape[1] // 2
    total_small = sum(sizes)
    n_lines = -(-total_small // line)
    packed = jnp.concatenate(small + (jnp.zeros((n_lines * line - total_small,), bf16),))
    packed = packed.reshape(n_lines, line)
    extra = jnp.concatenate([packed, jnp.zeros((16 - n_lines, line), bf16)])

    (full_qkv,), got_small = gather(links, [w_qkv], extra)
    all_small = jnp.stack([packed] + [g[:n_lines] for g in got_small]).reshape(ns, -1)
    all_small = jnp.concatenate(
        [lax.dynamic_index_in_dim(all_small, (z - j) % ns, 0) for j in range(ns)]
    )
    full_small = []
    base = 0
    for n in sizes:
        full_small.append(all_small[:, base : base + n].reshape(-1).astype(f32))
        base += n
    full_g1, full_s1, bias_f, full_bout, full_g2, full_s2, full_bup, full_bdown = full_small
    full_wout, full_wup = gather(links, [w_out, w_up])
    (full_wdown,) = gather(links, [w_down])

    first_slot = z * slots
    alive = (jnp.arange(slots, dtype=jnp.int32) + first_slot < counts[0]).astype(f32)
    alive_rows = jnp.broadcast_to(alive[:, None], (slots, seq_len)).reshape(n_rows, 1)
    tokens = inputs.reshape(n_rows, width).astype(f32)
    hidden_one, norm_one_back = jax.vjp(layer_norm, tokens, full_g1, full_s1)
    hidden_one_b = hidden_one.astype(bf16)
    projected = matmul(hidden_one_b, full_qkv)
    queries_b = (projected[:, :width] + bias_f[:width]).astype(bf16)
    keys_b = projected[:, width : 2 * width].astype(bf16)
    values_b = (projected[:, 2 * width :] + bias_f[width:]).astype(bf16)

    def arrange(values):
        return values.reshape(slots, seq_len, groups, head_block, HDIM).transpose(2, 0, 1, 3, 4)

    def restore(values):
        return values.transpose(1, 2, 0, 3, 4).reshape(n_rows, width)

    query_groups = arrange(queries_b)
    key_groups = arrange(keys_b)
    value_groups = arrange(values_b)

    def forward_group(operands):
        query_part, key_part, value_part = operands
        scores = (
            jnp.einsum("cqhd,ckhd->chqk", query_part, key_part, preferred_element_type=f32) * scale
        )
        largest = jnp.max(scores, -1, keepdims=True)
        exponent = jnp.exp(scores - largest)
        denominator = jnp.sum(exponent, -1, keepdims=True)
        probs_b = (exponent / denominator).astype(bf16)
        mixed = jnp.einsum("chqk,ckhd->cqhd", probs_b, value_part, preferred_element_type=f32)
        return (mixed, (largest + jnp.log(denominator))[..., 0])

    mixed_groups, log_totals = lax.map(forward_group, (query_groups, key_groups, value_groups))
    attended_b = restore(mixed_groups).astype(bf16)
    middle = tokens + matmul(attended_b, full_wout) + full_bout
    hidden_two, norm_two_back = jax.vjp(layer_norm, middle, full_g2, full_s2)
    hidden_two_b = hidden_two.astype(bf16)
    pre_act = matmul(hidden_two_b, full_wup) + full_bup
    activated, gelu_back = jax.vjp(gelu_exact, pre_act)
    activated_b = activated.astype(bf16)
    d_out = alive_rows * cotangent.reshape(n_rows, width).astype(f32)
    d_out_b = d_out.astype(bf16)
    grad_wdown = halves(links, activated_b, d_out_b)
    (o_wdown,) = scatter(links, [grad_wdown[0]], [grad_wdown[1]])
    result = middle + matmul(activated_b, full_wdown) + full_bdown
    output = (alive_rows * result).astype(bf16).reshape(inputs.shape)
    grad_bdown = jnp.sum(d_out, 0)
    d_act = right_trans(d_out_b, full_wdown)
    d_pre_b = gelu_back(d_act)[0].astype(bf16)
    grad_wup = halves(links, hidden_two_b, d_pre_b)
    grad_bup = jnp.sum(d_pre_b.astype(f32), 0)
    d_hidden_two = right_trans(d_pre_b, full_wup)
    d_mid_norm, grad_g2, grad_s2 = norm_two_back(d_hidden_two)
    d_mid = d_out + d_mid_norm
    d_proj_b = d_mid.astype(bf16)
    grad_wout = halves(links, attended_b, d_proj_b)
    o_wout, o_wup = scatter(links, [grad_wout[0], grad_wup[0]], [grad_wout[1], grad_wup[1]])
    grad_bout = jnp.sum(d_proj_b.astype(f32), 0)
    d_att_b = right_trans(d_proj_b, full_wout).astype(bf16)
    d_att_groups = arrange(d_att_b)

    def backward_group(operands):
        query_part, key_part, value_part, log_total, grad_part = operands
        scores = (
            jnp.einsum("cqhd,ckhd->chqk", query_part, key_part, preferred_element_type=f32) * scale
        )
        attn_probs = jnp.exp(scores - log_total[..., None])
        probs_b = attn_probs.astype(bf16)
        d_probs = jnp.einsum("cqhd,ckhd->chqk", grad_part, value_part, preferred_element_type=f32)
        row_inner = jnp.sum(d_probs * attn_probs, -1, keepdims=True)
        d_scores_b = (attn_probs * (d_probs - row_inner)).astype(bf16)
        d_query = (
            jnp.einsum("chqk,ckhd->cqhd", d_scores_b, key_part, preferred_element_type=f32) * scale
        )
        d_key = (
            jnp.einsum("chqk,cqhd->ckhd", d_scores_b, query_part, preferred_element_type=f32)
            * scale
        )
        d_value = jnp.einsum("chqk,cqhd->ckhd", probs_b, grad_part, preferred_element_type=f32)
        return (d_query, d_key, d_value)

    d_query_groups, d_key_groups, d_value_groups = lax.map(
        backward_group, (query_groups, key_groups, value_groups, log_totals, d_att_groups)
    )
    d_qkv_b = jnp.concatenate(
        [restore(d_query_groups), restore(d_key_groups), restore(d_value_groups)], 1
    ).astype(bf16)
    grad_qkv = halves(links, hidden_one_b, d_qkv_b)
    (o_qkv,) = scatter(links, [grad_qkv[0]], [grad_qkv[1]])
    column_sums = jnp.sum(d_qkv_b.astype(f32), 0)
    grad_qvb = jnp.concatenate([column_sums[:width], column_sums[2 * width :]])
    d_hidden_one = right_trans(d_qkv_b, full_qkv)
    d_in_norm, grad_g1, grad_s1 = norm_one_back(d_hidden_one)
    input_grad = (d_mid + d_in_norm).reshape(inputs.shape)
    small_grads = (grad_g1, grad_s1, grad_qvb, grad_bout, grad_g2, grad_s2, grad_bup, grad_bdown)
    joined = jnp.concatenate([g.reshape(ns, -1) for g in small_grads], 1)
    joined = lax.psum(joined, ("rep", "shard"))
    joined = lax.dynamic_index_in_dim(joined, z, 0, False)
    owned = []
    base = 0
    for n in sizes:
        owned.append(joined[base : base + n])
        base += n
    o_g1, o_s1, o_qvb, o_bout, o_g2, o_s2, o_bup, o_bdown = owned
    return (
        output,
        input_grad,
        o_g1,
        o_s1,
        o_qkv,
        o_qvb,
        o_wout,
        o_bout,
        o_g2,
        o_s2,
        o_wup,
        o_bup,
        o_wdown,
        o_bdown,
    )


def solution(mesh):
    tokens = P("rep", "shard", None, None)
    vector = P("shard")
    matrix = P("shard", None)
    return jax.shard_map(
        functools.partial(body, Links(mesh)),
        mesh=mesh,
        in_specs=(
            tokens,
            P("rep"),
            vector,
            vector,
            matrix,
            vector,
            matrix,
            vector,
            vector,
            vector,
            matrix,
            vector,
            matrix,
            vector,
            tokens,
        ),
        out_specs=(
            tokens,
            tokens,
            vector,
            vector,
            matrix,
            vector,
            matrix,
            vector,
            vector,
            vector,
            matrix,
            vector,
            matrix,
            vector,
        ),
        check_vma=False,
    )
```

time: 1340 us -> 1820 us (1.36)
  Pallas kernels: 0 us -> 767 us
  waiting for transfers between devices: 549 us -> 101 us
  starting transfers between devices: 0.36 us -> 153 us
  other arithmetic: 137 us -> 180 us
  matrix products: 475 us -> 446 us
    pallas_call x0 -> x3, Pallas kernels: none -> 767 us  [assemble(): pl.pallas_call(kernel, out_shape=[jax.ShapeDtypeStruct((ns * r, n), bf16)...]
    reduce_scatter x4 -> x0, waiting for transfers between devices: 291 us -> none  [the longest x1 148 us: body(): lax.psum_scatter(grad_wdown.astype(jnp.bfloat16), 'shard', scatter_dimens...]
    all_gather x4 -> x0, waiting for transfers between devices: 169 us -> none  [the longest x1 94.9 us: body(): lax.all_gather(w_down, 'shard', axis=0, tiled=True)]
    ppermute x0 -> x55, starting transfers between devices: none -> 153 us  [the longest x10 77.7 us: core(): return lax.ppermute(values, 'rep', [(i, i ^ 1) for i in range(self.nr)])]
    ppermute x0 -> x55, waiting for transfers between devices: none -> 101 us  [the longest x27 71.5 us: chip(): return lax.ppermute(values, 'rep', [(i, i ^ 2 * k) for i in range(self.nr)])]
    psum x1, blocking collectives: 14.6 us -> 112 us  [body(): joined = lax.psum(joined, ('rep', 'shard'))]
    psum x1 -> x0, waiting for transfers between devices: 85.6 us -> none  [body(): lax.psum(o_qkv.astype(jnp.bfloat16), 'rep').astype(jnp.float32)]
    all_gather x8 -> x0, blocking collectives: 70.4 us -> none  [the longest x1 13.1 us: body(): lax.all_gather(up_bias, 'shard', axis=0, tiled=True)]
  transfers between devices with their start and end apart: 9 -> 55, of which waited for: 6 -> 14; matrix products, arithmetic and copies ran while one was open for 43% -> 13% of each run, Pallas kernels for 0% -> 25%
where the time goes in v1:
time: 1820 us; the launch traced here: 1810 us
  Pallas kernels  767 us (42%)
  matrix products  446 us (25%)
  other arithmetic  180 us (10%)
  starting transfers between devices  153 us (8%)
  blocking collectives  112 us (6%)
  waiting for transfers between devices  101 us (6%)
  local copies, waits for them, and re-layouts  49.7 us (3%)
    pallas_call x3, Pallas kernels, assemble(): pl.pallas_call(kernel, out_shape=[jax.ShapeDtypeStruct((ns * r, n), bf16)...  767 us
    psum x1, blocking collectives, body(): joined = lax.psum(joined, ('rep', 'shard'))  112 us
    dot_general x4, matrix products, right_trans(): lax.dot_general(left, right, (((1,), (1,)), ((), ())), preferred_element_...  83 us
    ppermute x10, starting transfers between devices, core(): return lax.ppermute(values, 'rep', [(i, i ^ 1) for i in range(self.nr)])  77.7 us
    ppermute x27, waiting for transfers between devices, chip(): return lax.ppermute(values, 'rep', [(i, i ^ 2 * k) for i in range(self.nr)])  71.5 us
    dot_general x4, matrix products, backward_group(): jnp.einsum('cqhd,ckhd->chqk', grad_part, value_part, preferred_element_ty...  66.6 us
    convert_element_type x4, other arithmetic, backward_group(): d_scores_b = (attn_probs * (d_probs - row_inner)).astype(bf16)  54.1 us
    dot_general x8, matrix products, left_trans(): lax.dot_general(left, right, (((0,), (0,)), ((), ())), preferred_element_...  53.3 us
  transfers between devices with their start and end apart: 55, of which 14 were waited for; matrix products, arithmetic and copies ran while one was open for 13% of the time, Pallas kernels for 25%

profile of v1, /device:TPU:1, one launch (start us, length us, event | category | flops | bytes accessed | tf_op | source)
XLA Modules:
  0.0 1813.5 jit_solution(2331047220554693912)
XLA Ops:
  47.1 14.5 collective-permute-start.15
  61.6 10.8 collective-permute-start.14
  107.2 27.7 %collective-permute-start.20 = (bf16[4,3,256,512]{3,2,1,0:T(8,128)(2,1)}, bf16[4,3,256,512]{3,2,1,0:T(8,128)(2,1)}, u32[]{:S(2)}, u32[]{:S(2)}) collective-permute-start(bf16[4,3,256,512]{3,2,1,0:T(8,128)(2,1)} %pad_maximum_fusion.2), channel_id=1, source_target_pairs={{0,4},{4,0},{8,12},{12,8},{16,20},{20,16},{24,28},{28,24},{1,5},{5... | collective-permute-start | bytes 9437192 | tf_op jit(solution)/shard_map/ppermute | solution.py:58
  136.3 10.6 collective-permute-done.12.refs_5_
  149.2 14.4 collective-permute-start.13
  163.7 191.9 %assemble.3 = bf16[1024,3072]{1,0:T(8,128)(2,1)} custom-call(bf16[256,3072]{1,0:T(8,128)(2,1)} %refs_0_.3, bf16[3,64,1536]{2,1,0:T(8,128)(2,1)} %copy-done.36, bf16[3,64,1536]{2,1,0:T(8,128)(2,1)} %copy-done.33, bf16[3,64,1536]{2,1,0:T(8,128)(2,1)} %copy-done.34, bf16[3,64,1536]{2,1,0:T(8,128)(2,1)} %copy-done.35, ...), custom_call_target="tpu_custom_call" | custom-call | tf_op jit(solution)/shard_map/assemble/pallas_call | solution.py:110
  355.6 9.7 fusion.168
  381.2 130.1 %while.26 = (s32[]{:T(128)}, bf16[4,1,1104,4,64]{2,4,3,1,0:T(8,128)(2,1)}, f32[4,1,4,1104]{3,2,1,0:T(4,128)}, bf16[4,1,1104,4,64]{2,4,3,1,0:T(8,128)(2,1)}, bf16...) while((s32[]{:T(128)}, bf16[4,1,1104,4,64]{2,4,3,1,0:T(8,128)(2,1)}, ...), condition=%wide.region_5.6_spmd, body=%wide.region_2.5_spmd.sunk | while | flops 1282190080 | bytes 62444376 | solution.py:272
  381.4 10.8 fusion.218
  401.7 11.4 fusion.220
  413.8 10.8 fusion.218
  424.5 9.5 fusion.219
  434.1 11.4 fusion.220
  446.1 10.8 fusion.218
  466.4 11.5 fusion.220
  478.4 10.8 fusion.218
  498.7 11.4 fusion.220
  511.3 255.5 %assemble.5 = bf16[4096,1024]{1,0:T(8,128)(2,1)} custom-call(bf16[1024,1024]{1,0:T(8,128)(2,1)} %refs_0_.5, bf16[3,256,512]{2,1,0:T(8,128)(2,1)} %copy-done.30, bf16[3,256,512]{2,1,0:T(8,128)(2,1)} %copy-done.27, bf16[3,256,512]{2,1,0:T(8,128)(2,1)} %copy-done.28, bf16[3,256,512]{2,1,0:T(8,128)(2,1)} %copy-done.29, ...), custom_call_target="tpu_custom_call" | custom-call | tf_op jit(solution)/shard_map/assemble/pallas_call | solution.py:110
  766.8 319.2 %assemble.4 = (bf16[1024,1024]{1,0:T(8,128)(2,1)}, bf16[1024,4096]{1,0:T(8,128)(2,1)}) custom-call(bf16[256,1024]{1,0:T(8,128)(2,1)} %refs_0_.4, bf16[256,4096]{1,0:T(8,128)(2,1)} %refs_1_.1, bf16[3,64,2560]{2,1,0:T(8,128)(2,1)} %copy-done.23, bf16[3,64,2560]{2,1,0:T(8,128)(2,1)} %copy-done.24, bf16[3,64,2560]{2,1,0:T(8,128)(2,1)} %copy-done.25, ...), custom_call_target="tpu_custom_call" | custom-call | tf_op jit(solution)/shard_map/assemble/pallas_call | solution.py:110
  1093.9 12.8 convolution_add_fusion
  1106.8 54.3 %convert_reduce_fusion = (f32[4096]{0:T(1024)}, bf16[1104,4096]{1,0:T(8,128)(2,1)}, f32[1104,4096]{1,0:T(8,128)}) fusion(f32[1104,4096]{1,0:T(8,128)S(1)} %convolution_add_fusion, bf16[1104,1024]{1,0:T(8,128)(2,1)S(1)} %copy-done.40, bf16[4096,1024]{1,0:T(8,128)(2,1)} %assemble.5), kind=kOutput, calls=%fused_computation.55 | convolution fusion | flops 9595645952 | bytes 55885824 | tf_op jit(solution)/shard_map/dot_general | solution.py:38
  1161.1 13.6 multiply_convert_fusion.1
  1174.8 17.9 multiply_reduce_fusion.1
  1219.9 10.8 fusion.84
  1238.6 240.2 %while.27 = (s32[]{:T(128)}, bf16[4,1,1104,4,64]{2,4,3,1,0:T(8,128)(2,1)}, bf16[4,1,1104,4,64]{2,4,3,1,0:T(8,128)(2,1)}, bf16[4,1,1104,4,64]{2,4,3,1,0:T(8,128)(...) while((s32[]{:T(128)}, ...), condition=%wide.region_12.13_spmd, body=%wide.region_10.12_spmd.sunk | while | flops 3159731968 | bytes 201783552 | solution.py:321
  1239.7 11.1 fusion.229
  1250.8 16.7 multiply_reduce_fusion.5
  1267.4 13.5 multiply_convert_fusion.3
  1287.3 11.6 fusion.232
  1299.6 11.1 fusion.229
  1310.7 16.7 multiply_reduce_fusion.5
  1327.4 13.5 multiply_convert_fusion.3
  1347.3 11.6 fusion.232
  1359.6 11.1 fusion.229
  1370.7 16.7 multiply_reduce_fusion.5
  1387.4 13.5 multiply_convert_fusion.3
  1407.2 11.7 fusion.232
  1419.6 11.1 fusion.229
  1430.7 16.7 multiply_reduce_fusion.5
  1447.4 13.5 multiply_convert_fusion.3
  1467.2 11.6 fusion.232
  1505.7 9.7 fusion.78
  1520.4 9.7 fusion.75
  1546.0 11.5 collective-permute-done.24
  1557.5 17.1 collective-permute-done.23
  1608.1 112.2 %psum.7 = f32[4,3072]{1,0:T(4,128)S(1)} all-reduce(f32[4,3072]{1,0:T(4,128)S(1)} %constant_dynamic-update-slice_fusion), channel_id=1, replica_groups=mesh['rep'=8,'shard'=4] {'rep','shard'}, use_global_device_ids=true, to_apply=%region_23.24 | all-reduce | flops 12288 | bytes 98304 | tf_op jit(solution)/shard_map/psum | solution.py:336
  1738.9 12.1 collective-permute-done.49
  1750.9 21.8 %collective-permute-start.31 = (bf16[4,64,1536]{2,1,0:T(8,128)(2,1)S(1)}, bf16[4,64,1536]{2,1,0:T(8,128)(2,1)S(1)}, u32[]{:S(2)}, u32[]{:S(2)}) collective-permute-start(bf16[4,64,1536]{2,1,0:T(8,128)(2,1)S(1)} %pad_maximum_fusion.11), channel_id=1, source_target_pairs={{0,4},{4,0},{8,12},{12,8},{16,20},{20,16},{24,28},{28,24},{1,5},{5... | collective-permute-start | bytes 2359304 | tf_op jit(solution)/shard_map/ppermute | solution.py:58
  (474 shorter events, 340.9 us)
Async XLA Ops:
  8.7 18.9 %collective-permute-start.2 = (bf16[80,1536]{1,0:T(8,128)(2,1)S(1)}, bf16[80,1536]{1,0:T(8,128)(2,1)S(1)}, u32[]{:S(2)}, u32[]{:S(2)}) collective-permute-start(bf16[80,1536]{1,0:T(8,128)(2,1)S(1)} %maximum_maximum_fusion), channel_id=1, source_target_pairs={{0,3},{1,0},{2,1},{3,2},{4,7},{5,4},{6,5},{7,6},{8,11},{9,8},{10,9... | collective-permute-start | bytes 737288 | tf_op jit(solution)/shard_map/ppermute | solution.py:52
  12.9 20.4 %collective-permute-start.1 = (bf16[80,1536]{1,0:T(8,128)(2,1)S(1)}, bf16[80,1536]{1,0:T(8,128)(2,1)S(1)}, u32[]{:S(2)}, u32[]{:S(2)}) collective-permute-start(bf16[80,1536]{1,0:T(8,128)(2,1)S(1)} %maximum_maximum_fusion), channel_id=1, source_target_pairs={{0,2},{1,3},{2,0},{3,1},{4,6},{5,7},{6,4},{7,5},{8,10},{9,11},{10,... | collective-permute-start | bytes 737288 | tf_op jit(solution)/shard_map/ppermute | solution.py:52
  12.9 20.4 %collective-permute-start = (bf16[80,1536]{1,0:T(8,128)(2,1)S(1)}, bf16[80,1536]{1,0:T(8,128)(2,1)S(1)}, u32[]{:S(2)}, u32[]{:S(2)}) collective-permute-start(bf16[80,1536]{1,0:T(8,128)(2,1)S(1)} %maximum_maximum_fusion), channel_id=1, source_target_pairs={{0,1},{1,2},{2,3},{3,0},{4,5},{5,6},{6,7},{7,4},{8,9},{9,10},{10,1... | collective-permute-start | bytes 737288 | tf_op jit(solution)/shard_map/ppermute | solution.py:52
  16.0 66.9 %collective-permute-start.9 = (bf16[64,2560]{1,0:T(8,128)(2,1)}, bf16[64,2560]{1,0:T(8,128)(2,1)}, u32[]{:S(2)}, u32[]{:S(2)}) collective-permute-start(bf16[64,2560]{1,0:T(8,128)(2,1)} %pad_maximum_fusion.13), channel_id=1, source_target_pairs={{0,3},{1,0},{2,1},{3,2},{4,7},{5,4},{6,5},{7,6},{8,11},{9,8},{10,9... | collective-permute-start | bytes 983048 | tf_op jit(solution)/shard_map/ppermute | solution.py:52
  18.8 64.7 %collective-permute-start.8 = (bf16[64,2560]{1,0:T(8,128)(2,1)}, bf16[64,2560]{1,0:T(8,128)(2,1)}, u32[]{:S(2)}, u32[]{:S(2)}) collective-permute-start(bf16[64,2560]{1,0:T(8,128)(2,1)} %pad_maximum_fusion.13), channel_id=1, source_target_pairs={{0,2},{1,3},{2,0},{3,1},{4,6},{5,7},{6,4},{7,5},{8,10},{9,11},{10,... | collective-permute-start | bytes 983048 | tf_op jit(solution)/shard_map/ppermute | solution.py:52
  34.1 12.1 collective-permute-start.3
  35.3 11.8 collective-permute-start.4
  36.5 25.1 %collective-permute-start.5 = (bf16[3,64,1536]{2,1,0:T(8,128)(2,1)S(1)}, bf16[3,64,1536]{2,1,0:T(8,128)(2,1)S(1)}, u32[]{:S(2)}, u32[]{:S(2)}) collective-permute-start(bf16[3,64,1536]{2,1,0:T(8,128)(2,1)S(1)} %get-tuple-element.217.refs_1_), channel_id=1, source_target_pairs={{0,24},{4,28},{8,16},{12,20},{16,8},{20,12},{24,0},{28,4},{1,25},{... | collective-permute-start | bytes 1769480 | tf_op jit(solution)/shard_map/ppermute | solution.py:55
  46.2 26.5 %collective-permute-start.16 = (bf16[256,512]{1,0:T(8,128)(2,1)}, bf16[256,512]{1,0:T(8,128)(2,1)S(1)}, u32[]{:S(2)}, u32[]{:S(2)}) collective-permute-start(bf16[256,512]{1,0:T(8,128)(2,1)} %dynamic_slice.277), channel_id=1, source_target_pairs={{0,3},{1,0},{2,1},{3,2},{4,7},{5,4},{6,5},{7,6},{8,11},{9,8},{10,9... | collective-permute-start | bytes 786440 | tf_op jit(solution)/shard_map/ppermute | solution.py:52
  47.1 34.0 %collective-permute-start.15 = (bf16[256,512]{1,0:T(8,128)(2,1)}, bf16[256,512]{1,0:T(8,128)(2,1)S(1)}, u32[]{:S(2)}, u32[]{:S(2)}) collective-permute-start(bf16[256,512]{1,0:T(8,128)(2,1)} %dynamic_slice.277), channel_id=1, source_target_pairs={{0,2},{1,3},{2,0},{3,1},{4,6},{5,7},{6,4},{7,5},{8,10},{9,11},{10,... | collective-permute-start | bytes 786440 | tf_op jit(solution)/shard_map/ppermute | solution.py:52
  61.6 19.5 %collective-permute-start.14 = (bf16[256,512]{1,0:T(8,128)(2,1)}, bf16[256,512]{1,0:T(8,128)(2,1)S(1)}, u32[]{:S(2)}, u32[]{:S(2)}) collective-permute-start(bf16[256,512]{1,0:T(8,128)(2,1)} %dynamic_slice.277), channel_id=1, source_target_pairs={{0,1},{1,2},{2,3},{3,0},{4,5},{5,6},{6,7},{7,4},{8,9},{9,10},{10,1... | collective-permute-start | bytes 786440 | tf_op jit(solution)/shard_map/ppermute | solution.py:52
  72.7 91.0 %collective-permute-start.6 = (bf16[4,3,64,1536]{3,2,1,0:T(8,128)(2,1)S(1)}, bf16[4,3,64,1536]{3,2,1,0:T(8,128)(2,1)}, u32[]{:S(2)}, u32[]{:S(2)}) collective-permute-start(bf16[4,3,64,1536]{3,2,1,0:T(8,128)(2,1)S(1)} %pad_maximum_fusion.3), channel_id=1, source_target_pairs={{0,4},{4,0},{8,12},{12,8},{16,20},{20,16},{24,28},{28,24},{1,5},{5... | collective-permute-start | bytes 7077896 | tf_op jit(solution)/shard_map/ppermute | solution.py:58
  81.3 12.7 collective-permute-start.17
  81.3 13.5 collective-permute-start.18
  83.5 21.7 %collective-permute-start.19 = (bf16[3,256,512]{2,1,0:T(8,128)(2,1)S(1)}, bf16[3,256,512]{2,1,0:T(8,128)(2,1)S(1)}, u32[]{:S(2)}, u32[]{:S(2)}) collective-permute-start(bf16[3,256,512]{2,1,0:T(8,128)(2,1)S(1)} %get-tuple-element.215.refs_1_), channel_id=1, source_target_pairs={{0,24},{4,28},{8,16},{12,20},{16,8},{20,12},{24,0},{28,4},{1,25},{... | collective-permute-start | bytes 2359304 | tf_op jit(solution)/shard_map/ppermute | solution.py:55
  93.3 41.6 %collective-permute-start.10 = (bf16[3,64,2560]{2,1,0:T(8,128)(2,1)S(1)}, bf16[3,64,2560]{2,1,0:T(8,128)(2,1)S(1)}, u32[]{:S(2)}, u32[]{:S(2)}) collective-permute-start(bf16[3,64,2560]{2,1,0:T(8,128)(2,1)S(1)} %get-tuple-element.210.refs_2_), channel_id=1, source_target_pairs={{0,8},{4,12},{8,0},{12,4},{16,24},{20,28},{24,16},{28,20},{1,9},{5... | collective-permute-start | bytes 2949128 | tf_op jit(solution)/shard_map/ppermute | solution.py:55
  94.0 42.4 %collective-permute-start.11 = (bf16[3,64,2560]{2,1,0:T(8,128)(2,1)S(1)}, bf16[3,64,2560]{2,1,0:T(8,128)(2,1)S(1)}, u32[]{:S(2)}, u32[]{:S(2)}) collective-permute-start(bf16[3,64,2560]{2,1,0:T(8,128)(2,1)S(1)} %get-tuple-element.210.refs_2_), channel_id=1, source_target_pairs={{0,16},{4,20},{8,24},{12,28},{16,0},{20,4},{24,8},{28,12},{1,17},{... | collective-permute-start | bytes 2949128 | tf_op jit(solution)/shard_map/ppermute | solution.py:55
  94.9 52.0 %collective-permute-start.12 = (bf16[3,64,2560]{2,1,0:T(8,128)(2,1)S(1)}, bf16[3,64,2560]{2,1,0:T(8,128)(2,1)S(1)}, u32[]{:S(2)}, u32[]{:S(2)}) collective-permute-start(bf16[3,64,2560]{2,1,0:T(8,128)(2,1)S(1)} %get-tuple-element.210.refs_2_), channel_id=1, source_target_pairs={{0,24},{4,28},{8,16},{12,20},{16,8},{20,12},{24,0},{28,4},{1,25},{... | collective-permute-start | bytes 2949128 | tf_op jit(solution)/shard_map/ppermute | solution.py:55
  107.2 404.1 %collective-permute-start.20 = (bf16[4,3,256,512]{3,2,1,0:T(8,128)(2,1)}, bf16[4,3,256,512]{3,2,1,0:T(8,128)(2,1)}, u32[]{:S(2)}, u32[]{:S(2)}) collective-permute-start(bf16[4,3,256,512]{3,2,1,0:T(8,128)(2,1)} %pad_maximum_fusion.2), channel_id=1, source_target_pairs={{0,4},{4,0},{8,12},{12,8},{16,20},{20,16},{24,28},{28,24},{1,5},{5... | collective-permute-start | bytes 9437192 | tf_op jit(solution)/shard_map/ppermute | solution.py:58
  149.2 617.5 %collective-permute-start.13 = (bf16[4,3,64,2560]{3,2,1,0:T(8,128)(2,1)}, bf16[4,3,64,2560]{3,2,1,0:T(8,128)(2,1)}, u32[]{:S(2)}, u32[]{:S(2)}) collective-permute-start(bf16[4,3,64,2560]{3,2,1,0:T(8,128)(2,1)} %pad_maximum_fusion.1), channel_id=1, source_target_pairs={{0,4},{4,0},{8,12},{12,8},{16,20},{20,16},{24,28},{28,24},{1,5},{5... | collective-permute-start | bytes 11796488 | tf_op jit(solution)/shard_map/ppermute | solution.py:58
  1505.6 30.4 %collective-permute-start.21 = (bf16[1024,1536]{1,0:T(8,128)(2,1)S(1)}, bf16[1024,1536]{1,0:T(8,128)(2,1)S(1)}, u32[]{:S(2)}, u32[]{:S(2)}) collective-permute-start(bf16[1024,1536]{1,0:T(8,128)(2,1)S(1)} %convolution_convert_fusion.3), channel_id=1, source_target_pairs={{0,4},{4,0},{8,12},{12,8},{16,20},{20,16},{24,28},{28,24},{1,5},{5... | collective-permute-start | bytes 9437192 | tf_op jit(solution)/shard_map/ppermute | solution.py:58
  1515.5 72.6 %collective-permute-start.33 = (bf16[1024,2048]{1,0:T(8,128)(2,1)}, bf16[1024,2048]{1,0:T(8,128)(2,1)}, u32[]{:S(2)}, u32[]{:S(2)}) collective-permute-start(bf16[1024,2048]{1,0:T(8,128)(2,1)} %fusion.78), channel_id=1, source_target_pairs={{0,4},{4,0},{8,12},{12,8},{16,20},{20,16},{24,28},{28,24},{1,5},{5... | collective-permute-start | bytes 12582920 | tf_op jit(solution)/shard_map/ppermute | solution.py:58
  1516.0 24.4 %collective-permute-start.32 = (bf16[1024,512]{1,0:T(8,128)(2,1)S(1)}, bf16[1024,512]{1,0:T(8,128)(2,1)}, u32[]{:S(2)}, u32[]{:S(2)}) collective-permute-start(bf16[1024,512]{1,0:T(8,128)(2,1)S(1)} %copy-done.80), channel_id=1, source_target_pairs={{0,4},{4,0},{8,12},{12,8},{16,20},{20,16},{24,28},{28,24},{1,5},{5... | collective-permute-start | bytes 3145736 | tf_op jit(solution)/shard_map/ppermute | solution.py:58
  1516.0 65.1 %collective-permute-start.44 = (bf16[4096,512]{1,0:T(8,128)(2,1)}, bf16[4096,512]{1,0:T(8,128)(2,1)}, u32[]{:S(2)}, u32[]{:S(2)}) collective-permute-start(bf16[4096,512]{1,0:T(8,128)(2,1)} %convolution_convert_fusion), channel_id=1, source_target_pairs={{0,4},{4,0},{8,12},{12,8},{16,20},{20,16},{24,28},{28,24},{1,5},{5... | collective-permute-start | bytes 12582920 | tf_op jit(solution)/shard_map/ppermute | solution.py:58
  1537.1 20.4 %collective-permute-start.24 = (bf16[4,64,1536]{2,1,0:T(8,128)(2,1)}, bf16[4,64,1536]{2,1,0:T(8,128)(2,1)}, u32[]{:S(2)}, u32[]{:S(2)}) collective-permute-start(bf16[4,64,1536]{2,1,0:T(8,128)(2,1)} %fusion.107), channel_id=1, source_target_pairs={{0,24},{4,28},{8,16},{12,20},{16,8},{20,12},{24,0},{28,4},{1,25},{... | collective-permute-start | bytes 2359304 | tf_op jit(solution)/shard_map/ppermute | solution.py:55
  1540.2 34.4 %collective-permute-start.23 = (bf16[4,64,1536]{2,1,0:T(8,128)(2,1)}, bf16[4,64,1536]{2,1,0:T(8,128)(2,1)}, u32[]{:S(2)}, u32[]{:S(2)}) collective-permute-start(bf16[4,64,1536]{2,1,0:T(8,128)(2,1)} %get-tuple-element.178), channel_id=1, source_target_pairs={{0,16},{4,20},{8,24},{12,28},{16,0},{20,4},{24,8},{28,12},{1,17},{... | collective-permute-start | bytes 2359304 | tf_op jit(solution)/shard_map/ppermute | solution.py:55
  1540.4 34.2 %collective-permute-start.22 = (bf16[4,64,1536]{2,1,0:T(8,128)(2,1)}, bf16[4,64,1536]{2,1,0:T(8,128)(2,1)}, u32[]{:S(2)}, u32[]{:S(2)}) collective-permute-start(bf16[4,64,1536]{2,1,0:T(8,128)(2,1)} %get-tuple-element.177), channel_id=1, source_target_pairs={{0,8},{4,12},{8,0},{12,4},{16,24},{20,28},{24,16},{28,20},{1,9},{5... | collective-permute-start | bytes 2359304 | tf_op jit(solution)/shard_map/ppermute | solution.py:55
  1577.3 18.0 collective-permute-start.27
  1580.8 16.5 collective-permute-start.26
  1580.8 18.1 collective-permute-start.25
  1582.8 24.7 %collective-permute-start.47 = (bf16[4,256,512]{2,1,0:T(8,128)(2,1)S(1)}, bf16[4,256,512]{2,1,0:T(8,128)(2,1)}, u32[]{:S(2)}, u32[]{:S(2)}) collective-permute-start(bf16[4,256,512]{2,1,0:T(8,128)(2,1)S(1)} %fusion.104), channel_id=1, source_target_pairs={{0,24},{4,28},{8,16},{12,20},{16,8},{20,12},{24,0},{28,4},{1,25},{... | collective-permute-start | bytes 3145736 | tf_op jit(solution)/shard_map/ppermute | solution.py:55
  1588.0 135.5 %collective-permute-start.46 = (bf16[4,256,512]{2,1,0:T(8,128)(2,1)}, bf16[4,256,512]{2,1,0:T(8,128)(2,1)}, u32[]{:S(2)}, u32[]{:S(2)}) collective-permute-start(bf16[4,256,512]{2,1,0:T(8,128)(2,1)} %get-tuple-element.173), channel_id=1, source_target_pairs={{0,16},{4,20},{8,24},{12,28},{16,0},{20,4},{24,8},{28,12},{1,17},{... | collective-permute-start | bytes 3145736 | tf_op jit(solution)/shard_map/ppermute | solution.py:55
  1595.3 130.3 %collective-permute-start.45 = (bf16[4,256,512]{2,1,0:T(8,128)(2,1)}, bf16[4,256,512]{2,1,0:T(8,128)(2,1)}, u32[]{:S(2)}, u32[]{:S(2)}) collective-permute-start(bf16[4,256,512]{2,1,0:T(8,128)(2,1)} %get-tuple-element.172), channel_id=1, source_target_pairs={{0,8},{4,12},{8,0},{12,4},{16,24},{20,28},{24,16},{28,20},{1,9},{5... | collective-permute-start | bytes 3145736 | tf_op jit(solution)/shard_map/ppermute | solution.py:55
  1597.3 132.3 %collective-permute-start.36 = (bf16[4,64,2560]{2,1,0:T(8,128)(2,1)}, bf16[4,64,2560]{2,1,0:T(8,128)(2,1)}, u32[]{:S(2)}, u32[]{:S(2)}) collective-permute-start(bf16[4,64,2560]{2,1,0:T(8,128)(2,1)} %pad_maximum_fusion.6), channel_id=1, source_target_pairs={{0,24},{4,28},{8,16},{12,20},{16,8},{20,12},{24,0},{28,4},{1,25},{... | collective-permute-start | bytes 3932168 | tf_op jit(solution)/shard_map/ppermute | solution.py:55
  1598.9 130.8 %collective-permute-start.35 = (bf16[4,64,2560]{2,1,0:T(8,128)(2,1)}, bf16[4,64,2560]{2,1,0:T(8,128)(2,1)}, u32[]{:S(2)}, u32[]{:S(2)}) collective-permute-start(bf16[4,64,2560]{2,1,0:T(8,128)(2,1)} %pad_maximum_fusion.5), channel_id=1, source_target_pairs={{0,16},{4,20},{8,24},{12,28},{16,0},{20,4},{24,8},{28,12},{1,17},{... | collective-permute-start | bytes 3932168 | tf_op jit(solution)/shard_map/ppermute | solution.py:55
  1607.6 123.4 %collective-permute-start.34 = (bf16[4,64,2560]{2,1,0:T(8,128)(2,1)}, bf16[4,64,2560]{2,1,0:T(8,128)(2,1)}, u32[]{:S(2)}, u32[]{:S(2)}) collective-permute-start(bf16[4,64,2560]{2,1,0:T(8,128)(2,1)} %pad_maximum_fusion.4), channel_id=1, source_target_pairs={{0,8},{4,12},{8,0},{12,4},{16,24},{20,28},{24,16},{28,20},{1,9},{5... | collective-permute-start | bytes 3932168 | tf_op jit(solution)/shard_map/ppermute | solution.py:55
  1723.6 10.7 collective-permute-start.30
  1731.0 19.9 %collective-permute-start.49 = (bf16[256,512]{1,0:T(8,128)(2,1)S(1)}, bf16[256,512]{1,0:T(8,128)(2,1)S(1)}, u32[]{:S(2)}, u32[]{:S(2)}) collective-permute-start(bf16[256,512]{1,0:T(8,128)(2,1)S(1)} %get-tuple-element.208), channel_id=1, source_target_pairs={{0,2},{1,3},{2,0},{3,1},{4,6},{5,7},{6,4},{7,5},{8,10},{9,11},{10,... | collective-permute-start | bytes 786440 | tf_op jit(solution)/shard_map/ppermute | solution.py:52
  1734.3 38.4 %collective-permute-start.48 = (bf16[256,512]{1,0:T(8,128)(2,1)S(1)}, bf16[256,512]{1,0:T(8,128)(2,1)S(1)}, u32[]{:S(2)}, u32[]{:S(2)}) collective-permute-start(bf16[256,512]{1,0:T(8,128)(2,1)S(1)} %get-tuple-element.206), channel_id=1, source_target_pairs={{0,1},{1,2},{2,3},{3,0},{4,5},{5,6},{6,7},{7,4},{8,9},{9,10},{10,1... | collective-permute-start | bytes 786440 | tf_op jit(solution)/shard_map/ppermute | solution.py:52
  1735.6 39.4 %collective-permute-start.39 = (bf16[64,2560]{1,0:T(8,128)(2,1)S(1)}, bf16[64,2560]{1,0:T(8,128)(2,1)S(1)}, u32[]{:S(2)}, u32[]{:S(2)}) collective-permute-start(bf16[64,2560]{1,0:T(8,128)(2,1)S(1)} %get-tuple-element.204), channel_id=1, source_target_pairs={{0,3},{1,0},{2,1},{3,2},{4,7},{5,4},{6,5},{7,6},{8,11},{9,8},{10,9... | collective-permute-start | bytes 983048 | tf_op jit(solution)/shard_map/ppermute | solution.py:52
  1737.7 42.5 %collective-permute-start.38 = (bf16[64,2560]{1,0:T(8,128)(2,1)S(1)}, bf16[64,2560]{1,0:T(8,128)(2,1)S(1)}, u32[]{:S(2)}, u32[]{:S(2)}) collective-permute-start(bf16[64,2560]{1,0:T(8,128)(2,1)S(1)} %get-tuple-element.205), channel_id=1, source_target_pairs={{0,2},{1,3},{2,0},{3,1},{4,6},{5,7},{6,4},{7,5},{8,10},{9,11},{10,... | collective-permute-start | bytes 983048 | tf_op jit(solution)/shard_map/ppermute | solution.py:52
  1737.8 43.6 %collective-permute-start.37 = (bf16[64,2560]{1,0:T(8,128)(2,1)S(1)}, bf16[64,2560]{1,0:T(8,128)(2,1)S(1)}, u32[]{:S(2)}, u32[]{:S(2)}) collective-permute-start(bf16[64,2560]{1,0:T(8,128)(2,1)S(1)} %get-tuple-element.203), channel_id=1, source_target_pairs={{0,1},{1,2},{2,3},{3,0},{4,5},{5,6},{6,7},{7,4},{8,9},{9,10},{10,1... | collective-permute-start | bytes 983048 | tf_op jit(solution)/shard_map/ppermute | solution.py:52
  1750.9 31.8 %collective-permute-start.31 = (bf16[4,64,1536]{2,1,0:T(8,128)(2,1)S(1)}, bf16[4,64,1536]{2,1,0:T(8,128)(2,1)S(1)}, u32[]{:S(2)}, u32[]{:S(2)}) collective-permute-start(bf16[4,64,1536]{2,1,0:T(8,128)(2,1)S(1)} %pad_maximum_fusion.11), channel_id=1, source_target_pairs={{0,4},{4,0},{8,12},{12,8},{16,20},{20,16},{24,28},{28,24},{1,5},{5... | collective-permute-start | bytes 2359304 | tf_op jit(solution)/shard_map/ppermute | solution.py:58
  1775.0 15.2 collective-permute-start.52
  1781.6 11.6 collective-permute-start.42
  1782.7 19.0 %collective-permute-start.41 = (bf16[64,2560]{1,0:T(8,128)(2,1)S(1)}, bf16[64,2560]{1,0:T(8,128)(2,1)S(1)}, u32[]{:S(2)}, u32[]{:S(2)}) collective-permute-start(bf16[64,2560]{1,0:T(8,128)(2,1)S(1)} %fusion.110), channel_id=1, source_target_pairs={{0,16},{4,20},{8,24},{12,28},{16,0},{20,4},{24,8},{28,12},{1,17},{... | collective-permute-start | bytes 983048 | tf_op jit(solution)/shard_map/ppermute | solution.py:55
  1783.2 18.5 %collective-permute-start.40 = (bf16[64,2560]{1,0:T(8,128)(2,1)S(1)}, bf16[64,2560]{1,0:T(8,128)(2,1)S(1)}, u32[]{:S(2)}, u32[]{:S(2)}) collective-permute-start(bf16[64,2560]{1,0:T(8,128)(2,1)S(1)} %fusion.110), channel_id=1, source_target_pairs={{0,8},{4,12},{8,0},{12,4},{16,24},{20,28},{24,16},{28,20},{1,9},{5... | collective-permute-start | bytes 983048 | tf_op jit(solution)/shard_map/ppermute | solution.py:55
  1790.4 15.2 collective-permute-start.54
  (109 other events, 3232.9 us)

commit v2 on v1

--- a/solution.py
+++ b/solution.py
@@ -7,11 +7,9 @@
 from jax.experimental.pallas import tpu as pltpu
 from jax.sharding import PartitionSpec as P
 
-HEADS = 16
 HDIM = 64
 
 eps = 1e-06
-head_block = 4
 bf16 = jnp.bfloat16
 f32 = jnp.float32
 
@@ -36,6 +34,140 @@
 
 def right_trans(left, right):
     return lax.dot_general(left, right, (((1,), (1,)), ((), ())), preferred_element_type=f32)
+
+
+LOG2E = 1.4426950408889634
+
+
+def contract(left, right, left_dim, right_dim):
+    return lax.dot_general(
+        left, right, (((left_dim,), (right_dim,)), ((), ())), preferred_element_type=f32
+    )
+
+
+def query_blocks(rows, tile=256):
+    return [(i, min(tile, rows - i)) for i in range(0, rows, tile)]
+
+
+def head_mask(head, rows, dtype):
+    lane = lax.broadcasted_iota(jnp.int32, (rows, 2 * HDIM), 1)
+    return (lane // HDIM == head).astype(dtype)
+
+
+def attend_kernel(q_ref, k_ref, v_ref, o_ref, inv_ref, p_ref):
+    rows = q_ref.shape[0]
+    factor = HDIM ** (-0.5) * LOG2E
+    keys = k_ref[...]
+    values = v_ref[...]
+    ones = jnp.ones(values.shape, bf16)
+    for start, n in query_blocks(rows):
+        queries = q_ref[start : start + n, :]
+        mixed = inverse = None
+        for head in range(2):
+            mask = head_mask(head, rows, bf16)
+            scores = contract(keys * mask, queries, 1, 1)
+            largest = jnp.max(scores, axis=0, keepdims=True)
+            probs = jnp.exp2((scores - largest) * factor).astype(bf16)
+            p_ref[head, :, start : start + n] = probs
+            both = contract(probs, jnp.concatenate([values * mask, ones], 1), 0, 0)
+            inv = 1.0 / both[:, 2 * HDIM :]
+            part = both[:, : 2 * HDIM] * inv
+            share = head_mask(head, n, f32) * inv
+            mixed = part if mixed is None else mixed + part
+            inverse = share if inverse is None else inverse + share
+        o_ref[start : start + n, :] = mixed.astype(bf16)
+        inv_ref[start : start + n, :] = inverse
+
+
+def attend(qkv):
+    rows, wide = qkv.shape
+    width = wide // 3
+    pairs = width // (2 * HDIM)
+
+    def column(offset):
+        return pl.BlockSpec((rows, 2 * HDIM), lambda j: (0, offset + j))
+
+    return pl.pallas_call(
+        attend_kernel,
+        grid=(pairs,),
+        in_specs=[column(0), column(pairs), column(2 * pairs)],
+        out_specs=[column(0), column(0), pl.BlockSpec((2, rows, rows), lambda j: (j, 0, 0))],
+        out_shape=[
+            jax.ShapeDtypeStruct((rows, width), bf16),
+            jax.ShapeDtypeStruct((rows, width), f32),
+            jax.ShapeDtypeStruct((2 * pairs, rows, rows), bf16),
+        ],
+        compiler_params=pltpu.CompilerParams(vmem_limit_bytes=56 * 1024 * 1024),
+        cost_estimate=pl.CostEstimate(
+            flops=16 * rows * rows * width, transcendentals=2 * pairs * rows * rows,
+            bytes_accessed=4 * pairs * rows * rows + 12 * rows * width,
+        ),
+        name="attend",
+    )(qkv, qkv, qkv)
+
+
+def attend_back_kernel(
+    q_ref, k_ref, v_ref, d_ref, o_ref, inv_ref, p_ref, dq_ref, dk_ref, dv_ref
+):
+    rows = q_ref.shape[0]
+    scale = HDIM ** (-0.5)
+    queries = q_ref[...]
+    keys = k_ref[...]
+    values = v_ref[...]
+    grads = (d_ref[...].astype(f32) * inv_ref[...]).astype(bf16)
+    product = grads.astype(f32) * o_ref[...].astype(f32)
+    lane = lax.broadcasted_iota(jnp.int32, (rows, 2 * HDIM), 1)
+    blocks = query_blocks(rows)
+    d_queries = [None] * len(blocks)
+    d_keys = d_values = None
+    for head in range(2):
+        mask = head_mask(head, rows, bf16)
+        inner = -jnp.sum(jnp.where(lane // HDIM == head, product, 0.0), 1, keepdims=True)
+        high = inner.astype(bf16)
+        low = (inner - high.astype(f32)).astype(bf16)
+        tail = jnp.where(lane == 0, high, jnp.where(lane == 1, low, jnp.zeros_like(low)))
+        grads_wide = jnp.concatenate([grads, tail], 1)
+        values_wide = jnp.concatenate([values * mask, (lane < 2).astype(bf16)], 1)
+        keys_h, queries_h, grads_h = keys * mask, queries * mask, grads * mask
+        for b, (start, n) in enumerate(blocks):
+            d_probs = contract(values_wide, grads_wide[start : start + n, :], 1, 1)
+            probs = p_ref[head, :, start : start + n]
+            d_scores = probs * d_probs.astype(bf16)
+            to_values = contract(probs, grads_h[start : start + n, :], 1, 0)
+            to_keys = contract(d_scores, queries_h[start : start + n, :], 1, 0)
+            to_queries = contract(d_scores, keys_h, 0, 0)
+            d_values = to_values if d_values is None else d_values + to_values
+            d_keys = to_keys if d_keys is None else d_keys + to_keys
+            d_queries[b] = to_queries if d_queries[b] is None else d_queries[b] + to_queries
+    dk_ref[...] = (d_keys * scale).astype(bf16)
+    dv_ref[...] = d_values.astype(bf16)
+    for b, (start, n) in enumerate(blocks):
+        dq_ref[start : start + n, :] = (d_queries[b] * scale).astype(bf16)
+
+
+def attend_back(qkv, grad, attended, inverse, probs):
+    rows, wide = qkv.shape
+    width = wide // 3
+    pairs = width // (2 * HDIM)
+
+    def column(offset):
+        return pl.BlockSpec((rows, 2 * HDIM), lambda j: (0, offset + j))
+
+    return pl.pallas_call(
+        attend_back_kernel,
+        grid=(pairs,),
+        in_specs=[column(0), column(pairs), column(2 * pairs)]
+        + [column(0)] * 3
+        + [pl.BlockSpec((2, rows, rows), lambda j: (j, 0, 0))],
+        out_specs=[column(0)] * 3,
+        out_shape=[jax.ShapeDtypeStruct((rows, width), bf16)] * 3,
+        compiler_params=pltpu.CompilerParams(vmem_limit_bytes=56 * 1024 * 1024),
+        cost_estimate=pl.CostEstimate(
+            flops=32 * rows * rows * width, transcendentals=0,
+            bytes_accessed=4 * pairs * rows * rows + 24 * rows * width,
+        ),
+        name="attend_back",
+    )(qkv, qkv, qkv, grad, attended, inverse, probs)
 
 
 class Links:
@@ -111,8 +243,9 @@
         kernel,
         out_shape=[jax.ShapeDtypeStruct((ns * r, n), bf16) for r, n in zip(rows, cols)],
         in_specs=[anywhere] * (len(weights) + nq + 1),
-        out_specs=[anywhere] * len(weights),
+        out_specs=[pl.BlockSpec(memory_space=pltpu.VMEM)] * len(weights),
         scratch_shapes=[pltpu.SemaphoreType.DMA((count,))],
+        compiler_params=pltpu.CompilerParams(vmem_limit_bytes=32 * 1024 * 1024),
         name="assemble",
     )(*weights, own, *crossed, mate)
 
@@ -178,6 +311,22 @@
     return outs
 
 
+def total_of(links, lines):
+    z, _, _ = links.here()
+    lines = lines + links.core(lines)
+    crossed = [links.chip(lines, k) for k in range(1, links.nq)]
+    for x in crossed:
+        lines = lines + x
+    moved = [
+        links.along(lax.dynamic_index_in_dim(lines, (z + s) % links.ns, 0, False), s)
+        for s in range(1, links.ns)
+    ]
+    line = lax.dynamic_index_in_dim(lines, z, 0, False)
+    for x in moved:
+        line = line + x
+    return line
+
+
 def halves(links, left, right):
     _, _, c = links.here()
     half = right.shape[1] // 2
@@ -209,8 +358,6 @@
     seq_len = inputs.shape[2]
     width = inputs.shape[3]
     n_rows = slots * seq_len
-    groups = HEADS // head_block
-    scale = HDIM ** (-0.5)
     z = lax.axis_index("shard")
 
     small = (ln1_gain, ln1_shift, qv_bias, out_bias, ln2_gain, ln2_shift, up_bias, down_bias)
@@ -243,34 +390,10 @@
     hidden_one, norm_one_back = jax.vjp(layer_norm, tokens, full_g1, full_s1)
     hidden_one_b = hidden_one.astype(bf16)
     projected = matmul(hidden_one_b, full_qkv)
-    queries_b = (projected[:, :width] + bias_f[:width]).astype(bf16)
-    keys_b = projected[:, width : 2 * width].astype(bf16)
-    values_b = (projected[:, 2 * width :] + bias_f[width:]).astype(bf16)
-
-    def arrange(values):
-        return values.reshape(slots, seq_len, groups, head_block, HDIM).transpose(2, 0, 1, 3, 4)
-
-    def restore(values):
-        return values.transpose(1, 2, 0, 3, 4).reshape(n_rows, width)
-
-    query_groups = arrange(queries_b)
-    key_groups = arrange(keys_b)
-    value_groups = arrange(values_b)
-
-    def forward_group(operands):
-        query_part, key_part, value_part = operands
-        scores = (
-            jnp.einsum("cqhd,ckhd->chqk", query_part, key_part, preferred_element_type=f32) * scale
-        )
-        largest = jnp.max(scores, -1, keepdims=True)
-        exponent = jnp.exp(scores - largest)
-        denominator = jnp.sum(exponent, -1, keepdims=True)
-        probs_b = (exponent / denominator).astype(bf16)
-        mixed = jnp.einsum("chqk,ckhd->cqhd", probs_b, value_part, preferred_element_type=f32)
-        return (mixed, (largest + jnp.log(denominator))[..., 0])
-
-    mixed_groups, log_totals = lax.map(forward_group, (query_groups, key_groups, value_groups))
-    attended_b = restore(mixed_groups).astype(bf16)
+    none = jnp.zeros((width,), f32)
+    qkv_bias = jnp.concatenate([bias_f[:width], none, bias_f[width:]])
+    qkv_b = (projected + qkv_bias).astype(bf16)
+    attended_b, inverse, probs_b = attend(qkv_b)
     middle = tokens + matmul(attended_b, full_wout) + full_bout
     hidden_two, norm_two_back = jax.vjp(layer_norm, middle, full_g2, full_s2)
     hidden_two_b = hidden_two.astype(bf16)
@@ -296,34 +419,7 @@
     o_wout, o_wup = scatter(links, [grad_wout[0], grad_wup[0]], [grad_wout[1], grad_wup[1]])
     grad_bout = jnp.sum(d_proj_b.astype(f32), 0)
     d_att_b = right_trans(d_proj_b, full_wout).astype(bf16)
-    d_att_groups = arrange(d_att_b)
-
-    def backward_group(operands):
-        query_part, key_part, value_part, log_total, grad_part = operands
-        scores = (
-            jnp.einsum("cqhd,ckhd->chqk", query_part, key_part, preferred_element_type=f32) * scale
-        )
-        attn_probs = jnp.exp(scores - log_total[..., None])
-        probs_b = attn_probs.astype(bf16)
-        d_probs = jnp.einsum("cqhd,ckhd->chqk", grad_part, value_part, preferred_element_type=f32)
-        row_inner = jnp.sum(d_probs * attn_probs, -1, keepdims=True)
-        d_scores_b = (attn_probs * (d_probs - row_inner)).astype(bf16)
-        d_query = (
-            jnp.einsum("chqk,ckhd->cqhd", d_scores_b, key_part, preferred_element_type=f32) * scale
-        )
-        d_key = (
-            jnp.einsum("chqk,cqhd->ckhd", d_scores_b, query_part, preferred_element_type=f32)
-            * scale
-        )
-        d_value = jnp.einsum("chqk,cqhd->ckhd", probs_b, grad_part, preferred_element_type=f32)
-        return (d_query, d_key, d_value)
-
-    d_query_groups, d_key_groups, d_value_groups = lax.map(
-        backward_group, (query_groups, key_groups, value_groups, log_totals, d_att_groups)
-    )
-    d_qkv_b = jnp.concatenate(
-        [restore(d_query_groups), restore(d_key_groups), restore(d_value_groups)], 1
-    ).astype(bf16)
+    d_qkv_b = jnp.concatenate(attend_back(qkv_b, d_att_b, attended_b, inverse, probs_b), 1)
     grad_qkv = halves(links, hidden_one_b, d_qkv_b)
     (o_qkv,) = scatter(links, [grad_qkv[0]], [grad_qkv[1]])
     column_sums = jnp.sum(d_qkv_b.astype(f32), 0)
@@ -333,8 +429,7 @@
     input_grad = (d_mid + d_in_norm).reshape(inputs.shape)
     small_grads = (grad_g1, grad_s1, grad_qvb, grad_bout, grad_g2, grad_s2, grad_bup, grad_bdown)
     joined = jnp.concatenate([g.reshape(ns, -1) for g in small_grads], 1)
-    joined = lax.psum(joined, ("rep", "shard"))
-    joined = lax.dynamic_index_in_dim(joined, z, 0, False)
+    joined = total_of(links, joined)
     owned = []
     base = 0
     for n in sizes:

time: 1820 us -> 756 us (0.42)
  Pallas kernels: 767 us -> 103 us
  matrix products: 446 us -> 181 us
  waiting for transfers between devices: 101 us -> 257 us
  other arithmetic: 180 us -> 66.4 us
  blocking collectives: 112 us -> 0 us
  starting transfers between devices: 153 us -> 92.5 us
    pallas_call x3, Pallas kernels: 767 us -> 3.83 us  [assemble(): pl.pallas_call(kernel, out_shape=[jax.ShapeDtypeStruct((ns * r, n), bf16)...]
    dot_general x28 -> x0, matrix products: 271 us -> none  [the longest x4 66.6 us: backward_group(): jnp.einsum('cqhd,ckhd->chqk', grad_part, value_part, preferred_element_ty...]
    ppermute x27 -> x30, waiting for transfers between devices: 71.5 us -> 187 us  [chip(): return lax.ppermute(values, 'rep', [(i, i ^ 2 * k) for i in range(self.nr)])]
    psum x1 -> x0, blocking collectives: 112 us -> none  [body(): joined = lax.psum(joined, ('rep', 'shard'))]
    pallas_call x0 -> x2, Pallas kernels: none -> 98.7 us  [the longest x1 53.8 us: attend_back(): pl.pallas_call(attend_back_kernel, grid=(pairs,), in_specs=[column(0), co...]
    ppermute x10 -> x11, starting transfers between devices: 77.7 us -> 18.1 us  [core(): return lax.ppermute(values, 'rep', [(i, i ^ 1) for i in range(self.nr)])]
    convert_element_type x5 -> x0, other arithmetic: 56.9 us -> none  [the longest x4 54.1 us: backward_group(): d_scores_b = (attn_probs * (d_probs - row_inner)).astype(bf16)]
    ppermute x18 -> x21, waiting for transfers between devices: 29.5 us -> 70 us  [along(): lax.ppermute(values, 'shard', [(i, (i + step) % self.ns) for i in range(s...]
  transfers between devices with their start and end apart: 55 -> 62, of which waited for: 14 -> 27; matrix products, arithmetic and copies ran while one was open for 13% -> 13% of each run, Pallas kernels for 25% -> 6%
where the time goes in v2:
time: 756 us; the launch traced here: 750 us
  waiting for transfers between devices  257 us (34%)
  matrix products  181 us (24%)
  Pallas kernels  103 us (14%)
  starting transfers between devices  92.5 us (12%)
  other arithmetic  66.4 us (9%)
  local copies, waits for them, and re-layouts  48.1 us (6%)
    ppermute x30, waiting for transfers between devices, chip(): return lax.ppermute(values, 'rep', [(i, i ^ 2 * k) for i in range(self.nr)])  187 us
    dot_general x4, matrix products, right_trans(): lax.dot_general(left, right, (((1,), (1,)), ((), ())), preferred_element_...  84.7 us
    ppermute x21, waiting for transfers between devices, along(): lax.ppermute(values, 'shard', [(i, (i + step) % self.ns) for i in range(s...  70 us
    pallas_call x1, Pallas kernels, attend_back(): pl.pallas_call(attend_back_kernel, grid=(pairs,), in_specs=[column(0), co...  53.8 us
    dot_general x8, matrix products, left_trans(): lax.dot_general(left, right, (((0,), (0,)), ((), ())), preferred_element_...  49.9 us
    ppermute x21, starting transfers between devices, along(): lax.ppermute(values, 'shard', [(i, (i + step) % self.ns) for i in range(s...  47.4 us
    dot_general x4, matrix products, matmul(): return jnp.dot(left, right, preferred_element_type=f32)  46.3 us
    pallas_call x1, Pallas kernels, attend(): pl.pallas_call(attend_kernel, grid=(pairs,), in_specs=[column(0), column(...  44.9 us
  transfers between devices with their start and end apart: 62, of which 27 were waited for; matrix products, arithmetic and copies ran while one was open for 13% of the time, Pallas kernels for 6%

profile of v2, /device:TPU:1, one launch (start us, length us, event | category | flops | bytes accessed | tf_op | source)
XLA Modules:
  0.0 750.5 jit_solution(4306498321540244716)
XLA Ops:
  8.7 4.2 collective-permute-start.2
  14.4 2.9 collective-permute-start.16
  22.3 3.8 fusion.27
  27.7 5.7 collective-permute-done.1
  40.6 7.1 collective-permute-done.5.refs_4_
  47.7 12.4 %collective-permute-start.14 = (bf16[256,512]{1,0:T(8,128)(2,1)S(1)}, bf16[256,512]{1,0:T(8,128)(2,1)S(1)}, u32[]{:S(2)}, u32[]{:S(2)}) collective-permute-start(bf16[256,512]{1,0:T(8,128)(2,1)S(1)} %dynamic_slice.260), channel_id=1, source_target_pairs={{0,1},{1,2},{2,3},{3,0},{4,5},{5,6},{6,7},{7,4},{8,9},{9,10},{10,1... | collective-permute-start | bytes 786440 | tf_op jit(solution)/shard_map/ppermute | solution.py:184
  60.1 4.1 collective-permute-done.4.refs_3_
  64.2 13.1 %collective-permute-start.8 = (bf16[64,2560]{1,0:T(8,128)(2,1)S(1)}, bf16[64,2560]{1,0:T(8,128)(2,1)S(1)}, u32[]{:S(2)}, u32[]{:S(2)}) collective-permute-start(bf16[64,2560]{1,0:T(8,128)(2,1)S(1)} %pad_maximum_fusion.12), channel_id=1, source_target_pairs={{0,2},{1,3},{2,0},{3,1},{4,6},{5,7},{6,4},{7,5},{8,10},{9,11},{10,... | collective-permute-start | bytes 983048 | tf_op jit(solution)/shard_map/ppermute | solution.py:184
  85.8 20.2 %collective-permute-done.8 = bf16[64,2560]{1,0:T(8,128)(2,1)S(1)} collective-permute-done((bf16[64,2560]{1,0:T(8,128)(2,1)S(1)}, bf16[64,2560]{1,0:T(8,128)(2,1)S(1)}, u32[]{:S(2)}, u32[]{:S(2)}) %collective-permute-start.8) | collective-permute-done | bytes 327712 | tf_op jit(solution)/shard_map/ppermute | solution.py:184
  108.9 7.1 collective-permute-done.18.refs_3_
  118.2 5.8 collective-permute-done.17.refs_2_
  127.7 3.5 collective-permute-start.20
  131.2 14.9 %collective-permute-done.12.refs_5_ = bf16[3,64,2560]{2,1,0:T(8,128)(2,1)S(1)} collective-permute-done((bf16[3,64,2560]{2,1,0:T(8,128)(2,1)S(1)}, bf16[3,64,2560]{2,1,0:T(8,128)(2,1)S(1)}, u32[]{:S(2)}, u32[]{:S(2)}) %collective-permute-start.12) | collective-permute-done | bytes 983072 | tf_op jit(solution)/shard_map/ppermute | solution.py:187
  146.1 12.0 %collective-permute-done.11.refs_4_ = bf16[3,64,2560]{2,1,0:T(8,128)(2,1)S(1)} collective-permute-done((bf16[3,64,2560]{2,1,0:T(8,128)(2,1)S(1)}, bf16[3,64,2560]{2,1,0:T(8,128)(2,1)S(1)}, u32[]{:S(2)}, u32[]{:S(2)}) %collective-permute-start.11) | collective-permute-done | bytes 983072 | tf_op jit(solution)/shard_map/ppermute | solution.py:187
  158.1 8.1 %collective-permute-done.10.refs_3_ = bf16[3,64,2560]{2,1,0:T(8,128)(2,1)S(1)} collective-permute-done((bf16[3,64,2560]{2,1,0:T(8,128)(2,1)S(1)}, bf16[3,64,2560]{2,1,0:T(8,128)(2,1)S(1)}, u32[]{:S(2)}, u32[]{:S(2)}) %collective-permute-start.10) | collective-permute-done | bytes 983072 | tf_op jit(solution)/shard_map/ppermute | solution.py:187
  174.3 9.4 %fusion.6.q_ref.k_ref.v_ref = bf16[1104,3072]{1,0:T(8,128)(2,1)} fusion(bf16[1024,3072]{1,0:T(8,128)(2,1)S(1)} %assemble.3, f32[3072]{0:T(1024)S(1)} %pad_maximum_fusion.15, bf16[1,1,1104,1024]{3,2,1,0:T(8,128)(2,1)S(1)} %copy-done.32, f32[1024]{0:T(1024)S(1)} %bitcast.381, f32[1024]{0:T(1024)S(1)} %bitcast.368, f32[1104]{0:T(1024)S(1)} %fusion.113, ...), kind=kOutput, calls=%fused_computation.21 | convolution fusion | flops 6959333376 | bytes 15364736 | tf_op jit(solution)/shard_map/dot_general | solution.py:28
  183.7 44.9 %attend.1 = (bf16[1104,1024]{1,0:T(8,128)(2,1)}, f32[1104,1024]{1,0:T(8,128)}, bf16[16,1104,1104]{2,1,0:T(8,128)(2,1)}) custom-call(bf16[1104,3072]{1,0:T(8,128)(2,1)} %fusion.6.q_ref.k_ref.v_ref, bf16[1104,3072]{1,0:T(8,128)(2,1)} %fusion.6.q_ref.k_ref.v_ref, bf16[1104,3072]{1,0:T(8,128)(2,1)} %fusion.6.q_ref.k_ref.v_ref), custom_call_target="tpu_custom_call" | custom-call | flops 19969081344 | bytes 52568064 | tf_op jit(solution)/shard_map/attend/pallas_call | solution.py:90
  244.4 6.1 fusion.128
  256.4 14.6 %convolution_add_fusion = f32[1104,4096]{1,0:T(8,128)} fusion(bf16[1104,1024]{1,0:T(8,128)(2,1)} %add_convert_fusion.1, bf16[1024,4096]{1,0:T(8,128)(2,1)S(1)} %copy-done.25, f32[4096]{0:T(1024)S(1)} %bitcast.374), kind=kOutput, calls=%fused_computation.1 | convolution fusion | flops 9265545216 | bytes 28753920 | tf_op jit(solution)/shard_map/dot_general | solution.py:28
  271.1 54.2 %convert_reduce_fusion = (f32[4096]{0:T(1024)}, bf16[1104,4096]{1,0:T(8,128)(2,1)}, f32[1104,4096]{1,0:T(8,128)}) fusion(f32[1104,4096]{1,0:T(8,128)} %convolution_add_fusion, bf16[1104,1024]{1,0:T(8,128)(2,1)S(1)} %copy-done.43, bf16[4096,1024]{1,0:T(8,128)(2,1)S(1)} %assemble.5), kind=kOutput, calls=%fused_computation.3 | convolution fusion | flops 9595645952 | bytes 55885824 | tf_op jit(solution)/shard_map/dot_general | solution.py:36
  325.3 17.1 %multiply_reduce_fusion = (f32[1024]{0:T(1024)S(1)}, f32[1104]{0:T(1024)S(1)}, f32[1024]{0:T(1024)S(1)}, f32[1104,1024]{1,0:T(8,128)S(1)}) fusion(f32[1104,1024]{1,0:T(8,128)S(1)} %copy-done.30, f32[1104]{0:T(1024)S(1)} %copy-done.56, f32[1104]{0:T(1024)S(1)} %copy-done.48, f32[1024]{0:T(1024)S(1)} %bitcast.366, bf16[1104,4096]{1,0:T(8,128)(2,1)} %get-tuple-element.38, ...), kind=kOutput, calls=%fused_computation.51 | convolution fusion | flops 9270064128 | bytes 26502080 | tf_op jit(solution)/shard_map/dot_general | solution.py:36
  343.8 14.4 %multiply_convert_fusion = bf16[1104,4096]{1,0:T(8,128)(2,1)S(1)} fusion(f32[1104,4096]{1,0:T(8,128)} %get-tuple-element.39, f32[1104,4096]{1,0:T(8,128)} %convolution_add_fusion), kind=kLoop, calls=%fused_computation.5 | loop fusion | flops 13565952 | bytes 45219840 | tf_op jit(solution)/shard_map/convert_element_type | solution.py:402
  361.3 3.9 convolution_convert_fusion.2.d_ref
  367.8 7.6 %convolution_convert_fusion = bf16[4096,512]{1,0:T(8,128)(2,1)} fusion(bf16[1104,4096]{1,0:T(8,128)(2,1)S(1)} %multiply_convert_fusion, bf16[1104,1024]{1,0:T(8,128)(2,1)S(1)} %copy-done.43, s32[]{:T(128)S(6)} %select_n.287), kind=kOutput, calls=%fused_computation.24 | convolution fusion | flops 4632608768 | bytes 14368772 | tf_op jit(solution)/shard_map/dot_general | solution.py:32
  375.4 7.2 convolution_convert_fusion.1
  382.6 53.8 %attend_back.1 = (bf16[1104,1024]{1,0:T(8,128)(2,1)}, bf16[1104,1024]{1,0:T(8,128)(2,1)}, bf16[1104,1024]{1,0:T(8,128)(2,1)}) custom-call(bf16[1104,3072]{1,0:T(8,128)(2,1)} %fusion.6.q_ref.k_ref.v_ref, bf16[1104,3072]{1,0:T(8,128)(2,1)} %fusion.6.q_ref.k_ref.v_ref, bf16[1104,3072]{1,0:T(8,128)(2,1)} %fusion.6.q_ref.k_ref.v_ref, ...), custom_call_target="tpu_custom_call" | custom-call | flops 39938162688 | bytes 66134016 | tf_op jit(solution)/shard_map/attend_back/pallas_call | solution.py:156
  442.1 9.5 %fusion.122 = (f32[1024]{0:T(1024)S(1)}, f32[1104]{0:T(1024)S(1)}, f32[1104,1024]{1,0:T(8,128)}) fusion(f32[1024]{0:T(1024)S(1)} %bitcast.369, f32[1104]{0:T(1024)S(1)} %copy-done.46, bf16[1,1,1104,1024]{3,2,1,0:T(8,128)(2,1)S(1)} %copy-done.34, bf16[1104,3072]{1,0:T(8,128)(2,1)S(1)} %constant_dynamic-update-slice_fusion, bf16[1024,3072]{1,0:T(8,128)(2,1)S(1)} %bitcast.306), kind=kOutput, calls=%fused_computation.285 | convolution fusion | flops 6952548352 | bytes 19874432 | tf_op jit(solution)/shard_map/dot_general | solution.py:36
  452.6 16.1 %fusion.37 = bf16[1,1,1104,1024]{3,2,1,0:T(8,128)(2,1)} fusion(f32[1104,1024]{1,0:T(8,128)} %copy-done.29, bf16[1104,4096]{1,0:T(8,128)(2,1)} %copy-done.37, bf16[4096,1024]{1,0:T(8,128)(2,1)} %copy-done, f32[1024]{0:T(1024)S(1)} %bitcast.384, f32[]{:T(128)} %bitcast.1), kind=kOutput, calls=%fused_computation.68 | convolution fusion | flops 9265545216 | bytes 24219652 | tf_op jit(solution)/shard_map/dot_general | solution.py:28
  468.8 10.0 %fusion.31 = bf16[1024,2048]{1,0:T(8,128)(2,1)} fusion(bf16[1104,1024]{1,0:T(8,128)(2,1)} %add_convert_fusion.1, bf16[1104,4096]{1,0:T(8,128)(2,1)} %get-tuple-element.38, s32[]{:T(128)S(6)} %select_n.288), kind=kOutput, calls=%fused_computation.61 | convolution fusion | flops 4632608768 | bytes 10977284 | tf_op jit(solution)/shard_map/dot_general | solution.py:32
  479.6 4.4 fusion.20
  484.0 6.7 add_bitcast_fusion
  490.8 6.9 convolution_convert_fusion.3
  498.3 8.4 %fusion.28 = bf16[1024,2048]{1,0:T(8,128)(2,1)S(1)} fusion(bf16[1104,1024]{1,0:T(8,128)(2,1)S(1)} %copy-done.44, bf16[1104,4096]{1,0:T(8,128)(2,1)} %get-tuple-element.38, s32[]{:T(128)S(6)} %select_n.269), kind=kOutput, calls=%fused_computation.60 | convolution fusion | flops 4632608768 | bytes 10977284 | tf_op jit(solution)/shard_map/dot_general | solution.py:32
  506.8 5.6 convolution_convert_fusion.4
  522.9 16.2 %collective-permute-done.31 = bf16[4,64,1536]{2,1,0:T(8,128)(2,1)S(1)} collective-permute-done((bf16[4,64,1536]{2,1,0:T(8,128)(2,1)S(1)}, bf16[4,64,1536]{2,1,0:T(8,128)(2,1)S(1)}, u32[]{:S(2)}, u32[]{:S(2)}) %collective-permute-start.31) | collective-permute-done | bytes 786464 | tf_op jit(solution)/shard_map/ppermute | solution.py:187
  539.1 16.9 %collective-permute-done.29 = bf16[4,64,1536]{2,1,0:T(8,128)(2,1)S(1)} collective-permute-done((bf16[4,64,1536]{2,1,0:T(8,128)(2,1)S(1)}, bf16[4,64,1536]{2,1,0:T(8,128)(2,1)S(1)}, u32[]{:S(2)}, u32[]{:S(2)}) %collective-permute-start.29) | collective-permute-done | bytes 786464 | tf_op jit(solution)/shard_map/ppermute | solution.py:187
  562.8 3.1 fusion.52
  575.1 8.7 %collective-permute-done.33 = bf16[64,1536]{1,0:T(8,128)(2,1)S(1)} collective-permute-done((bf16[64,1536]{1,0:T(8,128)(2,1)S(1)}, bf16[64,1536]{1,0:T(8,128)(2,1)S(1)}, u32[]{:S(2)}, u32[]{:S(2)}) %collective-permute-start.33) | collective-permute-done | bytes 196640 | tf_op jit(solution)/shard_map/ppermute | solution.py:184
  587.5 18.4 %collective-permute-done.52 = bf16[4,256,512]{2,1,0:T(8,128)(2,1)S(1)} collective-permute-done((bf16[4,256,512]{2,1,0:T(8,128)(2,1)S(1)}, bf16[4,256,512]{2,1,0:T(8,128)(2,1)S(1)}, u32[]{:S(2)}, u32[]{:S(2)}) %collective-permute-start.52) | collective-permute-done | bytes 1048608 | tf_op jit(solution)/shard_map/ppermute | solution.py:187
  606.9 6.1 collective-permute-done.53
  615.8 52.7 %collective-permute-done.42 = bf16[4,64,2560]{2,1,0:T(8,128)(2,1)S(1)} collective-permute-done((bf16[4,64,2560]{2,1,0:T(8,128)(2,1)S(1)}, bf16[4,64,2560]{2,1,0:T(8,128)(2,1)S(1)}, u32[]{:S(2)}, u32[]{:S(2)}) %collective-permute-start.42) | collective-permute-done | bytes 1310752 | tf_op jit(solution)/shard_map/ppermute | solution.py:187
  675.5 2.9 collective-permute-start.46
  678.5 4.2 collective-permute-done.57
  682.7 7.4 collective-permute-start.38
  690.1 10.6 %collective-permute-done.56 = bf16[256,512]{1,0:T(8,128)(2,1)S(1)} collective-permute-done((bf16[256,512]{1,0:T(8,128)(2,1)S(1)}, bf16[256,512]{1,0:T(8,128)(2,1)S(1)}, u32[]{:S(2)}, u32[]{:S(2)}) %collective-permute-start.56) | collective-permute-done | bytes 262176 | tf_op jit(solution)/shard_map/ppermute | solution.py:184
  703.6 18.2 %collective-permute-done.45 = bf16[64,2560]{1,0:T(8,128)(2,1)S(1)} collective-permute-done((bf16[64,2560]{1,0:T(8,128)(2,1)S(1)}, bf16[64,2560]{1,0:T(8,128)(2,1)S(1)}, u32[]{:S(2)}, u32[]{:S(2)}) %collective-permute-start.45) | collective-permute-done | bytes 327712 | tf_op jit(solution)/shard_map/ppermute | solution.py:184
  727.4 3.4 collective-permute-done.49
  730.7 8.8 %collective-permute-done.48 = bf16[64,2560]{1,0:T(8,128)(2,1)S(1)} collective-permute-done((bf16[64,2560]{1,0:T(8,128)(2,1)S(1)}, bf16[64,2560]{1,0:T(8,128)(2,1)S(1)}, u32[]{:S(2)}, u32[]{:S(2)}) %collective-permute-start.48) | collective-permute-done | bytes 327712 | tf_op jit(solution)/shard_map/ppermute | solution.py:187
  (381 shorter events, 143.6 us)
Async XLA Ops:
  8.7 18.0 %collective-permute-start.2 = (bf16[80,1536]{1,0:T(8,128)(2,1)S(1)}, bf16[80,1536]{1,0:T(8,128)(2,1)}, u32[]{:S(2)}, u32[]{:S(2)}) collective-permute-start(bf16[80,1536]{1,0:T(8,128)(2,1)S(1)} %maximum_maximum_fusion), channel_id=1, source_target_pairs={{0,3},{1,0},{2,1},{3,2},{4,7},{5,4},{6,5},{7,6},{8,11},{9,8},{10,9... | collective-permute-start | bytes 737288 | tf_op jit(solution)/shard_map/ppermute | solution.py:184
  12.9 20.4 %collective-permute-start.1 = (bf16[80,1536]{1,0:T(8,128)(2,1)S(1)}, bf16[80,1536]{1,0:T(8,128)(2,1)}, u32[]{:S(2)}, u32[]{:S(2)}) collective-permute-start(bf16[80,1536]{1,0:T(8,128)(2,1)S(1)} %maximum_maximum_fusion), channel_id=1, source_target_pairs={{0,2},{1,3},{2,0},{3,1},{4,6},{5,7},{6,4},{7,5},{8,10},{9,11},{10,... | collective-permute-start | bytes 737288 | tf_op jit(solution)/shard_map/ppermute | solution.py:184
  13.0 21.4 %collective-permute-start = (bf16[80,1536]{1,0:T(8,128)(2,1)S(1)}, bf16[80,1536]{1,0:T(8,128)(2,1)}, u32[]{:S(2)}, u32[]{:S(2)}) collective-permute-start(bf16[80,1536]{1,0:T(8,128)(2,1)S(1)} %maximum_maximum_fusion), channel_id=1, source_target_pairs={{0,1},{1,2},{2,3},{3,0},{4,5},{5,6},{6,7},{7,4},{8,9},{9,10},{10,1... | collective-permute-start | bytes 737288 | tf_op jit(solution)/shard_map/ppermute | solution.py:184
  14.4 63.2 %collective-permute-start.16 = (bf16[256,512]{1,0:T(8,128)(2,1)S(1)}, bf16[256,512]{1,0:T(8,128)(2,1)S(1)}, u32[]{:S(2)}, u32[]{:S(2)}) collective-permute-start(bf16[256,512]{1,0:T(8,128)(2,1)S(1)} %dynamic_slice.260), channel_id=1, source_target_pairs={{0,3},{1,0},{2,1},{3,2},{4,7},{5,4},{6,5},{7,6},{8,11},{9,8},{10,9... | collective-permute-start | bytes 786440 | tf_op jit(solution)/shard_map/ppermute | solution.py:184
  17.3 61.3 %collective-permute-start.15 = (bf16[256,512]{1,0:T(8,128)(2,1)S(1)}, bf16[256,512]{1,0:T(8,128)(2,1)S(1)}, u32[]{:S(2)}, u32[]{:S(2)}) collective-permute-start(bf16[256,512]{1,0:T(8,128)(2,1)S(1)} %dynamic_slice.260), channel_id=1, source_target_pairs={{0,2},{1,3},{2,0},{3,1},{4,6},{5,7},{6,4},{7,5},{8,10},{9,11},{10,... | collective-permute-start | bytes 786440 | tf_op jit(solution)/shard_map/ppermute | solution.py:184
  37.6 26.6 %collective-permute-start.4 = (bf16[3,64,1536]{2,1,0:T(8,128)(2,1)S(1)}, bf16[3,64,1536]{2,1,0:T(8,128)(2,1)S(1)}, u32[]{:S(2)}, u32[]{:S(2)}) collective-permute-start(bf16[3,64,1536]{2,1,0:T(8,128)(2,1)S(1)} %get-tuple-element.89.refs_1_), channel_id=1, source_target_pairs={{0,16},{4,20},{8,24},{12,28},{16,0},{20,4},{24,8},{28,12},{1,17},{... | collective-permute-start | bytes 1769480 | tf_op jit(solution)/shard_map/ppermute | solution.py:187
  37.8 26.4 %collective-permute-start.3 = (bf16[3,64,1536]{2,1,0:T(8,128)(2,1)S(1)}, bf16[3,64,1536]{2,1,0:T(8,128)(2,1)S(1)}, u32[]{:S(2)}, u32[]{:S(2)}) collective-permute-start(bf16[3,64,1536]{2,1,0:T(8,128)(2,1)S(1)} %get-tuple-element.89.refs_1_), channel_id=1, source_target_pairs={{0,8},{4,12},{8,0},{12,4},{16,24},{20,28},{24,16},{28,20},{1,9},{5... | collective-permute-start | bytes 1769480 | tf_op jit(solution)/shard_map/ppermute | solution.py:187
  47.7 30.9 %collective-permute-start.14 = (bf16[256,512]{1,0:T(8,128)(2,1)S(1)}, bf16[256,512]{1,0:T(8,128)(2,1)S(1)}, u32[]{:S(2)}, u32[]{:S(2)}) collective-permute-start(bf16[256,512]{1,0:T(8,128)(2,1)S(1)} %dynamic_slice.260), channel_id=1, source_target_pairs={{0,1},{1,2},{2,3},{3,0},{4,5},{5,6},{6,7},{7,4},{8,9},{9,10},{10,1... | collective-permute-start | bytes 786440 | tf_op jit(solution)/shard_map/ppermute | solution.py:184
  64.2 18.7 %collective-permute-start.9 = (bf16[64,2560]{1,0:T(8,128)(2,1)S(1)}, bf16[64,2560]{1,0:T(8,128)(2,1)S(1)}, u32[]{:S(2)}, u32[]{:S(2)}) collective-permute-start(bf16[64,2560]{1,0:T(8,128)(2,1)S(1)} %pad_maximum_fusion.12), channel_id=1, source_target_pairs={{0,3},{1,0},{2,1},{3,2},{4,7},{5,4},{6,5},{7,6},{8,11},{9,8},{10,9... | collective-permute-start | bytes 983048 | tf_op jit(solution)/shard_map/ppermute | solution.py:184
  64.2 41.8 %collective-permute-start.8 = (bf16[64,2560]{1,0:T(8,128)(2,1)S(1)}, bf16[64,2560]{1,0:T(8,128)(2,1)S(1)}, u32[]{:S(2)}, u32[]{:S(2)}) collective-permute-start(bf16[64,2560]{1,0:T(8,128)(2,1)S(1)} %pad_maximum_fusion.12), channel_id=1, source_target_pairs={{0,2},{1,3},{2,0},{3,1},{4,6},{5,7},{6,4},{7,5},{8,10},{9,11},{10,... | collective-permute-start | bytes 983048 | tf_op jit(solution)/shard_map/ppermute | solution.py:184
  77.6 92.8 %collective-permute-start.6 = (bf16[4,3,64,1536]{3,2,1,0:T(8,128)(2,1)S(1)}, bf16[4,3,64,1536]{3,2,1,0:T(8,128)(2,1)S(1)}, u32[]{:S(2)}, u32[]{:S(2)}) collective-permute-start(bf16[4,3,64,1536]{3,2,1,0:T(8,128)(2,1)S(1)} %pad_maximum_fusion.2), channel_id=1, source_target_pairs={{0,4},{4,0},{8,12},{12,8},{16,20},{20,16},{24,28},{28,24},{1,5},{5... | collective-permute-start | bytes 7077896 | tf_op jit(solution)/shard_map/ppermute | solution.py:190
  78.7 30.0 %collective-permute-start.19 = (bf16[3,256,512]{2,1,0:T(8,128)(2,1)S(1)}, bf16[3,256,512]{2,1,0:T(8,128)(2,1)S(1)}, u32[]{:S(2)}, u32[]{:S(2)}) collective-permute-start(bf16[3,256,512]{2,1,0:T(8,128)(2,1)S(1)} %get-tuple-element.87.refs_1_), channel_id=1, source_target_pairs={{0,24},{4,28},{8,16},{12,20},{16,8},{20,12},{24,0},{28,4},{1,25},{... | collective-permute-start | bytes 2359304 | tf_op jit(solution)/shard_map/ppermute | solution.py:187
  80.1 35.9 %collective-permute-start.18 = (bf16[3,256,512]{2,1,0:T(8,128)(2,1)S(1)}, bf16[3,256,512]{2,1,0:T(8,128)(2,1)S(1)}, u32[]{:S(2)}, u32[]{:S(2)}) collective-permute-start(bf16[3,256,512]{2,1,0:T(8,128)(2,1)S(1)} %get-tuple-element.87.refs_1_), channel_id=1, source_target_pairs={{0,16},{4,20},{8,24},{12,28},{16,0},{20,4},{24,8},{28,12},{1,17},{... | collective-permute-start | bytes 2359304 | tf_op jit(solution)/shard_map/ppermute | solution.py:187
  82.9 24.3 %collective-permute-start.7 = (bf16[64,2560]{1,0:T(8,128)(2,1)S(1)}, bf16[64,2560]{1,0:T(8,128)(2,1)S(1)}, u32[]{:S(2)}, u32[]{:S(2)}) collective-permute-start(bf16[64,2560]{1,0:T(8,128)(2,1)S(1)} %pad_maximum_fusion.12), channel_id=1, source_target_pairs={{0,1},{1,2},{2,3},{3,0},{4,5},{5,6},{6,7},{7,4},{8,9},{9,10},{10,1... | collective-permute-start | bytes 983048 | tf_op jit(solution)/shard_map/ppermute | solution.py:184
  106.0 18.0 %collective-permute-start.17 = (bf16[3,256,512]{2,1,0:T(8,128)(2,1)S(1)}, bf16[3,256,512]{2,1,0:T(8,128)(2,1)S(1)}, u32[]{:S(2)}, u32[]{:S(2)}) collective-permute-start(bf16[3,256,512]{2,1,0:T(8,128)(2,1)S(1)} %get-tuple-element.87.refs_1_), channel_id=1, source_target_pairs={{0,8},{4,12},{8,0},{12,4},{16,24},{20,28},{24,16},{28,20},{1,9},{5... | collective-permute-start | bytes 2359304 | tf_op jit(solution)/shard_map/ppermute | solution.py:187
  107.4 38.7 %collective-permute-start.12 = (bf16[3,64,2560]{2,1,0:T(8,128)(2,1)S(1)}, bf16[3,64,2560]{2,1,0:T(8,128)(2,1)S(1)}, u32[]{:S(2)}, u32[]{:S(2)}) collective-permute-start(bf16[3,64,2560]{2,1,0:T(8,128)(2,1)S(1)} %get-tuple-element.82.refs_2_), channel_id=1, source_target_pairs={{0,24},{4,28},{8,16},{12,20},{16,8},{20,12},{24,0},{28,4},{1,25},{... | collective-permute-start | bytes 2949128 | tf_op jit(solution)/shard_map/ppermute | solution.py:187
  108.7 49.5 %collective-permute-start.11 = (bf16[3,64,2560]{2,1,0:T(8,128)(2,1)S(1)}, bf16[3,64,2560]{2,1,0:T(8,128)(2,1)S(1)}, u32[]{:S(2)}, u32[]{:S(2)}) collective-permute-start(bf16[3,64,2560]{2,1,0:T(8,128)(2,1)S(1)} %get-tuple-element.82.refs_2_), channel_id=1, source_target_pairs={{0,16},{4,20},{8,24},{12,28},{16,0},{20,4},{24,8},{28,12},{1,17},{... | collective-permute-start | bytes 2949128 | tf_op jit(solution)/shard_map/ppermute | solution.py:187
  116.0 50.2 %collective-permute-start.10 = (bf16[3,64,2560]{2,1,0:T(8,128)(2,1)S(1)}, bf16[3,64,2560]{2,1,0:T(8,128)(2,1)S(1)}, u32[]{:S(2)}, u32[]{:S(2)}) collective-permute-start(bf16[3,64,2560]{2,1,0:T(8,128)(2,1)S(1)} %get-tuple-element.82.refs_2_), channel_id=1, source_target_pairs={{0,8},{4,12},{8,0},{12,4},{16,24},{20,28},{24,16},{28,20},{1,9},{5... | collective-permute-start | bytes 2949128 | tf_op jit(solution)/shard_map/ppermute | solution.py:187
  127.7 100.9 %collective-permute-start.20 = (bf16[4,3,256,512]{3,2,1,0:T(8,128)(2,1)}, bf16[4,3,256,512]{3,2,1,0:T(8,128)(2,1)S(1)}, u32[]{:S(2)}, u32[]{:S(2)}) collective-permute-start(bf16[4,3,256,512]{3,2,1,0:T(8,128)(2,1)} %pad_maximum_fusion.1), channel_id=1, source_target_pairs={{0,4},{4,0},{8,12},{12,8},{16,20},{20,16},{24,28},{28,24},{1,5},{5... | collective-permute-start | bytes 9437192 | tf_op jit(solution)/shard_map/ppermute | solution.py:190
  168.5 71.1 %collective-permute-start.13 = (bf16[4,3,64,2560]{3,2,1,0:T(8,128)(2,1)}, bf16[4,3,64,2560]{3,2,1,0:T(8,128)(2,1)S(1)}, u32[]{:S(2)}, u32[]{:S(2)}) collective-permute-start(bf16[4,3,64,2560]{3,2,1,0:T(8,128)(2,1)} %pad_maximum_fusion), channel_id=1, source_target_pairs={{0,4},{4,0},{8,12},{12,8},{16,20},{20,16},{24,28},{28,24},{1,5},{5... | collective-permute-start | bytes 11796488 | tf_op jit(solution)/shard_map/ppermute | solution.py:190
  468.8 53.6 %collective-permute-start.39 = (bf16[1024,512]{1,0:T(8,128)(2,1)}, bf16[1024,512]{1,0:T(8,128)(2,1)S(1)}, u32[]{:S(2)}, u32[]{:S(2)}) collective-permute-start(bf16[1024,512]{1,0:T(8,128)(2,1)} %convolution_convert_fusion.5), channel_id=1, source_target_pairs={{0,4},{4,0},{8,12},{12,8},{16,20},{20,16},{24,28},{28,24},{1,5},{5... | collective-permute-start | bytes 3145736 | tf_op jit(solution)/shard_map/ppermute | solution.py:190
  478.9 82.9 %collective-permute-start.40 = (bf16[1024,2048]{1,0:T(8,128)(2,1)}, bf16[1024,2048]{1,0:T(8,128)(2,1)}, u32[]{:S(2)}, u32[]{:S(2)}) collective-permute-start(bf16[1024,2048]{1,0:T(8,128)(2,1)} %fusion.31), channel_id=1, source_target_pairs={{0,4},{4,0},{8,12},{12,8},{16,20},{20,16},{24,28},{28,24},{1,5},{5... | collective-permute-start | bytes 12582920 | tf_op jit(solution)/shard_map/ppermute | solution.py:190
  479.4 78.7 %collective-permute-start.51 = (bf16[4096,512]{1,0:T(8,128)(2,1)}, bf16[4096,512]{1,0:T(8,128)(2,1)}, u32[]{:S(2)}, u32[]{:S(2)}) collective-permute-start(bf16[4096,512]{1,0:T(8,128)(2,1)} %convolution_convert_fusion), channel_id=1, source_target_pairs={{0,4},{4,0},{8,12},{12,8},{16,20},{20,16},{24,28},{28,24},{1,5},{5... | collective-permute-start | bytes 12582920 | tf_op jit(solution)/shard_map/ppermute | solution.py:190
  497.7 17.6 %collective-permute-start.28 = (bf16[1024,1536]{1,0:T(8,128)(2,1)S(1)}, bf16[1024,1536]{1,0:T(8,128)(2,1)S(1)}, u32[]{:S(2)}, u32[]{:S(2)}) collective-permute-start(bf16[1024,1536]{1,0:T(8,128)(2,1)S(1)} %convolution_convert_fusion.3), channel_id=1, source_target_pairs={{0,4},{4,0},{8,12},{12,8},{16,20},{20,16},{24,28},{28,24},{1,5},{5... | collective-permute-start | bytes 9437192 | tf_op jit(solution)/shard_map/ppermute | solution.py:190
  519.8 19.3 %collective-permute-start.31 = (bf16[4,64,1536]{2,1,0:T(8,128)(2,1)S(1)}, bf16[4,64,1536]{2,1,0:T(8,128)(2,1)S(1)}, u32[]{:S(2)}, u32[]{:S(2)}) collective-permute-start(bf16[4,64,1536]{2,1,0:T(8,128)(2,1)S(1)} %fusion.60), channel_id=1, source_target_pairs={{0,24},{4,28},{8,16},{12,20},{16,8},{20,12},{24,0},{28,4},{1,25},{... | collective-permute-start | bytes 2359304 | tf_op jit(solution)/shard_map/ppermute | solution.py:187
  521.2 34.8 %collective-permute-start.29 = (bf16[4,64,1536]{2,1,0:T(8,128)(2,1)S(1)}, bf16[4,64,1536]{2,1,0:T(8,128)(2,1)S(1)}, u32[]{:S(2)}, u32[]{:S(2)}) collective-permute-start(bf16[4,64,1536]{2,1,0:T(8,128)(2,1)S(1)} %get-tuple-element.49), channel_id=1, source_target_pairs={{0,8},{4,12},{8,0},{12,4},{16,24},{20,28},{24,16},{28,20},{1,9},{5... | collective-permute-start | bytes 2359304 | tf_op jit(solution)/shard_map/ppermute | solution.py:187
  522.4 35.2 %collective-permute-start.30 = (bf16[4,64,1536]{2,1,0:T(8,128)(2,1)S(1)}, bf16[4,64,1536]{2,1,0:T(8,128)(2,1)S(1)}, u32[]{:S(2)}, u32[]{:S(2)}) collective-permute-start(bf16[4,64,1536]{2,1,0:T(8,128)(2,1)S(1)} %get-tuple-element.50), channel_id=1, source_target_pairs={{0,16},{4,20},{8,24},{12,28},{16,0},{20,4},{24,8},{28,12},{1,17},{... | collective-permute-start | bytes 2359304 | tf_op jit(solution)/shard_map/ppermute | solution.py:187
  539.1 30.8 %collective-permute-start.27 = (f32[3072]{0:T(1024)S(1)}, f32[3072]{0:T(1024)S(1)}, u32[]{:S(2)}, u32[]{:S(2)}) collective-permute-start(f32[3072]{0:T(1024)S(1)} %bitcast.380), channel_id=1, source_target_pairs={{0,3},{1,0},{2,1},{3,2},{4,7},{5,4},{6,5},{7,6},{8,11},{9,8},{10,9... | collective-permute-start | bytes 36872 | tf_op jit(solution)/shard_map/ppermute | solution.py:184
  556.0 15.3 %collective-permute-start.25 = (f32[3072]{0:T(1024)S(1)}, f32[3072]{0:T(1024)S(1)}, u32[]{:S(2)}, u32[]{:S(2)}) collective-permute-start(f32[3072]{0:T(1024)S(1)} %bitcast.379), channel_id=1, source_target_pairs={{0,1},{1,2},{2,3},{3,0},{4,5},{5,6},{6,7},{7,4},{8,9},{9,10},{10,1... | collective-permute-start | bytes 36872 | tf_op jit(solution)/shard_map/ppermute | solution.py:184
  561.7 23.3 %collective-permute-start.54 = (bf16[4,256,512]{2,1,0:T(8,128)(2,1)S(1)}, bf16[4,256,512]{2,1,0:T(8,128)(2,1)S(1)}, u32[]{:S(2)}, u32[]{:S(2)}) collective-permute-start(bf16[4,256,512]{2,1,0:T(8,128)(2,1)S(1)} %fusion.57), channel_id=1, source_target_pairs={{0,24},{4,28},{8,16},{12,20},{16,8},{20,12},{24,0},{28,4},{1,25},{... | collective-permute-start | bytes 3145736 | tf_op jit(solution)/shard_map/ppermute | solution.py:187
  571.9 34.0 %collective-permute-start.52 = (bf16[4,256,512]{2,1,0:T(8,128)(2,1)S(1)}, bf16[4,256,512]{2,1,0:T(8,128)(2,1)S(1)}, u32[]{:S(2)}, u32[]{:S(2)}) collective-permute-start(bf16[4,256,512]{2,1,0:T(8,128)(2,1)S(1)} %get-tuple-element.44), channel_id=1, source_target_pairs={{0,8},{4,12},{8,0},{12,4},{16,24},{20,28},{24,16},{28,20},{1,9},{5... | collective-permute-start | bytes 3145736 | tf_op jit(solution)/shard_map/ppermute | solution.py:187
  572.7 40.3 %collective-permute-start.53 = (bf16[4,256,512]{2,1,0:T(8,128)(2,1)S(1)}, bf16[4,256,512]{2,1,0:T(8,128)(2,1)S(1)}, u32[]{:S(2)}, u32[]{:S(2)}) collective-permute-start(bf16[4,256,512]{2,1,0:T(8,128)(2,1)S(1)} %get-tuple-element.45), channel_id=1, source_target_pairs={{0,16},{4,20},{8,24},{12,28},{16,0},{20,4},{24,8},{28,12},{1,17},{... | collective-permute-start | bytes 3145736 | tf_op jit(solution)/shard_map/ppermute | solution.py:187
  574.8 93.7 %collective-permute-start.42 = (bf16[4,64,2560]{2,1,0:T(8,128)(2,1)S(1)}, bf16[4,64,2560]{2,1,0:T(8,128)(2,1)S(1)}, u32[]{:S(2)}, u32[]{:S(2)}) collective-permute-start(bf16[4,64,2560]{2,1,0:T(8,128)(2,1)S(1)} %pad_maximum_fusion.4), channel_id=1, source_target_pairs={{0,16},{4,20},{8,24},{12,28},{16,0},{20,4},{24,8},{28,12},{1,17},{... | collective-permute-start | bytes 3932168 | tf_op jit(solution)/shard_map/ppermute | solution.py:187
  583.8 84.8 %collective-permute-start.43 = (bf16[4,64,2560]{2,1,0:T(8,128)(2,1)S(1)}, bf16[4,64,2560]{2,1,0:T(8,128)(2,1)S(1)}, u32[]{:S(2)}, u32[]{:S(2)}) collective-permute-start(bf16[4,64,2560]{2,1,0:T(8,128)(2,1)S(1)} %pad_maximum_fusion.5), channel_id=1, source_target_pairs={{0,24},{4,28},{8,16},{12,20},{16,8},{20,12},{24,0},{28,4},{1,25},{... | collective-permute-start | bytes 3932168 | tf_op jit(solution)/shard_map/ppermute | solution.py:187
  585.0 84.6 %collective-permute-start.41 = (bf16[4,64,2560]{2,1,0:T(8,128)(2,1)S(1)}, bf16[4,64,2560]{2,1,0:T(8,128)(2,1)S(1)}, u32[]{:S(2)}, u32[]{:S(2)}) collective-permute-start(bf16[4,64,2560]{2,1,0:T(8,128)(2,1)S(1)} %pad_maximum_fusion.3), channel_id=1, source_target_pairs={{0,8},{4,12},{8,0},{12,4},{16,24},{20,28},{24,16},{28,20},{1,9},{5... | collective-permute-start | bytes 3932168 | tf_op jit(solution)/shard_map/ppermute | solution.py:187
  605.9 66.6 %collective-permute-start.37 = (bf16[64,1536]{1,0:T(8,128)(2,1)S(1)}, bf16[64,1536]{1,0:T(8,128)(2,1)S(1)}, u32[]{:S(2)}, u32[]{:S(2)}) collective-permute-start(bf16[64,1536]{1,0:T(8,128)(2,1)S(1)} %fusion.93), channel_id=1, source_target_pairs={{0,24},{4,28},{8,16},{12,20},{16,8},{20,12},{24,0},{28,4},{1,25},{... | collective-permute-start | bytes 589832 | tf_op jit(solution)/shard_map/ppermute | solution.py:187
  613.0 61.8 %collective-permute-start.36 = (bf16[64,1536]{1,0:T(8,128)(2,1)S(1)}, bf16[64,1536]{1,0:T(8,128)(2,1)S(1)}, u32[]{:S(2)}, u32[]{:S(2)}) collective-permute-start(bf16[64,1536]{1,0:T(8,128)(2,1)S(1)} %fusion.93), channel_id=1, source_target_pairs={{0,16},{4,20},{8,24},{12,28},{16,0},{20,4},{24,8},{28,12},{1,17},{... | collective-permute-start | bytes 589832 | tf_op jit(solution)/shard_map/ppermute | solution.py:187
  672.5 28.2 %collective-permute-start.56 = (bf16[256,512]{1,0:T(8,128)(2,1)S(1)}, bf16[256,512]{1,0:T(8,128)(2,1)S(1)}, u32[]{:S(2)}, u32[]{:S(2)}) collective-permute-start(bf16[256,512]{1,0:T(8,128)(2,1)S(1)} %get-tuple-element.80), channel_id=1, source_target_pairs={{0,2},{1,3},{2,0},{3,1},{4,6},{5,7},{6,4},{7,5},{8,10},{9,11},{10,... | collective-permute-start | bytes 786440 | tf_op jit(solution)/shard_map/ppermute | solution.py:184
  674.9 27.3 %collective-permute-start.44 = (bf16[64,2560]{1,0:T(8,128)(2,1)S(1)}, bf16[64,2560]{1,0:T(8,128)(2,1)S(1)}, u32[]{:S(2)}, u32[]{:S(2)}) collective-permute-start(bf16[64,2560]{1,0:T(8,128)(2,1)S(1)} %get-tuple-element.75), channel_id=1, source_target_pairs={{0,1},{1,2},{2,3},{3,0},{4,5},{5,6},{6,7},{7,4},{8,9},{9,10},{10,1... | collective-permute-start | bytes 983048 | tf_op jit(solution)/shard_map/ppermute | solution.py:184
  675.5 26.9 %collective-permute-start.46 = (bf16[64,2560]{1,0:T(8,128)(2,1)S(1)}, bf16[64,2560]{1,0:T(8,128)(2,1)S(1)}, u32[]{:S(2)}, u32[]{:S(2)}) collective-permute-start(bf16[64,2560]{1,0:T(8,128)(2,1)S(1)} %get-tuple-element.76), channel_id=1, source_target_pairs={{0,3},{1,0},{2,1},{3,2},{4,7},{5,4},{6,5},{7,6},{8,11},{9,8},{10,9... | collective-permute-start | bytes 983048 | tf_op jit(solution)/shard_map/ppermute | solution.py:184
  678.4 43.4 %collective-permute-start.45 = (bf16[64,2560]{1,0:T(8,128)(2,1)S(1)}, bf16[64,2560]{1,0:T(8,128)(2,1)S(1)}, u32[]{:S(2)}, u32[]{:S(2)}) collective-permute-start(bf16[64,2560]{1,0:T(8,128)(2,1)S(1)} %get-tuple-element.77), channel_id=1, source_target_pairs={{0,2},{1,3},{2,0},{3,1},{4,6},{5,7},{6,4},{7,5},{8,10},{9,11},{10,... | collective-permute-start | bytes 983048 | tf_op jit(solution)/shard_map/ppermute | solution.py:184
  682.7 40.5 %collective-permute-start.38 = (bf16[4,64,1536]{2,1,0:T(8,128)(2,1)S(1)}, bf16[4,64,1536]{2,1,0:T(8,128)(2,1)S(1)}, u32[]{:S(2)}, u32[]{:S(2)}) collective-permute-start(bf16[4,64,1536]{2,1,0:T(8,128)(2,1)S(1)} %pad_maximum_fusion.10), channel_id=1, source_target_pairs={{0,4},{4,0},{8,12},{12,8},{16,20},{20,16},{24,28},{28,24},{1,5},{5... | collective-permute-start | bytes 2359304 | tf_op jit(solution)/shard_map/ppermute | solution.py:190
  700.9 22.6 %collective-permute-start.60 = (bf16[256,512]{1,0:T(8,128)(2,1)S(1)}, bf16[256,512]{1,0:T(8,128)(2,1)S(1)}, u32[]{:S(2)}, u32[]{:S(2)}) collective-permute-start(bf16[256,512]{1,0:T(8,128)(2,1)S(1)} %fusion.82), channel_id=1, source_target_pairs={{0,24},{4,28},{8,16},{12,20},{16,8},{20,12},{24,0},{28,4},{1,25},{... | collective-permute-start | bytes 786440 | tf_op jit(solution)/shard_map/ppermute | solution.py:187
  702.1 22.8 %collective-permute-start.59 = (bf16[256,512]{1,0:T(8,128)(2,1)S(1)}, bf16[256,512]{1,0:T(8,128)(2,1)S(1)}, u32[]{:S(2)}, u32[]{:S(2)}) collective-permute-start(bf16[256,512]{1,0:T(8,128)(2,1)S(1)} %fusion.82), channel_id=1, source_target_pairs={{0,16},{4,20},{8,24},{12,28},{16,0},{20,4},{24,8},{28,12},{1,17},{... | collective-permute-start | bytes 786440 | tf_op jit(solution)/shard_map/ppermute | solution.py:187
  702.4 22.5 %collective-permute-start.58 = (bf16[256,512]{1,0:T(8,128)(2,1)S(1)}, bf16[256,512]{1,0:T(8,128)(2,1)S(1)}, u32[]{:S(2)}, u32[]{:S(2)}) collective-permute-start(bf16[256,512]{1,0:T(8,128)(2,1)S(1)} %fusion.82), channel_id=1, source_target_pairs={{0,8},{4,12},{8,0},{12,4},{16,24},{20,28},{24,16},{28,20},{1,9},{5... | collective-permute-start | bytes 786440 | tf_op jit(solution)/shard_map/ppermute | solution.py:187
  723.2 16.4 %collective-permute-start.48 = (bf16[64,2560]{1,0:T(8,128)(2,1)S(1)}, bf16[64,2560]{1,0:T(8,128)(2,1)S(1)}, u32[]{:S(2)}, u32[]{:S(2)}) collective-permute-start(bf16[64,2560]{1,0:T(8,128)(2,1)S(1)} %fusion.63), channel_id=1, source_target_pairs={{0,16},{4,20},{8,24},{12,28},{16,0},{20,4},{24,8},{28,12},{1,17},{... | collective-permute-start | bytes 983048 | tf_op jit(solution)/shard_map/ppermute | solution.py:187
  723.5 16.1 %collective-permute-start.47 = (bf16[64,2560]{1,0:T(8,128)(2,1)S(1)}, bf16[64,2560]{1,0:T(8,128)(2,1)S(1)}, u32[]{:S(2)}, u32[]{:S(2)}) collective-permute-start(bf16[64,2560]{1,0:T(8,128)(2,1)S(1)} %fusion.63), channel_id=1, source_target_pairs={{0,8},{4,12},{8,0},{12,4},{16,24},{20,28},{24,16},{28,20},{1,9},{5... | collective-permute-start | bytes 983048 | tf_op jit(solution)/shard_map/ppermute | solution.py:187
  725.0 17.5 %collective-permute-start.61 = (bf16[4,256,512]{2,1,0:T(8,128)(2,1)S(1)}, bf16[4,256,512]{2,1,0:T(8,128)(2,1)S(1)}, u32[]{:S(2)}, u32[]{:S(2)}) collective-permute-start(bf16[4,256,512]{2,1,0:T(8,128)(2,1)S(1)} %pad_maximum_fusion.7), channel_id=1, source_target_pairs={{0,4},{4,0},{8,12},{12,8},{16,20},{20,16},{24,28},{28,24},{1,5},{5... | collective-permute-start | bytes 3145736 | tf_op jit(solution)/shard_map/ppermute | solution.py:190
  (87 other events, 1690.7 us)

commit v3 on v2

v3 whole, which is shorter than its diff:
```python
import functools

import jax
import jax.numpy as jnp
from jax import lax
from jax.experimental import pallas as pl
from jax.experimental.pallas import tpu as pltpu
from jax.sharding import PartitionSpec as P

HDIM = 64

eps = 1e-06
bf16 = jnp.bfloat16
HINT = pl.CostEstimate(flops=1, transcendentals=0, bytes_accessed=1)
f32 = jnp.float32


def layer_norm(values, gain, shift):
    centre = values - jnp.mean(values, -1, keepdims=True)
    spread = jnp.mean(centre * centre, -1, keepdims=True)
    return centre * lax.rsqrt(spread + eps) * gain + shift


def matmul(left, right):
    return jnp.dot(left, right, preferred_element_type=f32)


LOG2E = 1.4426950408889634


def contract(left, right, left_dim, right_dim):
    return lax.dot_general(
        left, right, (((left_dim,), (right_dim,)), ((), ())), preferred_element_type=f32
    )


def query_blocks(rows, tile=256):
    return [(i, min(tile, rows - i)) for i in range(0, rows, tile)]


def head_mask(head, rows, dtype):
    lane = lax.broadcasted_iota(jnp.int32, (rows, 2 * HDIM), 1)
    return (lane // HDIM == head).astype(dtype)


def attend_kernel(q_ref, k_ref, v_ref, o_ref, inv_ref, p_ref):
    rows = q_ref.shape[0]
    factor = HDIM ** (-0.5) * LOG2E
    keys = k_ref[...]
    values = v_ref[...]
    ones = jnp.ones(values.shape, bf16)
    for start, n in query_blocks(rows):
        queries = q_ref[start : start + n, :]
        mixed = inverse = None
        for head in range(2):
            mask = head_mask(head, rows, bf16)
            scores = contract(keys * mask, queries, 1, 1)
            largest = jnp.max(scores, axis=0, keepdims=True)
            probs = jnp.exp2((scores - largest) * factor).astype(bf16)
            p_ref[head, :, start : start + n] = probs
            both = contract(probs, jnp.concatenate([values * mask, ones], 1), 0, 0)
            inv = 1.0 / both[:, 2 * HDIM :]
            part = both[:, : 2 * HDIM] * inv
            share = head_mask(head, n, f32) * inv
            mixed = part if mixed is None else mixed + part
            inverse = share if inverse is None else inverse + share
        o_ref[start : start + n, :] = mixed.astype(bf16)
        inv_ref[start : start + n, :] = inverse


def whole(count):
    return [pl.BlockSpec(memory_space=pl.ANY)] * count


def attend(qkv, first, last, before=None):
    rows, wide = qkv.shape
    width = wide // 3
    pairs = width // (2 * HDIM)
    count = last - first

    def column(offset):
        return pl.BlockSpec((rows, 2 * HDIM), lambda j: (0, offset + first + j))

    def kernel(*refs):
        attend_kernel(*refs[:3], *refs[-3:])

    given = () if before is None else tuple(before)
    return pl.pallas_call(
        kernel,
        grid=(count,),
        in_specs=[column(0), column(pairs), column(2 * pairs)] + whole(len(given)),
        out_specs=[
            column(0),
            column(0),
            pl.BlockSpec((2, rows, rows), lambda j: (first + j, 0, 0)),
        ],
        out_shape=[
            jax.ShapeDtypeStruct((rows, width), bf16),
            jax.ShapeDtypeStruct((rows, width), f32),
            jax.ShapeDtypeStruct((2 * pairs, rows, rows), bf16),
        ],
        input_output_aliases={3 + i: i for i in range(len(given))},
        compiler_params=pltpu.CompilerParams(vmem_limit_bytes=56 * 1024 * 1024),
        cost_estimate=HINT,
        name="attend",
    )(qkv, qkv, qkv, *given)


def attend_back_kernel(
    q_ref, k_ref, v_ref, d_ref, o_ref, inv_ref, p_ref, out_ref, sum_ref
):
    rows = q_ref.shape[0]
    scale = HDIM ** (-0.5)
    queries = q_ref[...]
    keys = k_ref[...]
    values = v_ref[...]
    grads = (d_ref[...].astype(f32) * inv_ref[...]).astype(bf16)
    product = grads.astype(f32) * o_ref[...].astype(f32)
    lane = lax.broadcasted_iota(jnp.int32, (rows, 2 * HDIM), 1)
    blocks = query_blocks(rows)
    d_queries = [None] * len(blocks)
    d_keys = d_values = None
    for head in range(2):
        mask = head_mask(head, rows, bf16)
        inner = -jnp.sum(jnp.where(lane // HDIM == head, product, 0.0), 1, keepdims=True)
        high = inner.astype(bf16)
        low = (inner - high.astype(f32)).astype(bf16)
        tail = jnp.where(lane == 0, high, jnp.where(lane == 1, low, jnp.zeros_like(low)))
        grads_wide = jnp.concatenate([grads, tail], 1)
        values_wide = jnp.concatenate([values * mask, (lane < 2).astype(bf16)], 1)
        keys_h, queries_h, grads_h = keys * mask, queries * mask, grads * mask
        for b, (start, n) in enumerate(blocks):
            d_probs = contract(values_wide, grads_wide[start : start + n, :], 1, 1)
            probs = p_ref[head, :, start : start + n]
            d_scores = probs * d_probs.astype(bf16)
            to_values = contract(probs, grads_h[start : start + n, :], 1, 0)
            to_keys = contract(d_scores, queries_h[start : start + n, :], 1, 0)
            to_queries = contract(d_scores, keys_h, 0, 0)
            d_values = to_values if d_values is None else d_values + to_values
            d_keys = to_keys if d_keys is None else d_keys + to_keys
            d_queries[b] = to_queries if d_queries[b] is None else d_queries[b] + to_queries
    d_values = d_values.astype(bf16)
    out_ref[1] = (d_keys * scale).astype(bf16)
    out_ref[2] = d_values
    sums = jnp.zeros((1, 2 * HDIM), f32)
    for b, (start, n) in enumerate(blocks):
        block = (d_queries[b] * scale).astype(bf16)
        out_ref[0, start : start + n, :] = block
        sums = sums + jnp.sum(block.astype(f32), 0, keepdims=True)
    sum_ref[0] = sums
    sum_ref[1] = jnp.sum(d_values.astype(f32), 0, keepdims=True)


def attend_back(qkv, grad, attended, inverse, probs, first, last, before=None):
    rows, wide = qkv.shape
    width = wide // 3
    pairs = width // (2 * HDIM)
    count = last - first

    def column(offset):
        return pl.BlockSpec((rows, 2 * HDIM), lambda j: (0, offset + first + j))

    def kernel(*refs):
        attend_back_kernel(*refs[:7], *refs[-2:])

    given = () if before is None else tuple(before)
    return pl.pallas_call(
        kernel,
        grid=(count,),
        in_specs=[column(0), column(pairs), column(2 * pairs)]
        + [column(0)] * 3
        + [pl.BlockSpec((2, rows, rows), lambda j: (first + j, 0, 0))]
        + whole(len(given)),
        out_specs=[
            pl.BlockSpec((3, rows, 2 * HDIM), lambda j: (0, 0, first + j)),
            pl.BlockSpec((2, 1, 2 * HDIM), lambda j: (0, 0, first + j)),
        ],
        out_shape=[
            jax.ShapeDtypeStruct((3, rows, width), bf16),
            jax.ShapeDtypeStruct((2, 1, width), f32),
        ],
        input_output_aliases={7 + i: i for i in range(len(given))},
        compiler_params=pltpu.CompilerParams(vmem_limit_bytes=56 * 1024 * 1024),
        cost_estimate=HINT,
        name="attend_back",
    )(qkv, qkv, qkv, grad, attended, inverse, probs, *given)


def gelu_pair(values):
    bell = jnp.exp2(values * values * (-0.5 * LOG2E))
    t = 1.0 / (1.0 + 0.23164189 * jnp.abs(values))
    poly = 0.5307027145 * t - 0.7265760135
    poly = poly * t + 0.7107068705
    poly = poly * t - 0.142248368
    poly = poly * t + 0.127414796
    tail = poly * t * bell
    area = jnp.where(values >= 0, 1.0 - tail, tail)
    return values * area, area + values * bell * 0.3989422804014327


def feed_forward_kernel(
    h_ref, dm_ref, up_ref, bias_ref, down_ref, alive_ref, last_ref, y0_ref, g0_ref,
    y_ref, g_ref, down_away, down_home, up_away, up_home, gb_ref,
    act_ref, dp_ref, y_acc, g_acc,
):
    j = pl.program_id(0)

    @pl.when(j == 0)
    def _():
        if g0_ref is None:
            y_acc[...] = y0_ref[...] + last_ref[...]
            g_acc[...] = jnp.zeros_like(g_acc)
        else:
            y_acc[...] = y0_ref[...]
            g_acc[...] = g0_ref[...]

    rows = h_ref.shape[0]
    up, down = up_ref[...], down_ref[...]
    bias = bias_ref[...]
    chunk = 368
    for start in range(0, rows, chunk):
        r = slice(start, min(start + chunk, rows))
        act, slope = gelu_pair(contract(h_ref[r, :], up, 1, 0) + bias)
        act = act.astype(bf16)
        act_ref[r, :] = act
        d_pre = (contract(dm_ref[r, :], down, 1, 1) * slope).astype(bf16)
        dp_ref[r, :] = d_pre
        y_acc[r, :] += contract(act, down, 1, 0)
        g_acc[r, :] += contract(d_pre, up, 1, 1)
    gb_ref[...] = jnp.sum(dp_ref[...].astype(f32), 0, keepdims=True)[None]
    first_core = lax.axis_index("rep") % 2 == 0
    for left, right, away, home in (
        (act_ref, dm_ref, down_away, down_home),
        (h_ref, dp_ref, up_away, up_home),
    ):
        grad = contract(left[...], right[...], 0, 0)
        half = grad.shape[1] // 2
        low, high = grad[:, :half], grad[:, half:]
        away[...] = jnp.where(first_core, high, low).reshape(away.shape).astype(bf16)
        home[...] = jnp.where(first_core, low, high).reshape(home.shape).astype(bf16)

    @pl.when(j == pl.num_programs(0) - 1)
    def _():
        y = y_acc[...]
        y_ref[...] = y if g0_ref is None else (alive_ref[0] * y).astype(bf16)
        g_ref[...] = g_acc[...]


def feed_forward(links, hidden, d_out, up, bias, down, alive, last_bias, y0, g0, part):
    ns, nq = links.ns, links.nq
    rows, width = hidden.shape
    block = up.shape[1] // (2 * ns)
    rq = width // (ns * nq)
    per = width // block
    wide = dict(pipeline_mode=pl.Buffered(1))

    def full():
        return pl.BlockSpec((rows, width), lambda j: (0, 0), **wide)

    def kernel(*refs):
        refs = list(refs)
        if g0 is None:
            refs.insert(8, None)
        feed_forward_kernel(*refs)

    down_spec = pl.BlockSpec((1, block, width // 2), lambda j: (j, 0, 0))
    up_spec = pl.BlockSpec((ns, nq, 1, rq, block // 2), lambda j: (0, 0, j // per, 0, j % per))
    down_shape = jax.ShapeDtypeStruct((ns, block, width // 2), bf16)
    up_shape = jax.ShapeDtypeStruct((ns, nq, ns // per, rq, width // 2), bf16)
    sums = jax.ShapeDtypeStruct((rows, width), f32)
    given = (y0,) if g0 is None else (y0, g0)
    y, g, d_away, d_home, u_away, u_home, gb = pl.pallas_call(
        kernel,
        grid=(ns,),
        in_specs=[
            full(),
            full(),
            pl.BlockSpec((width, block), lambda j: (0, 2 * j + part)),
            pl.BlockSpec((1, block), lambda j: (0, 2 * j + part)),
            pl.BlockSpec((block, width), lambda j: (2 * j + part, 0)),
            pl.BlockSpec(memory_space=pltpu.SMEM),
            pl.BlockSpec((1, width), lambda j: (0, 0)),
        ]
        + [full() for _ in given],
        out_specs=[
            full(),
            full(),
            down_spec,
            down_spec,
            up_spec,
            up_spec,
            pl.BlockSpec((1, 1, block), lambda j: (j, 0, 0)),
        ],
        out_shape=[
            sums if g0 is None else jax.ShapeDtypeStruct((rows, width), bf16),
            sums,
            down_shape,
            down_shape,
            up_shape,
            up_shape,
            jax.ShapeDtypeStruct((ns, 1, block), f32),
        ],
        scratch_shapes=[
            pltpu.VMEM((rows, block), bf16),
            pltpu.VMEM((rows, block), bf16),
            pltpu.VMEM((rows, width), f32),
            pltpu.VMEM((rows, width), f32),
        ],
        compiler_params=pltpu.CompilerParams(vmem_limit_bytes=58 * 1024 * 1024),
        cost_estimate=HINT,
        name="feed_forward",
    )(hidden, d_out, up, bias, down, alive, last_bias, *given)

    def pieces(down_grad, up_grad):
        lanes = width // 2
        return [
            down_grad.reshape(ns, nq, block // nq, lanes),
            up_grad.reshape(ns, nq, ns // per * rq, lanes),
        ]

    return y, g, pieces(d_away, u_away), pieces(d_home, u_home), gb.reshape(ns, block)


def grad_kernel(left_ref, right_ref, away_ref, home_ref):
    grad = contract(left_ref[...], right_ref[0], 0, 0)
    half = grad.shape[1] // 2
    low, high = grad[:, :half], grad[:, half:]
    first_core = lax.axis_index("rep") % 2 == 0
    away_ref[...] = jnp.where(first_core, high, low).reshape(away_ref.shape).astype(bf16)
    home_ref[...] = jnp.where(first_core, low, high).reshape(home_ref.shape).astype(bf16)


def weight_grads(links, left, rights):
    ns, nq = links.ns, links.nq
    rows, width = left.shape
    count, _, wide = rights.shape
    rq = width // (ns * nq)
    spec = pl.BlockSpec((ns, nq, 1, rq, wide // 2), lambda i: (0, 0, i, 0, 0))
    shape = jax.ShapeDtypeStruct((ns, nq, count, rq, wide // 2), bf16)
    away, home = pl.pallas_call(
        grad_kernel,
        grid=(count,),
        in_specs=[
            pl.BlockSpec((rows, width), lambda i: (0, 0)),
            pl.BlockSpec((1, rows, wide), lambda i: (i, 0, 0)),
        ],
        out_specs=[spec, spec],
        out_shape=[shape, shape],
        compiler_params=pltpu.CompilerParams(vmem_limit_bytes=48 * 1024 * 1024),
        cost_estimate=HINT,
        name="weight_grads",
    )(left, rights)
    flat = (ns, nq, count * rq, wide // 2)
    return [away.reshape(flat)], [home.reshape(flat)]


def row_block(rows):
    return 368 if rows % 368 == 0 else rows


def normal(values):
    centre = values - jnp.mean(values, -1, keepdims=True)
    scale = lax.rsqrt(jnp.mean(centre * centre, -1, keepdims=True) + eps)
    return centre * scale, scale


def normal_back(unit, scale, grad):
    inner = jnp.mean(grad * unit, -1, keepdims=True)
    return scale * (grad - jnp.mean(grad, -1, keepdims=True) - unit * inner)


def column_sum(values):
    return jnp.sum(values, 0, keepdims=True)


def middle_kernel(x_ref, att_ref, w_ref, bias_ref, gain_ref, shift_ref, mid_ref, h_ref):
    mid = x_ref[...].astype(f32) + contract(att_ref[...], w_ref[...], 1, 0) + bias_ref[...]
    mid_ref[...] = mid
    unit, _ = normal(mid)
    h_ref[...] = (unit * gain_ref[...] + shift_ref[...]).astype(bf16)


def middle_of(tokens, attended, weight, bias, gain, shift):
    rows, width = tokens.shape
    n = row_block(rows)
    block = pl.BlockSpec((n, width), lambda i: (i, 0))
    line = pl.BlockSpec((1, width), lambda i: (0, 0))
    return pl.pallas_call(
        middle_kernel,
        grid=(rows // n,),
        in_specs=[block, block, pl.BlockSpec(weight.shape, lambda i: (0, 0)), line, line, line],
        out_specs=[block, block],
        out_shape=[
            jax.ShapeDtypeStruct((rows, width), f32),
            jax.ShapeDtypeStruct((rows, width), bf16),
        ],
        compiler_params=pltpu.CompilerParams(vmem_limit_bytes=48 * 1024 * 1024),
        cost_estimate=HINT,
        name="middle",
    )(tokens, attended, weight, bias, gain, shift)


def middle_back_kernel(
    g_ref, mid_ref, dm_ref, att_ref, w_ref, gain_ref,
    d_mid_ref, d_att_ref, away_ref, home_ref, sum_ref, acc_ref,
):
    i = pl.program_id(0)

    @pl.when(i == 0)
    def _():
        acc_ref[...] = jnp.zeros_like(acc_ref)
        sum_ref[...] = jnp.zeros_like(sum_ref)

    unit, scale = normal(mid_ref[...])
    g = g_ref[...]
    d_out = dm_ref[...].astype(f32)
    d_mid = d_out + normal_back(unit, scale, g * gain_ref[...])
    d_mid_ref[...] = d_mid
    d_proj = d_mid.astype(bf16)
    d_att_ref[...] = contract(d_proj, w_ref[...], 1, 1).astype(bf16)
    acc_ref[...] += contract(att_ref[...], d_proj, 0, 0)
    sum_ref[0:1, :] += column_sum(g * unit)
    sum_ref[1:2, :] += column_sum(g)
    sum_ref[2:3, :] += column_sum(d_proj.astype(f32))
    sum_ref[3:4, :] += column_sum(d_out)

    @pl.when(i == pl.num_programs(0) - 1)
    def _():
        grad = acc_ref[...]
        half = grad.shape[1] // 2
        low, high = grad[:, :half], grad[:, half:]
        first_core = lax.axis_index("rep") % 2 == 0
        away_ref[...] = jnp.where(first_core, high, low).reshape(away_ref.shape).astype(bf16)
        home_ref[...] = jnp.where(first_core, low, high).reshape(home_ref.shape).astype(bf16)


def middle_back(links, grad, middle, d_out, attended, weight, gain):
    ns, nq = links.ns, links.nq
    rows, width = middle.shape
    n = row_block(rows)
    block = pl.BlockSpec((n, width), lambda i: (i, 0))
    pieces = (ns, nq, width // (ns * nq), width // 2)
    whole_piece = pl.BlockSpec(pieces, lambda i: (0, 0, 0, 0))
    return pl.pallas_call(
        middle_back_kernel,
        grid=(rows // n,),
        in_specs=[block] * 4
        + [
            pl.BlockSpec(weight.shape, lambda i: (0, 0)),
            pl.BlockSpec((1, width), lambda i: (0, 0)),
        ],
        out_specs=[
            block,
            block,
            whole_piece,
            whole_piece,
            pl.BlockSpec((8, width), lambda i: (0, 0)),
        ],
        out_shape=[
            jax.ShapeDtypeStruct((rows, width), f32),
            jax.ShapeDtypeStruct((rows, width), bf16),
            jax.ShapeDtypeStruct(pieces, bf16),
            jax.ShapeDtypeStruct(pieces, bf16),
            jax.ShapeDtypeStruct((8, width), f32),
        ],
        scratch_shapes=[pltpu.VMEM((width, width), f32)],
        compiler_params=pltpu.CompilerParams(vmem_limit_bytes=48 * 1024 * 1024),
        cost_estimate=HINT,
        name="middle_back",
    )(grad, middle, d_out, attended, weight, gain)


def entry_back_kernel(d_ref, w_ref, x_ref, d_mid_ref, gain_ref, out_ref, sum_ref):
    @pl.when(pl.program_id(0) == 0)
    def _():
        sum_ref[...] = jnp.zeros_like(sum_ref)

    width = x_ref.shape[1]
    g = contract(d_ref[0], w_ref[:, :width], 1, 1)
    for t in range(1, 3):
        g = g + contract(d_ref[t], w_ref[:, t * width : (t + 1) * width], 1, 1)
    unit, scale = normal(x_ref[...].astype(f32))
    out_ref[...] = d_mid_ref[...] + normal_back(unit, scale, g * gain_ref[...])
    sum_ref[0:1, :] += column_sum(g * unit)
    sum_ref[1:2, :] += column_sum(g)


def entry_back(grads, weight, tokens, d_mid, gain):
    rows, width = tokens.shape
    n = row_block(rows)
    block = pl.BlockSpec((n, width), lambda i: (i, 0))
    return pl.pallas_call(
        entry_back_kernel,
        grid=(rows // n,),
        in_specs=[
            pl.BlockSpec((3, n, width), lambda i: (0, i, 0)),
            pl.BlockSpec(weight.shape, lambda i: (0, 0), pipeline_mode=pl.Buffered(1)),
            block,
            block,
            pl.BlockSpec((1, width), lambda i: (0, 0)),
        ],
        out_specs=[block, pl.BlockSpec((8, width), lambda i: (0, 0))],
        out_shape=[
            jax.ShapeDtypeStruct((rows, width), f32),
            jax.ShapeDtypeStruct((8, width), f32),
        ],
        compiler_params=pltpu.CompilerParams(vmem_limit_bytes=48 * 1024 * 1024),
        cost_estimate=HINT,
        name="entry_back",
    )(grads, weight, tokens, d_mid, gain)


class Links:
    def __init__(self, mesh):
        self.ns = mesh.shape["shard"]
        self.nr = mesh.shape["rep"]
        self.nq = self.nr // 2
        self.bits = self.nq.bit_length() - 1
        assert 1 << self.bits == self.nq

    def here(self):
        rep = lax.axis_index("rep")
        return lax.axis_index("shard"), rep // 2, rep % 2

    def along(self, values, step):
        return lax.ppermute(values, "shard", [(i, (i + step) % self.ns) for i in range(self.ns)])

    def chip(self, values, k):
        return lax.ppermute(values, "rep", [(i, i ^ (2 * k)) for i in range(self.nr)])

    def core(self, values):
        return lax.ppermute(values, "rep", [(i, i ^ 1) for i in range(self.nr)])


def meet(*values):
    return lax.optimization_barrier(values)


def tie(values, others):
    return lax.optimization_barrier((values, others))[0]


def piece_of(links, weights):
    _, q, c = links.here()
    parts = []
    for w in weights:
        rq, half = w.shape[0] // links.nq, w.shape[1] // 2
        parts.append(lax.dynamic_slice(w, (q * rq, c * half), (rq, half)))
    return jnp.concatenate(parts, 1)


def pack(links, weight, small, line):
    rq = weight.shape[0] // links.nq
    total = sum(v.shape[0] for v in small)
    fits = all(sum(v.shape[0] for v in part) == line for part in (small[:6], small[6:]))
    if rq % 16 or line % 128 or not fits:
        filled = jnp.concatenate(small + (jnp.zeros((-total % line,), bf16),)).reshape(-1, line)
        filler = jnp.zeros((16 - filled.shape[0], line), bf16)
        return jnp.concatenate([piece_of(links, [weight]), filled, filler])

    def kernel(w_ref, *refs):
        *vectors, out_ref, sem = refs
        rep = lax.axis_index("rep")
        q, c = rep // 2, rep % 2
        rows = pl.ds(pl.multiple_of(q * rq, rq), rq)
        copy = pltpu.make_async_copy(
            w_ref.at[rows, pl.ds(pl.multiple_of(c * line, line), line)], out_ref.at[:rq], sem
        )
        copy.start()
        lines = [[], []]
        for at, ref in enumerate(vectors):
            lines[at // 6].append(ref[...].astype(f32).reshape(1, -1))
        block = [jnp.concatenate(x, 1) for x in lines]
        row = lax.broadcasted_iota(jnp.int32, (16, line), 0)
        filled = jnp.where(row == 0, block[0], jnp.where(row == 1, block[1], 0.0))
        out_ref[rq:, :] = filled.astype(bf16)
        copy.wait()

    return pl.pallas_call(
        kernel,
        in_specs=whole(1) + [pl.BlockSpec(memory_space=pltpu.VMEM)] * len(small),
        out_specs=pl.BlockSpec(memory_space=pltpu.VMEM),
        out_shape=jax.ShapeDtypeStruct((rq + 16, line), bf16),
        scratch_shapes=[pltpu.SemaphoreType.DMA(())],
        cost_estimate=HINT,
        name="pack",
    )(weight, *small)


def gather_along(links, piece):
    return [links.along(piece, s) for s in range(1, links.ns)]


def lanes_of(links, values, part):
    n = values.shape[-1] // links.bits
    return values[..., part * n : (part + 1) * n]


def gather_step(links, held, step):
    out = []
    for part, pieces in enumerate(held):
        bit = 1 << ((part + step) % links.bits)
        known = sorted(pieces)
        sent = jnp.stack([pieces[k] for k in known])
        got = links.chip(sent, bit)
        out.append((bit, known, got))
    return out


def gather_merge(links, held, got):
    merged = []
    for pieces, (bit, known, values) in zip(held, got):
        more = dict(pieces)
        for i, k in enumerate(known):
            more[k ^ bit] = values[i]
        merged.append(more)
    return merged


def assemble(links, weights, got_mine, got_mate):
    ns, nq, bits = links.ns, links.nq, links.bits
    rows = [w.shape[0] for w in weights]
    cols = [w.shape[1] for w in weights]
    rq = [r // nq for r in rows]
    total = sum(cols) // 2
    lanes = total // bits
    n = len(weights)
    per_side = len(got_mine)

    def kernel(*refs):
        w_refs = refs[:n]
        sides = (refs[n : n + per_side], refs[n + per_side : n + 2 * per_side])
        out_refs = refs[n + 2 * per_side : n + 2 * per_side + n]
        sem = refs[-1]
        z = lax.axis_index("shard")
        rep = lax.axis_index("rep")
        q, c = rep // 2, rep % 2
        copies = []

        def go(src, dst):
            copy = pltpu.make_async_copy(src, dst, sem.at[len(copies)])
            copy.start()
            copies.append(copy)

        for i in range(n):
            go(w_refs[i], out_refs[i].at[pl.ds(pl.multiple_of(z * rows[i], rows[i]), rows[i]), :])
        for side, parts in enumerate(sides):
            core = c if side == 0 else 1 - c
            base = 0
            for i in range(n):
                half = cols[i] // 2

                def place(source, k, s, low, high):
                    zs = lax.rem(z + (ns - s), ns)
                    at = pl.ds(pl.multiple_of(zs * rows[i] + (q ^ k) * rq[i], rq[i]), rq[i])
                    to = pl.ds(pl.multiple_of(core * half + (low - base), 128), high - low)
                    go(source, out_refs[i].at[at, to])

                for s in range(1, ns):
                    own = parts[0].at[s - 1, :, pl.ds(base, half)]
                    place(own, 0, s, base, base + half)
                    at = 1
                    for step in range(bits):
                        for part in range(bits):
                            known = [0]
                            for t in range(step):
                                bit = 1 << ((part + t) % bits)
                                known = known + [k ^ bit for k in known]
                            known = sorted(known)
                            bit = 1 << ((part + step) % bits)
                            low = max(base, part * lanes)
                            high = min(base + half, (part + 1) * lanes)
                            if low < high:
                                cut = pl.ds(low - part * lanes, high - low)
                                for j, k in enumerate(known):
                                    source = parts[at].at[j, s - 1, :, cut]
                                    place(source, k ^ bit, s, low, high)
                            at += 1
                base += half
        for copy in copies:
            copy.wait()

    pieces = 0
    base = 0
    for i in range(n):
        half = cols[i] // 2
        for part in range(bits):
            if max(base, part * lanes) < min(base + half, (part + 1) * lanes):
                pieces += nq - 1
        pieces += 1
        base += half
    count = n + 2 * (ns - 1) * pieces
    return pl.pallas_call(
        kernel,
        out_shape=[jax.ShapeDtypeStruct((ns * r, c), bf16) for r, c in zip(rows, cols)],
        in_specs=whole(n + 2 * per_side),
        out_specs=[pl.BlockSpec(memory_space=pltpu.VMEM)] * n,
        scratch_shapes=[pltpu.SemaphoreType.DMA((count,))],
        compiler_params=pltpu.CompilerParams(vmem_limit_bytes=32 * 1024 * 1024),
        cost_estimate=HINT,
        name="assemble",
    )(*weights, *got_mine, *got_mate)


class Gather:
    def __init__(self, links, weights):
        self.links, self.weights = links, weights

    def start(self, own):
        self.own = own
        self.held = [{0: lanes_of(self.links, own, p)} for p in range(self.links.bits)]
        self.mine = [own]
        self.mate = [self.links.core(own)]
        self.done = 0
        return own

    def step(self, after=None):
        held = self.held if after is None else tie(self.held, after)
        got = gather_step(self.links, held, self.done)
        self.held = gather_merge(self.links, held, got)
        self.done += 1
        for _, _, values in got:
            self.mine.append(values)
            self.mate.append(self.links.core(values))
        return self.mine[-1]

    def full(self):
        while self.done < self.links.bits:
            self.step()
        return assemble(self.links, self.weights, self.mine, self.mate)


class Scatter:
    def __init__(self, links, sent, kept):
        self.links = links
        self.rows = [s.shape[2] for s in sent]
        self.lanes = sent[0].shape[3]
        self.got = [links.core(s) for s in sent]
        self.kept = kept
        self.done = 0
        total = sum(self.rows)
        if links.bits == 2 and all(n % 32 == 0 for n in self.rows):
            first = []
            second = []
            taken = 0
            for i, n in enumerate(self.rows):
                cut = min(n, total // 2 - taken)
                if len(self.rows) == 3:
                    cut = (n, 0, n // 2)[i]
                taken += cut
                if cut:
                    first.append((i, 0, cut))
                if cut < n:
                    second.append((i, cut, n))
            self.parts = [first, second]
        else:
            self.parts = None

    def plan(self):
        if self.parts is None:
            return [(i, 0, n) for i, n in enumerate(self.rows)]
        return self.parts[0] + self.parts[1]

    def blocks(self):
        links = self.links
        ns, nq, lanes = links.ns, links.nq, self.lanes
        n = len(self.rows)
        sizes = [sum(high - low for _, low, high in part) for part in self.parts]

        def kernel(*refs):
            kept, got, outs = refs[:n], refs[n : 2 * n], refs[2 * n :]
            q = lax.axis_index("rep") // 2
            for p, part in enumerate(self.parts):
                bit = 1 << p
                for at, k in enumerate([k for k in range(nq) if not k & bit]):
                    for out, chip in ((outs[2 * p], k ^ bit), (outs[2 * p + 1], k)):
                        base = 0
                        for i, low, high in part:
                            a = kept[i][0, q ^ chip, low:high, :].astype(f32)
                            b = got[i][0, q ^ chip, low:high, :].astype(f32)
                            out[at, 0, base : base + high - low, :] = (a + b).astype(bf16)
                            base += high - low

        return pl.pallas_call(
            kernel,
            grid=(ns,),
            in_specs=[pl.BlockSpec((1, nq, r, lanes), lambda j: (j, 0, 0, 0)) for r in self.rows] * 2,
            out_specs=[
                pl.BlockSpec((nq // 2, 1, r, lanes), lambda j: (0, j, 0, 0))
                for r in sizes
                for _ in range(2)
            ],
            out_shape=[
                jax.ShapeDtypeStruct((nq // 2, ns, r, lanes), bf16) for r in sizes for _ in range(2)
            ],
            compiler_params=pltpu.CompilerParams(vmem_limit_bytes=32 * 1024 * 1024),
            cost_estimate=HINT,
            name="core_sums",
        )(*self.kept, *self.got)

    def prepare(self):
        links = self.links
        if self.done == 0 and self.parts is not None:
            s0, k0, s1, k1 = self.blocks()
            self.buffers = [s0, s1]
            self.stay = [[0, 2], [0, 1]]
            self.held = [{0: k0[0], 2: k0[1]}, {0: k1[0], 1: k1[1]}]
            return self.buffers
        if self.done == 0:
            _, q, _ = links.here()
            total = sum(self.rows)
            size = total // links.bits
            self.held = []
            both = [a.astype(f32) + b.astype(f32) for a, b in zip(self.kept, self.got)]
            both = jnp.concatenate(both, 2).astype(bf16)
            for p in range(links.bits):
                high = (p + 1) * size if p < links.bits - 1 else total
                cut = both[:, :, p * size : high]
                self.held.append(
                    {k: lax.dynamic_index_in_dim(cut, q ^ k, 1, False) for k in range(links.nq)}
                )
        self.buffers = []
        self.stay = []
        for part, pieces in enumerate(self.held):
            bit = 1 << ((part + self.done) % links.bits)
            stay = [k for k in sorted(pieces) if not k & bit]
            self.stay.append(stay)
            self.buffers.append(jnp.stack([pieces[k ^ bit] for k in stay]))
        return self.buffers

    def send(self):
        links = self.links
        last = self.done == links.bits - 1 and self.parts is not None
        out = []
        for part, (pieces, buffer, stay) in enumerate(zip(self.held, self.buffers, self.stay)):
            got = links.chip(buffer, 1 << ((part + self.done) % links.bits))
            if last:
                out.append((pieces[0], got[0]))
                continue
            out.append(
                {
                    k: (pieces[k].astype(f32) + got[i].astype(f32)).astype(bf16)
                    for i, k in enumerate(stay)
                }
            )
        self.held = out
        self.done += 1

    def prepare_along(self):
        links = self.links
        ns = links.ns
        if self.parts is not None:
            lanes = self.lanes
            total = sum(self.rows)

            def kernel(a0, b0, a1, b1, *outs):
                z = lax.axis_index("shard")
                for s, out in enumerate(outs):
                    at = lax.rem(z + s, ns)
                    base = 0
                    for a, b in ((a0, b0), (a1, b1)):
                        n = a.shape[1]
                        out[base : base + n, :] = (a[at].astype(f32) + b[at].astype(f32)).astype(bf16)
                        base += n

            pairs = [x for pair in self.held for x in pair]
            self.buffers = pl.pallas_call(
                kernel,
                in_specs=[pl.BlockSpec(memory_space=pltpu.VMEM)] * 4,
                out_specs=[pl.BlockSpec(memory_space=pltpu.VMEM)] * ns,
                out_shape=[jax.ShapeDtypeStruct((total, lanes), bf16)] * ns,
                compiler_params=pltpu.CompilerParams(vmem_limit_bytes=32 * 1024 * 1024),
                cost_estimate=HINT,
                name="chip_sums",
            )(*pairs)
            return self.buffers
        z, _, _ = links.here()
        total = jnp.concatenate([p[0] for p in self.held], 1)
        self.buffers = [
            lax.dynamic_index_in_dim(total, (z + s) % ns, 0, False) for s in range(ns)
        ]
        return self.buffers

    def send_along(self):
        final = self.buffers[0].astype(f32)
        for s in range(1, self.links.ns):
            final = final + self.links.along(self.buffers[s], s).astype(f32)
        self.final = final.astype(bf16)
        return self.final

    def spread(self, after=None):
        links = self.links
        final = self.final if after is None else tie(self.final, after)
        others = [links.chip(final, k) for k in range(1, links.nq)]
        self.mine = [final] + others
        self.mate = [links.core(v) for v in self.mine]
        return self.mate

    def owned(self):
        links = self.links
        _, q, c = links.here()
        mine, mate = jnp.stack(self.mine), jnp.stack(self.mate)
        both = jnp.stack([jnp.where(c == 0, mine, mate), jnp.where(c == 0, mate, mine)])
        ordered = [lax.dynamic_index_in_dim(both, q ^ j, 1) for j in range(links.nq)]
        full = jnp.concatenate(ordered, 1).astype(f32)
        outs = []
        base = 0
        for n in self.rows:
            outs.append(full[:, :, base : base + n])
            base += n
        return outs


def owned_by_kernel(links, scatters, shapes, place):
    sides = [x for s in scatters for x in s.mine + s.mate]
    nq = links.nq

    def kernel(*refs):
        ins, outs = refs[: len(sides)], refs[len(sides) :]
        rep = lax.axis_index("rep")
        q, first_core = rep // 2, rep % 2 == 0
        for at, scatter in enumerate(scatters):
            refs_here = ins[2 * nq * at : 2 * nq * (at + 1)]
            for k in range(nq):
                mine, mate = refs_here[k], refs_here[nq + k]
                chip = q ^ k
                base = 0
                for i, low, high in scatter.plan():
                    for lo, hi, left, right, out, factor, offset, zero, one in place(at, i):
                        a, b = max(lo, low), min(hi, high)
                        if a >= b:
                            continue
                        r = slice(base + a - low, base + b - low)
                        x, y = mine[r, left:right].astype(f32), mate[r, left:right].astype(f32)
                        row = pl.multiple_of(chip * factor + (offset + a - lo), 8)
                        rows = pl.ds(row, b - a)
                        wide = right - left
                        outs[out][rows, zero : zero + wide] = jnp.where(first_core, x, y)
                        outs[out][rows, one : one + wide] = jnp.where(first_core, y, x)
                    base += high - low

    return pl.pallas_call(
        kernel,
        in_specs=[pl.BlockSpec(memory_space=pltpu.VMEM)] * len(sides),
        out_specs=[pl.BlockSpec(memory_space=pltpu.VMEM)] * len(shapes),
        out_shape=[jax.ShapeDtypeStruct(s, f32) for s in shapes],
        compiler_params=pltpu.CompilerParams(vmem_limit_bytes=48 * 1024 * 1024),
        cost_estimate=HINT,
        name="owned",
    )(*sides)


def owned_feed_forward(links, scatter_1, scatter_2, w_up, w_down, w_out):
    lanes = scatter_1.lanes
    block = w_down.shape[0] // 2
    if scatter_1.parts is None or scatter_2.parts is None:
        down_first, up_first = scatter_1.owned()
        down_second, up_second, o_wout = scatter_2.owned()
        o_wdown = jnp.concatenate([side_by_side(down_first, 1), side_by_side(down_second, 1)])
        return o_wdown, up_columns(links, up_first, up_second), side_by_side(o_wout, 1)
    down_rows, up_rows = scatter_1.rows
    rq = w_up.shape[0] // links.nq
    half = block // 2

    def place(at, i):
        if i == 0:
            return [(0, down_rows, 0, lanes, 0, down_rows, at * block, 0, lanes)]
        if i == 2:
            return [(0, rq, 0, lanes, 2, rq, 0, 0, lanes)]
        out = []
        per = lanes // half
        for g in range(up_rows // rq):
            for p in range(per):
                column = (g * per + p) * 2 * block + at * block
                out.append(
                    (g * rq, (g + 1) * rq, p * half, (p + 1) * half, 1, rq, 0, column, column + half)
                )
        return out

    return owned_by_kernel(
        links, [scatter_1, scatter_2], [w_down.shape, w_up.shape, w_out.shape], place
    )


def owned_qkv(links, scatter, w_qkv):
    if scatter.parts is None:
        (grad,) = scatter.owned()
        return side_by_side(grad, 3)
    lanes = scatter.lanes
    rq = w_qkv.shape[0] // links.nq

    def place(at, i):
        return [
            (t * rq, (t + 1) * rq, 0, lanes, 0, rq, 0, 2 * t * lanes, (2 * t + 1) * lanes)
            for t in range(3)
        ]

    return owned_by_kernel(links, [scatter], [w_qkv.shape], place)[0]


def up_columns(links, first, second):
    cores, chips, _, lanes = first.shape
    both = jnp.stack([first, second])
    groups = first.shape[2] * chips * links.ns // (2 * lanes)
    rows = first.shape[2] // groups
    per = links.ns // groups
    both = both.reshape(2, cores, chips, groups, rows, per, lanes // per)
    return both.transpose(2, 4, 3, 5, 0, 1, 6).reshape(chips * rows, -1)


def side_by_side(grad, groups):
    cores, chips, rows, lanes = grad.shape
    grad = grad.reshape(cores, chips, groups, rows // groups, lanes)
    return grad.transpose(1, 3, 2, 0, 4).reshape(chips * rows // groups, groups * cores * lanes)


def total_of(links, lines):
    z, _, _ = links.here()
    lines = lines + links.core(lines)
    crossed = [links.chip(lines, k) for k in range(1, links.nq)]
    for x in crossed:
        lines = lines + x
    moved = [
        links.along(lax.dynamic_index_in_dim(lines, (z + s) % links.ns, 0, False), s)
        for s in range(1, links.ns)
    ]
    line = lax.dynamic_index_in_dim(lines, z, 0, False)
    for x in moved:
        line = line + x
    return line


def body(
    links,
    inputs,
    counts,
    ln1_gain,
    ln1_shift,
    w_qkv,
    qv_bias,
    w_out,
    out_bias,
    ln2_gain,
    ln2_shift,
    w_up,
    up_bias,
    w_down,
    down_bias,
    cotangent,
):
    ns = links.ns
    slots = inputs.shape[1]
    seq_len = inputs.shape[2]
    width = inputs.shape[3]
    n_rows = slots * seq_len
    z = lax.axis_index("shard")

    small = (ln1_gain, ln1_shift, out_bias, ln2_gain, ln2_shift, down_bias, qv_bias, up_bias)
    sizes = [v.shape[0] for v in small]
    line = w_qkv.shape[1] // 2
    n_lines = -(-sum(sizes) // line)

    gather_a, gather_b, gather_c = (
        Gather(links, [w_qkv]),
        Gather(links, [w_out, w_up]),
        Gather(links, [w_down]),
    )
    n = w_qkv.shape[0] // links.nq
    packed_a = pack(links, w_qkv, small, line)
    got = gather_along(links, packed_a)
    got_small = [g[n : n + n_lines] for g in got]
    own_a = gather_a.start(jnp.stack([g[:n] for g in got]))
    got_b = gather_along(links, tie(piece_of(links, [w_out, w_up]), own_a))
    while gather_a.done < links.bits:
        last_a = gather_a.step()
    (full_qkv,) = gather_a.full()
    all_small = jnp.stack([packed_a[n : n + n_lines]] + got_small).reshape(ns, -1)
    all_small = jnp.concatenate(
        [lax.dynamic_index_in_dim(all_small, (z - j) % ns, 0) for j in range(ns)]
    )
    full_small = []
    base = 0
    for n in sizes:
        full_small.append(all_small[:, base : base + n].reshape(-1).astype(f32))
        base += n
    full_g1, full_s1, full_bout, full_g2, full_s2, full_bdown, bias_f, full_bup = full_small
    first_slot = z * slots
    alive = (jnp.arange(slots, dtype=jnp.int32) + first_slot < counts[0]).astype(f32)
    assert slots == 1
    d_out_b = jnp.where(alive[0] > 0, cotangent, jnp.zeros_like(cotangent)).reshape(n_rows, width)
    tokens_b = inputs.reshape(n_rows, width)
    hidden_one_b = layer_norm(tokens_b.astype(f32), full_g1, full_s1).astype(bf16)
    projected = matmul(hidden_one_b, full_qkv)
    none = jnp.zeros((width,), f32)
    qkv_bias = jnp.concatenate([bias_f[:width], none, bias_f[width:]])
    qkv_b = (projected + qkv_bias).astype(bf16)
    pairs = width // (2 * HDIM)
    cuts = (0, pairs // 4, pairs * 3 // 4, pairs)
    qkv_b, got_b = meet(qkv_b, got_b)
    got_c = gather_along(links, tie(piece_of(links, [w_down]), got_b))
    gather_b.start(jnp.stack(got_b))
    gather_b.step()
    kept = attend(qkv_b, cuts[0], cuts[1])
    kept, gather_b.held = meet(kept, gather_b.held)
    while gather_b.done < links.bits:
        gather_b.step()
    kept = attend(qkv_b, cuts[1], cuts[2], kept)
    kept, gather_b.mine, got_c = meet(kept, gather_b.mine, got_c)
    gather_c.start(jnp.stack(got_c))
    while gather_c.done < links.bits - 1:
        gather_c.step()
    kept = attend(qkv_b, cuts[2], cuts[3], kept)
    kept, gather_c.held = meet(kept, gather_c.held)
    gather_c.step()
    attended_b, inverse, probs_b = kept
    full_wout, full_wup = gather_b.full()
    gain_two = full_g2[None]
    middle, hidden_two_b = middle_of(
        tokens_b, attended_b, full_wout, full_bout[None], gain_two, full_s2[None]
    )
    middle, gather_c.mine = meet(middle, gather_c.mine)
    (full_wdown,) = gather_c.full()
    bias_up = full_bup[None]
    last_bias = full_bdown[None]
    y, g, away, home, gb_first = feed_forward(
        links, hidden_two_b, d_out_b, full_wup, bias_up, full_wdown, alive, last_bias, middle, None, 0
    )
    scatter_1 = Scatter(links, away, home)
    output, g, away, home, gb_second = feed_forward(
        links, hidden_two_b, d_out_b, full_wup, bias_up, full_wdown, alive, last_bias, y, g, 1
    )
    output = output.reshape(inputs.shape)
    grad_bup = jnp.concatenate([gb_first, gb_second], 1)
    g, scatter_1.kept = meet(g, scatter_1.kept)
    g, scatter_1.buffers = meet(g, scatter_1.prepare())
    scatter_1.send()
    d_mid, d_att_b, out_away, out_home, sums = middle_back(
        links, g, middle, d_out_b, attended_b, full_wout, gain_two
    )
    grad_g2, grad_s2, grad_bout, grad_bdown = (sums[i] for i in range(4))
    scatter_2 = Scatter(links, away + [out_away], home + [out_home])
    d_att_b, scatter_2.kept = meet(d_att_b, scatter_2.kept)
    d_att_b, scatter_2.buffers = meet(d_att_b, scatter_2.prepare())
    scatter_2.send()
    half = pairs // 2
    grads = attend_back(qkv_b, d_att_b, attended_b, inverse, probs_b, 0, half)
    grads, scatter_1.held, scatter_2.held = meet(grads, scatter_1.held, scatter_2.held)
    grads, scatter_1.buffers, scatter_2.buffers = meet(
        grads, scatter_1.prepare(), scatter_2.prepare()
    )
    scatter_1.send()
    scatter_2.send()
    grads = attend_back(qkv_b, d_att_b, attended_b, inverse, probs_b, half, pairs, grads)
    grads, scatter_1.held, scatter_2.held = meet(grads, scatter_1.held, scatter_2.held)
    grads, scatter_1.buffers, scatter_2.buffers = meet(
        grads, scatter_1.prepare_along(), scatter_2.prepare_along()
    )
    scatter_1.send_along()
    d_qkv, qv_sums = grads
    scatter_3 = Scatter(links, *weight_grads(links, hidden_one_b, d_qkv))
    scatter_3.kept, scatter_2.buffers = meet(scatter_3.kept, scatter_2.buffers)
    scatter_2.send_along()
    d_qkv, scatter_3.buffers = meet(d_qkv, scatter_3.prepare())
    scatter_3.send()
    input_grad, entry_sums = entry_back(d_qkv, full_qkv, tokens_b, d_mid, full_g1[None])
    grad_g1, grad_s1 = entry_sums[0], entry_sums[1]
    grad_qvb = qv_sums.reshape(-1)
    input_grad, scatter_1.final = meet(input_grad, scatter_1.final)
    scatter_1.spread()
    input_grad, scatter_3.held = meet(input_grad, scatter_3.held)
    input_grad = input_grad.reshape(inputs.shape)
    grad_g1, scatter_3.buffers, scatter_2.final = meet(
        grad_g1, scatter_3.prepare(), scatter_2.final
    )
    scatter_3.send()
    scatter_2.spread()
    scatter_3.buffers = scatter_3.prepare_along()
    scatter_3.send_along()
    scatter_3.final, scatter_1.mate, scatter_2.mate = meet(
        scatter_3.final, scatter_1.mate, scatter_2.mate
    )
    scatter_3.spread()
    o_wdown, o_wup, o_wout = owned_feed_forward(links, scatter_1, scatter_2, w_up, w_down, w_out)
    o_qkv = owned_qkv(links, scatter_3, w_qkv)
    small_grads = (grad_g1, grad_s1, grad_bout, grad_g2, grad_s2, grad_bdown, grad_qvb, grad_bup)
    joined = jnp.concatenate([g.reshape(ns, -1) for g in small_grads], 1)
    joined = total_of(links, joined)
    owned = []
    base = 0
    for n in sizes:
        owned.append(joined[base : base + n])
        base += n
    o_g1, o_s1, o_bout, o_g2, o_s2, o_bdown, o_qvb, o_bup = owned
    return (
        output,
        input_grad,
        o_g1,
        o_s1,
        o_qkv,
        o_qvb,
        o_wout,
        o_bout,
        o_g2,
        o_s2,
        o_wup,
        o_bup,
        o_wdown,
        o_bdown,
    )


def solution(mesh):
    tokens = P("rep", "shard", None, None)
    vector = P("shard")
    matrix = P("shard", None)
    return jax.shard_map(
        functools.partial(body, Links(mesh)),
        mesh=mesh,
        in_specs=(
            tokens,
            P("rep"),
            vector,
            vector,
            matrix,
            vector,
            matrix,
            vector,
            vector,
            vector,
            matrix,
            vector,
            matrix,
            vector,
            tokens,
        ),
        out_specs=(
            tokens,
            tokens,
            vector,
            vector,
            matrix,
            vector,
            matrix,
            vector,
            vector,
            vector,
            matrix,
            vector,
            matrix,
            vector,
        ),
        check_vma=False,
    )
```

time: 756 us -> 576 us (0.76)
  Pallas kernels: 103 us -> 276 us
  matrix products: 181 us -> 9 us
  waiting for transfers between devices: 257 us -> 106 us
  other arithmetic: 66.4 us -> 24.4 us
  starting transfers between devices: 92.5 us -> 125 us
  local copies, waits for them, and re-layouts: 48.1 us -> 28.6 us
    pallas_call x5 -> x23, Pallas kernels: 103 us -> 276 us  [the longest x2 91.7 us: feed_forward(): pl.pallas_call(kernel, grid=(ns,), in_specs=[full(), full(), pl.BlockSpec...]
    ppermute x30 -> x36, waiting for transfers between devices: 187 us -> 48.2 us  [chip(): return lax.ppermute(values, 'rep', [(i, i ^ 2 * k) for i in range(self.nr)])]
    dot_general x12 -> x0, matrix products: 135 us -> none  [the longest x4 84.7 us: right_trans(): lax.dot_general(left, right, (((1,), (1,)), ((), ())), preferred_element_...]
    dot_general x4 -> x1, matrix products: 46.3 us -> 9 us  [matmul(): return jnp.dot(left, right, preferred_element_type=f32)]
    ppermute x11 -> x34, starting transfers between devices: 18.1 us -> 39.2 us  [core(): return lax.ppermute(values, 'rep', [(i, i ^ 1) for i in range(self.nr)])]
    convert_element_type x16 -> x10, other arithmetic: 32.5 us -> 15.5 us  [the longest x6 12 us: send(): (pieces[k].astype(f32) + got[i].astype(f32)).astype(bf16)]
    unnamed x175 -> x121, local copies, waits for them, and re-layouts: 38.1 us -> 21.7 us
    ppermute x21, waiting for transfers between devices: 70 us -> 53.9 us  [along(): lax.ppermute(values, 'shard', [(i, (i + step) % self.ns) for i in range(s...]
  transfers between devices with their start and end apart: 62 -> 91, of which waited for: 27 -> 16; matrix products, arithmetic and copies ran while one was open for 13% -> 7% of each run, Pallas kernels for 6% -> 37%
where the time goes in v3:
time: 576 us; the launch traced here: 571 us
  Pallas kernels  276 us (48%)
  starting transfers between devices  125 us (22%)
  waiting for transfers between devices  106 us (18%)
  local copies, waits for them, and re-layouts  28.6 us (5%)
  other arithmetic  24.4 us (4%)
  matrix products  9 us (2%)
    pallas_call x2, Pallas kernels, feed_forward(): pl.pallas_call(kernel, grid=(ns,), in_specs=[full(), full(), pl.BlockSpec...  91.7 us
    pallas_call x2, Pallas kernels, attend_back(): pl.pallas_call(kernel, grid=(count,), in_specs=[column(0), column(pairs),...  58.2 us
    ppermute x21, starting transfers between devices, along(): lax.ppermute(values, 'shard', [(i, (i + step) % self.ns) for i in range(s...  56.4 us
    ppermute x21, waiting for transfers between devices, along(): lax.ppermute(values, 'shard', [(i, (i + step) % self.ns) for i in range(s...  53.9 us
    pallas_call x3, Pallas kernels, attend(): pl.pallas_call(kernel, grid=(count,), in_specs=[column(0), column(pairs),...  52.5 us
    ppermute x36, waiting for transfers between devices, chip(): return lax.ppermute(values, 'rep', [(i, i ^ 2 * k) for i in range(self.nr)])  48.2 us
    ppermute x34, starting transfers between devices, core(): return lax.ppermute(values, 'rep', [(i, i ^ 1) for i in range(self.nr)])  39.2 us
    ppermute x36, starting transfers between devices, chip(): return lax.ppermute(values, 'rep', [(i, i ^ 2 * k) for i in range(self.nr)])  29.2 us
  transfers between devices with their start and end apart: 91, of which 16 were waited for; matrix products, arithmetic and copies ran while one was open for 7% of the time, Pallas kernels for 37%

profile of v3, /device:TPU:1, one launch (start us, length us, event | category | flops | bytes accessed | tf_op | source)
XLA Modules:
  0.0 571.3 jit_solution(6260438531576082054)
XLA Ops:
  0.6 2.4 pack.1
  14.2 6.6 %collective-permute-done.2 = bf16[80,1536]{1,0:T(8,128)(2,1)S(1)} collective-permute-done((bf16[80,1536]{1,0:T(8,128)(2,1)}, bf16[80,1536]{1,0:T(8,128)(2,1)S(1)}, u32[]{:S(2)}, u32[]{:S(2)}) %collective-permute-start.2) | collective-permute-done | bytes 245792 | tf_op jit(solution)/shard_map/ppermute | solution.py:526
  20.8 3.7 collective-permute-done.1
  28.7 5.4 collective-permute-done.4.refs_3_
  37.7 10.6 %collective-permute-done.6.refs_5_ = bf16[2,3,64,768]{3,2,1,0:T(8,128)(2,1)S(1)} collective-permute-done((bf16[2,3,64,768]{3,2,1,0:T(8,128)(2,1)S(1)}, bf16[2,3,64,768]{3,2,1,0:T(8,128)(2,1)S(1)}, u32[]{:S(2)}, u32[]{:S(2)}) %collective-permute-start.6) | collective-permute-done | bytes 589856 | tf_op jit(solution)/shard_map/ppermute | solution.py:529
  52.0 5.6 collective-permute-start.12
  58.9 2.6 collective-permute-start.14
  63.0 9.0 %fusion.refs_0_.refs_1_.refs_2_ = bf16[1104,3072]{1,0:T(8,128)(2,1)} fusion(bf16[1104,1024]{1,0:T(8,128)(2,1)S(1)} %fusion.6.left_ref, bf16[1024,3072]{1,0:T(8,128)(2,1)S(1)} %assemble.3.w_ref, f32[3072]{0:T(1024)S(1)} %pad_maximum_fusion.12), kind=kOutput, calls=%fused_computation.1 | convolution fusion | flops 6952550400 | bytes 15347712 | tf_op jit(solution)/shard_map/dot_general | solution.py:25
  72.0 8.8 %collective-permute-done.13 = bf16[64,2560]{1,0:T(8,128)(2,1)S(1)} collective-permute-done((bf16[64,2560]{1,0:T(8,128)(2,1)S(1)}, bf16[64,2560]{1,0:T(8,128)(2,1)S(1)}, u32[]{:S(2)}, u32[]{:S(2)}) %collective-permute-start.13) | collective-permute-done | bytes 327712 | tf_op jit(solution)/shard_map/ppermute | solution.py:526
  82.7 14.0 %attend.3 = (bf16[1104,1024]{1,0:T(8,128)(2,1)}, f32[1104,1024]{1,0:T(8,128)}, bf16[16,1104,1104]{2,1,0:T(8,128)(2,1)}) custom-call(bf16[1104,3072]{1,0:T(8,128)(2,1)} %fusion.refs_0_.refs_1_.refs_2_, bf16[1104,3072]{1,0:T(8,128)(2,1)} %fusion.refs_0_.refs_1_.refs_2_, bf16[1104,3072]{1,0:T(8,128)(2,1)} %fusion.refs_0_.refs_1_.refs_2_), custom_call_target="tpu_custom_call" | custom-call | flops 1 | bytes 1 | tf_op jit(solution)/shard_map/attend/pallas_call | solution.py:88
  100.3 7.4 %collective-permute-start.19 = (bf16[256,512]{1,0:T(8,128)(2,1)S(1)}, bf16[256,512]{1,0:T(8,128)(2,1)S(1)}, u32[]{:S(2)}, u32[]{:S(2)}) collective-permute-start(bf16[256,512]{1,0:T(8,128)(2,1)S(1)} %dynamic_slice.41), channel_id=1, source_target_pairs={{0,1},{1,2},{2,3},{3,0},{4,5},{5,6},{6,7},{7,4},{8,9},{9,10},{10,1... | collective-permute-start | bytes 786440 | tf_op jit(solution)/shard_map/ppermute | solution.py:526
  109.8 24.5 %attend.4 = (bf16[1104,1024]{1,0:T(8,128)(2,1)}, f32[1104,1024]{1,0:T(8,128)}, bf16[16,1104,1104]{2,1,0:T(8,128)(2,1)}) custom-call(bf16[1104,3072]{1,0:T(8,128)(2,1)} %fusion.refs_0_.refs_1_.refs_2_, bf16[1104,3072]{1,0:T(8,128)(2,1)} %fusion.refs_0_.refs_1_.refs_2_, ...), custom_call_target="tpu_custom_call", output_to_operand_aliasing={{0}: (3, {}), {1}: (4, {}), {2}: (5, {})} | custom-call | flops 1 | bytes 1 | tf_op jit(solution)/shard_map/attend/pallas_call | solution.py:88
  136.9 2.7 collective-permute-start.25
  140.1 14.0 %attend.5 = (bf16[1104,1024]{1,0:T(8,128)(2,1)}, f32[1104,1024]{1,0:T(8,128)}, bf16[16,1104,1104]{2,1,0:T(8,128)(2,1)}) custom-call(bf16[1104,3072]{1,0:T(8,128)(2,1)} %fusion.refs_0_.refs_1_.refs_2_, bf16[1104,3072]{1,0:T(8,128)(2,1)} %fusion.refs_0_.refs_1_.refs_2_, ...), custom_call_target="tpu_custom_call", output_to_operand_aliasing={{0}: (3, {}), {1}: (4, {}), {2}: (5, {})} | custom-call | flops 1 | bytes 1 | tf_op jit(solution)/shard_map/attend/pallas_call | solution.py:88
  159.4 15.7 %collective-permute-done.30.refs_5_ = bf16[2,3,256,256]{3,2,1,0:T(8,128)(2,1)S(1)} collective-permute-done((bf16[2,3,256,256]{3,2,1,0:T(8,128)(2,1)S(1)}, bf16[2,3,256,256]{3,2,1,0:T(8,128)(2,1)S(1)}, u32[]{:S(2)}, u32[]{:S(2)}) %collective-permute-start.30) | collective-permute-done | bytes 786464 | tf_op jit(solution)/shard_map/ppermute | solution.py:529
  183.4 2.5 assemble.4
  185.9 3.3 copy-done.3
  189.2 6.7 %middle.1 = (f32[1104,1024]{1,0:T(8,128)}, bf16[1104,1024]{1,0:T(8,128)(2,1)S(1)}) custom-call(bf16[1104,1024]{1,0:T(8,128)(2,1)} %bitcast.155, bf16[1104,1024]{1,0:T(8,128)(2,1)} %get-tuple-element.223.att_ref.refs_4_, bf16[1024,1024]{1,0:T(8,128)(2,1)S(1)} %get-tuple-element.229.w_ref, f32[1,1024]{1,0:T(1,128)S(1)} %bitcast.171, f32[1,1024]{1,0:T(1,128)S(1)} %bitcast.168, ...), custom_call_target="tpu_custom_call" | custom-call | flops 1 | bytes 1 | tf_op jit(solution)/shard_map/middle/pallas_call | solution.py:388
  198.1 3.3 copy-done
  201.4 45.3 %feed_forward.2 = (f32[1104,1024]{1,0:T(8,128)}, f32[1104,1024]{1,0:T(8,128)}, bf16[4,512,512]{2,1,0:T(8,128)(2,1)}, bf16[4,512,512]{2,1,0:T(8,128)(2,1)}, bf16[...) custom-call(bf16[1104,1024]{1,0:T(8,128)(2,1)} %copy-done.7, ...), custom_call_target="tpu_custom_call" | custom-call | flops 1 | bytes 1 | tf_op jit(solution)/shard_map/feed_forward/pallas_call | solution.py:272
  247.3 46.4 %feed_forward.3 = (bf16[1104,1024]{1,0:T(8,128)(2,1)}, f32[1104,1024]{1,0:T(8,128)}, bf16[4,512,512]{2,1,0:T(8,128)(2,1)}, bf16[4,512,512]{2,1,0:T(8,128)(2,1)},...) custom-call(bf16[1104,1024]{1,0:T(8,128)(2,1)} %copy-done.7, ...), custom_call_target="tpu_custom_call" | custom-call | flops 1 | bytes 1 | tf_op jit(solution)/shard_map/feed_forward/pallas_call | solution.py:272
  297.4 4.5 core_sums.3
  303.0 13.7 %middle_back.1 = (f32[1104,1024]{1,0:T(8,128)}, bf16[1104,1024]{1,0:T(8,128)(2,1)}, bf16[4,4,64,512]{3,2,1,0:T(8,128)(2,1)S(1)}, bf16[4,4,64,512]{3,2,1,0:T(8,128)(2,1)S(1)}, f32[8,1024]{1,0:T(8,128)S(1)}) custom-call(f32[1104,1024]{1,0:T(8,128)} %get-tuple-element.256.g_ref, f32[1104,1024]{1,0:T(8,128)} %get-tuple-element.242.refs_7_.mid_ref, ...), custom_call_target="tpu_custom_call" | custom-call | flops 1 | bytes 1 | tf_op jit(solution)/shard_map/middle_back/pallas_call | solution.py:444
  319.4 2.7 core_sums.4
  323.1 29.2 %attend_back.2 = (bf16[3,1104,1024]{2,1,0:T(8,128)(2,1)}, f32[2,1,1024]{2,1,0:T(1,128)}) custom-call(bf16[1104,3072]{1,0:T(8,128)(2,1)} %fusion.refs_0_.refs_1_.refs_2_, bf16[1104,3072]{1,0:T(8,128)(2,1)} %fusion.refs_0_.refs_1_.refs_2_, bf16[1104,3072]{1,0:T(8,128)(2,1)} %fusion.refs_0_.refs_1_.refs_2_, bf16[1104,1024]{1,0:T(8,128)(2,1)} %get-tuple-element.270.refs_3_, ...), custom_call_target="tpu_custom_call" | custom-call | flops 1 | bytes 1 | tf_op jit(solution)/shard_map/attend_back/pallas_call | solution.py:167
  357.0 12.5 %collective-permute-done.44 = bf16[2,4,160,512]{3,2,1,0:T(8,128)(2,1)} collective-permute-done((bf16[2,4,160,512]{3,2,1,0:T(8,128)(2,1)}, bf16[2,4,160,512]{3,2,1,0:T(8,128)(2,1)}, u32[]{:S(2)}, u32[]{:S(2)}) %collective-permute-start.44) | collective-permute-done | bytes 1310752 | tf_op jit(solution)/shard_map/ppermute | solution.py:529
  369.5 2.5 fusion.10
  375.4 29.0 %attend_back.3 = (bf16[3,1104,1024]{2,1,0:T(8,128)(2,1)}, f32[2,1,1024]{2,1,0:T(1,128)}) custom-call(bf16[1104,3072]{1,0:T(8,128)(2,1)} %fusion.refs_0_.refs_1_.refs_2_, bf16[1104,3072]{1,0:T(8,128)(2,1)} %fusion.refs_0_.refs_1_.refs_2_, bf16[1104,3072]{1,0:T(8,128)(2,1)} %fusion.refs_0_.refs_1_.refs_2_, ...), custom_call_target="tpu_custom_call", output_to_operand_aliasing={{0}: (7, {}), {1}: (8, {})} | custom-call | flops 1 | bytes 1 | tf_op jit(solution)/shard_map/attend_back/pallas_call | solution.py:167
  406.4 11.6 %weight_grads.1 = (bf16[4,4,3,64,512]{4,3,2,1,0:T(8,128)(2,1)S(1)}, bf16[4,4,3,64,512]{4,3,2,1,0:T(8,128)(2,1)}) custom-call(bf16[1104,1024]{1,0:T(8,128)(2,1)S(1)} %copy-done.6, bf16[3,1104,1024]{2,1,0:T(8,128)(2,1)} %get-tuple-element.329.right_ref.d_ref), custom_call_target="tpu_custom_call" | custom-call | flops 1 | bytes 1 | tf_op jit(solution)/shard_map/weight_grads/pallas_call | solution.py:340
  418.0 2.4 collective-permute-start.49
  431.5 2.8 collective-permute-start.57
  434.4 6.9 %collective-permute-done.51 = bf16[256,512]{1,0:T(8,128)(2,1)S(1)} collective-permute-done((bf16[256,512]{1,0:T(8,128)(2,1)S(1)}, bf16[256,512]{1,0:T(8,128)(2,1)S(1)}, u32[]{:S(2)}, u32[]{:S(2)}) %collective-permute-start.51) | collective-permute-done | bytes 262176 | tf_op jit(solution)/shard_map/ppermute | solution.py:526
  445.5 3.1 collective-permute-done.55
  448.6 19.4 %collective-permute-done.56 = bf16[320,512]{1,0:T(8,128)(2,1)} collective-permute-done((bf16[320,512]{1,0:T(8,128)(2,1)}, bf16[320,512]{1,0:T(8,128)(2,1)}, u32[]{:S(2)}, u32[]{:S(2)}) %collective-permute-start.56) | collective-permute-done | bytes 327712 | tf_op jit(solution)/shard_map/ppermute | solution.py:526
  469.4 14.8 %entry_back.1 = (f32[1104,1024]{1,0:T(8,128)}, f32[8,1024]{1,0:T(8,128)S(1)}) custom-call(bf16[3,1104,1024]{2,1,0:T(8,128)(2,1)} %get-tuple-element.329.right_ref.d_ref, bf16[1024,3072]{1,0:T(8,128)(2,1)} %copy-done.4, bf16[1104,1024]{1,0:T(8,128)(2,1)S(1)} %bitcast.156, f32[1104,1024]{1,0:T(8,128)} %get-tuple-element.330.d_mid_ref, f32[1,1024]{1,0:T(1,128)S(1)} %bitcast.172), custom_call_target="tpu_custom_call" | custom-call | flops 1 | bytes 1 | tf_op jit(solution)/shard_map/entry_back/pallas_call | solution.py:492
  488.8 2.4 fusion.18
  494.5 4.8 collective-permute-start.58
  502.8 3.8 collective-permute-done.65
  511.5 2.4 collective-permute-start.77
  513.9 7.3 %collective-permute-start.67 = (bf16[192,512]{1,0:T(8,128)(2,1)S(1)}, bf16[192,512]{1,0:T(8,128)(2,1)S(1)}, u32[]{:S(2)}, u32[]{:S(2)}) collective-permute-start(bf16[192,512]{1,0:T(8,128)(2,1)S(1)} %get-tuple-element.359), channel_id=1, source_target_pairs={{0,1},{1,2},{2,3},{3,0},{4,5},{5,6},{6,7},{7,4},{8,9},{9,10},{10,1... | collective-permute-start | bytes 589832 | tf_op jit(solution)/shard_map/ppermute | solution.py:526
  521.6 5.6 collective-permute-start.81
  527.2 6.2 %collective-permute-start.68 = (bf16[192,512]{1,0:T(8,128)(2,1)S(1)}, bf16[192,512]{1,0:T(8,128)(2,1)S(1)}, u32[]{:S(2)}, u32[]{:S(2)}) collective-permute-start(bf16[192,512]{1,0:T(8,128)(2,1)S(1)} %get-tuple-element.360), channel_id=1, source_target_pairs={{0,2},{1,3},{2,0},{3,1},{4,6},{5,7},{6,4},{7,5},{8,10},{9,11},{10,... | collective-permute-start | bytes 589832 | tf_op jit(solution)/shard_map/ppermute | solution.py:526
  533.5 3.2 collective-permute-start.69
  536.7 5.4 collective-permute-done.68
  542.1 5.5 collective-permute-start.62
  547.6 3.1 collective-permute-start.63
  556.7 3.1 collective-permute-start.88
  563.7 5.4 owned.3
  (341 shorter events, 114.9 us)
Async XLA Ops:
  3.1 21.4 %collective-permute-start = (bf16[80,1536]{1,0:T(8,128)(2,1)}, bf16[80,1536]{1,0:T(8,128)(2,1)S(1)}, u32[]{:S(2)}, u32[]{:S(2)}) collective-permute-start(bf16[80,1536]{1,0:T(8,128)(2,1)} %pack.1), channel_id=1, source_target_pairs={{0,1},{1,2},{2,3},{3,0},{4,5},{5,6},{6,7},{7,4},{8,9},{9,10},{10,1... | collective-permute-start | bytes 737288 | tf_op jit(solution)/shard_map/ppermute | solution.py:526
  5.3 19.2 %collective-permute-start.1 = (bf16[80,1536]{1,0:T(8,128)(2,1)}, bf16[80,1536]{1,0:T(8,128)(2,1)S(1)}, u32[]{:S(2)}, u32[]{:S(2)}) collective-permute-start(bf16[80,1536]{1,0:T(8,128)(2,1)} %pack.1), channel_id=1, source_target_pairs={{0,2},{1,3},{2,0},{3,1},{4,6},{5,7},{6,4},{7,5},{8,10},{9,11},{10,... | collective-permute-start | bytes 737288 | tf_op jit(solution)/shard_map/ppermute | solution.py:526
  24.7 27.3 %collective-permute-start.7 = (bf16[3,64,1536]{2,1,0:T(8,128)(2,1)S(1)}, bf16[3,64,1536]{2,1,0:T(8,128)(2,1)S(1)}, u32[]{:S(2)}, u32[]{:S(2)}) collective-permute-start(bf16[3,64,1536]{2,1,0:T(8,128)(2,1)S(1)} %pad_maximum_fusion.6.refs_1_), channel_id=1, source_target_pairs={{0,4},{4,0},{8,12},{12,8},{16,20},{20,16},{24,28},{28,24},{1,5},{5... | collective-permute-start | bytes 1769480 | tf_op jit(solution)/shard_map/ppermute | solution.py:532
  52.0 20.0 %collective-permute-start.12 = (bf16[64,2560]{1,0:T(8,128)(2,1)S(1)}, bf16[64,2560]{1,0:T(8,128)(2,1)S(1)}, u32[]{:S(2)}, u32[]{:S(2)}) collective-permute-start(bf16[64,2560]{1,0:T(8,128)(2,1)S(1)} %pad_maximum_fusion.9), channel_id=1, source_target_pairs={{0,1},{1,2},{2,3},{3,0},{4,5},{5,6},{6,7},{7,4},{8,9},{9,10},{10,1... | collective-permute-start | bytes 983048 | tf_op jit(solution)/shard_map/ppermute | solution.py:526
  57.6 23.3 %collective-permute-start.13 = (bf16[64,2560]{1,0:T(8,128)(2,1)S(1)}, bf16[64,2560]{1,0:T(8,128)(2,1)S(1)}, u32[]{:S(2)}, u32[]{:S(2)}) collective-permute-start(bf16[64,2560]{1,0:T(8,128)(2,1)S(1)} %pad_maximum_fusion.9), channel_id=1, source_target_pairs={{0,2},{1,3},{2,0},{3,1},{4,6},{5,7},{6,4},{7,5},{8,10},{9,11},{10,... | collective-permute-start | bytes 983048 | tf_op jit(solution)/shard_map/ppermute | solution.py:526
  58.9 22.0 %collective-permute-start.14 = (bf16[64,2560]{1,0:T(8,128)(2,1)S(1)}, bf16[64,2560]{1,0:T(8,128)(2,1)S(1)}, u32[]{:S(2)}, u32[]{:S(2)}) collective-permute-start(bf16[64,2560]{1,0:T(8,128)(2,1)S(1)} %pad_maximum_fusion.9), channel_id=1, source_target_pairs={{0,3},{1,0},{2,1},{3,2},{4,7},{5,4},{6,5},{7,6},{8,11},{9,8},{10,9... | collective-permute-start | bytes 983048 | tf_op jit(solution)/shard_map/ppermute | solution.py:526
  97.7 36.5 %collective-permute-start.18 = (bf16[2,3,64,1280]{3,2,1,0:T(8,128)(2,1)}, bf16[2,3,64,1280]{3,2,1,0:T(8,128)(2,1)}, u32[]{:S(2)}, u32[]{:S(2)}) collective-permute-start(bf16[2,3,64,1280]{3,2,1,0:T(8,128)(2,1)} %pad_maximum_fusion.2), channel_id=1, source_target_pairs={{0,8},{4,12},{8,0},{12,4},{16,24},{20,28},{24,16},{28,20},{1,9},{5... | collective-permute-start | bytes 2949128 | tf_op jit(solution)/shard_map/ppermute | solution.py:529
  100.0 34.3 %collective-permute-start.17 = (bf16[2,3,64,1280]{3,2,1,0:T(8,128)(2,1)}, bf16[2,3,64,1280]{3,2,1,0:T(8,128)(2,1)}, u32[]{:S(2)}, u32[]{:S(2)}) collective-permute-start(bf16[2,3,64,1280]{3,2,1,0:T(8,128)(2,1)} %pad_maximum_fusion.1), channel_id=1, source_target_pairs={{0,16},{4,20},{8,24},{12,28},{16,0},{20,4},{24,8},{28,12},{1,17},{... | collective-permute-start | bytes 2949128 | tf_op jit(solution)/shard_map/ppermute | solution.py:529
  100.3 34.0 %collective-permute-start.19 = (bf16[256,512]{1,0:T(8,128)(2,1)S(1)}, bf16[256,512]{1,0:T(8,128)(2,1)S(1)}, u32[]{:S(2)}, u32[]{:S(2)}) collective-permute-start(bf16[256,512]{1,0:T(8,128)(2,1)S(1)} %dynamic_slice.41), channel_id=1, source_target_pairs={{0,1},{1,2},{2,3},{3,0},{4,5},{5,6},{6,7},{7,4},{8,9},{9,10},{10,1... | collective-permute-start | bytes 786440 | tf_op jit(solution)/shard_map/ppermute | solution.py:526
  107.6 26.7 %collective-permute-start.20 = (bf16[256,512]{1,0:T(8,128)(2,1)S(1)}, bf16[256,512]{1,0:T(8,128)(2,1)S(1)}, u32[]{:S(2)}, u32[]{:S(2)}) collective-permute-start(bf16[256,512]{1,0:T(8,128)(2,1)S(1)} %dynamic_slice.41), channel_id=1, source_target_pairs={{0,2},{1,3},{2,0},{3,1},{4,6},{5,7},{6,4},{7,5},{8,10},{9,11},{10,... | collective-permute-start | bytes 786440 | tf_op jit(solution)/shard_map/ppermute | solution.py:526
  108.5 25.8 %collective-permute-start.21 = (bf16[256,512]{1,0:T(8,128)(2,1)S(1)}, bf16[256,512]{1,0:T(8,128)(2,1)S(1)}, u32[]{:S(2)}, u32[]{:S(2)}) collective-permute-start(bf16[256,512]{1,0:T(8,128)(2,1)S(1)} %dynamic_slice.41), channel_id=1, source_target_pairs={{0,3},{1,0},{2,1},{3,2},{4,7},{5,4},{6,5},{7,6},{8,11},{9,8},{10,9... | collective-permute-start | bytes 786440 | tf_op jit(solution)/shard_map/ppermute | solution.py:526
  135.4 18.7 %collective-permute-start.22 = (bf16[1,3,256,256]{3,2,1,0:T(8,128)(2,1)}, bf16[1,3,256,256]{3,2,1,0:T(8,128)(2,1)S(1)}, u32[]{:S(2)}, u32[]{:S(2)}) collective-permute-start(bf16[1,3,256,256]{3,2,1,0:T(8,128)(2,1)} %get-tuple-element.399), channel_id=1, source_target_pairs={{0,8},{4,12},{8,0},{12,4},{16,24},{20,28},{24,16},{28,20},{1,9},{5... | collective-permute-start | bytes 1179656 | tf_op jit(solution)/shard_map/ppermute | solution.py:529
  136.2 18.1 %collective-permute-start.23 = (bf16[1,3,256,256]{3,2,1,0:T(8,128)(2,1)}, bf16[1,3,256,256]{3,2,1,0:T(8,128)(2,1)}, u32[]{:S(2)}, u32[]{:S(2)}) collective-permute-start(bf16[1,3,256,256]{3,2,1,0:T(8,128)(2,1)} %get-tuple-element.398), channel_id=1, source_target_pairs={{0,16},{4,20},{8,24},{12,28},{16,0},{20,4},{24,8},{28,12},{1,17},{... | collective-permute-start | bytes 1179656 | tf_op jit(solution)/shard_map/ppermute | solution.py:529
  136.9 19.1 %collective-permute-start.25 = (bf16[1,3,64,1280]{3,2,1,0:T(8,128)(2,1)S(1)}, bf16[1,3,64,1280]{3,2,1,0:T(8,128)(2,1)S(1)}, u32[]{:S(2)}, u32[]{:S(2)}) collective-permute-start(bf16[1,3,64,1280]{3,2,1,0:T(8,128)(2,1)S(1)} %copy-done.17), channel_id=1, source_target_pairs={{0,4},{4,0},{8,12},{12,8},{16,20},{20,16},{24,28},{28,24},{1,5},{5... | collective-permute-start | bytes 1474568 | tf_op jit(solution)/shard_map/ppermute | solution.py:532
  139.6 17.6 %collective-permute-start.26 = (bf16[1,3,64,1280]{3,2,1,0:T(8,128)(2,1)S(1)}, bf16[1,3,64,1280]{3,2,1,0:T(8,128)(2,1)S(1)}, u32[]{:S(2)}, u32[]{:S(2)}) collective-permute-start(bf16[1,3,64,1280]{3,2,1,0:T(8,128)(2,1)S(1)} %copy-done.20), channel_id=1, source_target_pairs={{0,4},{4,0},{8,12},{12,8},{16,20},{20,16},{24,28},{28,24},{1,5},{5... | collective-permute-start | bytes 1474568 | tf_op jit(solution)/shard_map/ppermute | solution.py:532
  139.7 18.5 %collective-permute-start.24 = (bf16[3,64,2560]{2,1,0:T(8,128)(2,1)S(1)}, bf16[3,64,2560]{2,1,0:T(8,128)(2,1)S(1)}, u32[]{:S(2)}, u32[]{:S(2)}) collective-permute-start(bf16[3,64,2560]{2,1,0:T(8,128)(2,1)S(1)} %pad_maximum_fusion.refs_2_), channel_id=1, source_target_pairs={{0,4},{4,0},{8,12},{12,8},{16,20},{20,16},{24,28},{28,24},{1,5},{5... | collective-permute-start | bytes 2949128 | tf_op jit(solution)/shard_map/ppermute | solution.py:532
  156.0 19.2 %collective-permute-start.30 = (bf16[2,3,256,256]{3,2,1,0:T(8,128)(2,1)S(1)}, bf16[2,3,256,256]{3,2,1,0:T(8,128)(2,1)S(1)}, u32[]{:S(2)}, u32[]{:S(2)}) collective-permute-start(bf16[2,3,256,256]{3,2,1,0:T(8,128)(2,1)S(1)} %pad_maximum_fusion.5), channel_id=1, source_target_pairs={{0,8},{4,12},{8,0},{12,4},{16,24},{20,28},{24,16},{28,20},{1,9},{5... | collective-permute-start | bytes 2359304 | tf_op jit(solution)/shard_map/ppermute | solution.py:529
  157.3 18.8 %collective-permute-start.29 = (bf16[2,3,256,256]{3,2,1,0:T(8,128)(2,1)S(1)}, bf16[2,3,256,256]{3,2,1,0:T(8,128)(2,1)S(1)}, u32[]{:S(2)}, u32[]{:S(2)}) collective-permute-start(bf16[2,3,256,256]{3,2,1,0:T(8,128)(2,1)S(1)} %pad_maximum_fusion.4), channel_id=1, source_target_pairs={{0,16},{4,20},{8,24},{12,28},{16,0},{20,4},{24,8},{28,12},{1,17},{... | collective-permute-start | bytes 2359304 | tf_op jit(solution)/shard_map/ppermute | solution.py:529
  158.2 37.7 %collective-permute-start.31 = (bf16[3,256,512]{2,1,0:T(8,128)(2,1)S(1)}, bf16[3,256,512]{2,1,0:T(8,128)(2,1)S(1)}, u32[]{:S(2)}, u32[]{:S(2)}) collective-permute-start(bf16[3,256,512]{2,1,0:T(8,128)(2,1)S(1)} %pad_maximum_fusion.3.refs_1_), channel_id=1, source_target_pairs={{0,4},{4,0},{8,12},{12,8},{16,20},{20,16},{24,28},{28,24},{1,5},{5... | collective-permute-start | bytes 2359304 | tf_op jit(solution)/shard_map/ppermute | solution.py:532
  158.9 37.0 %collective-permute-start.32 = (bf16[1,3,256,256]{3,2,1,0:T(8,128)(2,1)S(1)}, bf16[1,3,256,256]{3,2,1,0:T(8,128)(2,1)S(1)}, u32[]{:S(2)}, u32[]{:S(2)}) collective-permute-start(bf16[1,3,256,256]{3,2,1,0:T(8,128)(2,1)S(1)} %collective-permute-done.22.refs_2_), channel_id=1, source_target_pairs={{0,4},{4,0},{8,12},{12,8},{16,20},{20,16},{24,28},{28,24},{1,5},{5... | collective-permute-start | bytes 1179656 | tf_op jit(solution)/shard_map/ppermute | solution.py:532
  159.0 36.9 %collective-permute-start.33 = (bf16[1,3,256,256]{3,2,1,0:T(8,128)(2,1)}, bf16[1,3,256,256]{3,2,1,0:T(8,128)(2,1)S(1)}, u32[]{:S(2)}, u32[]{:S(2)}) collective-permute-start(bf16[1,3,256,256]{3,2,1,0:T(8,128)(2,1)} %collective-permute-done.23.refs_3_), channel_id=1, source_target_pairs={{0,4},{4,0},{8,12},{12,8},{16,20},{20,16},{24,28},{28,24},{1,5},{5... | collective-permute-start | bytes 1179656 | tf_op jit(solution)/shard_map/ppermute | solution.py:532
  175.1 20.8 %collective-permute-start.35 = (bf16[2,3,256,256]{3,2,1,0:T(8,128)(2,1)S(1)}, bf16[2,3,256,256]{3,2,1,0:T(8,128)(2,1)S(1)}, u32[]{:S(2)}, u32[]{:S(2)}) collective-permute-start(bf16[2,3,256,256]{3,2,1,0:T(8,128)(2,1)S(1)} %collective-permute-done.30.refs_5_), channel_id=1, source_target_pairs={{0,4},{4,0},{8,12},{12,8},{16,20},{20,16},{24,28},{28,24},{1,5},{5... | collective-permute-start | bytes 2359304 | tf_op jit(solution)/shard_map/ppermute | solution.py:532
  176.1 19.9 %collective-permute-start.34 = (bf16[2,3,256,256]{3,2,1,0:T(8,128)(2,1)S(1)}, bf16[2,3,256,256]{3,2,1,0:T(8,128)(2,1)S(1)}, u32[]{:S(2)}, u32[]{:S(2)}) collective-permute-start(bf16[2,3,256,256]{3,2,1,0:T(8,128)(2,1)S(1)} %collective-permute-done.29.refs_4_), channel_id=1, source_target_pairs={{0,4},{4,0},{8,12},{12,8},{16,20},{20,16},{24,28},{28,24},{1,5},{5... | collective-permute-start | bytes 2359304 | tf_op jit(solution)/shard_map/ppermute | solution.py:532
  246.7 47.5 %collective-permute-start.36 = (bf16[4,4,128,512]{3,2,1,0:T(8,128)(2,1)}, bf16[4,4,128,512]{3,2,1,0:T(8,128)(2,1)}, u32[]{:S(2)}, u32[]{:S(2)}) collective-permute-start(bf16[4,4,128,512]{3,2,1,0:T(8,128)(2,1)} %bitcast.208), channel_id=1, source_target_pairs={{0,4},{4,0},{8,12},{12,8},{16,20},{20,16},{24,28},{28,24},{1,5},{5... | collective-permute-start | bytes 6291464 | tf_op jit(solution)/shard_map/ppermute | solution.py:532
  246.8 47.4 %collective-permute-start.37 = (bf16[4,4,128,512]{3,2,1,0:T(8,128)(2,1)}, bf16[4,4,128,512]{3,2,1,0:T(8,128)(2,1)}, u32[]{:S(2)}, u32[]{:S(2)}) collective-permute-start(bf16[4,4,128,512]{3,2,1,0:T(8,128)(2,1)} %bitcast.207), channel_id=1, source_target_pairs={{0,4},{4,0},{8,12},{12,8},{16,20},{20,16},{24,28},{28,24},{1,5},{5... | collective-permute-start | bytes 6291464 | tf_op jit(solution)/shard_map/ppermute | solution.py:532
  293.6 24.2 %collective-permute-start.38 = (bf16[4,4,128,512]{3,2,1,0:T(8,128)(2,1)}, bf16[4,4,128,512]{3,2,1,0:T(8,128)(2,1)S(1)}, u32[]{:S(2)}, u32[]{:S(2)}) collective-permute-start(bf16[4,4,128,512]{3,2,1,0:T(8,128)(2,1)} %bitcast.206), channel_id=1, source_target_pairs={{0,4},{4,0},{8,12},{12,8},{16,20},{20,16},{24,28},{28,24},{1,5},{5... | collective-permute-start | bytes 6291464 | tf_op jit(solution)/shard_map/ppermute | solution.py:532
  293.8 24.0 %collective-permute-start.39 = (bf16[4,4,128,512]{3,2,1,0:T(8,128)(2,1)}, bf16[4,4,128,512]{3,2,1,0:T(8,128)(2,1)S(1)}, u32[]{:S(2)}, u32[]{:S(2)}) collective-permute-start(bf16[4,4,128,512]{3,2,1,0:T(8,128)(2,1)} %bitcast.205), channel_id=1, source_target_pairs={{0,4},{4,0},{8,12},{12,8},{16,20},{20,16},{24,28},{28,24},{1,5},{5... | collective-permute-start | bytes 6291464 | tf_op jit(solution)/shard_map/ppermute | solution.py:532
  316.8 35.5 %collective-permute-start.42 = (bf16[2,4,128,512]{3,2,1,0:T(8,128)(2,1)}, bf16[2,4,128,512]{3,2,1,0:T(8,128)(2,1)}, u32[]{:S(2)}, u32[]{:S(2)}) collective-permute-start(bf16[2,4,128,512]{3,2,1,0:T(8,128)(2,1)} %get-tuple-element.278), channel_id=1, source_target_pairs={{0,16},{4,20},{8,24},{12,28},{16,0},{20,4},{24,8},{28,12},{1,17},{... | collective-permute-start | bytes 3145736 | tf_op jit(solution)/shard_map/ppermute | solution.py:529
  317.0 37.6 %collective-permute-start.41 = (bf16[2,4,128,512]{3,2,1,0:T(8,128)(2,1)}, bf16[2,4,128,512]{3,2,1,0:T(8,128)(2,1)}, u32[]{:S(2)}, u32[]{:S(2)}) collective-permute-start(bf16[2,4,128,512]{3,2,1,0:T(8,128)(2,1)} %get-tuple-element.276), channel_id=1, source_target_pairs={{0,8},{4,12},{8,0},{12,4},{16,24},{20,28},{24,16},{28,20},{1,9},{5... | collective-permute-start | bytes 3145736 | tf_op jit(solution)/shard_map/ppermute | solution.py:529
  322.1 47.4 %collective-permute-start.44 = (bf16[2,4,160,512]{3,2,1,0:T(8,128)(2,1)}, bf16[2,4,160,512]{3,2,1,0:T(8,128)(2,1)}, u32[]{:S(2)}, u32[]{:S(2)}) collective-permute-start(bf16[2,4,160,512]{3,2,1,0:T(8,128)(2,1)} %get-tuple-element.282), channel_id=1, source_target_pairs={{0,16},{4,20},{8,24},{12,28},{16,0},{20,4},{24,8},{28,12},{1,17},{... | collective-permute-start | bytes 3932168 | tf_op jit(solution)/shard_map/ppermute | solution.py:529
  322.4 49.6 %collective-permute-start.43 = (bf16[2,4,160,512]{3,2,1,0:T(8,128)(2,1)}, bf16[2,4,160,512]{3,2,1,0:T(8,128)(2,1)S(1)}, u32[]{:S(2)}, u32[]{:S(2)}) collective-permute-start(bf16[2,4,160,512]{3,2,1,0:T(8,128)(2,1)} %get-tuple-element.280), channel_id=1, source_target_pairs={{0,8},{4,12},{8,0},{12,4},{16,24},{20,28},{24,16},{28,20},{1,9},{5... | collective-permute-start | bytes 3932168 | tf_op jit(solution)/shard_map/ppermute | solution.py:529
  372.4 32.1 %collective-permute-start.47 = (bf16[1,4,160,512]{3,2,1,0:T(8,128)(2,1)S(1)}, bf16[1,4,160,512]{3,2,1,0:T(8,128)(2,1)S(1)}, u32[]{:S(2)}, u32[]{:S(2)}) collective-permute-start(bf16[1,4,160,512]{3,2,1,0:T(8,128)(2,1)S(1)} %bitcast.178), channel_id=1, source_target_pairs={{0,16},{4,20},{8,24},{12,28},{16,0},{20,4},{24,8},{28,12},{1,17},{... | collective-permute-start | bytes 1966088 | tf_op jit(solution)/shard_map/ppermute | solution.py:529
  372.7 31.8 %collective-permute-start.48 = (bf16[1,4,160,512]{3,2,1,0:T(8,128)(2,1)}, bf16[1,4,160,512]{3,2,1,0:T(8,128)(2,1)S(1)}, u32[]{:S(2)}, u32[]{:S(2)}) collective-permute-start(bf16[1,4,160,512]{3,2,1,0:T(8,128)(2,1)} %bitcast.51), channel_id=1, source_target_pairs={{0,8},{4,12},{8,0},{12,4},{16,24},{20,28},{24,16},{28,20},{1,9},{5... | collective-permute-start | bytes 1966088 | tf_op jit(solution)/shard_map/ppermute | solution.py:529
  373.5 31.0 %collective-permute-start.45 = (bf16[1,4,128,512]{3,2,1,0:T(8,128)(2,1)}, bf16[1,4,128,512]{3,2,1,0:T(8,128)(2,1)S(1)}, u32[]{:S(2)}, u32[]{:S(2)}) collective-permute-start(bf16[1,4,128,512]{3,2,1,0:T(8,128)(2,1)} %bitcast.48), channel_id=1, source_target_pairs={{0,16},{4,20},{8,24},{12,28},{16,0},{20,4},{24,8},{28,12},{1,17},{... | collective-permute-start | bytes 1572872 | tf_op jit(solution)/shard_map/ppermute | solution.py:529
  374.6 29.9 %collective-permute-start.46 = (bf16[1,4,128,512]{3,2,1,0:T(8,128)(2,1)}, bf16[1,4,128,512]{3,2,1,0:T(8,128)(2,1)S(1)}, u32[]{:S(2)}, u32[]{:S(2)}) collective-permute-start(bf16[1,4,128,512]{3,2,1,0:T(8,128)(2,1)} %bitcast.49), channel_id=1, source_target_pairs={{0,8},{4,12},{8,0},{12,4},{16,24},{20,28},{24,16},{28,20},{1,9},{5... | collective-permute-start | bytes 1572872 | tf_op jit(solution)/shard_map/ppermute | solution.py:529
  421.0 20.2 %collective-permute-start.51 = (bf16[256,512]{1,0:T(8,128)(2,1)S(1)}, bf16[256,512]{1,0:T(8,128)(2,1)S(1)}, u32[]{:S(2)}, u32[]{:S(2)}) collective-permute-start(bf16[256,512]{1,0:T(8,128)(2,1)S(1)} %get-tuple-element.334), channel_id=1, source_target_pairs={{0,2},{1,3},{2,0},{3,1},{4,6},{5,7},{6,4},{7,5},{8,10},{9,11},{10,... | collective-permute-start | bytes 786440 | tf_op jit(solution)/shard_map/ppermute | solution.py:526
  422.3 21.5 %collective-permute-start.52 = (bf16[256,512]{1,0:T(8,128)(2,1)S(1)}, bf16[256,512]{1,0:T(8,128)(2,1)}, u32[]{:S(2)}, u32[]{:S(2)}) collective-permute-start(bf16[256,512]{1,0:T(8,128)(2,1)S(1)} %get-tuple-element.335), channel_id=1, source_target_pairs={{0,3},{1,0},{2,1},{3,2},{4,7},{5,4},{6,5},{7,6},{8,11},{9,8},{10,9... | collective-permute-start | bytes 786440 | tf_op jit(solution)/shard_map/ppermute | solution.py:526
  423.6 25.0 %collective-permute-start.55 = (bf16[320,512]{1,0:T(8,128)(2,1)}, bf16[320,512]{1,0:T(8,128)(2,1)}, u32[]{:S(2)}, u32[]{:S(2)}) collective-permute-start(bf16[320,512]{1,0:T(8,128)(2,1)} %get-tuple-element.346), channel_id=1, source_target_pairs={{0,1},{1,2},{2,3},{3,0},{4,5},{5,6},{6,7},{7,4},{8,9},{9,10},{10,1... | collective-permute-start | bytes 983048 | tf_op jit(solution)/shard_map/ppermute | solution.py:526
  425.7 42.4 %collective-permute-start.56 = (bf16[320,512]{1,0:T(8,128)(2,1)}, bf16[320,512]{1,0:T(8,128)(2,1)}, u32[]{:S(2)}, u32[]{:S(2)}) collective-permute-start(bf16[320,512]{1,0:T(8,128)(2,1)} %get-tuple-element.347), channel_id=1, source_target_pairs={{0,2},{1,3},{2,0},{3,1},{4,6},{5,7},{6,4},{7,5},{8,10},{9,11},{10,... | collective-permute-start | bytes 983048 | tf_op jit(solution)/shard_map/ppermute | solution.py:526
  431.5 36.5 %collective-permute-start.57 = (bf16[320,512]{1,0:T(8,128)(2,1)S(1)}, bf16[320,512]{1,0:T(8,128)(2,1)}, u32[]{:S(2)}, u32[]{:S(2)}) collective-permute-start(bf16[320,512]{1,0:T(8,128)(2,1)S(1)} %get-tuple-element.348), channel_id=1, source_target_pairs={{0,3},{1,0},{2,1},{3,2},{4,7},{5,4},{6,5},{7,6},{8,11},{9,8},{10,9... | collective-permute-start | bytes 983048 | tf_op jit(solution)/shard_map/ppermute | solution.py:526
  441.2 45.6 %collective-permute-start.54 = (bf16[2,4,96,512]{3,2,1,0:T(8,128)(2,1)}, bf16[2,4,96,512]{3,2,1,0:T(8,128)(2,1)}, u32[]{:S(2)}, u32[]{:S(2)}) collective-permute-start(bf16[2,4,96,512]{3,2,1,0:T(8,128)(2,1)} %get-tuple-element.340), channel_id=1, source_target_pairs={{0,16},{4,20},{8,24},{12,28},{16,0},{20,4},{24,8},{28,12},{1,17},{... | collective-permute-start | bytes 2359304 | tf_op jit(solution)/shard_map/ppermute | solution.py:529
  443.8 47.4 %collective-permute-start.53 = (bf16[2,4,96,512]{3,2,1,0:T(8,128)(2,1)}, bf16[2,4,96,512]{3,2,1,0:T(8,128)(2,1)}, u32[]{:S(2)}, u32[]{:S(2)}) collective-permute-start(bf16[2,4,96,512]{3,2,1,0:T(8,128)(2,1)} %copy-done.36), channel_id=1, source_target_pairs={{0,8},{4,12},{8,0},{12,4},{16,24},{20,28},{24,16},{28,20},{1,9},{5... | collective-permute-start | bytes 2359304 | tf_op jit(solution)/shard_map/ppermute | solution.py:529
  510.6 16.6 %collective-permute-start.82 = (bf16[320,512]{1,0:T(8,128)(2,1)S(1)}, bf16[320,512]{1,0:T(8,128)(2,1)S(1)}, u32[]{:S(2)}, u32[]{:S(2)}) collective-permute-start(bf16[320,512]{1,0:T(8,128)(2,1)S(1)} %add_convert_fusion.12.refs_8_), channel_id=1, source_target_pairs={{0,24},{4,28},{8,16},{12,20},{16,8},{20,12},{24,0},{28,4},{1,25},{... | collective-permute-start | bytes 983048 | tf_op jit(solution)/shard_map/ppermute | solution.py:529
  511.5 15.7 %collective-permute-start.77 = (bf16[320,512]{1,0:T(8,128)(2,1)S(1)}, bf16[320,512]{1,0:T(8,128)(2,1)S(1)}, u32[]{:S(2)}, u32[]{:S(2)}) collective-permute-start(bf16[320,512]{1,0:T(8,128)(2,1)S(1)} %add_convert_fusion.12.refs_8_), channel_id=1, source_target_pairs={{0,4},{4,0},{8,12},{12,8},{16,20},{20,16},{24,28},{28,24},{1,5},{5... | collective-permute-start | bytes 983048 | tf_op jit(solution)/shard_map/ppermute | solution.py:532
  513.9 19.6 %collective-permute-start.67 = (bf16[192,512]{1,0:T(8,128)(2,1)S(1)}, bf16[192,512]{1,0:T(8,128)(2,1)S(1)}, u32[]{:S(2)}, u32[]{:S(2)}) collective-permute-start(bf16[192,512]{1,0:T(8,128)(2,1)S(1)} %get-tuple-element.359), channel_id=1, source_target_pairs={{0,1},{1,2},{2,3},{3,0},{4,5},{5,6},{6,7},{7,4},{8,9},{9,10},{10,1... | collective-permute-start | bytes 589832 | tf_op jit(solution)/shard_map/ppermute | solution.py:526
  521.2 29.5 %collective-permute-start.79 = (bf16[320,512]{1,0:T(8,128)(2,1)S(1)}, bf16[320,512]{1,0:T(8,128)(2,1)S(1)}, u32[]{:S(2)}, u32[]{:S(2)}) collective-permute-start(bf16[320,512]{1,0:T(8,128)(2,1)S(1)} %collective-permute-done.78.refs_9_), channel_id=1, source_target_pairs={{0,4},{4,0},{8,12},{12,8},{16,20},{20,16},{24,28},{28,24},{1,5},{5... | collective-permute-start | bytes 983048 | tf_op jit(solution)/shard_map/ppermute | solution.py:532
  521.6 29.2 %collective-permute-start.81 = (bf16[320,512]{1,0:T(8,128)(2,1)S(1)}, bf16[320,512]{1,0:T(8,128)(2,1)S(1)}, u32[]{:S(2)}, u32[]{:S(2)}) collective-permute-start(bf16[320,512]{1,0:T(8,128)(2,1)S(1)} %collective-permute-done.80.refs_10_), channel_id=1, source_target_pairs={{0,4},{4,0},{8,12},{12,8},{16,20},{20,16},{24,28},{28,24},{1,5},{5... | collective-permute-start | bytes 983048 | tf_op jit(solution)/shard_map/ppermute | solution.py:532
  527.2 23.6 %collective-permute-start.83 = (bf16[320,512]{1,0:T(8,128)(2,1)S(1)}, bf16[320,512]{1,0:T(8,128)(2,1)S(1)}, u32[]{:S(2)}, u32[]{:S(2)}) collective-permute-start(bf16[320,512]{1,0:T(8,128)(2,1)S(1)} %collective-permute-done.82.refs_11_), channel_id=1, source_target_pairs={{0,4},{4,0},{8,12},{12,8},{16,20},{20,16},{24,28},{28,24},{1,5},{5... | collective-permute-start | bytes 983048 | tf_op jit(solution)/shard_map/ppermute | solution.py:532
  (90 other events, 867.4 us)

commit v4 on v3

--- a/solution.py
+++ b/solution.py
@@ -11,7 +11,8 @@
 
 eps = 1e-06
 bf16 = jnp.bfloat16
-HINT = pl.CostEstimate(flops=1, transcendentals=0, bytes_accessed=1)
+LIGHT = pl.CostEstimate(flops=1, transcendentals=0, bytes_accessed=1)
+HEAVY = pl.CostEstimate(flops=20_000_000_000, transcendentals=0, bytes_accessed=10_000_000)
 f32 = jnp.float32
 
 
@@ -101,7 +102,7 @@
         ],
         input_output_aliases={3 + i: i for i in range(len(given))},
         compiler_params=pltpu.CompilerParams(vmem_limit_bytes=56 * 1024 * 1024),
-        cost_estimate=HINT,
+        cost_estimate=HEAVY,
         name="attend",
     )(qkv, qkv, qkv, *given)
 
@@ -181,7 +182,7 @@
         ],
         input_output_aliases={7 + i: i for i in range(len(given))},
         compiler_params=pltpu.CompilerParams(vmem_limit_bytes=56 * 1024 * 1024),
-        cost_estimate=HINT,
+        cost_estimate=HEAVY,
         name="attend_back",
     )(qkv, qkv, qkv, grad, attended, inverse, probs, *given)
 
@@ -307,7 +308,7 @@
             pltpu.VMEM((rows, width), f32),
         ],
         compiler_params=pltpu.CompilerParams(vmem_limit_bytes=58 * 1024 * 1024),
-        cost_estimate=HINT,
+        cost_estimate=HEAVY,
         name="feed_forward",
     )(hidden, d_out, up, bias, down, alive, last_bias, *given)
 
@@ -347,7 +348,7 @@
         out_specs=[spec, spec],
         out_shape=[shape, shape],
         compiler_params=pltpu.CompilerParams(vmem_limit_bytes=48 * 1024 * 1024),
-        cost_estimate=HINT,
+        cost_estimate=HEAVY,
         name="weight_grads",
     )(left, rights)
     flat = (ns, nq, count * rq, wide // 2)
@@ -395,7 +396,7 @@
             jax.ShapeDtypeStruct((rows, width), bf16),
         ],
         compiler_params=pltpu.CompilerParams(vmem_limit_bytes=48 * 1024 * 1024),
-        cost_estimate=HINT,
+        cost_estimate=HEAVY,
         name="middle",
     )(tokens, attended, weight, bias, gain, shift)
 
@@ -465,7 +466,7 @@
         ],
         scratch_shapes=[pltpu.VMEM((width, width), f32)],
         compiler_params=pltpu.CompilerParams(vmem_limit_bytes=48 * 1024 * 1024),
-        cost_estimate=HINT,
+        cost_estimate=HEAVY,
         name="middle_back",
     )(grad, middle, d_out, attended, weight, gain)
 
@@ -505,7 +506,7 @@
             jax.ShapeDtypeStruct((8, width), f32),
         ],
         compiler_params=pltpu.CompilerParams(vmem_limit_bytes=48 * 1024 * 1024),
-        cost_estimate=HINT,
+        cost_estimate=HEAVY,
         name="entry_back",
     )(grads, weight, tokens, d_mid, gain)
 
@@ -582,7 +583,7 @@
         out_specs=pl.BlockSpec(memory_space=pltpu.VMEM),
         out_shape=jax.ShapeDtypeStruct((rq + 16, line), bf16),
         scratch_shapes=[pltpu.SemaphoreType.DMA(())],
-        cost_estimate=HINT,
+        cost_estimate=LIGHT,
         name="pack",
     )(weight, *small)
 
@@ -594,27 +595,6 @@
 def lanes_of(links, values, part):
     n = values.shape[-1] // links.bits
     return values[..., part * n : (part + 1) * n]
-
-
-def gather_step(links, held, step):
-    out = []
-    for part, pieces in enumerate(held):
-        bit = 1 << ((part + step) % links.bits)
-        known = sorted(pieces)
-        sent = jnp.stack([pieces[k] for k in known])
-        got = links.chip(sent, bit)
-        out.append((bit, known, got))
-    return out
-
-
-def gather_merge(links, held, got):
-    merged = []
-    for pieces, (bit, known, values) in zip(held, got):
-        more = dict(pieces)
-        for i, k in enumerate(known):
-            more[k ^ bit] = values[i]
-        merged.append(more)
-    return merged
 
 
 def assemble(links, weights, got_mine, got_mate):
@@ -697,7 +677,7 @@
         out_specs=[pl.BlockSpec(memory_space=pltpu.VMEM)] * n,
         scratch_shapes=[pltpu.SemaphoreType.DMA((count,))],
         compiler_params=pltpu.CompilerParams(vmem_limit_bytes=32 * 1024 * 1024),
-        cost_estimate=HINT,
+        cost_estimate=LIGHT,
         name="assemble",
     )(*weights, *got_mine, *got_mate)
 
@@ -714,19 +694,24 @@
         self.done = 0
         return own
 
-    def step(self, after=None):
-        held = self.held if after is None else tie(self.held, after)
-        got = gather_step(self.links, held, self.done)
-        self.held = gather_merge(self.links, held, got)
-        self.done += 1
-        for _, _, values in got:
+    def send(self):
+        self.arrived = [
+            self.links.chip(jnp.stack([pieces[k] for k in sorted(pieces)]), self.bit(part))
+            for part, pieces in enumerate(self.held)
+        ]
+
+    def bit(self, part):
+        return 1 << ((part + self.done) % self.links.bits)
+
+    def absorb(self):
+        for part, (pieces, values) in enumerate(zip(self.held, self.arrived)):
+            for i, k in enumerate(sorted(pieces)):
+                pieces[k ^ self.bit(part)] = values[i]
             self.mine.append(values)
             self.mate.append(self.links.core(values))
-        return self.mine[-1]
+        self.done += 1
 
     def full(self):
-        while self.done < self.links.bits:
-            self.step()
         return assemble(self.links, self.weights, self.mine, self.mate)
 
 
@@ -794,7 +779,7 @@
                 jax.ShapeDtypeStruct((nq // 2, ns, r, lanes), bf16) for r in sizes for _ in range(2)
             ],
             compiler_params=pltpu.CompilerParams(vmem_limit_bytes=32 * 1024 * 1024),
-            cost_estimate=HINT,
+            cost_estimate=LIGHT,
             name="core_sums",
         )(*self.kept, *self.got)
 
@@ -829,11 +814,15 @@
         return self.buffers
 
     def send(self):
-        links = self.links
-        last = self.done == links.bits - 1 and self.parts is not None
+        self.arrived = [
+            self.links.chip(buffer, 1 << ((part + self.done) % self.links.bits))
+            for part, buffer in enumerate(self.buffers)
+        ]
+
+    def absorb(self):
+        last = self.done == self.links.bits - 1 and self.parts is not None
         out = []
-        for part, (pieces, buffer, stay) in enumerate(zip(self.held, self.buffers, self.stay)):
-            got = links.chip(buffer, 1 << ((part + self.done) % links.bits))
+        for pieces, got, stay in zip(self.held, self.arrived, self.stay):
             if last:
                 out.append((pieces[0], got[0]))
                 continue
@@ -846,14 +835,16 @@
         self.held = out
         self.done += 1
 
-    def prepare_along(self):
+    def prepare_along(self, lines=None):
         links = self.links
         ns = links.ns
         if self.parts is not None:
             lanes = self.lanes
             total = sum(self.rows)
-
-            def kernel(a0, b0, a1, b1, *outs):
+            more = 0 if lines is None else lines.shape[1]
+
+            def kernel(a0, b0, a1, b1, *refs):
+                outs = refs[-ns:]
                 z = lax.axis_index("shard")
                 for s, out in enumerate(outs):
                     at = lax.rem(z + s, ns)
@@ -862,15 +853,19 @@
                         n = a.shape[1]
                         out[base : base + n, :] = (a[at].astype(f32) + b[at].astype(f32)).astype(bf16)
                         base += n
+                    if more:
+                        out[base : base + more, :] = refs[0][at].astype(bf16)
 
             pairs = [x for pair in self.held for x in pair]
+            if more:
+                pairs.append(lines)
             self.buffers = pl.pallas_call(
                 kernel,
-                in_specs=[pl.BlockSpec(memory_space=pltpu.VMEM)] * 4,
+                in_specs=[pl.BlockSpec(memory_space=pltpu.VMEM)] * len(pairs),
                 out_specs=[pl.BlockSpec(memory_space=pltpu.VMEM)] * ns,
-                out_shape=[jax.ShapeDtypeStruct((total, lanes), bf16)] * ns,
+                out_shape=[jax.ShapeDtypeStruct((total + more, lanes), bf16)] * ns,
                 compiler_params=pltpu.CompilerParams(vmem_limit_bytes=32 * 1024 * 1024),
-                cost_estimate=HINT,
+                cost_estimate=LIGHT,
                 name="chip_sums",
             )(*pairs)
             return self.buffers
@@ -882,24 +877,24 @@
         return self.buffers
 
     def send_along(self):
+        self.arrived = [
+            self.links.along(self.buffers[s], s) for s in range(1, self.links.ns)
+        ]
+
+    def settle(self):
         final = self.buffers[0].astype(f32)
-        for s in range(1, self.links.ns):
-            final = final + self.links.along(self.buffers[s], s).astype(f32)
-        self.final = final.astype(bf16)
-        return self.final
-
-    def spread(self, after=None):
-        links = self.links
-        final = self.final if after is None else tie(self.final, after)
-        others = [links.chip(final, k) for k in range(1, links.nq)]
-        self.mine = [final] + others
-        self.mate = [links.core(v) for v in self.mine]
-        return self.mate
+        for x in self.arrived:
+            final = final + x.astype(f32)
+        total = sum(self.rows)
+        self.final = final[:total].astype(bf16)
+        return final[total:]
 
     def owned(self):
         links = self.links
         _, q, c = links.here()
-        mine, mate = jnp.stack(self.mine), jnp.stack(self.mate)
+        rows = slice(self.base, self.base + sum(self.rows))
+        mine = jnp.stack([v[rows] for v in self.mine])
+        mate = jnp.stack([v[rows] for v in self.mate])
         both = jnp.stack([jnp.where(c == 0, mine, mate), jnp.where(c == 0, mate, mine)])
         ordered = [lax.dynamic_index_in_dim(both, q ^ j, 1) for j in range(links.nq)]
         full = jnp.concatenate(ordered, 1).astype(f32)
@@ -911,8 +906,24 @@
         return outs
 
 
+class Spread:
+    def __init__(self, links, scatters):
+        self.links, self.scatters = links, scatters
+        finals = [s.final for s in scatters]
+        self.final = jnp.concatenate(finals) if len(finals) > 1 else finals[0]
+        self.others = [links.chip(self.final, k) for k in range(1, links.nq)]
+
+    def pair(self):
+        mine = [self.final] + self.others
+        self.mate = [self.links.core(v) for v in mine]
+        base = 0
+        for s in self.scatters:
+            s.mine, s.mate, s.base = mine, self.mate, base
+            base += sum(s.rows)
+
+
 def owned_by_kernel(links, scatters, shapes, place):
-    sides = [x for s in scatters for x in s.mine + s.mate]
+    sides = scatters[0].mine + scatters[0].mate
     nq = links.nq
 
     def kernel(*refs):
@@ -920,11 +931,10 @@
         rep = lax.axis_index("rep")
         q, first_core = rep // 2, rep % 2 == 0
         for at, scatter in enumerate(scatters):
-            refs_here = ins[2 * nq * at : 2 * nq * (at + 1)]
             for k in range(nq):
-                mine, mate = refs_here[k], refs_here[nq + k]
+                mine, mate = ins[k], ins[nq + k]
                 chip = q ^ k
-                base = 0
+                base = scatter.base
                 for i, low, high in scatter.plan():
                     for lo, hi, left, right, out, factor, offset, zero, one in place(at, i):
                         a, b = max(lo, low), min(hi, high)
@@ -945,7 +955,7 @@
         out_specs=[pl.BlockSpec(memory_space=pltpu.VMEM)] * len(shapes),
         out_shape=[jax.ShapeDtypeStruct(s, f32) for s in shapes],
         compiler_params=pltpu.CompilerParams(vmem_limit_bytes=48 * 1024 * 1024),
-        cost_estimate=HINT,
+        cost_estimate=LIGHT,
         name="owned",
     )(*sides)
 
@@ -1014,12 +1024,16 @@
     return grad.transpose(1, 3, 2, 0, 4).reshape(chips * rows // groups, groups * cores * lanes)
 
 
-def total_of(links, lines):
-    z, _, _ = links.here()
+def total_over_rep(links, lines):
     lines = lines + links.core(lines)
     crossed = [links.chip(lines, k) for k in range(1, links.nq)]
     for x in crossed:
         lines = lines + x
+    return lines
+
+
+def total_over_shard(links, lines):
+    z, _, _ = links.here()
     moved = [
         links.along(lax.dynamic_index_in_dim(lines, (z + s) % links.ns, 0, False), s)
         for s in range(1, links.ns)
@@ -1072,8 +1086,13 @@
     own_a = gather_a.start(jnp.stack([g[:n] for g in got]))
     got_b = gather_along(links, tie(piece_of(links, [w_out, w_up]), own_a))
     while gather_a.done < links.bits:
-        last_a = gather_a.step()
+        gather_a.send()
+        gather_a.absorb()
+    gather_a.mine, got_b = meet(gather_a.mine, got_b)
     (full_qkv,) = gather_a.full()
+    got_c = gather_along(links, tie(piece_of(links, [w_down]), got_b))
+    gather_b.start(jnp.stack(got_b))
+    gather_b.send()
     all_small = jnp.stack([packed_a[n : n + n_lines]] + got_small).reshape(ns, -1)
     all_small = jnp.concatenate(
         [lax.dynamic_index_in_dim(all_small, (z - j) % ns, 0) for j in range(ns)]
@@ -1095,30 +1114,35 @@
     qkv_bias = jnp.concatenate([bias_f[:width], none, bias_f[width:]])
     qkv_b = (projected + qkv_bias).astype(bf16)
     pairs = width // (2 * HDIM)
-    cuts = (0, pairs // 4, pairs * 3 // 4, pairs)
-    qkv_b, got_b = meet(qkv_b, got_b)
-    got_c = gather_along(links, tie(piece_of(links, [w_down]), got_b))
-    gather_b.start(jnp.stack(got_b))
-    gather_b.step()
+    cuts = (0, pairs * 3 // 8, pairs * 5 // 8, pairs)
+    qkv_b, gather_b.arrived = meet(qkv_b, gather_b.arrived)
+    gather_b.absorb()
+    while gather_b.done < links.bits - 1:
+        gather_b.send()
+        gather_b.absorb()
+    gather_b.send()
     kept = attend(qkv_b, cuts[0], cuts[1])
-    kept, gather_b.held = meet(kept, gather_b.held)
-    while gather_b.done < links.bits:
-        gather_b.step()
+    kept, gather_b.arrived, got_c = meet(kept, gather_b.arrived, got_c)
+    gather_b.absorb()
+    gather_c.start(jnp.stack(got_c))
+    gather_c.send()
     kept = attend(qkv_b, cuts[1], cuts[2], kept)
-    kept, gather_b.mine, got_c = meet(kept, gather_b.mine, got_c)
-    gather_c.start(jnp.stack(got_c))
+    kept, gather_c.arrived = meet(kept, gather_c.arrived)
+    gather_c.absorb()
     while gather_c.done < links.bits - 1:
-        gather_c.step()
+        gather_c.send()
+        gather_c.absorb()
+    gather_c.send()
     kept = attend(qkv_b, cuts[2], cuts[3], kept)
-    kept, gather_c.held = meet(kept, gather_c.held)
-    gather_c.step()
+    kept, gather_c.arrived = meet(kept, gather_c.arrived)
+    gather_c.absorb()
     attended_b, inverse, probs_b = kept
     full_wout, full_wup = gather_b.full()
     gain_two = full_g2[None]
     middle, hidden_two_b = middle_of(
         tokens_b, attended_b, full_wout, full_bout[None], gain_two, full_s2[None]
     )
-    middle, gather_c.mine = meet(middle, gather_c.mine)
+    middle, gather_c.mate = meet(middle, gather_c.mate)
     (full_wdown,) = gather_c.full()
     bias_up = full_bup[None]
     last_bias = full_bdown[None]
@@ -1139,52 +1163,88 @@
     )
     grad_g2, grad_s2, grad_bout, grad_bdown = (sums[i] for i in range(4))
     scatter_2 = Scatter(links, away + [out_away], home + [out_home])
-    d_att_b, scatter_2.kept = meet(d_att_b, scatter_2.kept)
-    d_att_b, scatter_2.buffers = meet(d_att_b, scatter_2.prepare())
-    scatter_2.send()
-    half = pairs // 2
-    grads = attend_back(qkv_b, d_att_b, attended_b, inverse, probs_b, 0, half)
-    grads, scatter_1.held, scatter_2.held = meet(grads, scatter_1.held, scatter_2.held)
-    grads, scatter_1.buffers, scatter_2.buffers = meet(
-        grads, scatter_1.prepare(), scatter_2.prepare()
+    d_att_b, scatter_1.arrived = meet(d_att_b, scatter_1.arrived)
+    scatter_1.absorb()
+    d_att_b, scatter_1.buffers, scatter_2.buffers = meet(
+        d_att_b, scatter_1.prepare(), scatter_2.prepare()
     )
     scatter_1.send()
     scatter_2.send()
+    half = pairs * 5 // 8
+    grads = attend_back(qkv_b, d_att_b, attended_b, inverse, probs_b, 0, half)
+    for _ in range(links.bits - 2):
+        scatter_1.absorb()
+        scatter_1.prepare()
+        scatter_1.send()
+        scatter_2.absorb()
+        scatter_2.prepare()
+        scatter_2.send()
+    grads, scatter_1.arrived, scatter_2.arrived = meet(
+        grads, scatter_1.arrived, scatter_2.arrived
+    )
+    scatter_1.absorb()
+    scatter_2.absorb()
+    grads, scatter_1.buffers, scatter_2.buffers = meet(
+        grads, scatter_1.prepare_along(), scatter_2.prepare()
+    )
+    scatter_1.send_along()
+    scatter_2.send()
     grads = attend_back(qkv_b, d_att_b, attended_b, inverse, probs_b, half, pairs, grads)
-    grads, scatter_1.held, scatter_2.held = meet(grads, scatter_1.held, scatter_2.held)
-    grads, scatter_1.buffers, scatter_2.buffers = meet(
-        grads, scatter_1.prepare_along(), scatter_2.prepare_along()
-    )
-    scatter_1.send_along()
+    grads, scatter_1.arrived, scatter_2.arrived = meet(
+        grads, scatter_1.arrived, scatter_2.arrived
+    )
+    scatter_1.settle()
+    scatter_2.absorb()
+    grads, scatter_1.final, scatter_2.buffers = meet(
+        grads, scatter_1.final, scatter_2.prepare_along()
+    )
+    scatter_2.send_along()
     d_qkv, qv_sums = grads
     scatter_3 = Scatter(links, *weight_grads(links, hidden_one_b, d_qkv))
-    scatter_3.kept, scatter_2.buffers = meet(scatter_3.kept, scatter_2.buffers)
-    scatter_2.send_along()
     d_qkv, scatter_3.buffers = meet(d_qkv, scatter_3.prepare())
     scatter_3.send()
     input_grad, entry_sums = entry_back(d_qkv, full_qkv, tokens_b, d_mid, full_g1[None])
+    for _ in range(links.bits - 2):
+        scatter_3.absorb()
+        scatter_3.prepare()
+        scatter_3.send()
+    input_grad, entry_sums, scatter_3.arrived, scatter_2.arrived = meet(
+        input_grad, entry_sums, scatter_3.arrived, scatter_2.arrived
+    )
+    scatter_3.absorb()
+    scatter_3.prepare()
+    scatter_3.send()
+    scatter_2.settle()
+    input_grad = input_grad.reshape(inputs.shape)
     grad_g1, grad_s1 = entry_sums[0], entry_sums[1]
     grad_qvb = qv_sums.reshape(-1)
-    input_grad, scatter_1.final = meet(input_grad, scatter_1.final)
-    scatter_1.spread()
-    input_grad, scatter_3.held = meet(input_grad, scatter_3.held)
-    input_grad = input_grad.reshape(inputs.shape)
-    grad_g1, scatter_3.buffers, scatter_2.final = meet(
-        grad_g1, scatter_3.prepare(), scatter_2.final
-    )
-    scatter_3.send()
-    scatter_2.spread()
-    scatter_3.buffers = scatter_3.prepare_along()
-    scatter_3.send_along()
-    scatter_3.final, scatter_1.mate, scatter_2.mate = meet(
-        scatter_3.final, scatter_1.mate, scatter_2.mate
-    )
-    scatter_3.spread()
-    o_wdown, o_wup, o_wout = owned_feed_forward(links, scatter_1, scatter_2, w_up, w_down, w_out)
-    o_qkv = owned_qkv(links, scatter_3, w_qkv)
     small_grads = (grad_g1, grad_s1, grad_bout, grad_g2, grad_s2, grad_bdown, grad_qvb, grad_bup)
     joined = jnp.concatenate([g.reshape(ns, -1) for g in small_grads], 1)
-    joined = total_of(links, joined)
+    joined = total_over_rep(links, joined)
+    scatter_3.arrived, scatter_1.final, scatter_2.final = meet(
+        scatter_3.arrived, scatter_1.final, scatter_2.final
+    )
+    scatter_3.absorb()
+    n_small = joined.shape[1]
+    ride = scatter_3.parts is not None and n_small % scatter_3.lanes == 0
+    if ride:
+        lines = joined.reshape(ns, -1, scatter_3.lanes)
+        lines = jnp.pad(lines, ((0, 0), (0, -lines.shape[1] % 16), (0, 0)))
+        scatter_3.buffers = scatter_3.prepare_along(lines)
+    else:
+        scatter_3.prepare_along()
+        joined = total_over_shard(links, joined)
+    scatter_3.send_along()
+    spread_12 = Spread(links, [scatter_1, scatter_2])
+    scatter_3.arrived, spread_12.others = meet(scatter_3.arrived, spread_12.others)
+    spread_12.pair()
+    arrived_lines = scatter_3.settle()
+    spread_3 = Spread(links, [scatter_3])
+    if ride:
+        joined = arrived_lines.reshape(-1)[:n_small]
+    o_wdown, o_wup, o_wout = owned_feed_forward(links, scatter_1, scatter_2, w_up, w_down, w_out)
+    spread_3.pair()
+    o_qkv = owned_qkv(links, scatter_3, w_qkv)
     owned = []
     base = 0
     for n in sizes:

time: 576 us -> 501 us (0.87)
  waiting for transfers between devices: 106 us -> 55 us
  starting transfers between devices: 125 us -> 88.4 us
  local copies, waits for them, and re-layouts: 28.6 us -> 41.4 us
    ppermute x21 -> x18, starting transfers between devices: 56.4 us -> 26.4 us  [along(): lax.ppermute(values, 'shard', [(i, (i + step) % self.ns) for i in range(s...]
    ppermute x36 -> x33, waiting for transfers between devices: 48.2 us -> 20.2 us  [chip(): return lax.ppermute(values, 'rep', [(i, i ^ 2 * k) for i in range(self.nr)])]
    ppermute x21 -> x18, waiting for transfers between devices: 53.9 us -> 32.1 us  [along(): lax.ppermute(values, 'shard', [(i, (i + step) % self.ns) for i in range(s...]
    unnamed x121 -> x138, local copies, waits for them, and re-layouts: 21.7 us -> 29.7 us
    convert_element_type x9 -> x7, other arithmetic: 14.7 us -> 8.72 us  [the longest x5 7.72 us: absorb(): (pieces[k].astype(f32) + got[i].astype(f32)).astype(bf16)]
    ppermute x34 -> x30, starting transfers between devices: 39.2 us -> 33.6 us  [core(): return lax.ppermute(values, 'rep', [(i, i ^ 1) for i in range(self.nr)])]
    ppermute x36 -> x33, starting transfers between devices: 29.2 us -> 28.4 us  [chip(): return lax.ppermute(values, 'rep', [(i, i ^ 2 * k) for i in range(self.nr)])]
  transfers between devices with their start and end apart: 91 -> 81, of which waited for: 16 -> 18; matrix products, arithmetic and copies ran while one was open for 7% -> 8% of each run, Pallas kernels for 37% -> 42%
where the time goes in v4:
time: 501 us; the launch traced here: 495 us
  Pallas kernels  277 us (55%)
  starting transfers between devices  88.4 us (18%)
  waiting for transfers between devices  55 us (11%)
  local copies, waits for them, and re-layouts  41.4 us (8%)
  other arithmetic  21.6 us (4%)
  matrix products  9.01 us (2%)
    pallas_call x2, Pallas kernels, feed_forward(): pl.pallas_call(kernel, grid=(ns,), in_specs=[full(), full(), pl.BlockSpec...  91.8 us
    pallas_call x2, Pallas kernels, attend_back(): pl.pallas_call(kernel, grid=(count,), in_specs=[column(0), column(pairs),...  58.3 us
    pallas_call x3, Pallas kernels, attend(): pl.pallas_call(kernel, grid=(count,), in_specs=[column(0), column(pairs),...  52.4 us
    ppermute x30, starting transfers between devices, core(): return lax.ppermute(values, 'rep', [(i, i ^ 1) for i in range(self.nr)])  33.6 us
    ppermute x18, waiting for transfers between devices, along(): lax.ppermute(values, 'shard', [(i, (i + step) % self.ns) for i in range(s...  32.1 us
    unnamed x138, local copies, waits for them, and re-layouts  29.7 us
    ppermute x33, starting transfers between devices, chip(): return lax.ppermute(values, 'rep', [(i, i ^ 2 * k) for i in range(self.nr)])  28.4 us
    ppermute x18, starting transfers between devices, along(): lax.ppermute(values, 'shard', [(i, (i + step) % self.ns) for i in range(s...  26.4 us
  transfers between devices with their start and end apart: 81, of which 18 were waited for; matrix products, arithmetic and copies ran while one was open for 8% of the time, Pallas kernels for 42%

profile of v4, /device:TPU:1, one launch (start us, length us, event | category | flops | bytes accessed | tf_op | source)
XLA Modules:
  0.0 495.4 jit_solution(6313181521290435360)
XLA Ops:
  0.7 2.5 pack.1
  3.2 4.2 collective-permute-start.2
  9.3 2.0 convert_reduce_fusion
  12.4 3.3 select_bitcast_fusion.refs_1_.dm_ref
  18.3 9.7 %collective-permute-done.1 = bf16[80,1536]{1,0:T(8,128)(2,1)} collective-permute-done((bf16[80,1536]{1,0:T(8,128)(2,1)}, bf16[80,1536]{1,0:T(8,128)(2,1)}, u32[]{:S(2)}, u32[]{:S(2)}) %collective-permute-start.1) | collective-permute-done | bytes 245792 | tf_op jit(solution)/shard_map/ppermute | solution.py:527
  30.0 1.9 collective-permute-start.8
  39.9 3.9 collective-permute-done.3.refs_2_
  46.9 3.9 collective-permute-start.10
  50.8 8.9 %collective-permute-done.8 = bf16[64,2560]{1,0:T(8,128)(2,1)S(1)} collective-permute-done((bf16[64,2560]{1,0:T(8,128)(2,1)S(1)}, bf16[64,2560]{1,0:T(8,128)(2,1)S(1)}, u32[]{:S(2)}, u32[]{:S(2)}) %collective-permute-start.8) | collective-permute-done | bytes 327712 | tf_op jit(solution)/shard_map/ppermute | solution.py:527
  59.7 1.9 collective-permute-start.12
  68.9 9.0 %fusion.refs_0_.refs_1_.refs_2_ = bf16[1104,3072]{1,0:T(8,128)(2,1)} fusion(bf16[1104,1024]{1,0:T(8,128)(2,1)S(1)} %fusion.6.left_ref, bf16[1024,3072]{1,0:T(8,128)(2,1)S(1)} %assemble.3.w_ref, f32[3072]{0:T(1024)S(1)} %pad_maximum_fusion.12), kind=kOutput, calls=%fused_computation.1 | convolution fusion | flops 6952550400 | bytes 15347712 | tf_op jit(solution)/shard_map/dot_general | solution.py:26
  80.3 19.1 %attend.3 = (bf16[1104,1024]{1,0:T(8,128)(2,1)}, f32[1104,1024]{1,0:T(8,128)}, bf16[16,1104,1104]{2,1,0:T(8,128)(2,1)}) custom-call(bf16[1104,3072]{1,0:T(8,128)(2,1)} %fusion.refs_0_.refs_1_.refs_2_, bf16[1104,3072]{1,0:T(8,128)(2,1)} %fusion.refs_0_.refs_1_.refs_2_, bf16[1104,3072]{1,0:T(8,128)(2,1)} %fusion.refs_0_.refs_1_.refs_2_), custom_call_target="tpu_custom_call" | custom-call | flops 20000000000 | bytes 10000000 | tf_op jit(solution)/shard_map/attend/pallas_call | solution.py:89
  99.5 2.7 collective-permute-start.26
  105.3 14.1 %attend.4 = (bf16[1104,1024]{1,0:T(8,128)(2,1)}, f32[1104,1024]{1,0:T(8,128)}, bf16[16,1104,1104]{2,1,0:T(8,128)(2,1)}) custom-call(bf16[1104,3072]{1,0:T(8,128)(2,1)} %fusion.refs_0_.refs_1_.refs_2_, bf16[1104,3072]{1,0:T(8,128)(2,1)} %fusion.refs_0_.refs_1_.refs_2_, ...), custom_call_target="tpu_custom_call", output_to_operand_aliasing={{0}: (3, {}), {1}: (4, {}), {2}: (5, {})} | custom-call | flops 20000000000 | bytes 10000000 | tf_op jit(solution)/shard_map/attend/pallas_call | solution.py:89
  125.2 19.1 %attend.5 = (bf16[1104,1024]{1,0:T(8,128)(2,1)}, f32[1104,1024]{1,0:T(8,128)}, bf16[16,1104,1104]{2,1,0:T(8,128)(2,1)}) custom-call(bf16[1104,3072]{1,0:T(8,128)(2,1)} %fusion.refs_0_.refs_1_.refs_2_, bf16[1104,3072]{1,0:T(8,128)(2,1)} %fusion.refs_0_.refs_1_.refs_2_, ...), custom_call_target="tpu_custom_call", output_to_operand_aliasing={{0}: (3, {}), {1}: (4, {}), {2}: (5, {})} | custom-call | flops 20000000000 | bytes 10000000 | tf_op jit(solution)/shard_map/attend/pallas_call | solution.py:89
  145.9 3.6 assemble.4
  149.6 3.3 copy-done.28
  156.3 7.1 %middle.1 = (f32[1104,1024]{1,0:T(8,128)}, bf16[1104,1024]{1,0:T(8,128)(2,1)S(1)}) custom-call(bf16[1104,1024]{1,0:T(8,128)(2,1)} %bitcast.124, bf16[1104,1024]{1,0:T(8,128)(2,1)} %get-tuple-element.213.att_ref.refs_4_, bf16[1024,1024]{1,0:T(8,128)(2,1)S(1)} %copy-done.30, f32[1,1024]{1,0:T(1,128)S(1)} %bitcast.140, f32[1,1024]{1,0:T(1,128)S(1)} %bitcast.137, ...), custom_call_target="tpu_custom_call" | custom-call | flops 20000000000 | bytes 10000000 | tf_op jit(solution)/shard_map/middle/pallas_call | solution.py:389
  164.7 2.4 assemble.5.refs_4_
  167.1 3.2 copy-done.2
  170.4 45.3 %feed_forward.2 = (f32[1104,1024]{1,0:T(8,128)}, f32[1104,1024]{1,0:T(8,128)}, bf16[4,512,512]{2,1,0:T(8,128)(2,1)}, bf16[4,512,512]{2,1,0:T(8,128)(2,1)}, bf16[...) custom-call(bf16[1104,1024]{1,0:T(8,128)(2,1)} %copy-done.34, ...), custom_call_target="tpu_custom_call" | custom-call | flops 20000000000 | bytes 10000000 | tf_op jit(solution)/shard_map/feed_forward/pallas_call | solution.py:273
  216.2 46.5 %feed_forward.3 = (bf16[1104,1024]{1,0:T(8,128)(2,1)}, f32[1104,1024]{1,0:T(8,128)}, bf16[4,512,512]{2,1,0:T(8,128)(2,1)}, bf16[4,512,512]{2,1,0:T(8,128)(2,1)},...) custom-call(bf16[1104,1024]{1,0:T(8,128)(2,1)} %copy-done.34, ...), custom_call_target="tpu_custom_call" | custom-call | flops 20000000000 | bytes 10000000 | tf_op jit(solution)/shard_map/feed_forward/pallas_call | solution.py:273
  263.3 4.4 core_sums.3
  270.9 13.6 %middle_back.1 = (f32[1104,1024]{1,0:T(8,128)}, bf16[1104,1024]{1,0:T(8,128)(2,1)}, bf16[4,4,64,512]{3,2,1,0:T(8,128)(2,1)S(1)}, bf16[4,4,64,512]{3,2,1,0:T(8,128)(2,1)S(1)}, f32[8,1024]{1,0:T(8,128)S(1)}) custom-call(f32[1104,1024]{1,0:T(8,128)} %get-tuple-element.241.g_ref, f32[1104,1024]{1,0:T(8,128)} %get-tuple-element.227.refs_7_.mid_ref, ...), custom_call_target="tpu_custom_call" | custom-call | flops 20000000000 | bytes 10000000 | tf_op jit(solution)/shard_map/middle_back/pallas_call | solution.py:445
  285.1 8.5 %collective-permute-done.38 = bf16[2,4,128,512]{3,2,1,0:T(8,128)(2,1)S(1)} collective-permute-done((bf16[2,4,128,512]{3,2,1,0:T(8,128)(2,1)}, bf16[2,4,128,512]{3,2,1,0:T(8,128)(2,1)S(1)}, u32[]{:S(2)}, u32[]{:S(2)}) %collective-permute-start.38) | collective-permute-done | bytes 1048608 | tf_op jit(solution)/shard_map/ppermute | solution.py:530
  294.6 2.8 fusion.9
  297.4 2.5 core_sums.4
  302.9 35.5 %attend_back.2 = (bf16[3,1104,1024]{2,1,0:T(8,128)(2,1)}, f32[2,1,1024]{2,1,0:T(1,128)}) custom-call(bf16[1104,3072]{1,0:T(8,128)(2,1)} %fusion.refs_0_.refs_1_.refs_2_, bf16[1104,3072]{1,0:T(8,128)(2,1)} %fusion.refs_0_.refs_1_.refs_2_, bf16[1104,3072]{1,0:T(8,128)(2,1)} %fusion.refs_0_.refs_1_.refs_2_, bf16[1104,1024]{1,0:T(8,128)(2,1)} %get-tuple-element.258.refs_3_, ...), custom_call_target="tpu_custom_call" | custom-call | flops 20000000000 | bytes 10000000 | tf_op jit(solution)/shard_map/attend_back/pallas_call | solution.py:168
  338.4 2.0 collective-permute-done.45
  341.8 2.6 fusion.7
  346.0 1.8 collective-permute-start.48
  350.7 22.8 %attend_back.3 = (bf16[3,1104,1024]{2,1,0:T(8,128)(2,1)}, f32[2,1,1024]{2,1,0:T(1,128)}) custom-call(bf16[1104,3072]{1,0:T(8,128)(2,1)} %fusion.refs_0_.refs_1_.refs_2_, bf16[1104,3072]{1,0:T(8,128)(2,1)} %fusion.refs_0_.refs_1_.refs_2_, bf16[1104,3072]{1,0:T(8,128)(2,1)} %fusion.refs_0_.refs_1_.refs_2_, ...), custom_call_target="tpu_custom_call", output_to_operand_aliasing={{0}: (7, {}), {1}: (8, {})} | custom-call | flops 20000000000 | bytes 10000000 | tf_op jit(solution)/shard_map/attend_back/pallas_call | solution.py:168
  376.9 11.8 %weight_grads.1 = (bf16[4,4,3,64,512]{4,3,2,1,0:T(8,128)(2,1)}, bf16[4,4,3,64,512]{4,3,2,1,0:T(8,128)(2,1)}) custom-call(bf16[1104,1024]{1,0:T(8,128)(2,1)S(1)} %copy-done.9, bf16[3,1104,1024]{2,1,0:T(8,128)(2,1)} %get-tuple-element.305.right_ref.d_ref), custom_call_target="tpu_custom_call" | custom-call | flops 20000000000 | bytes 10000000 | tf_op jit(solution)/shard_map/weight_grads/pallas_call | solution.py:341
  388.6 3.8 collective-permute-start.52
  394.8 2.3 collective-permute-start.57
  397.9 1.9 copy-done.5
  402.3 14.7 %entry_back.1 = (f32[1104,1024]{1,0:T(8,128)}, f32[8,1024]{1,0:T(8,128)S(1)}) custom-call(bf16[3,1104,1024]{2,1,0:T(8,128)(2,1)} %get-tuple-element.305.right_ref.d_ref, bf16[1024,3072]{1,0:T(8,128)(2,1)} %copy-done.3, bf16[1104,1024]{1,0:T(8,128)(2,1)S(1)} %bitcast.125, f32[1104,1024]{1,0:T(8,128)} %get-tuple-element.306.d_mid_ref, f32[1,1024]{1,0:T(1,128)S(1)} %bitcast.141), custom_call_target="tpu_custom_call" | custom-call | flops 20000000000 | bytes 10000000 | tf_op jit(solution)/shard_map/entry_back/pallas_call | solution.py:493
  424.5 2.1 collective-permute-start.60
  427.5 1.8 collective-permute-start.63
  430.3 2.0 collective-permute-done.59
  441.1 6.6 %collective-permute-start.64 = (bf16[208,512]{1,0:T(8,128)(2,1)S(1)}, bf16[208,512]{1,0:T(8,128)(2,1)S(1)}, u32[]{:S(2)}, u32[]{:S(2)}) collective-permute-start(bf16[208,512]{1,0:T(8,128)(2,1)S(1)} %get-tuple-element.332), channel_id=1, source_target_pairs={{0,1},{1,2},{2,3},{3,0},{4,5},{5,6},{6,7},{7,4},{8,9},{9,10},{10,1... | collective-permute-start | bytes 638984 | tf_op jit(solution)/shard_map/ppermute | solution.py:527
  448.4 3.0 collective-permute-done.64
  453.1 9.4 %collective-permute-done.65 = bf16[208,512]{1,0:T(8,128)(2,1)S(1)} collective-permute-done((bf16[208,512]{1,0:T(8,128)(2,1)S(1)}, bf16[208,512]{1,0:T(8,128)(2,1)S(1)}, u32[]{:S(2)}, u32[]{:S(2)}) %collective-permute-start.65) | collective-permute-done | bytes 213024 | tf_op jit(solution)/shard_map/ppermute | solution.py:527
  463.8 5.2 %collective-permute-start.73 = (bf16[192,512]{1,0:T(8,128)(2,1)S(1)}, bf16[192,512]{1,0:T(8,128)(2,1)S(1)}, u32[]{:S(2)}, u32[]{:S(2)}) collective-permute-start(bf16[192,512]{1,0:T(8,128)(2,1)S(1)} %slice.353.refs_0_), channel_id=1, source_target_pairs={{0,4},{4,0},{8,12},{12,8},{16,20},{20,16},{24,28},{28,24},{1,5},{5... | collective-permute-start | bytes 589832 | tf_op jit(solution)/shard_map/ppermute | solution.py:533
  469.0 2.8 collective-permute-start.70
  471.9 5.8 %collective-permute-start.76 = (bf16[192,512]{1,0:T(8,128)(2,1)S(1)}, bf16[192,512]{1,0:T(8,128)(2,1)S(1)}, u32[]{:S(2)}, u32[]{:S(2)}) collective-permute-start(bf16[192,512]{1,0:T(8,128)(2,1)S(1)} %collective-permute-done.72.refs_3_), channel_id=1, source_target_pairs={{0,4},{4,0},{8,12},{12,8},{16,20},{20,16},{24,28},{28,24},{1,5},{5... | collective-permute-start | bytes 589832 | tf_op jit(solution)/shard_map/ppermute | solution.py:533
  486.4 3.0 owned.2
  489.3 5.8 %owned.3 = (f32[1024,1024]{1,0:T(8,128)}, f32[256,4096]{1,0:T(8,128)}, f32[256,1024]{1,0:T(8,128)}) custom-call(bf16[576,512]{1,0:T(8,128)(2,1)S(1)} %constant_dynamic-update-slice_fusion.9.refs_0_, bf16[576,512]{1,0:T(8,128)(2,1)S(1)} %collective-permute-done.67.refs_1_, bf16[576,512]{1,0:T(8,128)(2,1)S(1)} %collective-permute-done.68.refs_2_, ...), custom_call_target="tpu_custom_call" | custom-call | flops 1 | bytes 1 | tf_op jit(solution)/shard_map/owned/pallas_call | solution.py:952
  (340 shorter events, 96.5 us)
Async XLA Ops:
  7.4 20.6 %collective-permute-start.1 = (bf16[80,1536]{1,0:T(8,128)(2,1)}, bf16[80,1536]{1,0:T(8,128)(2,1)}, u32[]{:S(2)}, u32[]{:S(2)}) collective-permute-start(bf16[80,1536]{1,0:T(8,128)(2,1)} %pack.1), channel_id=1, source_target_pairs={{0,2},{1,3},{2,0},{3,1},{4,6},{5,7},{6,4},{7,5},{8,10},{9,11},{10,... | collective-permute-start | bytes 737288 | tf_op jit(solution)/shard_map/ppermute | solution.py:527
  7.4 21.6 %collective-permute-start = (bf16[80,1536]{1,0:T(8,128)(2,1)}, bf16[80,1536]{1,0:T(8,128)(2,1)}, u32[]{:S(2)}, u32[]{:S(2)}) collective-permute-start(bf16[80,1536]{1,0:T(8,128)(2,1)} %pack.1), channel_id=1, source_target_pairs={{0,1},{1,2},{2,3},{3,0},{4,5},{5,6},{6,7},{7,4},{8,9},{9,10},{10,1... | collective-permute-start | bytes 737288 | tf_op jit(solution)/shard_map/ppermute | solution.py:527
  30.0 16.9 %collective-permute-start.9 = (bf16[64,2560]{1,0:T(8,128)(2,1)S(1)}, bf16[64,2560]{1,0:T(8,128)(2,1)S(1)}, u32[]{:S(2)}, u32[]{:S(2)}) collective-permute-start(bf16[64,2560]{1,0:T(8,128)(2,1)S(1)} %pad_maximum_fusion.9), channel_id=1, source_target_pairs={{0,3},{1,0},{2,1},{3,2},{4,7},{5,4},{6,5},{7,6},{8,11},{9,8},{10,9... | collective-permute-start | bytes 983048 | tf_op jit(solution)/shard_map/ppermute | solution.py:527
  30.0 29.6 %collective-permute-start.8 = (bf16[64,2560]{1,0:T(8,128)(2,1)S(1)}, bf16[64,2560]{1,0:T(8,128)(2,1)S(1)}, u32[]{:S(2)}, u32[]{:S(2)}) collective-permute-start(bf16[64,2560]{1,0:T(8,128)(2,1)S(1)} %pad_maximum_fusion.9), channel_id=1, source_target_pairs={{0,2},{1,3},{2,0},{3,1},{4,6},{5,7},{6,4},{7,5},{8,10},{9,11},{10,... | collective-permute-start | bytes 983048 | tf_op jit(solution)/shard_map/ppermute | solution.py:527
  31.9 29.7 %collective-permute-start.7 = (bf16[64,2560]{1,0:T(8,128)(2,1)S(1)}, bf16[64,2560]{1,0:T(8,128)(2,1)S(1)}, u32[]{:S(2)}, u32[]{:S(2)}) collective-permute-start(bf16[64,2560]{1,0:T(8,128)(2,1)S(1)} %pad_maximum_fusion.9), channel_id=1, source_target_pairs={{0,1},{1,2},{2,3},{3,0},{4,5},{5,6},{6,7},{7,4},{8,9},{9,10},{10,1... | collective-permute-start | bytes 983048 | tf_op jit(solution)/shard_map/ppermute | solution.py:527
  43.9 17.7 %collective-permute-start.5 = (bf16[2,3,64,768]{3,2,1,0:T(8,128)(2,1)S(1)}, bf16[2,3,64,768]{3,2,1,0:T(8,128)(2,1)S(1)}, u32[]{:S(2)}, u32[]{:S(2)}) collective-permute-start(bf16[2,3,64,768]{3,2,1,0:T(8,128)(2,1)S(1)} %pad_maximum_fusion.7), channel_id=1, source_target_pairs={{0,16},{4,20},{8,24},{12,28},{16,0},{20,4},{24,8},{28,12},{1,17},{... | collective-permute-start | bytes 1769480 | tf_op jit(solution)/shard_map/ppermute | solution.py:530
  44.3 17.4 %collective-permute-start.6 = (bf16[2,3,64,768]{3,2,1,0:T(8,128)(2,1)S(1)}, bf16[2,3,64,768]{3,2,1,0:T(8,128)(2,1)S(1)}, u32[]{:S(2)}, u32[]{:S(2)}) collective-permute-start(bf16[2,3,64,768]{3,2,1,0:T(8,128)(2,1)S(1)} %pad_maximum_fusion.8), channel_id=1, source_target_pairs={{0,8},{4,12},{8,0},{12,4},{16,24},{20,28},{24,16},{28,20},{1,9},{5... | collective-permute-start | bytes 1769480 | tf_op jit(solution)/shard_map/ppermute | solution.py:530
  46.9 15.5 %collective-permute-start.10 = (bf16[3,64,1536]{2,1,0:T(8,128)(2,1)S(1)}, bf16[3,64,1536]{2,1,0:T(8,128)(2,1)S(1)}, u32[]{:S(2)}, u32[]{:S(2)}) collective-permute-start(bf16[3,64,1536]{2,1,0:T(8,128)(2,1)S(1)} %pad_maximum_fusion.6.refs_1_), channel_id=1, source_target_pairs={{0,4},{4,0},{8,12},{12,8},{16,20},{20,16},{24,28},{28,24},{1,5},{5... | collective-permute-start | bytes 1769480 | tf_op jit(solution)/shard_map/ppermute | solution.py:533
  62.4 37.1 %collective-permute-start.21 = (bf16[256,512]{1,0:T(8,128)(2,1)}, bf16[256,512]{1,0:T(8,128)(2,1)S(1)}, u32[]{:S(2)}, u32[]{:S(2)}) collective-permute-start(bf16[256,512]{1,0:T(8,128)(2,1)} %dynamic_slice.28), channel_id=1, source_target_pairs={{0,3},{1,0},{2,1},{3,2},{4,7},{5,4},{6,5},{7,6},{8,11},{9,8},{10,9... | collective-permute-start | bytes 786440 | tf_op jit(solution)/shard_map/ppermute | solution.py:527
  62.8 39.3 %collective-permute-start.20 = (bf16[256,512]{1,0:T(8,128)(2,1)}, bf16[256,512]{1,0:T(8,128)(2,1)S(1)}, u32[]{:S(2)}, u32[]{:S(2)}) collective-permute-start(bf16[256,512]{1,0:T(8,128)(2,1)} %dynamic_slice.28), channel_id=1, source_target_pairs={{0,2},{1,3},{2,0},{3,1},{4,6},{5,7},{6,4},{7,5},{8,10},{9,11},{10,... | collective-permute-start | bytes 786440 | tf_op jit(solution)/shard_map/ppermute | solution.py:527
  63.2 39.0 %collective-permute-start.19 = (bf16[256,512]{1,0:T(8,128)(2,1)}, bf16[256,512]{1,0:T(8,128)(2,1)}, u32[]{:S(2)}, u32[]{:S(2)}) collective-permute-start(bf16[256,512]{1,0:T(8,128)(2,1)} %dynamic_slice.28), channel_id=1, source_target_pairs={{0,1},{1,2},{2,3},{3,0},{4,5},{5,6},{6,7},{7,4},{8,9},{9,10},{10,1... | collective-permute-start | bytes 786440 | tf_op jit(solution)/shard_map/ppermute | solution.py:527
  79.1 23.6 %collective-permute-start.18 = (bf16[2,3,64,1280]{3,2,1,0:T(8,128)(2,1)}, bf16[2,3,64,1280]{3,2,1,0:T(8,128)(2,1)S(1)}, u32[]{:S(2)}, u32[]{:S(2)}) collective-permute-start(bf16[2,3,64,1280]{3,2,1,0:T(8,128)(2,1)} %pad_maximum_fusion.2), channel_id=1, source_target_pairs={{0,8},{4,12},{8,0},{12,4},{16,24},{20,28},{24,16},{28,20},{1,9},{5... | collective-permute-start | bytes 2949128 | tf_op jit(solution)/shard_map/ppermute | solution.py:530
  80.1 22.5 %collective-permute-start.17 = (bf16[2,3,64,1280]{3,2,1,0:T(8,128)(2,1)S(1)}, bf16[2,3,64,1280]{3,2,1,0:T(8,128)(2,1)S(1)}, u32[]{:S(2)}, u32[]{:S(2)}) collective-permute-start(bf16[2,3,64,1280]{3,2,1,0:T(8,128)(2,1)S(1)} %pad_maximum_fusion.1), channel_id=1, source_target_pairs={{0,16},{4,20},{8,24},{12,28},{16,0},{20,4},{24,8},{28,12},{1,17},{... | collective-permute-start | bytes 2949128 | tf_op jit(solution)/shard_map/ppermute | solution.py:530
  99.5 23.4 %collective-permute-start.26 = (bf16[3,64,2560]{2,1,0:T(8,128)(2,1)S(1)}, bf16[3,64,2560]{2,1,0:T(8,128)(2,1)}, u32[]{:S(2)}, u32[]{:S(2)}) collective-permute-start(bf16[3,64,2560]{2,1,0:T(8,128)(2,1)S(1)} %pad_maximum_fusion.refs_2_), channel_id=1, source_target_pairs={{0,4},{4,0},{8,12},{12,8},{16,20},{20,16},{24,28},{28,24},{1,5},{5... | collective-permute-start | bytes 2949128 | tf_op jit(solution)/shard_map/ppermute | solution.py:533
  102.1 21.8 %collective-permute-start.27 = (bf16[1,3,64,1280]{3,2,1,0:T(8,128)(2,1)S(1)}, bf16[1,3,64,1280]{3,2,1,0:T(8,128)(2,1)}, u32[]{:S(2)}, u32[]{:S(2)}) collective-permute-start(bf16[1,3,64,1280]{3,2,1,0:T(8,128)(2,1)S(1)} %collective-permute-done.15.refs_3_), channel_id=1, source_target_pairs={{0,4},{4,0},{8,12},{12,8},{16,20},{20,16},{24,28},{28,24},{1,5},{5... | collective-permute-start | bytes 1474568 | tf_op jit(solution)/shard_map/ppermute | solution.py:533
  102.2 42.1 %collective-permute-start.28 = (bf16[1,3,64,1280]{3,2,1,0:T(8,128)(2,1)S(1)}, bf16[1,3,64,1280]{3,2,1,0:T(8,128)(2,1)}, u32[]{:S(2)}, u32[]{:S(2)}) collective-permute-start(bf16[1,3,64,1280]{3,2,1,0:T(8,128)(2,1)S(1)} %collective-permute-done.16.refs_4_), channel_id=1, source_target_pairs={{0,4},{4,0},{8,12},{12,8},{16,20},{20,16},{24,28},{28,24},{1,5},{5... | collective-permute-start | bytes 1474568 | tf_op jit(solution)/shard_map/ppermute | solution.py:533
  103.8 15.7 %collective-permute-start.23 = (bf16[1,3,256,256]{3,2,1,0:T(8,128)(2,1)S(1)}, bf16[1,3,256,256]{3,2,1,0:T(8,128)(2,1)S(1)}, u32[]{:S(2)}, u32[]{:S(2)}) collective-permute-start(bf16[1,3,256,256]{3,2,1,0:T(8,128)(2,1)S(1)} %get-tuple-element.368), channel_id=1, source_target_pairs={{0,16},{4,20},{8,24},{12,28},{16,0},{20,4},{24,8},{28,12},{1,17},{... | collective-permute-start | bytes 1179656 | tf_op jit(solution)/shard_map/ppermute | solution.py:530
  105.1 15.8 %collective-permute-start.22 = (bf16[1,3,256,256]{3,2,1,0:T(8,128)(2,1)S(1)}, bf16[1,3,256,256]{3,2,1,0:T(8,128)(2,1)S(1)}, u32[]{:S(2)}, u32[]{:S(2)}) collective-permute-start(bf16[1,3,256,256]{3,2,1,0:T(8,128)(2,1)S(1)} %get-tuple-element.369), channel_id=1, source_target_pairs={{0,8},{4,12},{8,0},{12,4},{16,24},{20,28},{24,16},{28,20},{1,9},{5... | collective-permute-start | bytes 1179656 | tf_op jit(solution)/shard_map/ppermute | solution.py:530
  119.5 25.9 %collective-permute-start.29 = (bf16[2,3,64,1280]{3,2,1,0:T(8,128)(2,1)S(1)}, bf16[2,3,64,1280]{3,2,1,0:T(8,128)(2,1)}, u32[]{:S(2)}, u32[]{:S(2)}) collective-permute-start(bf16[2,3,64,1280]{3,2,1,0:T(8,128)(2,1)S(1)} %collective-permute-done.17.refs_5_), channel_id=1, source_target_pairs={{0,4},{4,0},{8,12},{12,8},{16,20},{20,16},{24,28},{28,24},{1,5},{5... | collective-permute-start | bytes 2949128 | tf_op jit(solution)/shard_map/ppermute | solution.py:533
  120.9 24.6 %collective-permute-start.30 = (bf16[2,3,64,1280]{3,2,1,0:T(8,128)(2,1)S(1)}, bf16[2,3,64,1280]{3,2,1,0:T(8,128)(2,1)}, u32[]{:S(2)}, u32[]{:S(2)}) collective-permute-start(bf16[2,3,64,1280]{3,2,1,0:T(8,128)(2,1)S(1)} %collective-permute-done.18.refs_6_), channel_id=1, source_target_pairs={{0,4},{4,0},{8,12},{12,8},{16,20},{20,16},{24,28},{28,24},{1,5},{5... | collective-permute-start | bytes 2949128 | tf_op jit(solution)/shard_map/ppermute | solution.py:533
  122.9 31.3 %collective-permute-start.25 = (bf16[2,3,256,256]{3,2,1,0:T(8,128)(2,1)}, bf16[2,3,256,256]{3,2,1,0:T(8,128)(2,1)}, u32[]{:S(2)}, u32[]{:S(2)}) collective-permute-start(bf16[2,3,256,256]{3,2,1,0:T(8,128)(2,1)} %pad_maximum_fusion.5), channel_id=1, source_target_pairs={{0,8},{4,12},{8,0},{12,4},{16,24},{20,28},{24,16},{28,20},{1,9},{5... | collective-permute-start | bytes 2359304 | tf_op jit(solution)/shard_map/ppermute | solution.py:530
  123.9 30.3 %collective-permute-start.24 = (bf16[2,3,256,256]{3,2,1,0:T(8,128)(2,1)}, bf16[2,3,256,256]{3,2,1,0:T(8,128)(2,1)}, u32[]{:S(2)}, u32[]{:S(2)}) collective-permute-start(bf16[2,3,256,256]{3,2,1,0:T(8,128)(2,1)} %pad_maximum_fusion.4), channel_id=1, source_target_pairs={{0,16},{4,20},{8,24},{12,28},{16,0},{20,4},{24,8},{28,12},{1,17},{... | collective-permute-start | bytes 2359304 | tf_op jit(solution)/shard_map/ppermute | solution.py:530
  144.3 20.4 %collective-permute-start.31 = (bf16[3,256,512]{2,1,0:T(8,128)(2,1)S(1)}, bf16[3,256,512]{2,1,0:T(8,128)(2,1)S(1)}, u32[]{:S(2)}, u32[]{:S(2)}) collective-permute-start(bf16[3,256,512]{2,1,0:T(8,128)(2,1)S(1)} %pad_maximum_fusion.3.refs_1_), channel_id=1, source_target_pairs={{0,4},{4,0},{8,12},{12,8},{16,20},{20,16},{24,28},{28,24},{1,5},{5... | collective-permute-start | bytes 2359304 | tf_op jit(solution)/shard_map/ppermute | solution.py:533
  145.4 19.3 %collective-permute-start.32 = (bf16[1,3,256,256]{3,2,1,0:T(8,128)(2,1)S(1)}, bf16[1,3,256,256]{3,2,1,0:T(8,128)(2,1)}, u32[]{:S(2)}, u32[]{:S(2)}) collective-permute-start(bf16[1,3,256,256]{3,2,1,0:T(8,128)(2,1)S(1)} %collective-permute-done.22.refs_2_), channel_id=1, source_target_pairs={{0,4},{4,0},{8,12},{12,8},{16,20},{20,16},{24,28},{28,24},{1,5},{5... | collective-permute-start | bytes 1179656 | tf_op jit(solution)/shard_map/ppermute | solution.py:533
  145.5 19.2 %collective-permute-start.33 = (bf16[1,3,256,256]{3,2,1,0:T(8,128)(2,1)S(1)}, bf16[1,3,256,256]{3,2,1,0:T(8,128)(2,1)}, u32[]{:S(2)}, u32[]{:S(2)}) collective-permute-start(bf16[1,3,256,256]{3,2,1,0:T(8,128)(2,1)S(1)} %collective-permute-done.23.refs_3_), channel_id=1, source_target_pairs={{0,4},{4,0},{8,12},{12,8},{16,20},{20,16},{24,28},{28,24},{1,5},{5... | collective-permute-start | bytes 1179656 | tf_op jit(solution)/shard_map/ppermute | solution.py:533
  215.6 47.7 %collective-permute-start.36 = (bf16[4,4,128,512]{3,2,1,0:T(8,128)(2,1)}, bf16[4,4,128,512]{3,2,1,0:T(8,128)(2,1)}, u32[]{:S(2)}, u32[]{:S(2)}) collective-permute-start(bf16[4,4,128,512]{3,2,1,0:T(8,128)(2,1)} %bitcast.164), channel_id=1, source_target_pairs={{0,4},{4,0},{8,12},{12,8},{16,20},{20,16},{24,28},{28,24},{1,5},{5... | collective-permute-start | bytes 6291464 | tf_op jit(solution)/shard_map/ppermute | solution.py:533
  215.8 47.5 %collective-permute-start.37 = (bf16[4,4,128,512]{3,2,1,0:T(8,128)(2,1)}, bf16[4,4,128,512]{3,2,1,0:T(8,128)(2,1)}, u32[]{:S(2)}, u32[]{:S(2)}) collective-permute-start(bf16[4,4,128,512]{3,2,1,0:T(8,128)(2,1)} %bitcast.163), channel_id=1, source_target_pairs={{0,4},{4,0},{8,12},{12,8},{16,20},{20,16},{24,28},{28,24},{1,5},{5... | collective-permute-start | bytes 6291464 | tf_op jit(solution)/shard_map/ppermute | solution.py:533
  262.7 34.7 %collective-permute-start.40 = (bf16[4,4,128,512]{3,2,1,0:T(8,128)(2,1)}, bf16[4,4,128,512]{3,2,1,0:T(8,128)(2,1)S(1)}, u32[]{:S(2)}, u32[]{:S(2)}) collective-permute-start(bf16[4,4,128,512]{3,2,1,0:T(8,128)(2,1)} %bitcast.162), channel_id=1, source_target_pairs={{0,4},{4,0},{8,12},{12,8},{16,20},{20,16},{24,28},{28,24},{1,5},{5... | collective-permute-start | bytes 6291464 | tf_op jit(solution)/shard_map/ppermute | solution.py:533
  262.9 34.5 %collective-permute-start.41 = (bf16[4,4,128,512]{3,2,1,0:T(8,128)(2,1)}, bf16[4,4,128,512]{3,2,1,0:T(8,128)(2,1)S(1)}, u32[]{:S(2)}, u32[]{:S(2)}) collective-permute-start(bf16[4,4,128,512]{3,2,1,0:T(8,128)(2,1)} %bitcast.161), channel_id=1, source_target_pairs={{0,4},{4,0},{8,12},{12,8},{16,20},{20,16},{24,28},{28,24},{1,5},{5... | collective-permute-start | bytes 6291464 | tf_op jit(solution)/shard_map/ppermute | solution.py:533
  268.7 24.9 %collective-permute-start.38 = (bf16[2,4,128,512]{3,2,1,0:T(8,128)(2,1)}, bf16[2,4,128,512]{3,2,1,0:T(8,128)(2,1)S(1)}, u32[]{:S(2)}, u32[]{:S(2)}) collective-permute-start(bf16[2,4,128,512]{3,2,1,0:T(8,128)(2,1)} %get-tuple-element.243), channel_id=1, source_target_pairs={{0,8},{4,12},{8,0},{12,4},{16,24},{20,28},{24,16},{28,20},{1,9},{5... | collective-permute-start | bytes 3145736 | tf_op jit(solution)/shard_map/ppermute | solution.py:530
  269.1 24.5 %collective-permute-start.39 = (bf16[2,4,128,512]{3,2,1,0:T(8,128)(2,1)S(1)}, bf16[2,4,128,512]{3,2,1,0:T(8,128)(2,1)S(1)}, u32[]{:S(2)}, u32[]{:S(2)}) collective-permute-start(bf16[2,4,128,512]{3,2,1,0:T(8,128)(2,1)S(1)} %get-tuple-element.244), channel_id=1, source_target_pairs={{0,16},{4,20},{8,24},{12,28},{16,0},{20,4},{24,8},{28,12},{1,17},{... | collective-permute-start | bytes 3145736 | tf_op jit(solution)/shard_map/ppermute | solution.py:530
  300.0 38.4 %collective-permute-start.43 = (bf16[1,4,128,512]{3,2,1,0:T(8,128)(2,1)}, bf16[1,4,128,512]{3,2,1,0:T(8,128)(2,1)S(1)}, u32[]{:S(2)}, u32[]{:S(2)}) collective-permute-start(bf16[1,4,128,512]{3,2,1,0:T(8,128)(2,1)} %get-tuple-element.263), channel_id=1, source_target_pairs={{0,16},{4,20},{8,24},{12,28},{16,0},{20,4},{24,8},{28,12},{1,17},{... | collective-permute-start | bytes 1572872 | tf_op jit(solution)/shard_map/ppermute | solution.py:530
  300.1 38.3 %collective-permute-start.44 = (bf16[1,4,128,512]{3,2,1,0:T(8,128)(2,1)S(1)}, bf16[1,4,128,512]{3,2,1,0:T(8,128)(2,1)S(1)}, u32[]{:S(2)}, u32[]{:S(2)}) collective-permute-start(bf16[1,4,128,512]{3,2,1,0:T(8,128)(2,1)S(1)} %get-tuple-element.264), channel_id=1, source_target_pairs={{0,8},{4,12},{8,0},{12,4},{16,24},{20,28},{24,16},{28,20},{1,9},{5... | collective-permute-start | bytes 1572872 | tf_op jit(solution)/shard_map/ppermute | solution.py:530
  301.1 39.3 %collective-permute-start.45 = (bf16[2,4,160,512]{3,2,1,0:T(8,128)(2,1)}, bf16[2,4,160,512]{3,2,1,0:T(8,128)(2,1)}, u32[]{:S(2)}, u32[]{:S(2)}) collective-permute-start(bf16[2,4,160,512]{3,2,1,0:T(8,128)(2,1)} %get-tuple-element.265), channel_id=1, source_target_pairs={{0,8},{4,12},{8,0},{12,4},{16,24},{20,28},{24,16},{28,20},{1,9},{5... | collective-permute-start | bytes 3932168 | tf_op jit(solution)/shard_map/ppermute | solution.py:530
  301.6 39.1 %collective-permute-start.46 = (bf16[2,4,160,512]{3,2,1,0:T(8,128)(2,1)S(1)}, bf16[2,4,160,512]{3,2,1,0:T(8,128)(2,1)S(1)}, u32[]{:S(2)}, u32[]{:S(2)}) collective-permute-start(bf16[2,4,160,512]{3,2,1,0:T(8,128)(2,1)S(1)} %get-tuple-element.266), channel_id=1, source_target_pairs={{0,16},{4,20},{8,24},{12,28},{16,0},{20,4},{24,8},{28,12},{1,17},{... | collective-permute-start | bytes 3932168 | tf_op jit(solution)/shard_map/ppermute | solution.py:530
  345.1 28.4 %collective-permute-start.47 = (bf16[256,512]{1,0:T(8,128)(2,1)S(1)}, bf16[256,512]{1,0:T(8,128)(2,1)S(1)}, u32[]{:S(2)}, u32[]{:S(2)}) collective-permute-start(bf16[256,512]{1,0:T(8,128)(2,1)S(1)} %get-tuple-element.283), channel_id=1, source_target_pairs={{0,1},{1,2},{2,3},{3,0},{4,5},{5,6},{6,7},{7,4},{8,9},{9,10},{10,1... | collective-permute-start | bytes 786440 | tf_op jit(solution)/shard_map/ppermute | solution.py:527
  346.0 27.5 %collective-permute-start.48 = (bf16[256,512]{1,0:T(8,128)(2,1)S(1)}, bf16[256,512]{1,0:T(8,128)(2,1)S(1)}, u32[]{:S(2)}, u32[]{:S(2)}) collective-permute-start(bf16[256,512]{1,0:T(8,128)(2,1)S(1)} %get-tuple-element.284), channel_id=1, source_target_pairs={{0,2},{1,3},{2,0},{3,1},{4,6},{5,7},{6,4},{7,5},{8,10},{9,11},{10,... | collective-permute-start | bytes 786440 | tf_op jit(solution)/shard_map/ppermute | solution.py:527
  347.8 25.7 %collective-permute-start.49 = (bf16[256,512]{1,0:T(8,128)(2,1)S(1)}, bf16[256,512]{1,0:T(8,128)(2,1)S(1)}, u32[]{:S(2)}, u32[]{:S(2)}) collective-permute-start(bf16[256,512]{1,0:T(8,128)(2,1)S(1)} %get-tuple-element.285), channel_id=1, source_target_pairs={{0,3},{1,0},{2,1},{3,2},{4,7},{5,4},{6,5},{7,6},{8,11},{9,8},{10,9... | collective-permute-start | bytes 786440 | tf_op jit(solution)/shard_map/ppermute | solution.py:527
  349.1 24.4 %collective-permute-start.50 = (bf16[1,4,160,512]{3,2,1,0:T(8,128)(2,1)}, bf16[1,4,160,512]{3,2,1,0:T(8,128)(2,1)S(1)}, u32[]{:S(2)}, u32[]{:S(2)}) collective-permute-start(bf16[1,4,160,512]{3,2,1,0:T(8,128)(2,1)} %get-tuple-element.286), channel_id=1, source_target_pairs={{0,16},{4,20},{8,24},{12,28},{16,0},{20,4},{24,8},{28,12},{1,17},{... | collective-permute-start | bytes 1966088 | tf_op jit(solution)/shard_map/ppermute | solution.py:530
  350.1 23.4 %collective-permute-start.51 = (bf16[1,4,160,512]{3,2,1,0:T(8,128)(2,1)S(1)}, bf16[1,4,160,512]{3,2,1,0:T(8,128)(2,1)S(1)}, u32[]{:S(2)}, u32[]{:S(2)}) collective-permute-start(bf16[1,4,160,512]{3,2,1,0:T(8,128)(2,1)S(1)} %get-tuple-element.287), channel_id=1, source_target_pairs={{0,8},{4,12},{8,0},{12,4},{16,24},{20,28},{24,16},{28,20},{1,9},{5... | collective-permute-start | bytes 1966088 | tf_op jit(solution)/shard_map/ppermute | solution.py:530
  393.7 23.3 %collective-permute-start.55 = (bf16[320,512]{1,0:T(8,128)(2,1)}, bf16[320,512]{1,0:T(8,128)(2,1)S(1)}, u32[]{:S(2)}, u32[]{:S(2)}) collective-permute-start(bf16[320,512]{1,0:T(8,128)(2,1)} %copy-done.33), channel_id=1, source_target_pairs={{0,1},{1,2},{2,3},{3,0},{4,5},{5,6},{6,7},{7,4},{8,9},{9,10},{10,1... | collective-permute-start | bytes 983048 | tf_op jit(solution)/shard_map/ppermute | solution.py:527
  394.0 24.2 %collective-permute-start.56 = (bf16[320,512]{1,0:T(8,128)(2,1)}, bf16[320,512]{1,0:T(8,128)(2,1)S(1)}, u32[]{:S(2)}, u32[]{:S(2)}) collective-permute-start(bf16[320,512]{1,0:T(8,128)(2,1)} %copy-done.32), channel_id=1, source_target_pairs={{0,2},{1,3},{2,0},{3,1},{4,6},{5,7},{6,4},{7,5},{8,10},{9,11},{10,... | collective-permute-start | bytes 983048 | tf_op jit(solution)/shard_map/ppermute | solution.py:527
  394.8 23.4 %collective-permute-start.57 = (bf16[320,512]{1,0:T(8,128)(2,1)S(1)}, bf16[320,512]{1,0:T(8,128)(2,1)S(1)}, u32[]{:S(2)}, u32[]{:S(2)}) collective-permute-start(bf16[320,512]{1,0:T(8,128)(2,1)S(1)} %get-tuple-element.313), channel_id=1, source_target_pairs={{0,3},{1,0},{2,1},{3,2},{4,7},{5,4},{6,5},{7,6},{8,11},{9,8},{10,9... | collective-permute-start | bytes 983048 | tf_op jit(solution)/shard_map/ppermute | solution.py:527
  401.1 18.8 %collective-permute-start.53 = (bf16[2,4,96,512]{3,2,1,0:T(8,128)(2,1)S(1)}, bf16[2,4,96,512]{3,2,1,0:T(8,128)(2,1)S(1)}, u32[]{:S(2)}, u32[]{:S(2)}) collective-permute-start(bf16[2,4,96,512]{3,2,1,0:T(8,128)(2,1)S(1)} %get-tuple-element.309), channel_id=1, source_target_pairs={{0,8},{4,12},{8,0},{12,4},{16,24},{20,28},{24,16},{28,20},{1,9},{5... | collective-permute-start | bytes 2359304 | tf_op jit(solution)/shard_map/ppermute | solution.py:530
  402.1 18.4 %collective-permute-start.54 = (bf16[2,4,96,512]{3,2,1,0:T(8,128)(2,1)S(1)}, bf16[2,4,96,512]{3,2,1,0:T(8,128)(2,1)S(1)}, u32[]{:S(2)}, u32[]{:S(2)}) collective-permute-start(bf16[2,4,96,512]{3,2,1,0:T(8,128)(2,1)S(1)} %get-tuple-element.310), channel_id=1, source_target_pairs={{0,16},{4,20},{8,24},{12,28},{16,0},{20,4},{24,8},{28,12},{1,17},{... | collective-permute-start | bytes 2359304 | tf_op jit(solution)/shard_map/ppermute | solution.py:530
  434.2 28.3 %collective-permute-start.69 = (bf16[576,512]{1,0:T(8,128)(2,1)S(1)}, bf16[576,512]{1,0:T(8,128)(2,1)S(1)}, u32[]{:S(2)}, u32[]{:S(2)}) collective-permute-start(bf16[576,512]{1,0:T(8,128)(2,1)S(1)} %constant_dynamic-update-slice_fusion.9.refs_0_), channel_id=1, source_target_pairs={{0,24},{4,28},{8,16},{12,20},{16,8},{20,12},{24,0},{28,4},{1,25},{... | collective-permute-start | bytes 1769480 | tf_op jit(solution)/shard_map/ppermute | solution.py:530
  434.6 27.9 %collective-permute-start.68 = (bf16[576,512]{1,0:T(8,128)(2,1)S(1)}, bf16[576,512]{1,0:T(8,128)(2,1)S(1)}, u32[]{:S(2)}, u32[]{:S(2)}) collective-permute-start(bf16[576,512]{1,0:T(8,128)(2,1)S(1)} %constant_dynamic-update-slice_fusion.9.refs_0_), channel_id=1, source_target_pairs={{0,16},{4,20},{8,24},{12,28},{16,0},{20,4},{24,8},{28,12},{1,17},{... | collective-permute-start | bytes 1769480 | tf_op jit(solution)/shard_map/ppermute | solution.py:530
  436.3 26.2 %collective-permute-start.67 = (bf16[576,512]{1,0:T(8,128)(2,1)S(1)}, bf16[576,512]{1,0:T(8,128)(2,1)S(1)}, u32[]{:S(2)}, u32[]{:S(2)}) collective-permute-start(bf16[576,512]{1,0:T(8,128)(2,1)S(1)} %constant_dynamic-update-slice_fusion.9.refs_0_), channel_id=1, source_target_pairs={{0,8},{4,12},{8,0},{12,4},{16,24},{20,28},{24,16},{28,20},{1,9},{5... | collective-permute-start | bytes 1769480 | tf_op jit(solution)/shard_map/ppermute | solution.py:530
  (87 other events, 693.1 us)

commit v5 on v4

--- a/solution.py
+++ b/solution.py
@@ -182,7 +182,7 @@
         ],
         input_output_aliases={7 + i: i for i in range(len(given))},
         compiler_params=pltpu.CompilerParams(vmem_limit_bytes=56 * 1024 * 1024),
-        cost_estimate=HEAVY,
+        cost_estimate=LIGHT if first == 0 else HEAVY,
         name="attend_back",
     )(qkv, qkv, qkv, grad, attended, inverse, probs, *given)
 
@@ -202,18 +202,24 @@
 def feed_forward_kernel(
     h_ref, dm_ref, up_ref, bias_ref, down_ref, alive_ref, last_ref, y0_ref, g0_ref,
     y_ref, g_ref, down_away, down_home, up_away, up_home, gb_ref,
-    act_ref, dp_ref, y_acc, g_acc,
+    act_ref, dp_ref, y_acc, g_acc, out_ref, sems,
 ):
     j = pl.program_id(0)
+    final = g0_ref is not None
+    given = [pltpu.make_async_copy(y0_ref, y_acc, sems.at[0])]
+    if final:
+        given.append(pltpu.make_async_copy(g0_ref, g_acc, sems.at[1]))
+    made = [
+        pltpu.make_async_copy(out_ref if final else y_acc, y_ref, sems.at[2]),
+        pltpu.make_async_copy(g_acc, g_ref, sems.at[3]),
+    ]
 
     @pl.when(j == 0)
     def _():
-        if g0_ref is None:
-            y_acc[...] = y0_ref[...] + last_ref[...]
+        for copy in given:
+            copy.start()
+        if not final:
             g_acc[...] = jnp.zeros_like(g_acc)
-        else:
-            y_acc[...] = y0_ref[...]
-            g_acc[...] = g0_ref[...]
 
     rows = h_ref.shape[0]
     up, down = up_ref[...], down_ref[...]
@@ -226,8 +232,23 @@
         act_ref[r, :] = act
         d_pre = (contract(dm_ref[r, :], down, 1, 1) * slope).astype(bf16)
         dp_ref[r, :] = d_pre
+        if start == 0:
+
+            @pl.when(j == 0)
+            def _():
+                for copy in given:
+                    copy.wait()
+
         y_acc[r, :] += contract(act, down, 1, 0)
         g_acc[r, :] += contract(d_pre, up, 1, 1)
+
+    @pl.when(j == pl.num_programs(0) - 1)
+    def _():
+        if final:
+            out_ref[...] = (alive_ref[0] * (y_acc[...] + last_ref[...])).astype(bf16)
+        for copy in made:
+            copy.start()
+
     gb_ref[...] = jnp.sum(dp_ref[...].astype(f32), 0, keepdims=True)[None]
     first_core = lax.axis_index("rep") % 2 == 0
     for left, right, away, home in (
@@ -242,9 +263,8 @@
 
     @pl.when(j == pl.num_programs(0) - 1)
     def _():
-        y = y_acc[...]
-        y_ref[...] = y if g0_ref is None else (alive_ref[0] * y).astype(bf16)
-        g_ref[...] = g_acc[...]
+        for copy in made:
+            copy.wait()
 
 
 def feed_forward(links, hidden, d_out, up, bias, down, alive, last_bias, y0, g0, part):
@@ -282,10 +302,9 @@
             pl.BlockSpec(memory_space=pltpu.SMEM),
             pl.BlockSpec((1, width), lambda j: (0, 0)),
         ]
-        + [full() for _ in given],
-        out_specs=[
-            full(),
-            full(),
+        + whole(len(given)),
+        out_specs=whole(2)
+        + [
             down_spec,
             down_spec,
             up_spec,
@@ -306,8 +325,10 @@
             pltpu.VMEM((rows, block), bf16),
             pltpu.VMEM((rows, width), f32),
             pltpu.VMEM((rows, width), f32),
+            pltpu.VMEM((rows, width), bf16),
+            pltpu.SemaphoreType.DMA((4,)),
         ],
-        compiler_params=pltpu.CompilerParams(vmem_limit_bytes=58 * 1024 * 1024),
+        compiler_params=pltpu.CompilerParams(vmem_limit_bytes=50 * 1024 * 1024),
         cost_estimate=HEAVY,
         name="feed_forward",
     )(hidden, d_out, up, bias, down, alive, last_bias, *given)
@@ -506,7 +527,7 @@
             jax.ShapeDtypeStruct((8, width), f32),
         ],
         compiler_params=pltpu.CompilerParams(vmem_limit_bytes=48 * 1024 * 1024),
-        cost_estimate=HEAVY,
+        cost_estimate=pl.CostEstimate(flops=6_000_000_000, transcendentals=0, bytes_accessed=1),
         name="entry_back",
     )(grads, weight, tokens, d_mid, gain)
 
@@ -834,6 +855,18 @@
             )
         self.held = out
         self.done += 1
+
+    def join(self, other):
+        n = len(self.rows)
+        self.held = [
+            {k: jnp.concatenate([mine[k], theirs[k]], 1) for k in mine}
+            for mine, theirs in zip(self.held, other.held)
+        ]
+        self.rows = self.rows + other.rows
+        self.parts = [
+            mine + [(i + n, low, high) for i, low, high in theirs]
+            for mine, theirs in zip(self.parts, other.parts)
+        ]
 
     def prepare_along(self, lines=None):
         links = self.links
@@ -1156,51 +1189,85 @@
     output = output.reshape(inputs.shape)
     grad_bup = jnp.concatenate([gb_first, gb_second], 1)
     g, scatter_1.kept = meet(g, scatter_1.kept)
-    g, scatter_1.buffers = meet(g, scatter_1.prepare())
+    scatter_2 = Scatter(links, away, home)
+    early = scatter_1.parts is not None
+    if early:
+        scatter_2.kept, scatter_1.buffers = meet(scatter_2.kept, scatter_1.prepare())
+        g, scatter_1.buffers, scatter_2.buffers = meet(
+            g, scatter_1.buffers, scatter_2.prepare()
+        )
+        scatter_2.send()
+    else:
+        g, scatter_1.buffers = meet(g, scatter_1.prepare())
     scatter_1.send()
     d_mid, d_att_b, out_away, out_home, sums = middle_back(
         links, g, middle, d_out_b, attended_b, full_wout, gain_two
     )
     grad_g2, grad_s2, grad_bout, grad_bdown = (sums[i] for i in range(4))
-    scatter_2 = Scatter(links, away + [out_away], home + [out_home])
-    d_att_b, scatter_1.arrived = meet(d_att_b, scatter_1.arrived)
+    if early:
+        d_att_b, out_away, out_home = meet(d_att_b, out_away, out_home)
+        scatter_o = Scatter(links, [out_away], [out_home])
+    else:
+        scatter_2 = Scatter(links, away + [out_away], home + [out_home])
+        d_att_b, scatter_2.buffers = meet(d_att_b, scatter_2.prepare())
+        scatter_2.send()
+    thirds = (0, pairs // 2, pairs * 3 // 4, pairs)
+
+    def back(part, before=None):
+        low, high = thirds[part], thirds[part + 1]
+        return attend_back(
+            qkv_b, d_att_b, attended_b, inverse, probs_b, low, high, before
+        )
+
+    grads = back(0)
+    grads, scatter_1.arrived, scatter_2.arrived = meet(
+        grads, scatter_1.arrived, scatter_2.arrived
+    )
     scatter_1.absorb()
-    d_att_b, scatter_1.buffers, scatter_2.buffers = meet(
-        d_att_b, scatter_1.prepare(), scatter_2.prepare()
-    )
-    scatter_1.send()
-    scatter_2.send()
-    half = pairs * 5 // 8
-    grads = attend_back(qkv_b, d_att_b, attended_b, inverse, probs_b, 0, half)
+    scatter_2.absorb()
     for _ in range(links.bits - 2):
-        scatter_1.absorb()
         scatter_1.prepare()
         scatter_1.send()
-        scatter_2.absorb()
+        scatter_1.absorb()
         scatter_2.prepare()
         scatter_2.send()
-    grads, scatter_1.arrived, scatter_2.arrived = meet(
-        grads, scatter_1.arrived, scatter_2.arrived
-    )
+        scatter_2.absorb()
+    if early:
+        grads, scatter_1.buffers, scatter_2.held, scatter_o.buffers = meet(
+            grads, scatter_1.prepare(), scatter_2.held, scatter_o.prepare()
+        )
+        scatter_o.send()
+    else:
+        grads, scatter_1.buffers, scatter_2.buffers = meet(
+            grads, scatter_1.prepare(), scatter_2.prepare()
+        )
+    scatter_1.send()
+    grads = back(1, grads)
+    if early:
+        grads, scatter_1.arrived, scatter_o.arrived = meet(
+            grads, scatter_1.arrived, scatter_o.arrived
+        )
+        scatter_o.absorb()
+        scatter_2.join(scatter_o)
+        scatter_2.prepare()
+    else:
+        grads, scatter_1.arrived = meet(grads, scatter_1.arrived)
     scatter_1.absorb()
+    grads, scatter_1.buffers, scatter_2.buffers = meet(
+        grads, scatter_1.prepare_along(), scatter_2.buffers
+    )
+    scatter_2.send()
+    scatter_1.send_along()
+    grads = back(2, grads)
+    grads, scatter_2.arrived = meet(grads, scatter_2.arrived)
     scatter_2.absorb()
-    grads, scatter_1.buffers, scatter_2.buffers = meet(
-        grads, scatter_1.prepare_along(), scatter_2.prepare()
-    )
-    scatter_1.send_along()
-    scatter_2.send()
-    grads = attend_back(qkv_b, d_att_b, attended_b, inverse, probs_b, half, pairs, grads)
-    grads, scatter_1.arrived, scatter_2.arrived = meet(
-        grads, scatter_1.arrived, scatter_2.arrived
-    )
-    scatter_1.settle()
-    scatter_2.absorb()
-    grads, scatter_1.final, scatter_2.buffers = meet(
-        grads, scatter_1.final, scatter_2.prepare_along()
-    )
+    grads, scatter_2.buffers = meet(grads, scatter_2.prepare_along())
     scatter_2.send_along()
     d_qkv, qv_sums = grads
-    scatter_3 = Scatter(links, *weight_grads(links, hidden_one_b, d_qkv))
+    qkv_away, qkv_home = weight_grads(links, hidden_one_b, d_qkv)
+    qkv_away, qkv_home, scatter_1.arrived = meet(qkv_away, qkv_home, scatter_1.arrived)
+    scatter_3 = Scatter(links, qkv_away, qkv_home)
+    scatter_1.settle()
     d_qkv, scatter_3.buffers = meet(d_qkv, scatter_3.prepare())
     scatter_3.send()
     input_grad, entry_sums = entry_back(d_qkv, full_qkv, tokens_b, d_mid, full_g1[None])
@@ -1220,29 +1287,33 @@
     grad_qvb = qv_sums.reshape(-1)
     small_grads = (grad_g1, grad_s1, grad_bout, grad_g2, grad_s2, grad_bdown, grad_qvb, grad_bup)
     joined = jnp.concatenate([g.reshape(ns, -1) for g in small_grads], 1)
+    n_small = joined.shape[1]
+    ride = scatter_3.parts is not None and n_small % scatter_3.lanes == 0
+    if ride:
+        joined = joined.reshape(ns, -1, scatter_3.lanes)
+        joined = jnp.pad(joined, ((0, 0), (0, -joined.shape[1] % 8), (0, 0)))
     joined = total_over_rep(links, joined)
     scatter_3.arrived, scatter_1.final, scatter_2.final = meet(
         scatter_3.arrived, scatter_1.final, scatter_2.final
     )
     scatter_3.absorb()
-    n_small = joined.shape[1]
-    ride = scatter_3.parts is not None and n_small % scatter_3.lanes == 0
     if ride:
-        lines = joined.reshape(ns, -1, scatter_3.lanes)
-        lines = jnp.pad(lines, ((0, 0), (0, -lines.shape[1] % 16), (0, 0)))
-        scatter_3.buffers = scatter_3.prepare_along(lines)
+        scatter_3.prepare_along(joined)
     else:
         scatter_3.prepare_along()
         joined = total_over_shard(links, joined)
     scatter_3.send_along()
     spread_12 = Spread(links, [scatter_1, scatter_2])
     scatter_3.arrived, spread_12.others = meet(scatter_3.arrived, spread_12.others)
-    spread_12.pair()
     arrived_lines = scatter_3.settle()
     spread_3 = Spread(links, [scatter_3])
+    spread_12.pair()
+    o_wdown, o_wup, o_wout = owned_feed_forward(links, scatter_1, scatter_2, w_up, w_down, w_out)
     if ride:
         joined = arrived_lines.reshape(-1)[:n_small]
-    o_wdown, o_wup, o_wout = owned_feed_forward(links, scatter_1, scatter_2, w_up, w_down, w_out)
+    joined, o_wdown, o_wup, o_wout, spread_3.others = meet(
+        joined, o_wdown, o_wup, o_wout, spread_3.others
+    )
     spread_3.pair()
     o_qkv = owned_qkv(links, scatter_3, w_qkv)
     owned = []

time: 501 us -> 479 us (0.956)
  local copies, waits for them, and re-layouts: 41.4 us -> 24.7 us
  starting transfers between devices: 88.4 us -> 80.7 us
    unnamed x138 -> x118, local copies, waits for them, and re-layouts: 29.7 us -> 17.3 us
    ppermute x30, starting transfers between devices: 33.6 us -> 25.1 us  [core(): return lax.ppermute(values, 'rep', [(i, i ^ 1) for i in range(self.nr)])]
    pallas_call x2 -> x3, Pallas kernels: 58.3 us -> 62.6 us  [attend_back(): pl.pallas_call(kernel, grid=(count,), in_specs=[column(0), column(pairs),...]
    ppermute x33 -> x35, starting transfers between devices: 28.4 us -> 31.6 us  [chip(): return lax.ppermute(values, 'rep', [(i, i ^ 2 * k) for i in range(self.nr)])]
    ppermute x33 -> x35, waiting for transfers between devices: 20.2 us -> 19.1 us  [chip(): return lax.ppermute(values, 'rep', [(i, i ^ 2 * k) for i in range(self.nr)])]
  transfers between devices with their start and end apart: 81 -> 83, of which waited for: 18 -> 21; matrix products, arithmetic and copies ran while one was open for 8% -> 8% of each run, Pallas kernels for 42% -> 47%
where the time goes in v5:
time: 479 us; the launch traced here: 471 us
  Pallas kernels  277 us (58%)
  starting transfers between devices  80.7 us (17%)
  waiting for transfers between devices  57.5 us (12%)
  local copies, waits for them, and re-layouts  24.7 us (5%)
  other arithmetic  19.8 us (4%)
  matrix products  9 us (2%)
    pallas_call x2, Pallas kernels, feed_forward(): pl.pallas_call(kernel, grid=(ns,), in_specs=[full(), full(), pl.BlockSpec...  87.6 us
    pallas_call x3, Pallas kernels, attend_back(): pl.pallas_call(kernel, grid=(count,), in_specs=[column(0), column(pairs),...  62.6 us
    pallas_call x3, Pallas kernels, attend(): pl.pallas_call(kernel, grid=(count,), in_specs=[column(0), column(pairs),...  52.5 us
    ppermute x35, starting transfers between devices, chip(): return lax.ppermute(values, 'rep', [(i, i ^ 2 * k) for i in range(self.nr)])  31.6 us
    ppermute x18, waiting for transfers between devices, along(): lax.ppermute(values, 'shard', [(i, (i + step) % self.ns) for i in range(s...  30.9 us
    ppermute x30, starting transfers between devices, core(): return lax.ppermute(values, 'rep', [(i, i ^ 1) for i in range(self.nr)])  25.1 us
    ppermute x18, starting transfers between devices, along(): lax.ppermute(values, 'shard', [(i, (i + step) % self.ns) for i in range(s...  24 us
    ppermute x35, waiting for transfers between devices, chip(): return lax.ppermute(values, 'rep', [(i, i ^ 2 * k) for i in range(self.nr)])  19.1 us
  transfers between devices with their start and end apart: 83, of which 21 were waited for; matrix products, arithmetic and copies ran while one was open for 8% of the time, Pallas kernels for 47%

profile of v5, /device:TPU:1, one launch (start us, length us, event | category | flops | bytes accessed | tf_op | source)
XLA Modules:
  0.0 471.5 jit_solution(8584780807009021787)
XLA Ops:
  0.7 2.5 pack.1
  3.2 4.2 collective-permute-start.2
  9.3 2.0 convert_reduce_fusion
  13.1 3.3 select_bitcast_fusion.refs_1_.dm_ref
  19.6 8.4 %collective-permute-done.1 = bf16[80,1536]{1,0:T(8,128)(2,1)} collective-permute-done((bf16[80,1536]{1,0:T(8,128)(2,1)}, bf16[80,1536]{1,0:T(8,128)(2,1)}, u32[]{:S(2)}, u32[]{:S(2)}) %collective-permute-start.1) | collective-permute-done | bytes 245792 | tf_op jit(solution)/shard_map/ppermute | solution.py:548
  30.0 1.9 collective-permute-start.8
  39.9 3.9 collective-permute-done.3.refs_2_
  45.7 3.9 collective-permute-start.10
  49.7 10.2 %collective-permute-done.8 = bf16[64,2560]{1,0:T(8,128)(2,1)S(1)} collective-permute-done((bf16[64,2560]{1,0:T(8,128)(2,1)}, bf16[64,2560]{1,0:T(8,128)(2,1)S(1)}, u32[]{:S(2)}, u32[]{:S(2)}) %collective-permute-start.8) | collective-permute-done | bytes 327712 | tf_op jit(solution)/shard_map/ppermute | solution.py:548
  59.9 1.9 collective-permute-start.12
  68.8 9.0 %fusion.refs_0_.refs_1_.refs_2_ = bf16[1104,3072]{1,0:T(8,128)(2,1)} fusion(bf16[1104,1024]{1,0:T(8,128)(2,1)S(1)} %fusion.6.left_ref, bf16[1024,3072]{1,0:T(8,128)(2,1)S(1)} %assemble.3.w_ref, f32[3072]{0:T(1024)S(1)} %pad_maximum_fusion.14), kind=kOutput, calls=%fused_computation.1 | convolution fusion | flops 6952550400 | bytes 15347712 | tf_op jit(solution)/shard_map/dot_general | solution.py:26
  79.5 19.1 %attend.3 = (bf16[1104,1024]{1,0:T(8,128)(2,1)}, f32[1104,1024]{1,0:T(8,128)}, bf16[16,1104,1104]{2,1,0:T(8,128)(2,1)}) custom-call(bf16[1104,3072]{1,0:T(8,128)(2,1)} %fusion.refs_0_.refs_1_.refs_2_, bf16[1104,3072]{1,0:T(8,128)(2,1)} %fusion.refs_0_.refs_1_.refs_2_, bf16[1104,3072]{1,0:T(8,128)(2,1)} %fusion.refs_0_.refs_1_.refs_2_), custom_call_target="tpu_custom_call" | custom-call | flops 20000000000 | bytes 10000000 | tf_op jit(solution)/shard_map/attend/pallas_call | solution.py:89
  98.7 2.6 collective-permute-start.26
  104.5 14.2 %attend.4 = (bf16[1104,1024]{1,0:T(8,128)(2,1)}, f32[1104,1024]{1,0:T(8,128)}, bf16[16,1104,1104]{2,1,0:T(8,128)(2,1)}) custom-call(bf16[1104,3072]{1,0:T(8,128)(2,1)} %fusion.refs_0_.refs_1_.refs_2_, bf16[1104,3072]{1,0:T(8,128)(2,1)} %fusion.refs_0_.refs_1_.refs_2_, ...), custom_call_target="tpu_custom_call", output_to_operand_aliasing={{0}: (3, {}), {1}: (4, {}), {2}: (5, {})} | custom-call | flops 20000000000 | bytes 10000000 | tf_op jit(solution)/shard_map/attend/pallas_call | solution.py:89
  124.4 19.1 %attend.5 = (bf16[1104,1024]{1,0:T(8,128)(2,1)}, f32[1104,1024]{1,0:T(8,128)}, bf16[16,1104,1104]{2,1,0:T(8,128)(2,1)}) custom-call(bf16[1104,3072]{1,0:T(8,128)(2,1)} %fusion.refs_0_.refs_1_.refs_2_, bf16[1104,3072]{1,0:T(8,128)(2,1)} %fusion.refs_0_.refs_1_.refs_2_, ...), custom_call_target="tpu_custom_call", output_to_operand_aliasing={{0}: (3, {}), {1}: (4, {}), {2}: (5, {})} | custom-call | flops 20000000000 | bytes 10000000 | tf_op jit(solution)/shard_map/attend/pallas_call | solution.py:89
  145.2 3.6 assemble.4
  148.8 3.3 copy-done.22
  152.7 7.5 %middle.1 = (f32[1104,1024]{1,0:T(8,128)}, bf16[1104,1024]{1,0:T(8,128)(2,1)S(1)}) custom-call(bf16[1104,1024]{1,0:T(8,128)(2,1)} %bitcast.136, bf16[1104,1024]{1,0:T(8,128)(2,1)} %get-tuple-element.244.att_ref.refs_4_, bf16[1024,1024]{1,0:T(8,128)(2,1)S(1)} %get-tuple-element.247.w_ref, f32[1,1024]{1,0:T(1,128)S(1)} %bitcast.156, f32[1,1024]{1,0:T(1,128)S(1)} %bitcast.151, ...), custom_call_target="tpu_custom_call" | custom-call | flops 20000000000 | bytes 10000000 | tf_op jit(solution)/shard_map/middle/pallas_call | solution.py:410
  160.3 2.8 assemble.5.refs_4_
  163.1 3.2 copy-done.2
  166.4 44.0 %feed_forward.2 = (f32[1104,1024]{1,0:T(8,128)}, f32[1104,1024]{1,0:T(8,128)}, bf16[4,512,512]{2,1,0:T(8,128)(2,1)S(1)}, bf16[4,512,512]{2,1,0:T(8,128)(2,1)}, b...) custom-call(bf16[1104,1024]{1,0:T(8,128)(2,1)} %copy-done.28, ...), custom_call_target="tpu_custom_call" | custom-call | flops 20000000000 | bytes 10000000 | tf_op jit(solution)/shard_map/feed_forward/pallas_call | solution.py:293
  210.9 43.7 %feed_forward.3 = (bf16[1104,1024]{1,0:T(8,128)(2,1)}, f32[1104,1024]{1,0:T(8,128)}, bf16[4,512,512]{2,1,0:T(8,128)(2,1)S(1)}, bf16[4,512,512]{2,1,0:T(8,128)(2,...) custom-call(bf16[1104,1024]{1,0:T(8,128)(2,1)} %copy-done.28, ...), custom_call_target="tpu_custom_call" | custom-call | flops 20000000000 | bytes 10000000 | tf_op jit(solution)/shard_map/feed_forward/pallas_call | solution.py:293
  255.2 2.5 core_sums.4
  257.7 3.3 collective-permute-done.38.refs_2_
  262.1 2.3 core_sums.5
  267.3 14.0 %middle_back.1 = (f32[1104,1024]{1,0:T(8,128)}, bf16[1104,1024]{1,0:T(8,128)(2,1)}, bf16[4,4,64,512]{3,2,1,0:T(8,128)(2,1)}, bf16[4,4,64,512]{3,2,1,0:T(8,128)(2,1)S(1)}, f32[8,1024]{1,0:T(8,128)S(1)}) custom-call(f32[1104,1024]{1,0:T(8,128)} %get-tuple-element.282.g_ref, f32[1104,1024]{1,0:T(8,128)} %get-tuple-element.258.refs_7_.mid_ref, ...), custom_call_target="tpu_custom_call" | custom-call | flops 20000000000 | bytes 10000000 | tf_op jit(solution)/shard_map/middle_back/pallas_call | solution.py:466
  282.6 29.0 %attend_back.3 = (bf16[3,1104,1024]{2,1,0:T(8,128)(2,1)}, f32[2,1,1024]{2,1,0:T(1,128)}) custom-call(bf16[1104,3072]{1,0:T(8,128)(2,1)} %fusion.refs_0_.refs_1_.refs_2_, bf16[1104,3072]{1,0:T(8,128)(2,1)} %fusion.refs_0_.refs_1_.refs_2_, bf16[1104,3072]{1,0:T(8,128)(2,1)} %fusion.refs_0_.refs_1_.refs_2_, bf16[1104,1024]{1,0:T(8,128)(2,1)} %get-tuple-element.286.refs_3_, ...), custom_call_target="tpu_custom_call" | custom-call | flops 1 | bytes 1 | tf_op jit(solution)/shard_map/attend_back/pallas_call | solution.py:168
  311.8 3.2 fusion.11
  315.0 2.2 fusion.8
  320.6 16.9 %attend_back.4 = (bf16[3,1104,1024]{2,1,0:T(8,128)(2,1)}, f32[2,1,1024]{2,1,0:T(1,128)}) custom-call(bf16[1104,3072]{1,0:T(8,128)(2,1)} %fusion.refs_0_.refs_1_.refs_2_, bf16[1104,3072]{1,0:T(8,128)(2,1)} %fusion.refs_0_.refs_1_.refs_2_, bf16[1104,3072]{1,0:T(8,128)(2,1)} %fusion.refs_0_.refs_1_.refs_2_, ...), custom_call_target="tpu_custom_call", output_to_operand_aliasing={{0}: (7, {}), {1}: (8, {})} | custom-call | flops 20000000000 | bytes 10000000 | tf_op jit(solution)/shard_map/attend_back/pallas_call | solution.py:168
  341.4 1.7 collective-permute-start.53
  344.1 16.7 %attend_back.5 = (bf16[3,1104,1024]{2,1,0:T(8,128)(2,1)}, f32[2,1,1024]{2,1,0:T(1,128)}) custom-call(bf16[1104,3072]{1,0:T(8,128)(2,1)} %fusion.refs_0_.refs_1_.refs_2_, bf16[1104,3072]{1,0:T(8,128)(2,1)} %fusion.refs_0_.refs_1_.refs_2_, bf16[1104,3072]{1,0:T(8,128)(2,1)} %fusion.refs_0_.refs_1_.refs_2_, ...), custom_call_target="tpu_custom_call", output_to_operand_aliasing={{0}: (7, {}), {1}: (8, {})} | custom-call | flops 20000000000 | bytes 10000000 | tf_op jit(solution)/shard_map/attend_back/pallas_call | solution.py:168
  362.7 11.8 %weight_grads.1 = (bf16[4,4,3,64,512]{4,3,2,1,0:T(8,128)(2,1)}, bf16[4,4,3,64,512]{4,3,2,1,0:T(8,128)(2,1)}) custom-call(bf16[1104,1024]{1,0:T(8,128)(2,1)S(1)} %copy-done.9, bf16[3,1104,1024]{2,1,0:T(8,128)(2,1)} %get-tuple-element.357.right_ref.d_ref), custom_call_target="tpu_custom_call" | custom-call | flops 20000000000 | bytes 10000000 | tf_op jit(solution)/shard_map/weight_grads/pallas_call | solution.py:362
  375.4 3.8 collective-permute-start.54
  380.4 2.3 collective-permute-start.59
  382.7 1.9 collective-permute-done.54.refs_1_
  384.6 1.9 copy-done.5
  390.0 14.8 %entry_back.1 = (f32[1104,1024]{1,0:T(8,128)}, f32[8,1024]{1,0:T(8,128)S(1)}) custom-call(bf16[3,1104,1024]{2,1,0:T(8,128)(2,1)} %get-tuple-element.357.right_ref.d_ref, bf16[1024,3072]{1,0:T(8,128)(2,1)} %copy-done.3, bf16[1104,1024]{1,0:T(8,128)(2,1)S(1)} %bitcast.137, f32[1104,1024]{1,0:T(8,128)} %get-tuple-element.358.d_mid_ref, f32[1,1024]{1,0:T(1,128)S(1)} %bitcast.157), custom_call_target="tpu_custom_call" | custom-call | flops 6000000000 | bytes 1 | tf_op jit(solution)/shard_map/entry_back/pallas_call | solution.py:514
  404.9 1.8 collective-permute-done.55
  415.4 5.7 %collective-permute-done.61 = bf16[1,4,96,512]{3,2,1,0:T(8,128)(2,1)S(1)} collective-permute-done((bf16[1,4,96,512]{3,2,1,0:T(8,128)(2,1)S(1)}, bf16[1,4,96,512]{3,2,1,0:T(8,128)(2,1)S(1)}, u32[]{:S(2)}, u32[]{:S(2)}) %collective-permute-start.61) | collective-permute-done | bytes 393248 | tf_op jit(solution)/shard_map/ppermute | solution.py:551
  421.9 3.0 collective-permute-start.71
  425.6 4.3 collective-permute-start.66
  430.6 2.9 collective-permute-done.66
  433.5 1.7 collective-permute-start.68
  435.2 9.4 %collective-permute-done.67 = bf16[200,512]{1,0:T(8,128)(2,1)S(1)} collective-permute-done((bf16[200,512]{1,0:T(8,128)(2,1)S(1)}, bf16[200,512]{1,0:T(8,128)(2,1)S(1)}, u32[]{:S(2)}, u32[]{:S(2)}) %collective-permute-start.67) | collective-permute-done | bytes 204832 | tf_op jit(solution)/shard_map/ppermute | solution.py:548
  445.4 6.0 %collective-permute-done.70.refs_2_ = bf16[576,512]{1,0:T(8,128)(2,1)S(1)} collective-permute-done((bf16[576,512]{1,0:T(8,128)(2,1)S(1)}, bf16[576,512]{1,0:T(8,128)(2,1)S(1)}, u32[]{:S(2)}, u32[]{:S(2)}) %collective-permute-start.70) | collective-permute-done | bytes 589856 | tf_op jit(solution)/shard_map/ppermute | solution.py:551
  459.1 5.6 %owned.2 = (f32[1024,1024]{1,0:T(8,128)}, f32[256,4096]{1,0:T(8,128)}, f32[256,1024]{1,0:T(8,128)}) custom-call(bf16[576,512]{1,0:T(8,128)(2,1)S(1)} %constant_dynamic-update-slice_fusion.9.refs_0_, bf16[576,512]{1,0:T(8,128)(2,1)S(1)} %collective-permute-done.69.refs_1_, bf16[576,512]{1,0:T(8,128)(2,1)S(1)} %collective-permute-done.70.refs_2_, ...), custom_call_target="tpu_custom_call" | custom-call | flops 1 | bytes 1 | tf_op jit(solution)/shard_map/owned/pallas_call | solution.py:985
  468.4 2.9 owned.3
  (332 shorter events, 82.8 us)
Async XLA Ops:
  3.2 15.8 %collective-permute-start.2 = (bf16[80,1536]{1,0:T(8,128)(2,1)}, bf16[80,1536]{1,0:T(8,128)(2,1)S(1)}, u32[]{:S(2)}, u32[]{:S(2)}) collective-permute-start(bf16[80,1536]{1,0:T(8,128)(2,1)} %pack.1), channel_id=1, source_target_pairs={{0,3},{1,0},{2,1},{3,2},{4,7},{5,4},{6,5},{7,6},{8,11},{9,8},{10,9... | collective-permute-start | bytes 737288 | tf_op jit(solution)/shard_map/ppermute | solution.py:548
  7.4 20.6 %collective-permute-start.1 = (bf16[80,1536]{1,0:T(8,128)(2,1)}, bf16[80,1536]{1,0:T(8,128)(2,1)}, u32[]{:S(2)}, u32[]{:S(2)}) collective-permute-start(bf16[80,1536]{1,0:T(8,128)(2,1)} %pack.1), channel_id=1, source_target_pairs={{0,2},{1,3},{2,0},{3,1},{4,6},{5,7},{6,4},{7,5},{8,10},{9,11},{10,... | collective-permute-start | bytes 737288 | tf_op jit(solution)/shard_map/ppermute | solution.py:548
  7.4 21.6 %collective-permute-start = (bf16[80,1536]{1,0:T(8,128)(2,1)}, bf16[80,1536]{1,0:T(8,128)(2,1)}, u32[]{:S(2)}, u32[]{:S(2)}) collective-permute-start(bf16[80,1536]{1,0:T(8,128)(2,1)} %pack.1), channel_id=1, source_target_pairs={{0,1},{1,2},{2,3},{3,0},{4,5},{5,6},{6,7},{7,4},{8,9},{9,10},{10,1... | collective-permute-start | bytes 737288 | tf_op jit(solution)/shard_map/ppermute | solution.py:548
  30.0 15.7 %collective-permute-start.9 = (bf16[64,2560]{1,0:T(8,128)(2,1)}, bf16[64,2560]{1,0:T(8,128)(2,1)S(1)}, u32[]{:S(2)}, u32[]{:S(2)}) collective-permute-start(bf16[64,2560]{1,0:T(8,128)(2,1)} %pad_maximum_fusion.11), channel_id=1, source_target_pairs={{0,3},{1,0},{2,1},{3,2},{4,7},{5,4},{6,5},{7,6},{8,11},{9,8},{10,9... | collective-permute-start | bytes 983048 | tf_op jit(solution)/shard_map/ppermute | solution.py:548
  30.0 29.9 %collective-permute-start.8 = (bf16[64,2560]{1,0:T(8,128)(2,1)}, bf16[64,2560]{1,0:T(8,128)(2,1)S(1)}, u32[]{:S(2)}, u32[]{:S(2)}) collective-permute-start(bf16[64,2560]{1,0:T(8,128)(2,1)} %pad_maximum_fusion.11), channel_id=1, source_target_pairs={{0,2},{1,3},{2,0},{3,1},{4,6},{5,7},{6,4},{7,5},{8,10},{9,11},{10,... | collective-permute-start | bytes 983048 | tf_op jit(solution)/shard_map/ppermute | solution.py:548
  31.9 29.9 %collective-permute-start.7 = (bf16[64,2560]{1,0:T(8,128)(2,1)}, bf16[64,2560]{1,0:T(8,128)(2,1)S(1)}, u32[]{:S(2)}, u32[]{:S(2)}) collective-permute-start(bf16[64,2560]{1,0:T(8,128)(2,1)} %pad_maximum_fusion.11), channel_id=1, source_target_pairs={{0,1},{1,2},{2,3},{3,0},{4,5},{5,6},{6,7},{7,4},{8,9},{9,10},{10,1... | collective-permute-start | bytes 983048 | tf_op jit(solution)/shard_map/ppermute | solution.py:548
  43.9 17.9 %collective-permute-start.5 = (bf16[2,3,64,768]{3,2,1,0:T(8,128)(2,1)S(1)}, bf16[2,3,64,768]{3,2,1,0:T(8,128)(2,1)S(1)}, u32[]{:S(2)}, u32[]{:S(2)}) collective-permute-start(bf16[2,3,64,768]{3,2,1,0:T(8,128)(2,1)S(1)} %pad_maximum_fusion.9), channel_id=1, source_target_pairs={{0,16},{4,20},{8,24},{12,28},{16,0},{20,4},{24,8},{28,12},{1,17},{... | collective-permute-start | bytes 1769480 | tf_op jit(solution)/shard_map/ppermute | solution.py:551
  44.2 17.6 %collective-permute-start.6 = (bf16[2,3,64,768]{3,2,1,0:T(8,128)(2,1)S(1)}, bf16[2,3,64,768]{3,2,1,0:T(8,128)(2,1)S(1)}, u32[]{:S(2)}, u32[]{:S(2)}) collective-permute-start(bf16[2,3,64,768]{3,2,1,0:T(8,128)(2,1)S(1)} %pad_maximum_fusion.10), channel_id=1, source_target_pairs={{0,8},{4,12},{8,0},{12,4},{16,24},{20,28},{24,16},{28,20},{1,9},{5... | collective-permute-start | bytes 1769480 | tf_op jit(solution)/shard_map/ppermute | solution.py:551
  45.7 16.9 %collective-permute-start.10 = (bf16[3,64,1536]{2,1,0:T(8,128)(2,1)S(1)}, bf16[3,64,1536]{2,1,0:T(8,128)(2,1)S(1)}, u32[]{:S(2)}, u32[]{:S(2)}) collective-permute-start(bf16[3,64,1536]{2,1,0:T(8,128)(2,1)S(1)} %pad_maximum_fusion.8.refs_1_), channel_id=1, source_target_pairs={{0,4},{4,0},{8,12},{12,8},{16,20},{20,16},{24,28},{28,24},{1,5},{5... | collective-permute-start | bytes 1769480 | tf_op jit(solution)/shard_map/ppermute | solution.py:554
  62.6 36.1 %collective-permute-start.21 = (bf16[256,512]{1,0:T(8,128)(2,1)}, bf16[256,512]{1,0:T(8,128)(2,1)}, u32[]{:S(2)}, u32[]{:S(2)}) collective-permute-start(bf16[256,512]{1,0:T(8,128)(2,1)} %dynamic_slice.28), channel_id=1, source_target_pairs={{0,3},{1,0},{2,1},{3,2},{4,7},{5,4},{6,5},{7,6},{8,11},{9,8},{10,9... | collective-permute-start | bytes 786440 | tf_op jit(solution)/shard_map/ppermute | solution.py:548
  63.0 38.2 %collective-permute-start.20 = (bf16[256,512]{1,0:T(8,128)(2,1)}, bf16[256,512]{1,0:T(8,128)(2,1)}, u32[]{:S(2)}, u32[]{:S(2)}) collective-permute-start(bf16[256,512]{1,0:T(8,128)(2,1)} %dynamic_slice.28), channel_id=1, source_target_pairs={{0,2},{1,3},{2,0},{3,1},{4,6},{5,7},{6,4},{7,5},{8,10},{9,11},{10,... | collective-permute-start | bytes 786440 | tf_op jit(solution)/shard_map/ppermute | solution.py:548
  63.4 37.9 %collective-permute-start.19 = (bf16[256,512]{1,0:T(8,128)(2,1)}, bf16[256,512]{1,0:T(8,128)(2,1)}, u32[]{:S(2)}, u32[]{:S(2)}) collective-permute-start(bf16[256,512]{1,0:T(8,128)(2,1)} %dynamic_slice.28), channel_id=1, source_target_pairs={{0,1},{1,2},{2,3},{3,0},{4,5},{5,6},{6,7},{7,4},{8,9},{9,10},{10,1... | collective-permute-start | bytes 786440 | tf_op jit(solution)/shard_map/ppermute | solution.py:548
  78.0 23.7 %collective-permute-start.18 = (bf16[2,3,64,1280]{3,2,1,0:T(8,128)(2,1)S(1)}, bf16[2,3,64,1280]{3,2,1,0:T(8,128)(2,1)S(1)}, u32[]{:S(2)}, u32[]{:S(2)}) collective-permute-start(bf16[2,3,64,1280]{3,2,1,0:T(8,128)(2,1)S(1)} %pad_maximum_fusion.2), channel_id=1, source_target_pairs={{0,8},{4,12},{8,0},{12,4},{16,24},{20,28},{24,16},{28,20},{1,9},{5... | collective-permute-start | bytes 2949128 | tf_op jit(solution)/shard_map/ppermute | solution.py:551
  79.2 22.6 %collective-permute-start.17 = (bf16[2,3,64,1280]{3,2,1,0:T(8,128)(2,1)S(1)}, bf16[2,3,64,1280]{3,2,1,0:T(8,128)(2,1)S(1)}, u32[]{:S(2)}, u32[]{:S(2)}) collective-permute-start(bf16[2,3,64,1280]{3,2,1,0:T(8,128)(2,1)S(1)} %pad_maximum_fusion.1), channel_id=1, source_target_pairs={{0,16},{4,20},{8,24},{12,28},{16,0},{20,4},{24,8},{28,12},{1,17},{... | collective-permute-start | bytes 2949128 | tf_op jit(solution)/shard_map/ppermute | solution.py:551
  98.7 23.5 %collective-permute-start.26 = (bf16[3,64,2560]{2,1,0:T(8,128)(2,1)S(1)}, bf16[3,64,2560]{2,1,0:T(8,128)(2,1)}, u32[]{:S(2)}, u32[]{:S(2)}) collective-permute-start(bf16[3,64,2560]{2,1,0:T(8,128)(2,1)S(1)} %pad_maximum_fusion.refs_2_), channel_id=1, source_target_pairs={{0,4},{4,0},{8,12},{12,8},{16,20},{20,16},{24,28},{28,24},{1,5},{5... | collective-permute-start | bytes 2949128 | tf_op jit(solution)/shard_map/ppermute | solution.py:554
  101.2 22.1 %collective-permute-start.27 = (bf16[1,3,64,1280]{3,2,1,0:T(8,128)(2,1)S(1)}, bf16[1,3,64,1280]{3,2,1,0:T(8,128)(2,1)}, u32[]{:S(2)}, u32[]{:S(2)}) collective-permute-start(bf16[1,3,64,1280]{3,2,1,0:T(8,128)(2,1)S(1)} %collective-permute-done.15.refs_3_), channel_id=1, source_target_pairs={{0,4},{4,0},{8,12},{12,8},{16,20},{20,16},{24,28},{28,24},{1,5},{5... | collective-permute-start | bytes 1474568 | tf_op jit(solution)/shard_map/ppermute | solution.py:554
  101.3 42.3 %collective-permute-start.28 = (bf16[1,3,64,1280]{3,2,1,0:T(8,128)(2,1)S(1)}, bf16[1,3,64,1280]{3,2,1,0:T(8,128)(2,1)}, u32[]{:S(2)}, u32[]{:S(2)}) collective-permute-start(bf16[1,3,64,1280]{3,2,1,0:T(8,128)(2,1)S(1)} %collective-permute-done.16.refs_4_), channel_id=1, source_target_pairs={{0,4},{4,0},{8,12},{12,8},{16,20},{20,16},{24,28},{28,24},{1,5},{5... | collective-permute-start | bytes 1474568 | tf_op jit(solution)/shard_map/ppermute | solution.py:554
  103.0 15.7 %collective-permute-start.23 = (bf16[1,3,256,256]{3,2,1,0:T(8,128)(2,1)S(1)}, bf16[1,3,256,256]{3,2,1,0:T(8,128)(2,1)S(1)}, u32[]{:S(2)}, u32[]{:S(2)}) collective-permute-start(bf16[1,3,256,256]{3,2,1,0:T(8,128)(2,1)S(1)} %get-tuple-element.430), channel_id=1, source_target_pairs={{0,16},{4,20},{8,24},{12,28},{16,0},{20,4},{24,8},{28,12},{1,17},{... | collective-permute-start | bytes 1179656 | tf_op jit(solution)/shard_map/ppermute | solution.py:551
  104.3 16.0 %collective-permute-start.22 = (bf16[1,3,256,256]{3,2,1,0:T(8,128)(2,1)S(1)}, bf16[1,3,256,256]{3,2,1,0:T(8,128)(2,1)S(1)}, u32[]{:S(2)}, u32[]{:S(2)}) collective-permute-start(bf16[1,3,256,256]{3,2,1,0:T(8,128)(2,1)S(1)} %get-tuple-element.431), channel_id=1, source_target_pairs={{0,8},{4,12},{8,0},{12,4},{16,24},{20,28},{24,16},{28,20},{1,9},{5... | collective-permute-start | bytes 1179656 | tf_op jit(solution)/shard_map/ppermute | solution.py:551
  118.8 25.9 %collective-permute-start.29 = (bf16[2,3,64,1280]{3,2,1,0:T(8,128)(2,1)S(1)}, bf16[2,3,64,1280]{3,2,1,0:T(8,128)(2,1)}, u32[]{:S(2)}, u32[]{:S(2)}) collective-permute-start(bf16[2,3,64,1280]{3,2,1,0:T(8,128)(2,1)S(1)} %collective-permute-done.17.refs_5_), channel_id=1, source_target_pairs={{0,4},{4,0},{8,12},{12,8},{16,20},{20,16},{24,28},{28,24},{1,5},{5... | collective-permute-start | bytes 2949128 | tf_op jit(solution)/shard_map/ppermute | solution.py:554
  120.2 24.5 %collective-permute-start.30 = (bf16[2,3,64,1280]{3,2,1,0:T(8,128)(2,1)S(1)}, bf16[2,3,64,1280]{3,2,1,0:T(8,128)(2,1)}, u32[]{:S(2)}, u32[]{:S(2)}) collective-permute-start(bf16[2,3,64,1280]{3,2,1,0:T(8,128)(2,1)S(1)} %collective-permute-done.18.refs_6_), channel_id=1, source_target_pairs={{0,4},{4,0},{8,12},{12,8},{16,20},{20,16},{24,28},{28,24},{1,5},{5... | collective-permute-start | bytes 2949128 | tf_op jit(solution)/shard_map/ppermute | solution.py:554
  122.2 29.9 %collective-permute-start.25 = (bf16[2,3,256,256]{3,2,1,0:T(8,128)(2,1)}, bf16[2,3,256,256]{3,2,1,0:T(8,128)(2,1)}, u32[]{:S(2)}, u32[]{:S(2)}) collective-permute-start(bf16[2,3,256,256]{3,2,1,0:T(8,128)(2,1)} %pad_maximum_fusion.5), channel_id=1, source_target_pairs={{0,8},{4,12},{8,0},{12,4},{16,24},{20,28},{24,16},{28,20},{1,9},{5... | collective-permute-start | bytes 2359304 | tf_op jit(solution)/shard_map/ppermute | solution.py:551
  123.4 28.7 %collective-permute-start.24 = (bf16[2,3,256,256]{3,2,1,0:T(8,128)(2,1)}, bf16[2,3,256,256]{3,2,1,0:T(8,128)(2,1)}, u32[]{:S(2)}, u32[]{:S(2)}) collective-permute-start(bf16[2,3,256,256]{3,2,1,0:T(8,128)(2,1)} %pad_maximum_fusion.4), channel_id=1, source_target_pairs={{0,16},{4,20},{8,24},{12,28},{16,0},{20,4},{24,8},{28,12},{1,17},{... | collective-permute-start | bytes 2359304 | tf_op jit(solution)/shard_map/ppermute | solution.py:551
  143.6 16.7 %collective-permute-start.31 = (bf16[3,256,512]{2,1,0:T(8,128)(2,1)S(1)}, bf16[3,256,512]{2,1,0:T(8,128)(2,1)S(1)}, u32[]{:S(2)}, u32[]{:S(2)}) collective-permute-start(bf16[3,256,512]{2,1,0:T(8,128)(2,1)S(1)} %pad_maximum_fusion.3.refs_1_), channel_id=1, source_target_pairs={{0,4},{4,0},{8,12},{12,8},{16,20},{20,16},{24,28},{28,24},{1,5},{5... | collective-permute-start | bytes 2359304 | tf_op jit(solution)/shard_map/ppermute | solution.py:554
  210.4 44.8 %collective-permute-start.36 = (bf16[4,4,128,512]{3,2,1,0:T(8,128)(2,1)S(1)}, bf16[4,4,128,512]{3,2,1,0:T(8,128)(2,1)S(1)}, u32[]{:S(2)}, u32[]{:S(2)}) collective-permute-start(bf16[4,4,128,512]{3,2,1,0:T(8,128)(2,1)S(1)} %bitcast.159), channel_id=1, source_target_pairs={{0,4},{4,0},{8,12},{12,8},{16,20},{20,16},{24,28},{28,24},{1,5},{5... | collective-permute-start | bytes 6291464 | tf_op jit(solution)/shard_map/ppermute | solution.py:554
  210.5 44.7 %collective-permute-start.37 = (bf16[4,4,128,512]{3,2,1,0:T(8,128)(2,1)}, bf16[4,4,128,512]{3,2,1,0:T(8,128)(2,1)S(1)}, u32[]{:S(2)}, u32[]{:S(2)}) collective-permute-start(bf16[4,4,128,512]{3,2,1,0:T(8,128)(2,1)} %bitcast.172), channel_id=1, source_target_pairs={{0,4},{4,0},{8,12},{12,8},{16,20},{20,16},{24,28},{28,24},{1,5},{5... | collective-permute-start | bytes 6291464 | tf_op jit(solution)/shard_map/ppermute | solution.py:554
  264.3 47.2 %collective-permute-start.40 = (bf16[2,4,128,512]{3,2,1,0:T(8,128)(2,1)}, bf16[2,4,128,512]{3,2,1,0:T(8,128)(2,1)}, u32[]{:S(2)}, u32[]{:S(2)}) collective-permute-start(bf16[2,4,128,512]{3,2,1,0:T(8,128)(2,1)} %get-tuple-element.291), channel_id=1, source_target_pairs={{0,8},{4,12},{8,0},{12,4},{16,24},{20,28},{24,16},{28,20},{1,9},{5... | collective-permute-start | bytes 3145736 | tf_op jit(solution)/shard_map/ppermute | solution.py:551
  264.7 46.9 %collective-permute-start.41 = (bf16[2,4,128,512]{3,2,1,0:T(8,128)(2,1)}, bf16[2,4,128,512]{3,2,1,0:T(8,128)(2,1)}, u32[]{:S(2)}, u32[]{:S(2)}) collective-permute-start(bf16[2,4,128,512]{3,2,1,0:T(8,128)(2,1)} %get-tuple-element.292), channel_id=1, source_target_pairs={{0,16},{4,20},{8,24},{12,28},{16,0},{20,4},{24,8},{28,12},{1,17},{... | collective-permute-start | bytes 3145736 | tf_op jit(solution)/shard_map/ppermute | solution.py:551
  265.0 46.7 %collective-permute-start.42 = (bf16[2,4,128,512]{3,2,1,0:T(8,128)(2,1)}, bf16[2,4,128,512]{3,2,1,0:T(8,128)(2,1)}, u32[]{:S(2)}, u32[]{:S(2)}) collective-permute-start(bf16[2,4,128,512]{3,2,1,0:T(8,128)(2,1)} %get-tuple-element.293), channel_id=1, source_target_pairs={{0,8},{4,12},{8,0},{12,4},{16,24},{20,28},{24,16},{28,20},{1,9},{5... | collective-permute-start | bytes 3145736 | tf_op jit(solution)/shard_map/ppermute | solution.py:551
  266.2 45.6 %collective-permute-start.43 = (bf16[2,4,128,512]{3,2,1,0:T(8,128)(2,1)S(1)}, bf16[2,4,128,512]{3,2,1,0:T(8,128)(2,1)}, u32[]{:S(2)}, u32[]{:S(2)}) collective-permute-start(bf16[2,4,128,512]{3,2,1,0:T(8,128)(2,1)S(1)} %get-tuple-element.294), channel_id=1, source_target_pairs={{0,16},{4,20},{8,24},{12,28},{16,0},{20,4},{24,8},{28,12},{1,17},{... | collective-permute-start | bytes 3145736 | tf_op jit(solution)/shard_map/ppermute | solution.py:551
  281.2 35.9 %collective-permute-start.44 = (bf16[4,4,64,512]{3,2,1,0:T(8,128)(2,1)}, bf16[4,4,64,512]{3,2,1,0:T(8,128)(2,1)S(1)}, u32[]{:S(2)}, u32[]{:S(2)}) collective-permute-start(bf16[4,4,64,512]{3,2,1,0:T(8,128)(2,1)} %get-tuple-element.306), channel_id=1, source_target_pairs={{0,4},{4,0},{8,12},{12,8},{16,20},{20,16},{24,28},{28,24},{1,5},{5... | collective-permute-start | bytes 3145736 | tf_op jit(solution)/shard_map/ppermute | solution.py:554
  317.6 19.9 %collective-permute-start.47 = (bf16[2,4,32,512]{3,2,1,0:T(8,128)(2,1)S(1)}, bf16[2,4,32,512]{3,2,1,0:T(8,128)(2,1)S(1)}, u32[]{:S(2)}, u32[]{:S(2)}) collective-permute-start(bf16[2,4,32,512]{3,2,1,0:T(8,128)(2,1)S(1)} %get-tuple-element.315), channel_id=1, source_target_pairs={{0,8},{4,12},{8,0},{12,4},{16,24},{20,28},{24,16},{28,20},{1,9},{5... | collective-permute-start | bytes 786440 | tf_op jit(solution)/shard_map/ppermute | solution.py:551
  318.8 18.8 %collective-permute-start.48 = (bf16[2,4,32,512]{3,2,1,0:T(8,128)(2,1)S(1)}, bf16[2,4,32,512]{3,2,1,0:T(8,128)(2,1)S(1)}, u32[]{:S(2)}, u32[]{:S(2)}) collective-permute-start(bf16[2,4,32,512]{3,2,1,0:T(8,128)(2,1)S(1)} %get-tuple-element.316), channel_id=1, source_target_pairs={{0,16},{4,20},{8,24},{12,28},{16,0},{20,4},{24,8},{28,12},{1,17},{... | collective-permute-start | bytes 786440 | tf_op jit(solution)/shard_map/ppermute | solution.py:551
  319.2 18.4 %collective-permute-start.45 = (bf16[1,4,128,512]{3,2,1,0:T(8,128)(2,1)}, bf16[1,4,128,512]{3,2,1,0:T(8,128)(2,1)S(1)}, u32[]{:S(2)}, u32[]{:S(2)}) collective-permute-start(bf16[1,4,128,512]{3,2,1,0:T(8,128)(2,1)} %get-tuple-element.313), channel_id=1, source_target_pairs={{0,16},{4,20},{8,24},{12,28},{16,0},{20,4},{24,8},{28,12},{1,17},{... | collective-permute-start | bytes 1572872 | tf_op jit(solution)/shard_map/ppermute | solution.py:551
  320.2 17.3 %collective-permute-start.46 = (bf16[1,4,128,512]{3,2,1,0:T(8,128)(2,1)}, bf16[1,4,128,512]{3,2,1,0:T(8,128)(2,1)S(1)}, u32[]{:S(2)}, u32[]{:S(2)}) collective-permute-start(bf16[1,4,128,512]{3,2,1,0:T(8,128)(2,1)} %get-tuple-element.314), channel_id=1, source_target_pairs={{0,8},{4,12},{8,0},{12,4},{16,24},{20,28},{24,16},{28,20},{1,9},{5... | collective-permute-start | bytes 1572872 | tf_op jit(solution)/shard_map/ppermute | solution.py:551
  338.8 35.6 %collective-permute-start.51 = (bf16[256,512]{1,0:T(8,128)(2,1)S(1)}, bf16[256,512]{1,0:T(8,128)(2,1)S(1)}, u32[]{:S(2)}, u32[]{:S(2)}) collective-permute-start(bf16[256,512]{1,0:T(8,128)(2,1)S(1)} %get-tuple-element.350), channel_id=1, source_target_pairs={{0,1},{1,2},{2,3},{3,0},{4,5},{5,6},{6,7},{7,4},{8,9},{9,10},{10,1... | collective-permute-start | bytes 786440 | tf_op jit(solution)/shard_map/ppermute | solution.py:548
  339.9 34.6 %collective-permute-start.52 = (bf16[256,512]{1,0:T(8,128)(2,1)S(1)}, bf16[256,512]{1,0:T(8,128)(2,1)S(1)}, u32[]{:S(2)}, u32[]{:S(2)}) collective-permute-start(bf16[256,512]{1,0:T(8,128)(2,1)S(1)} %get-tuple-element.351), channel_id=1, source_target_pairs={{0,2},{1,3},{2,0},{3,1},{4,6},{5,7},{6,4},{7,5},{8,10},{9,11},{10,... | collective-permute-start | bytes 786440 | tf_op jit(solution)/shard_map/ppermute | solution.py:548
  341.4 33.1 %collective-permute-start.53 = (bf16[256,512]{1,0:T(8,128)(2,1)S(1)}, bf16[256,512]{1,0:T(8,128)(2,1)S(1)}, u32[]{:S(2)}, u32[]{:S(2)}) collective-permute-start(bf16[256,512]{1,0:T(8,128)(2,1)S(1)} %get-tuple-element.352), channel_id=1, source_target_pairs={{0,3},{1,0},{2,1},{3,2},{4,7},{5,4},{6,5},{7,6},{8,11},{9,8},{10,9... | collective-permute-start | bytes 786440 | tf_op jit(solution)/shard_map/ppermute | solution.py:548
  343.1 17.8 %collective-permute-start.49 = (bf16[1,4,160,512]{3,2,1,0:T(8,128)(2,1)S(1)}, bf16[1,4,160,512]{3,2,1,0:T(8,128)(2,1)S(1)}, u32[]{:S(2)}, u32[]{:S(2)}) collective-permute-start(bf16[1,4,160,512]{3,2,1,0:T(8,128)(2,1)S(1)} %maximum_bitcast_fusion), channel_id=1, source_target_pairs={{0,16},{4,20},{8,24},{12,28},{16,0},{20,4},{24,8},{28,12},{1,17},{... | collective-permute-start | bytes 1966088 | tf_op jit(solution)/shard_map/ppermute | solution.py:551
  343.3 17.6 %collective-permute-start.50 = (bf16[1,4,160,512]{3,2,1,0:T(8,128)(2,1)S(1)}, bf16[1,4,160,512]{3,2,1,0:T(8,128)(2,1)S(1)}, u32[]{:S(2)}, u32[]{:S(2)}) collective-permute-start(bf16[1,4,160,512]{3,2,1,0:T(8,128)(2,1)S(1)} %maximum_bitcast_fusion.1), channel_id=1, source_target_pairs={{0,8},{4,12},{8,0},{12,4},{16,24},{20,28},{24,16},{28,20},{1,9},{5... | collective-permute-start | bytes 1966088 | tf_op jit(solution)/shard_map/ppermute | solution.py:551
  379.3 25.5 %collective-permute-start.57 = (bf16[320,512]{1,0:T(8,128)(2,1)}, bf16[320,512]{1,0:T(8,128)(2,1)S(1)}, u32[]{:S(2)}, u32[]{:S(2)}) collective-permute-start(bf16[320,512]{1,0:T(8,128)(2,1)} %copy-done.27), channel_id=1, source_target_pairs={{0,1},{1,2},{2,3},{3,0},{4,5},{5,6},{6,7},{7,4},{8,9},{9,10},{10,1... | collective-permute-start | bytes 983048 | tf_op jit(solution)/shard_map/ppermute | solution.py:548
  379.7 25.2 %collective-permute-start.58 = (bf16[320,512]{1,0:T(8,128)(2,1)}, bf16[320,512]{1,0:T(8,128)(2,1)S(1)}, u32[]{:S(2)}, u32[]{:S(2)}) collective-permute-start(bf16[320,512]{1,0:T(8,128)(2,1)} %copy-done.26), channel_id=1, source_target_pairs={{0,2},{1,3},{2,0},{3,1},{4,6},{5,7},{6,4},{7,5},{8,10},{9,11},{10,... | collective-permute-start | bytes 983048 | tf_op jit(solution)/shard_map/ppermute | solution.py:548
  380.4 24.4 %collective-permute-start.59 = (bf16[320,512]{1,0:T(8,128)(2,1)}, bf16[320,512]{1,0:T(8,128)(2,1)S(1)}, u32[]{:S(2)}, u32[]{:S(2)}) collective-permute-start(bf16[320,512]{1,0:T(8,128)(2,1)} %copy-done.25), channel_id=1, source_target_pairs={{0,3},{1,0},{2,1},{3,2},{4,7},{5,4},{6,5},{7,6},{8,11},{9,8},{10,9... | collective-permute-start | bytes 983048 | tf_op jit(solution)/shard_map/ppermute | solution.py:548
  387.9 18.8 %collective-permute-start.55 = (bf16[2,4,96,512]{3,2,1,0:T(8,128)(2,1)S(1)}, bf16[2,4,96,512]{3,2,1,0:T(8,128)(2,1)S(1)}, u32[]{:S(2)}, u32[]{:S(2)}) collective-permute-start(bf16[2,4,96,512]{3,2,1,0:T(8,128)(2,1)S(1)} %get-tuple-element.361), channel_id=1, source_target_pairs={{0,8},{4,12},{8,0},{12,4},{16,24},{20,28},{24,16},{28,20},{1,9},{5... | collective-permute-start | bytes 2359304 | tf_op jit(solution)/shard_map/ppermute | solution.py:551
  388.6 18.4 %collective-permute-start.56 = (bf16[2,4,96,512]{3,2,1,0:T(8,128)(2,1)S(1)}, bf16[2,4,96,512]{3,2,1,0:T(8,128)(2,1)S(1)}, u32[]{:S(2)}, u32[]{:S(2)}) collective-permute-start(bf16[2,4,96,512]{3,2,1,0:T(8,128)(2,1)S(1)} %get-tuple-element.362), channel_id=1, source_target_pairs={{0,16},{4,20},{8,24},{12,28},{16,0},{20,4},{24,8},{28,12},{1,17},{... | collective-permute-start | bytes 2359304 | tf_op jit(solution)/shard_map/ppermute | solution.py:551
  421.9 23.5 %collective-permute-start.71 = (bf16[576,512]{1,0:T(8,128)(2,1)S(1)}, bf16[576,512]{1,0:T(8,128)(2,1)S(1)}, u32[]{:S(2)}, u32[]{:S(2)}) collective-permute-start(bf16[576,512]{1,0:T(8,128)(2,1)S(1)} %constant_dynamic-update-slice_fusion.9.refs_0_), channel_id=1, source_target_pairs={{0,24},{4,28},{8,16},{12,20},{16,8},{20,12},{24,0},{28,4},{1,25},{... | collective-permute-start | bytes 1769480 | tf_op jit(solution)/shard_map/ppermute | solution.py:551
  424.9 26.4 %collective-permute-start.70 = (bf16[576,512]{1,0:T(8,128)(2,1)S(1)}, bf16[576,512]{1,0:T(8,128)(2,1)S(1)}, u32[]{:S(2)}, u32[]{:S(2)}) collective-permute-start(bf16[576,512]{1,0:T(8,128)(2,1)S(1)} %constant_dynamic-update-slice_fusion.9.refs_0_), channel_id=1, source_target_pairs={{0,16},{4,20},{8,24},{12,28},{16,0},{20,4},{24,8},{28,12},{1,17},{... | collective-permute-start | bytes 1769480 | tf_op jit(solution)/shard_map/ppermute | solution.py:551
  424.9 26.4 %collective-permute-start.69 = (bf16[576,512]{1,0:T(8,128)(2,1)S(1)}, bf16[576,512]{1,0:T(8,128)(2,1)S(1)}, u32[]{:S(2)}, u32[]{:S(2)}) collective-permute-start(bf16[576,512]{1,0:T(8,128)(2,1)S(1)} %constant_dynamic-update-slice_fusion.9.refs_0_), channel_id=1, source_target_pairs={{0,8},{4,12},{8,0},{12,4},{16,24},{20,28},{24,16},{28,20},{1,9},{5... | collective-permute-start | bytes 1769480 | tf_op jit(solution)/shard_map/ppermute | solution.py:551
  (80 other events, 669.9 us)

commit v6 on v5

--- a/solution.py
+++ b/solution.py
@@ -352,10 +352,10 @@
     home_ref[...] = jnp.where(first_core, low, high).reshape(home_ref.shape).astype(bf16)
 
 
-def weight_grads(links, left, rights):
+def weight_grads(links, left, rights, first, count):
     ns, nq = links.ns, links.nq
     rows, width = left.shape
-    count, _, wide = rights.shape
+    wide = rights.shape[2]
     rq = width // (ns * nq)
     spec = pl.BlockSpec((ns, nq, 1, rq, wide // 2), lambda i: (0, 0, i, 0, 0))
     shape = jax.ShapeDtypeStruct((ns, nq, count, rq, wide // 2), bf16)
@@ -364,7 +364,7 @@
         grid=(count,),
         in_specs=[
             pl.BlockSpec((rows, width), lambda i: (0, 0)),
-            pl.BlockSpec((1, rows, wide), lambda i: (i, 0, 0)),
+            pl.BlockSpec((1, rows, wide), lambda i: (first + i, 0, 0)),
         ],
         out_specs=[spec, spec],
         out_shape=[shape, shape],
@@ -373,7 +373,7 @@
         name="weight_grads",
     )(left, rights)
     flat = (ns, nq, count * rq, wide // 2)
-    return [away.reshape(flat)], [home.reshape(flat)]
+    return away.reshape(flat), home.reshape(flat)
 
 
 def row_block(rows):
@@ -618,7 +618,7 @@
     return values[..., part * n : (part + 1) * n]
 
 
-def assemble(links, weights, got_mine, got_mate):
+def assemble(links, weights, got_mine, got_mate, through):
     ns, nq, bits = links.ns, links.nq, links.bits
     rows = [w.shape[0] for w in weights]
     cols = [w.shape[1] for w in weights]
@@ -631,17 +631,20 @@
     def kernel(*refs):
         w_refs = refs[:n]
         sides = (refs[n : n + per_side], refs[n + per_side : n + 2 * per_side])
-        out_refs = refs[n + 2 * per_side : n + 2 * per_side + n]
+        final_refs = refs[n + 2 * per_side : n + 2 * per_side + n]
+        out_refs = refs[n + 2 * per_side + n :][:n] if through else final_refs
         sem = refs[-1]
         z = lax.axis_index("shard")
         rep = lax.axis_index("rep")
         q, c = rep // 2, rep % 2
         copies = []
-
-        def go(src, dst):
+        by_step = [[] for _ in range(ns)]
+
+        def go(src, dst, s=0):
             copy = pltpu.make_async_copy(src, dst, sem.at[len(copies)])
             copy.start()
             copies.append(copy)
+            by_step[s].append(copy)
 
         for i in range(n):
             go(w_refs[i], out_refs[i].at[pl.ds(pl.multiple_of(z * rows[i], rows[i]), rows[i]), :])
@@ -655,7 +658,7 @@
                     zs = lax.rem(z + (ns - s), ns)
                     at = pl.ds(pl.multiple_of(zs * rows[i] + (q ^ k) * rq[i], rq[i]), rq[i])
                     to = pl.ds(pl.multiple_of(core * half + (low - base), 128), high - low)
-                    go(source, out_refs[i].at[at, to])
+                    go(source, out_refs[i].at[at, to], s)
 
                 for s in range(1, ns):
                     own = parts[0].at[s - 1, :, pl.ds(base, half)]
@@ -678,8 +681,23 @@
                                     place(source, k ^ bit, s, low, high)
                             at += 1
                 base += half
-        for copy in copies:
-            copy.wait()
+        onward = []
+        for s in range(ns):
+            for copy in by_step[s]:
+                copy.wait()
+            if through:
+                zs = lax.rem(z + (ns - s), ns)
+                for i in range(n):
+                    at = pl.ds(pl.multiple_of(zs * rows[i], rows[i]), rows[i])
+                    move = pltpu.make_async_copy(
+                        out_refs[i].at[at, :],
+                        final_refs[i].at[at, :],
+                        sem.at[len(copies) + len(onward)],
+                    )
+                    move.start()
+                    onward.append(move)
+        for move in onward:
+            move.wait()
 
     pieces = 0
     base = 0
@@ -695,8 +713,14 @@
         kernel,
         out_shape=[jax.ShapeDtypeStruct((ns * r, c), bf16) for r, c in zip(rows, cols)],
         in_specs=whole(n + 2 * per_side),
-        out_specs=[pl.BlockSpec(memory_space=pltpu.VMEM)] * n,
-        scratch_shapes=[pltpu.SemaphoreType.DMA((count,))],
+        out_specs=[
+            pl.BlockSpec(memory_space=pltpu.MemorySpace.HBM if through else pltpu.VMEM)
+        ]
+        * n,
+        scratch_shapes=[
+            pltpu.VMEM((ns * r, c), bf16) for r, c in zip(rows, cols) if through
+        ]
+        + [pltpu.SemaphoreType.DMA((count + ns * n,))],
         compiler_params=pltpu.CompilerParams(vmem_limit_bytes=32 * 1024 * 1024),
         cost_estimate=LIGHT,
         name="assemble",
@@ -732,8 +756,8 @@
             self.mate.append(self.links.core(values))
         self.done += 1
 
-    def full(self):
-        return assemble(self.links, self.weights, self.mine, self.mate)
+    def full(self, through=True):
+        return assemble(self.links, self.weights, self.mine, self.mate, through)
 
 
 class Scatter:
@@ -1027,15 +1051,14 @@
 
 def owned_qkv(links, scatter, w_qkv):
     if scatter.parts is None:
-        (grad,) = scatter.owned()
-        return side_by_side(grad, 3)
+        return side_by_side(jnp.concatenate(scatter.owned(), 2), 3)
     lanes = scatter.lanes
     rq = w_qkv.shape[0] // links.nq
 
     def place(at, i):
         return [
-            (t * rq, (t + 1) * rq, 0, lanes, 0, rq, 0, 2 * t * lanes, (2 * t + 1) * lanes)
-            for t in range(3)
+            (n * rq, (n + 1) * rq, 0, lanes, 0, rq, 0, 2 * t * lanes, (2 * t + 1) * lanes)
+            for n, t in enumerate(range(3))
         ]
 
     return owned_by_kernel(links, [scatter], [w_qkv.shape], place)[0]
@@ -1122,7 +1145,7 @@
         gather_a.send()
         gather_a.absorb()
     gather_a.mine, got_b = meet(gather_a.mine, got_b)
-    (full_qkv,) = gather_a.full()
+    (full_qkv,) = gather_a.full(False)
     got_c = gather_along(links, tie(piece_of(links, [w_down]), got_b))
     gather_b.start(jnp.stack(got_b))
     gather_b.send()
@@ -1264,9 +1287,9 @@
     grads, scatter_2.buffers = meet(grads, scatter_2.prepare_along())
     scatter_2.send_along()
     d_qkv, qv_sums = grads
-    qkv_away, qkv_home = weight_grads(links, hidden_one_b, d_qkv)
+    qkv_away, qkv_home = weight_grads(links, hidden_one_b, d_qkv, 0, 3)
     qkv_away, qkv_home, scatter_1.arrived = meet(qkv_away, qkv_home, scatter_1.arrived)
-    scatter_3 = Scatter(links, qkv_away, qkv_home)
+    scatter_3 = Scatter(links, [qkv_away], [qkv_home])
     scatter_1.settle()
     d_qkv, scatter_3.buffers = meet(d_qkv, scatter_3.prepare())
     scatter_3.send()
@@ -1311,16 +1334,16 @@
     o_wdown, o_wup, o_wout = owned_feed_forward(links, scatter_1, scatter_2, w_up, w_down, w_out)
     if ride:
         joined = arrived_lines.reshape(-1)[:n_small]
-    joined, o_wdown, o_wup, o_wout, spread_3.others = meet(
-        joined, o_wdown, o_wup, o_wout, spread_3.others
-    )
-    spread_3.pair()
-    o_qkv = owned_qkv(links, scatter_3, w_qkv)
     owned = []
     base = 0
     for n in sizes:
         owned.append(joined[base : base + n])
         base += n
+    owned, o_wdown, o_wup, o_wout, spread_3.others = meet(
+        owned, o_wdown, o_wup, o_wout, spread_3.others
+    )
+    spread_3.pair()
+    o_qkv = owned_qkv(links, scatter_3, w_qkv)
     o_g1, o_s1, o_bout, o_g2, o_s2, o_bdown, o_qvb, o_bup = owned
     return (
         output,

time: 479 us -> 478 us (level)
    unnamed x118 -> x114, local copies, waits for them, and re-layouts: 17.3 us -> 16 us
where the time goes in v6:
time: 478 us; the launch traced here: 471 us
  Pallas kernels  277 us (58%)
  starting transfers between devices  80.7 us (17%)
  waiting for transfers between devices  59.8 us (13%)
  local copies, waits for them, and re-layouts  22.2 us (5%)
  other arithmetic  19.8 us (4%)
  matrix products  8.99 us (2%)
    pallas_call x2, Pallas kernels, feed_forward(): pl.pallas_call(kernel, grid=(ns,), in_specs=[full(), full(), pl.BlockSpec...  87.6 us
    pallas_call x3, Pallas kernels, attend_back(): pl.pallas_call(kernel, grid=(count,), in_specs=[column(0), column(pairs),...  62.6 us
    pallas_call x3, Pallas kernels, attend(): pl.pallas_call(kernel, grid=(count,), in_specs=[column(0), column(pairs),...  52.5 us
    ppermute x35, starting transfers between devices, chip(): return lax.ppermute(values, 'rep', [(i, i ^ 2 * k) for i in range(self.nr)])  31.4 us
    ppermute x18, waiting for transfers between devices, along(): lax.ppermute(values, 'shard', [(i, (i + step) % self.ns) for i in range(s...  30.9 us
    ppermute x30, starting transfers between devices, core(): return lax.ppermute(values, 'rep', [(i, i ^ 1) for i in range(self.nr)])  25.2 us
    ppermute x18, starting transfers between devices, along(): lax.ppermute(values, 'shard', [(i, (i + step) % self.ns) for i in range(s...  24 us
    ppermute x35, waiting for transfers between devices, chip(): return lax.ppermute(values, 'rep', [(i, i ^ 2 * k) for i in range(self.nr)])  20.8 us
  transfers between devices with their start and end apart: 83, of which 21 were waited for; matrix products, arithmetic and copies ran while one was open for 8% of the time, Pallas kernels for 47%

profile of v6, /device:TPU:1, one launch (start us, length us, event | category | flops | bytes accessed | tf_op | source)
XLA Modules:
  0.0 470.9 jit_solution(9373936828277972450)
XLA Ops:
  0.7 2.5 pack.1
  3.2 4.2 collective-permute-start.2
  9.3 2.0 convert_reduce_fusion
  13.1 3.3 select_bitcast_fusion.refs_1_.dm_ref
  19.6 8.4 %collective-permute-done.1 = bf16[80,1536]{1,0:T(8,128)(2,1)} collective-permute-done((bf16[80,1536]{1,0:T(8,128)(2,1)}, bf16[80,1536]{1,0:T(8,128)(2,1)}, u32[]{:S(2)}, u32[]{:S(2)}) %collective-permute-start.1) | collective-permute-done | bytes 245792 | tf_op jit(solution)/shard_map/ppermute | solution.py:548
  30.0 1.9 collective-permute-start.8
  39.9 3.9 collective-permute-done.3.refs_2_
  45.7 3.9 collective-permute-start.10
  49.7 10.2 %collective-permute-done.8 = bf16[64,2560]{1,0:T(8,128)(2,1)S(1)} collective-permute-done((bf16[64,2560]{1,0:T(8,128)(2,1)}, bf16[64,2560]{1,0:T(8,128)(2,1)S(1)}, u32[]{:S(2)}, u32[]{:S(2)}) %collective-permute-start.8) | collective-permute-done | bytes 327712 | tf_op jit(solution)/shard_map/ppermute | solution.py:548
  59.9 1.9 collective-permute-start.12
  68.8 9.0 %fusion.refs_0_.refs_1_.refs_2_ = bf16[1104,3072]{1,0:T(8,128)(2,1)} fusion(bf16[1104,1024]{1,0:T(8,128)(2,1)S(1)} %fusion.6.left_ref, bf16[1024,3072]{1,0:T(8,128)(2,1)S(1)} %assemble.3.w_ref, f32[3072]{0:T(1024)S(1)} %pad_maximum_fusion.14), kind=kOutput, calls=%fused_computation.1 | convolution fusion | flops 6952550400 | bytes 15347712 | tf_op jit(solution)/shard_map/dot_general | solution.py:26
  79.5 19.1 %attend.3 = (bf16[1104,1024]{1,0:T(8,128)(2,1)}, f32[1104,1024]{1,0:T(8,128)}, bf16[16,1104,1104]{2,1,0:T(8,128)(2,1)}) custom-call(bf16[1104,3072]{1,0:T(8,128)(2,1)} %fusion.refs_0_.refs_1_.refs_2_, bf16[1104,3072]{1,0:T(8,128)(2,1)} %fusion.refs_0_.refs_1_.refs_2_, bf16[1104,3072]{1,0:T(8,128)(2,1)} %fusion.refs_0_.refs_1_.refs_2_), custom_call_target="tpu_custom_call" | custom-call | flops 20000000000 | bytes 10000000 | tf_op jit(solution)/shard_map/attend/pallas_call | solution.py:89
  98.7 2.6 collective-permute-start.26
  104.5 14.2 %attend.4 = (bf16[1104,1024]{1,0:T(8,128)(2,1)}, f32[1104,1024]{1,0:T(8,128)}, bf16[16,1104,1104]{2,1,0:T(8,128)(2,1)}) custom-call(bf16[1104,3072]{1,0:T(8,128)(2,1)} %fusion.refs_0_.refs_1_.refs_2_, bf16[1104,3072]{1,0:T(8,128)(2,1)} %fusion.refs_0_.refs_1_.refs_2_, ...), custom_call_target="tpu_custom_call", output_to_operand_aliasing={{0}: (3, {}), {1}: (4, {}), {2}: (5, {})} | custom-call | flops 20000000000 | bytes 10000000 | tf_op jit(solution)/shard_map/attend/pallas_call | solution.py:89
  124.4 19.1 %attend.5 = (bf16[1104,1024]{1,0:T(8,128)(2,1)}, f32[1104,1024]{1,0:T(8,128)}, bf16[16,1104,1104]{2,1,0:T(8,128)(2,1)}) custom-call(bf16[1104,3072]{1,0:T(8,128)(2,1)} %fusion.refs_0_.refs_1_.refs_2_, bf16[1104,3072]{1,0:T(8,128)(2,1)} %fusion.refs_0_.refs_1_.refs_2_, ...), custom_call_target="tpu_custom_call", output_to_operand_aliasing={{0}: (3, {}), {1}: (4, {}), {2}: (5, {})} | custom-call | flops 20000000000 | bytes 10000000 | tf_op jit(solution)/shard_map/attend/pallas_call | solution.py:89
  145.2 3.9 assemble.4
  149.0 3.3 copy-done.20
  152.9 7.5 %middle.1 = (f32[1104,1024]{1,0:T(8,128)}, bf16[1104,1024]{1,0:T(8,128)(2,1)S(1)}) custom-call(bf16[1104,1024]{1,0:T(8,128)(2,1)} %bitcast.140, bf16[1104,1024]{1,0:T(8,128)(2,1)} %get-tuple-element.251.att_ref.refs_4_, bf16[1024,1024]{1,0:T(8,128)(2,1)S(1)} %get-tuple-element.254.w_ref, f32[1,1024]{1,0:T(1,128)S(1)} %bitcast.160, f32[1,1024]{1,0:T(1,128)S(1)} %bitcast.155, ...), custom_call_target="tpu_custom_call" | custom-call | flops 20000000000 | bytes 10000000 | tf_op jit(solution)/shard_map/middle/pallas_call | solution.py:410
  160.5 3.2 assemble.5.refs_4_
  163.6 3.2 copy-done.2
  166.9 43.9 %feed_forward.2 = (f32[1104,1024]{1,0:T(8,128)}, f32[1104,1024]{1,0:T(8,128)}, bf16[4,512,512]{2,1,0:T(8,128)(2,1)S(1)}, bf16[4,512,512]{2,1,0:T(8,128)(2,1)}, b...) custom-call(bf16[1104,1024]{1,0:T(8,128)(2,1)} %copy-done.26, ...), custom_call_target="tpu_custom_call" | custom-call | flops 20000000000 | bytes 10000000 | tf_op jit(solution)/shard_map/feed_forward/pallas_call | solution.py:293
  211.4 43.7 %feed_forward.3 = (bf16[1104,1024]{1,0:T(8,128)(2,1)}, f32[1104,1024]{1,0:T(8,128)}, bf16[4,512,512]{2,1,0:T(8,128)(2,1)S(1)}, bf16[4,512,512]{2,1,0:T(8,128)(2,...) custom-call(bf16[1104,1024]{1,0:T(8,128)(2,1)} %copy-done.26, ...), custom_call_target="tpu_custom_call" | custom-call | flops 20000000000 | bytes 10000000 | tf_op jit(solution)/shard_map/feed_forward/pallas_call | solution.py:293
  255.7 2.4 core_sums.4
  258.1 3.3 collective-permute-done.38.refs_2_
  262.6 2.2 core_sums.5
  267.7 14.0 %middle_back.1 = (f32[1104,1024]{1,0:T(8,128)}, bf16[1104,1024]{1,0:T(8,128)(2,1)}, bf16[4,4,64,512]{3,2,1,0:T(8,128)(2,1)}, bf16[4,4,64,512]{3,2,1,0:T(8,128)(2,1)S(1)}, f32[8,1024]{1,0:T(8,128)S(1)}) custom-call(f32[1104,1024]{1,0:T(8,128)} %get-tuple-element.289.g_ref, f32[1104,1024]{1,0:T(8,128)} %get-tuple-element.265.refs_7_.mid_ref, ...), custom_call_target="tpu_custom_call" | custom-call | flops 20000000000 | bytes 10000000 | tf_op jit(solution)/shard_map/middle_back/pallas_call | solution.py:466
  283.0 29.0 %attend_back.3 = (bf16[3,1104,1024]{2,1,0:T(8,128)(2,1)}, f32[2,1,1024]{2,1,0:T(1,128)}) custom-call(bf16[1104,3072]{1,0:T(8,128)(2,1)} %fusion.refs_0_.refs_1_.refs_2_, bf16[1104,3072]{1,0:T(8,128)(2,1)} %fusion.refs_0_.refs_1_.refs_2_, bf16[1104,3072]{1,0:T(8,128)(2,1)} %fusion.refs_0_.refs_1_.refs_2_, bf16[1104,1024]{1,0:T(8,128)(2,1)} %get-tuple-element.293.refs_3_, ...), custom_call_target="tpu_custom_call" | custom-call | flops 1 | bytes 1 | tf_op jit(solution)/shard_map/attend_back/pallas_call | solution.py:168
  312.3 3.2 fusion.11
  315.4 2.2 fusion.8
  321.1 16.9 %attend_back.4 = (bf16[3,1104,1024]{2,1,0:T(8,128)(2,1)}, f32[2,1,1024]{2,1,0:T(1,128)}) custom-call(bf16[1104,3072]{1,0:T(8,128)(2,1)} %fusion.refs_0_.refs_1_.refs_2_, bf16[1104,3072]{1,0:T(8,128)(2,1)} %fusion.refs_0_.refs_1_.refs_2_, bf16[1104,3072]{1,0:T(8,128)(2,1)} %fusion.refs_0_.refs_1_.refs_2_, ...), custom_call_target="tpu_custom_call", output_to_operand_aliasing={{0}: (7, {}), {1}: (8, {})} | custom-call | flops 20000000000 | bytes 10000000 | tf_op jit(solution)/shard_map/attend_back/pallas_call | solution.py:168
  344.5 16.7 %attend_back.5 = (bf16[3,1104,1024]{2,1,0:T(8,128)(2,1)}, f32[2,1,1024]{2,1,0:T(1,128)}) custom-call(bf16[1104,3072]{1,0:T(8,128)(2,1)} %fusion.refs_0_.refs_1_.refs_2_, bf16[1104,3072]{1,0:T(8,128)(2,1)} %fusion.refs_0_.refs_1_.refs_2_, bf16[1104,3072]{1,0:T(8,128)(2,1)} %fusion.refs_0_.refs_1_.refs_2_, ...), custom_call_target="tpu_custom_call", output_to_operand_aliasing={{0}: (7, {}), {1}: (8, {})} | custom-call | flops 20000000000 | bytes 10000000 | tf_op jit(solution)/shard_map/attend_back/pallas_call | solution.py:168
  363.1 11.8 %weight_grads.1 = (bf16[4,4,3,64,512]{4,3,2,1,0:T(8,128)(2,1)}, bf16[4,4,3,64,512]{4,3,2,1,0:T(8,128)(2,1)}) custom-call(bf16[1104,1024]{1,0:T(8,128)(2,1)S(1)} %copy-done.9, bf16[3,1104,1024]{2,1,0:T(8,128)(2,1)} %get-tuple-element.364.right_ref.d_ref), custom_call_target="tpu_custom_call" | custom-call | flops 20000000000 | bytes 10000000 | tf_op jit(solution)/shard_map/weight_grads/pallas_call | solution.py:362
  375.8 3.8 collective-permute-start.54
  380.8 2.3 collective-permute-start.59
  383.1 1.9 collective-permute-done.54.refs_1_
  385.1 1.9 copy-done.5
  390.5 14.8 %entry_back.1 = (f32[1104,1024]{1,0:T(8,128)}, f32[8,1024]{1,0:T(8,128)S(1)}) custom-call(bf16[3,1104,1024]{2,1,0:T(8,128)(2,1)} %get-tuple-element.364.right_ref.d_ref, bf16[1024,3072]{1,0:T(8,128)(2,1)} %copy-done.3, bf16[1104,1024]{1,0:T(8,128)(2,1)S(1)} %bitcast.141, f32[1104,1024]{1,0:T(8,128)} %get-tuple-element.365.d_mid_ref, f32[1,1024]{1,0:T(1,128)S(1)} %bitcast.161), custom_call_target="tpu_custom_call" | custom-call | flops 6000000000 | bytes 1 | tf_op jit(solution)/shard_map/entry_back/pallas_call | solution.py:514
  405.3 1.8 collective-permute-done.55
  415.9 5.7 %collective-permute-done.61 = bf16[1,4,96,512]{3,2,1,0:T(8,128)(2,1)S(1)} collective-permute-done((bf16[1,4,96,512]{3,2,1,0:T(8,128)(2,1)S(1)}, bf16[1,4,96,512]{3,2,1,0:T(8,128)(2,1)S(1)}, u32[]{:S(2)}, u32[]{:S(2)}) %collective-permute-start.61) | collective-permute-done | bytes 393248 | tf_op jit(solution)/shard_map/ppermute | solution.py:551
  422.3 3.0 collective-permute-start.71
  426.0 4.3 collective-permute-start.66
  431.0 2.9 collective-permute-done.66
  433.9 1.7 collective-permute-start.68
  435.7 9.3 %collective-permute-done.67 = bf16[200,512]{1,0:T(8,128)(2,1)S(1)} collective-permute-done((bf16[200,512]{1,0:T(8,128)(2,1)S(1)}, bf16[200,512]{1,0:T(8,128)(2,1)S(1)}, u32[]{:S(2)}, u32[]{:S(2)}) %collective-permute-start.67) | collective-permute-done | bytes 204832 | tf_op jit(solution)/shard_map/ppermute | solution.py:548
  445.8 6.0 %collective-permute-done.70.refs_2_ = bf16[576,512]{1,0:T(8,128)(2,1)S(1)} collective-permute-done((bf16[576,512]{1,0:T(8,128)(2,1)S(1)}, bf16[576,512]{1,0:T(8,128)(2,1)S(1)}, u32[]{:S(2)}, u32[]{:S(2)}) %collective-permute-start.70) | collective-permute-done | bytes 589856 | tf_op jit(solution)/shard_map/ppermute | solution.py:551
  458.7 5.8 %owned.2 = (f32[1024,1024]{1,0:T(8,128)}, f32[256,4096]{1,0:T(8,128)}, f32[256,1024]{1,0:T(8,128)}) custom-call(bf16[576,512]{1,0:T(8,128)(2,1)S(1)} %constant_dynamic-update-slice_fusion.9.refs_0_, bf16[576,512]{1,0:T(8,128)(2,1)S(1)} %collective-permute-done.69.refs_1_, bf16[576,512]{1,0:T(8,128)(2,1)S(1)} %collective-permute-done.70.refs_2_, ...), custom_call_target="tpu_custom_call" | custom-call | flops 1 | bytes 1 | tf_op jit(solution)/shard_map/owned/pallas_call | solution.py:1009
  464.5 2.0 collective-permute-done.77.refs_2_
  468.7 1.9 owned.3
  (327 shorter events, 82.3 us)
Async XLA Ops:
  3.2 15.8 %collective-permute-start.2 = (bf16[80,1536]{1,0:T(8,128)(2,1)}, bf16[80,1536]{1,0:T(8,128)(2,1)S(1)}, u32[]{:S(2)}, u32[]{:S(2)}) collective-permute-start(bf16[80,1536]{1,0:T(8,128)(2,1)} %pack.1), channel_id=1, source_target_pairs={{0,3},{1,0},{2,1},{3,2},{4,7},{5,4},{6,5},{7,6},{8,11},{9,8},{10,9... | collective-permute-start | bytes 737288 | tf_op jit(solution)/shard_map/ppermute | solution.py:548
  7.4 20.6 %collective-permute-start.1 = (bf16[80,1536]{1,0:T(8,128)(2,1)}, bf16[80,1536]{1,0:T(8,128)(2,1)}, u32[]{:S(2)}, u32[]{:S(2)}) collective-permute-start(bf16[80,1536]{1,0:T(8,128)(2,1)} %pack.1), channel_id=1, source_target_pairs={{0,2},{1,3},{2,0},{3,1},{4,6},{5,7},{6,4},{7,5},{8,10},{9,11},{10,... | collective-permute-start | bytes 737288 | tf_op jit(solution)/shard_map/ppermute | solution.py:548
  7.4 21.6 %collective-permute-start = (bf16[80,1536]{1,0:T(8,128)(2,1)}, bf16[80,1536]{1,0:T(8,128)(2,1)}, u32[]{:S(2)}, u32[]{:S(2)}) collective-permute-start(bf16[80,1536]{1,0:T(8,128)(2,1)} %pack.1), channel_id=1, source_target_pairs={{0,1},{1,2},{2,3},{3,0},{4,5},{5,6},{6,7},{7,4},{8,9},{9,10},{10,1... | collective-permute-start | bytes 737288 | tf_op jit(solution)/shard_map/ppermute | solution.py:548
  30.0 15.7 %collective-permute-start.9 = (bf16[64,2560]{1,0:T(8,128)(2,1)}, bf16[64,2560]{1,0:T(8,128)(2,1)S(1)}, u32[]{:S(2)}, u32[]{:S(2)}) collective-permute-start(bf16[64,2560]{1,0:T(8,128)(2,1)} %pad_maximum_fusion.11), channel_id=1, source_target_pairs={{0,3},{1,0},{2,1},{3,2},{4,7},{5,4},{6,5},{7,6},{8,11},{9,8},{10,9... | collective-permute-start | bytes 983048 | tf_op jit(solution)/shard_map/ppermute | solution.py:548
  30.0 29.9 %collective-permute-start.8 = (bf16[64,2560]{1,0:T(8,128)(2,1)}, bf16[64,2560]{1,0:T(8,128)(2,1)S(1)}, u32[]{:S(2)}, u32[]{:S(2)}) collective-permute-start(bf16[64,2560]{1,0:T(8,128)(2,1)} %pad_maximum_fusion.11), channel_id=1, source_target_pairs={{0,2},{1,3},{2,0},{3,1},{4,6},{5,7},{6,4},{7,5},{8,10},{9,11},{10,... | collective-permute-start | bytes 983048 | tf_op jit(solution)/shard_map/ppermute | solution.py:548
  31.9 29.9 %collective-permute-start.7 = (bf16[64,2560]{1,0:T(8,128)(2,1)}, bf16[64,2560]{1,0:T(8,128)(2,1)S(1)}, u32[]{:S(2)}, u32[]{:S(2)}) collective-permute-start(bf16[64,2560]{1,0:T(8,128)(2,1)} %pad_maximum_fusion.11), channel_id=1, source_target_pairs={{0,1},{1,2},{2,3},{3,0},{4,5},{5,6},{6,7},{7,4},{8,9},{9,10},{10,1... | collective-permute-start | bytes 983048 | tf_op jit(solution)/shard_map/ppermute | solution.py:548
  43.9 17.9 %collective-permute-start.5 = (bf16[2,3,64,768]{3,2,1,0:T(8,128)(2,1)S(1)}, bf16[2,3,64,768]{3,2,1,0:T(8,128)(2,1)S(1)}, u32[]{:S(2)}, u32[]{:S(2)}) collective-permute-start(bf16[2,3,64,768]{3,2,1,0:T(8,128)(2,1)S(1)} %pad_maximum_fusion.9), channel_id=1, source_target_pairs={{0,16},{4,20},{8,24},{12,28},{16,0},{20,4},{24,8},{28,12},{1,17},{... | collective-permute-start | bytes 1769480 | tf_op jit(solution)/shard_map/ppermute | solution.py:551
  44.2 17.6 %collective-permute-start.6 = (bf16[2,3,64,768]{3,2,1,0:T(8,128)(2,1)S(1)}, bf16[2,3,64,768]{3,2,1,0:T(8,128)(2,1)S(1)}, u32[]{:S(2)}, u32[]{:S(2)}) collective-permute-start(bf16[2,3,64,768]{3,2,1,0:T(8,128)(2,1)S(1)} %pad_maximum_fusion.10), channel_id=1, source_target_pairs={{0,8},{4,12},{8,0},{12,4},{16,24},{20,28},{24,16},{28,20},{1,9},{5... | collective-permute-start | bytes 1769480 | tf_op jit(solution)/shard_map/ppermute | solution.py:551
  45.7 16.9 %collective-permute-start.10 = (bf16[3,64,1536]{2,1,0:T(8,128)(2,1)S(1)}, bf16[3,64,1536]{2,1,0:T(8,128)(2,1)S(1)}, u32[]{:S(2)}, u32[]{:S(2)}) collective-permute-start(bf16[3,64,1536]{2,1,0:T(8,128)(2,1)S(1)} %pad_maximum_fusion.8.refs_1_), channel_id=1, source_target_pairs={{0,4},{4,0},{8,12},{12,8},{16,20},{20,16},{24,28},{28,24},{1,5},{5... | collective-permute-start | bytes 1769480 | tf_op jit(solution)/shard_map/ppermute | solution.py:554
  62.6 36.1 %collective-permute-start.21 = (bf16[256,512]{1,0:T(8,128)(2,1)}, bf16[256,512]{1,0:T(8,128)(2,1)}, u32[]{:S(2)}, u32[]{:S(2)}) collective-permute-start(bf16[256,512]{1,0:T(8,128)(2,1)} %dynamic_slice.28), channel_id=1, source_target_pairs={{0,3},{1,0},{2,1},{3,2},{4,7},{5,4},{6,5},{7,6},{8,11},{9,8},{10,9... | collective-permute-start | bytes 786440 | tf_op jit(solution)/shard_map/ppermute | solution.py:548
  63.0 38.2 %collective-permute-start.20 = (bf16[256,512]{1,0:T(8,128)(2,1)}, bf16[256,512]{1,0:T(8,128)(2,1)}, u32[]{:S(2)}, u32[]{:S(2)}) collective-permute-start(bf16[256,512]{1,0:T(8,128)(2,1)} %dynamic_slice.28), channel_id=1, source_target_pairs={{0,2},{1,3},{2,0},{3,1},{4,6},{5,7},{6,4},{7,5},{8,10},{9,11},{10,... | collective-permute-start | bytes 786440 | tf_op jit(solution)/shard_map/ppermute | solution.py:548
  63.4 37.9 %collective-permute-start.19 = (bf16[256,512]{1,0:T(8,128)(2,1)}, bf16[256,512]{1,0:T(8,128)(2,1)}, u32[]{:S(2)}, u32[]{:S(2)}) collective-permute-start(bf16[256,512]{1,0:T(8,128)(2,1)} %dynamic_slice.28), channel_id=1, source_target_pairs={{0,1},{1,2},{2,3},{3,0},{4,5},{5,6},{6,7},{7,4},{8,9},{9,10},{10,1... | collective-permute-start | bytes 786440 | tf_op jit(solution)/shard_map/ppermute | solution.py:548
  78.0 23.7 %collective-permute-start.18 = (bf16[2,3,64,1280]{3,2,1,0:T(8,128)(2,1)S(1)}, bf16[2,3,64,1280]{3,2,1,0:T(8,128)(2,1)S(1)}, u32[]{:S(2)}, u32[]{:S(2)}) collective-permute-start(bf16[2,3,64,1280]{3,2,1,0:T(8,128)(2,1)S(1)} %pad_maximum_fusion.2), channel_id=1, source_target_pairs={{0,8},{4,12},{8,0},{12,4},{16,24},{20,28},{24,16},{28,20},{1,9},{5... | collective-permute-start | bytes 2949128 | tf_op jit(solution)/shard_map/ppermute | solution.py:551
  79.2 22.6 %collective-permute-start.17 = (bf16[2,3,64,1280]{3,2,1,0:T(8,128)(2,1)S(1)}, bf16[2,3,64,1280]{3,2,1,0:T(8,128)(2,1)S(1)}, u32[]{:S(2)}, u32[]{:S(2)}) collective-permute-start(bf16[2,3,64,1280]{3,2,1,0:T(8,128)(2,1)S(1)} %pad_maximum_fusion.1), channel_id=1, source_target_pairs={{0,16},{4,20},{8,24},{12,28},{16,0},{20,4},{24,8},{28,12},{1,17},{... | collective-permute-start | bytes 2949128 | tf_op jit(solution)/shard_map/ppermute | solution.py:551
  98.7 23.5 %collective-permute-start.26 = (bf16[3,64,2560]{2,1,0:T(8,128)(2,1)S(1)}, bf16[3,64,2560]{2,1,0:T(8,128)(2,1)}, u32[]{:S(2)}, u32[]{:S(2)}) collective-permute-start(bf16[3,64,2560]{2,1,0:T(8,128)(2,1)S(1)} %pad_maximum_fusion.refs_2_), channel_id=1, source_target_pairs={{0,4},{4,0},{8,12},{12,8},{16,20},{20,16},{24,28},{28,24},{1,5},{5... | collective-permute-start | bytes 2949128 | tf_op jit(solution)/shard_map/ppermute | solution.py:554
  101.2 22.1 %collective-permute-start.27 = (bf16[1,3,64,1280]{3,2,1,0:T(8,128)(2,1)S(1)}, bf16[1,3,64,1280]{3,2,1,0:T(8,128)(2,1)}, u32[]{:S(2)}, u32[]{:S(2)}) collective-permute-start(bf16[1,3,64,1280]{3,2,1,0:T(8,128)(2,1)S(1)} %collective-permute-done.15.refs_3_), channel_id=1, source_target_pairs={{0,4},{4,0},{8,12},{12,8},{16,20},{20,16},{24,28},{28,24},{1,5},{5... | collective-permute-start | bytes 1474568 | tf_op jit(solution)/shard_map/ppermute | solution.py:554
  101.3 42.3 %collective-permute-start.28 = (bf16[1,3,64,1280]{3,2,1,0:T(8,128)(2,1)S(1)}, bf16[1,3,64,1280]{3,2,1,0:T(8,128)(2,1)}, u32[]{:S(2)}, u32[]{:S(2)}) collective-permute-start(bf16[1,3,64,1280]{3,2,1,0:T(8,128)(2,1)S(1)} %collective-permute-done.16.refs_4_), channel_id=1, source_target_pairs={{0,4},{4,0},{8,12},{12,8},{16,20},{20,16},{24,28},{28,24},{1,5},{5... | collective-permute-start | bytes 1474568 | tf_op jit(solution)/shard_map/ppermute | solution.py:554
  104.3 16.0 %collective-permute-start.22 = (bf16[1,3,256,256]{3,2,1,0:T(8,128)(2,1)S(1)}, bf16[1,3,256,256]{3,2,1,0:T(8,128)(2,1)S(1)}, u32[]{:S(2)}, u32[]{:S(2)}) collective-permute-start(bf16[1,3,256,256]{3,2,1,0:T(8,128)(2,1)S(1)} %get-tuple-element.445), channel_id=1, source_target_pairs={{0,8},{4,12},{8,0},{12,4},{16,24},{20,28},{24,16},{28,20},{1,9},{5... | collective-permute-start | bytes 1179656 | tf_op jit(solution)/shard_map/ppermute | solution.py:551
  118.8 25.9 %collective-permute-start.29 = (bf16[2,3,64,1280]{3,2,1,0:T(8,128)(2,1)S(1)}, bf16[2,3,64,1280]{3,2,1,0:T(8,128)(2,1)}, u32[]{:S(2)}, u32[]{:S(2)}) collective-permute-start(bf16[2,3,64,1280]{3,2,1,0:T(8,128)(2,1)S(1)} %collective-permute-done.17.refs_5_), channel_id=1, source_target_pairs={{0,4},{4,0},{8,12},{12,8},{16,20},{20,16},{24,28},{28,24},{1,5},{5... | collective-permute-start | bytes 2949128 | tf_op jit(solution)/shard_map/ppermute | solution.py:554
  120.2 24.5 %collective-permute-start.30 = (bf16[2,3,64,1280]{3,2,1,0:T(8,128)(2,1)S(1)}, bf16[2,3,64,1280]{3,2,1,0:T(8,128)(2,1)}, u32[]{:S(2)}, u32[]{:S(2)}) collective-permute-start(bf16[2,3,64,1280]{3,2,1,0:T(8,128)(2,1)S(1)} %collective-permute-done.18.refs_6_), channel_id=1, source_target_pairs={{0,4},{4,0},{8,12},{12,8},{16,20},{20,16},{24,28},{28,24},{1,5},{5... | collective-permute-start | bytes 2949128 | tf_op jit(solution)/shard_map/ppermute | solution.py:554
  122.2 30.1 %collective-permute-start.25 = (bf16[2,3,256,256]{3,2,1,0:T(8,128)(2,1)}, bf16[2,3,256,256]{3,2,1,0:T(8,128)(2,1)}, u32[]{:S(2)}, u32[]{:S(2)}) collective-permute-start(bf16[2,3,256,256]{3,2,1,0:T(8,128)(2,1)} %pad_maximum_fusion.5), channel_id=1, source_target_pairs={{0,8},{4,12},{8,0},{12,4},{16,24},{20,28},{24,16},{28,20},{1,9},{5... | collective-permute-start | bytes 2359304 | tf_op jit(solution)/shard_map/ppermute | solution.py:551
  123.4 28.9 %collective-permute-start.24 = (bf16[2,3,256,256]{3,2,1,0:T(8,128)(2,1)}, bf16[2,3,256,256]{3,2,1,0:T(8,128)(2,1)}, u32[]{:S(2)}, u32[]{:S(2)}) collective-permute-start(bf16[2,3,256,256]{3,2,1,0:T(8,128)(2,1)} %pad_maximum_fusion.4), channel_id=1, source_target_pairs={{0,16},{4,20},{8,24},{12,28},{16,0},{20,4},{24,8},{28,12},{1,17},{... | collective-permute-start | bytes 2359304 | tf_op jit(solution)/shard_map/ppermute | solution.py:551
  143.6 16.8 %collective-permute-start.31 = (bf16[3,256,512]{2,1,0:T(8,128)(2,1)S(1)}, bf16[3,256,512]{2,1,0:T(8,128)(2,1)S(1)}, u32[]{:S(2)}, u32[]{:S(2)}) collective-permute-start(bf16[3,256,512]{2,1,0:T(8,128)(2,1)S(1)} %pad_maximum_fusion.3.refs_1_), channel_id=1, source_target_pairs={{0,4},{4,0},{8,12},{12,8},{16,20},{20,16},{24,28},{28,24},{1,5},{5... | collective-permute-start | bytes 2359304 | tf_op jit(solution)/shard_map/ppermute | solution.py:554
  144.6 15.8 %collective-permute-start.32 = (bf16[1,3,256,256]{3,2,1,0:T(8,128)(2,1)S(1)}, bf16[1,3,256,256]{3,2,1,0:T(8,128)(2,1)}, u32[]{:S(2)}, u32[]{:S(2)}) collective-permute-start(bf16[1,3,256,256]{3,2,1,0:T(8,128)(2,1)S(1)} %collective-permute-done.22.refs_2_), channel_id=1, source_target_pairs={{0,4},{4,0},{8,12},{12,8},{16,20},{20,16},{24,28},{28,24},{1,5},{5... | collective-permute-start | bytes 1179656 | tf_op jit(solution)/shard_map/ppermute | solution.py:554
  210.8 44.9 %collective-permute-start.36 = (bf16[4,4,128,512]{3,2,1,0:T(8,128)(2,1)S(1)}, bf16[4,4,128,512]{3,2,1,0:T(8,128)(2,1)S(1)}, u32[]{:S(2)}, u32[]{:S(2)}) collective-permute-start(bf16[4,4,128,512]{3,2,1,0:T(8,128)(2,1)S(1)} %bitcast.163), channel_id=1, source_target_pairs={{0,4},{4,0},{8,12},{12,8},{16,20},{20,16},{24,28},{28,24},{1,5},{5... | collective-permute-start | bytes 6291464 | tf_op jit(solution)/shard_map/ppermute | solution.py:554
  210.9 44.8 %collective-permute-start.37 = (bf16[4,4,128,512]{3,2,1,0:T(8,128)(2,1)}, bf16[4,4,128,512]{3,2,1,0:T(8,128)(2,1)S(1)}, u32[]{:S(2)}, u32[]{:S(2)}) collective-permute-start(bf16[4,4,128,512]{3,2,1,0:T(8,128)(2,1)} %bitcast.178), channel_id=1, source_target_pairs={{0,4},{4,0},{8,12},{12,8},{16,20},{20,16},{24,28},{28,24},{1,5},{5... | collective-permute-start | bytes 6291464 | tf_op jit(solution)/shard_map/ppermute | solution.py:554
  264.8 47.2 %collective-permute-start.40 = (bf16[2,4,128,512]{3,2,1,0:T(8,128)(2,1)}, bf16[2,4,128,512]{3,2,1,0:T(8,128)(2,1)}, u32[]{:S(2)}, u32[]{:S(2)}) collective-permute-start(bf16[2,4,128,512]{3,2,1,0:T(8,128)(2,1)} %get-tuple-element.298), channel_id=1, source_target_pairs={{0,8},{4,12},{8,0},{12,4},{16,24},{20,28},{24,16},{28,20},{1,9},{5... | collective-permute-start | bytes 3145736 | tf_op jit(solution)/shard_map/ppermute | solution.py:551
  265.2 46.8 %collective-permute-start.41 = (bf16[2,4,128,512]{3,2,1,0:T(8,128)(2,1)}, bf16[2,4,128,512]{3,2,1,0:T(8,128)(2,1)}, u32[]{:S(2)}, u32[]{:S(2)}) collective-permute-start(bf16[2,4,128,512]{3,2,1,0:T(8,128)(2,1)} %get-tuple-element.299), channel_id=1, source_target_pairs={{0,16},{4,20},{8,24},{12,28},{16,0},{20,4},{24,8},{28,12},{1,17},{... | collective-permute-start | bytes 3145736 | tf_op jit(solution)/shard_map/ppermute | solution.py:551
  265.5 46.7 %collective-permute-start.42 = (bf16[2,4,128,512]{3,2,1,0:T(8,128)(2,1)}, bf16[2,4,128,512]{3,2,1,0:T(8,128)(2,1)}, u32[]{:S(2)}, u32[]{:S(2)}) collective-permute-start(bf16[2,4,128,512]{3,2,1,0:T(8,128)(2,1)} %get-tuple-element.300), channel_id=1, source_target_pairs={{0,8},{4,12},{8,0},{12,4},{16,24},{20,28},{24,16},{28,20},{1,9},{5... | collective-permute-start | bytes 3145736 | tf_op jit(solution)/shard_map/ppermute | solution.py:551
  266.6 45.7 %collective-permute-start.43 = (bf16[2,4,128,512]{3,2,1,0:T(8,128)(2,1)S(1)}, bf16[2,4,128,512]{3,2,1,0:T(8,128)(2,1)}, u32[]{:S(2)}, u32[]{:S(2)}) collective-permute-start(bf16[2,4,128,512]{3,2,1,0:T(8,128)(2,1)S(1)} %get-tuple-element.301), channel_id=1, source_target_pairs={{0,16},{4,20},{8,24},{12,28},{16,0},{20,4},{24,8},{28,12},{1,17},{... | collective-permute-start | bytes 3145736 | tf_op jit(solution)/shard_map/ppermute | solution.py:551
  281.7 35.9 %collective-permute-start.44 = (bf16[4,4,64,512]{3,2,1,0:T(8,128)(2,1)}, bf16[4,4,64,512]{3,2,1,0:T(8,128)(2,1)S(1)}, u32[]{:S(2)}, u32[]{:S(2)}) collective-permute-start(bf16[4,4,64,512]{3,2,1,0:T(8,128)(2,1)} %get-tuple-element.313), channel_id=1, source_target_pairs={{0,4},{4,0},{8,12},{12,8},{16,20},{20,16},{24,28},{28,24},{1,5},{5... | collective-permute-start | bytes 3145736 | tf_op jit(solution)/shard_map/ppermute | solution.py:554
  318.1 19.9 %collective-permute-start.47 = (bf16[2,4,32,512]{3,2,1,0:T(8,128)(2,1)S(1)}, bf16[2,4,32,512]{3,2,1,0:T(8,128)(2,1)S(1)}, u32[]{:S(2)}, u32[]{:S(2)}) collective-permute-start(bf16[2,4,32,512]{3,2,1,0:T(8,128)(2,1)S(1)} %get-tuple-element.322), channel_id=1, source_target_pairs={{0,8},{4,12},{8,0},{12,4},{16,24},{20,28},{24,16},{28,20},{1,9},{5... | collective-permute-start | bytes 786440 | tf_op jit(solution)/shard_map/ppermute | solution.py:551
  319.2 18.8 %collective-permute-start.48 = (bf16[2,4,32,512]{3,2,1,0:T(8,128)(2,1)S(1)}, bf16[2,4,32,512]{3,2,1,0:T(8,128)(2,1)S(1)}, u32[]{:S(2)}, u32[]{:S(2)}) collective-permute-start(bf16[2,4,32,512]{3,2,1,0:T(8,128)(2,1)S(1)} %get-tuple-element.323), channel_id=1, source_target_pairs={{0,16},{4,20},{8,24},{12,28},{16,0},{20,4},{24,8},{28,12},{1,17},{... | collective-permute-start | bytes 786440 | tf_op jit(solution)/shard_map/ppermute | solution.py:551
  319.6 18.4 %collective-permute-start.45 = (bf16[1,4,128,512]{3,2,1,0:T(8,128)(2,1)}, bf16[1,4,128,512]{3,2,1,0:T(8,128)(2,1)S(1)}, u32[]{:S(2)}, u32[]{:S(2)}) collective-permute-start(bf16[1,4,128,512]{3,2,1,0:T(8,128)(2,1)} %get-tuple-element.320), channel_id=1, source_target_pairs={{0,16},{4,20},{8,24},{12,28},{16,0},{20,4},{24,8},{28,12},{1,17},{... | collective-permute-start | bytes 1572872 | tf_op jit(solution)/shard_map/ppermute | solution.py:551
  320.7 17.4 %collective-permute-start.46 = (bf16[1,4,128,512]{3,2,1,0:T(8,128)(2,1)}, bf16[1,4,128,512]{3,2,1,0:T(8,128)(2,1)S(1)}, u32[]{:S(2)}, u32[]{:S(2)}) collective-permute-start(bf16[1,4,128,512]{3,2,1,0:T(8,128)(2,1)} %get-tuple-element.321), channel_id=1, source_target_pairs={{0,8},{4,12},{8,0},{12,4},{16,24},{20,28},{24,16},{28,20},{1,9},{5... | collective-permute-start | bytes 1572872 | tf_op jit(solution)/shard_map/ppermute | solution.py:551
  339.3 35.6 %collective-permute-start.51 = (bf16[256,512]{1,0:T(8,128)(2,1)S(1)}, bf16[256,512]{1,0:T(8,128)(2,1)S(1)}, u32[]{:S(2)}, u32[]{:S(2)}) collective-permute-start(bf16[256,512]{1,0:T(8,128)(2,1)S(1)} %get-tuple-element.357), channel_id=1, source_target_pairs={{0,1},{1,2},{2,3},{3,0},{4,5},{5,6},{6,7},{7,4},{8,9},{9,10},{10,1... | collective-permute-start | bytes 786440 | tf_op jit(solution)/shard_map/ppermute | solution.py:548
  340.3 34.6 %collective-permute-start.52 = (bf16[256,512]{1,0:T(8,128)(2,1)S(1)}, bf16[256,512]{1,0:T(8,128)(2,1)S(1)}, u32[]{:S(2)}, u32[]{:S(2)}) collective-permute-start(bf16[256,512]{1,0:T(8,128)(2,1)S(1)} %get-tuple-element.358), channel_id=1, source_target_pairs={{0,2},{1,3},{2,0},{3,1},{4,6},{5,7},{6,4},{7,5},{8,10},{9,11},{10,... | collective-permute-start | bytes 786440 | tf_op jit(solution)/shard_map/ppermute | solution.py:548
  341.8 33.1 %collective-permute-start.53 = (bf16[256,512]{1,0:T(8,128)(2,1)S(1)}, bf16[256,512]{1,0:T(8,128)(2,1)S(1)}, u32[]{:S(2)}, u32[]{:S(2)}) collective-permute-start(bf16[256,512]{1,0:T(8,128)(2,1)S(1)} %get-tuple-element.359), channel_id=1, source_target_pairs={{0,3},{1,0},{2,1},{3,2},{4,7},{5,4},{6,5},{7,6},{8,11},{9,8},{10,9... | collective-permute-start | bytes 786440 | tf_op jit(solution)/shard_map/ppermute | solution.py:548
  343.5 17.8 %collective-permute-start.49 = (bf16[1,4,160,512]{3,2,1,0:T(8,128)(2,1)S(1)}, bf16[1,4,160,512]{3,2,1,0:T(8,128)(2,1)S(1)}, u32[]{:S(2)}, u32[]{:S(2)}) collective-permute-start(bf16[1,4,160,512]{3,2,1,0:T(8,128)(2,1)S(1)} %maximum_bitcast_fusion), channel_id=1, source_target_pairs={{0,16},{4,20},{8,24},{12,28},{16,0},{20,4},{24,8},{28,12},{1,17},{... | collective-permute-start | bytes 1966088 | tf_op jit(solution)/shard_map/ppermute | solution.py:551
  343.7 17.6 %collective-permute-start.50 = (bf16[1,4,160,512]{3,2,1,0:T(8,128)(2,1)S(1)}, bf16[1,4,160,512]{3,2,1,0:T(8,128)(2,1)S(1)}, u32[]{:S(2)}, u32[]{:S(2)}) collective-permute-start(bf16[1,4,160,512]{3,2,1,0:T(8,128)(2,1)S(1)} %maximum_bitcast_fusion.1), channel_id=1, source_target_pairs={{0,8},{4,12},{8,0},{12,4},{16,24},{20,28},{24,16},{28,20},{1,9},{5... | collective-permute-start | bytes 1966088 | tf_op jit(solution)/shard_map/ppermute | solution.py:551
  379.8 25.5 %collective-permute-start.57 = (bf16[320,512]{1,0:T(8,128)(2,1)}, bf16[320,512]{1,0:T(8,128)(2,1)S(1)}, u32[]{:S(2)}, u32[]{:S(2)}) collective-permute-start(bf16[320,512]{1,0:T(8,128)(2,1)} %copy-done.25), channel_id=1, source_target_pairs={{0,1},{1,2},{2,3},{3,0},{4,5},{5,6},{6,7},{7,4},{8,9},{9,10},{10,1... | collective-permute-start | bytes 983048 | tf_op jit(solution)/shard_map/ppermute | solution.py:548
  380.1 25.2 %collective-permute-start.58 = (bf16[320,512]{1,0:T(8,128)(2,1)}, bf16[320,512]{1,0:T(8,128)(2,1)S(1)}, u32[]{:S(2)}, u32[]{:S(2)}) collective-permute-start(bf16[320,512]{1,0:T(8,128)(2,1)} %copy-done.24), channel_id=1, source_target_pairs={{0,2},{1,3},{2,0},{3,1},{4,6},{5,7},{6,4},{7,5},{8,10},{9,11},{10,... | collective-permute-start | bytes 983048 | tf_op jit(solution)/shard_map/ppermute | solution.py:548
  380.8 24.5 %collective-permute-start.59 = (bf16[320,512]{1,0:T(8,128)(2,1)}, bf16[320,512]{1,0:T(8,128)(2,1)S(1)}, u32[]{:S(2)}, u32[]{:S(2)}) collective-permute-start(bf16[320,512]{1,0:T(8,128)(2,1)} %copy-done.23), channel_id=1, source_target_pairs={{0,3},{1,0},{2,1},{3,2},{4,7},{5,4},{6,5},{7,6},{8,11},{9,8},{10,9... | collective-permute-start | bytes 983048 | tf_op jit(solution)/shard_map/ppermute | solution.py:548
  388.3 18.8 %collective-permute-start.55 = (bf16[2,4,96,512]{3,2,1,0:T(8,128)(2,1)S(1)}, bf16[2,4,96,512]{3,2,1,0:T(8,128)(2,1)S(1)}, u32[]{:S(2)}, u32[]{:S(2)}) collective-permute-start(bf16[2,4,96,512]{3,2,1,0:T(8,128)(2,1)S(1)} %get-tuple-element.368), channel_id=1, source_target_pairs={{0,8},{4,12},{8,0},{12,4},{16,24},{20,28},{24,16},{28,20},{1,9},{5... | collective-permute-start | bytes 2359304 | tf_op jit(solution)/shard_map/ppermute | solution.py:551
  389.1 18.4 %collective-permute-start.56 = (bf16[2,4,96,512]{3,2,1,0:T(8,128)(2,1)S(1)}, bf16[2,4,96,512]{3,2,1,0:T(8,128)(2,1)S(1)}, u32[]{:S(2)}, u32[]{:S(2)}) collective-permute-start(bf16[2,4,96,512]{3,2,1,0:T(8,128)(2,1)S(1)} %get-tuple-element.369), channel_id=1, source_target_pairs={{0,16},{4,20},{8,24},{12,28},{16,0},{20,4},{24,8},{28,12},{1,17},{... | collective-permute-start | bytes 2359304 | tf_op jit(solution)/shard_map/ppermute | solution.py:551
  422.3 23.5 %collective-permute-start.71 = (bf16[576,512]{1,0:T(8,128)(2,1)S(1)}, bf16[576,512]{1,0:T(8,128)(2,1)S(1)}, u32[]{:S(2)}, u32[]{:S(2)}) collective-permute-start(bf16[576,512]{1,0:T(8,128)(2,1)S(1)} %constant_dynamic-update-slice_fusion.9.refs_0_), channel_id=1, source_target_pairs={{0,24},{4,28},{8,16},{12,20},{16,8},{20,12},{24,0},{28,4},{1,25},{... | collective-permute-start | bytes 1769480 | tf_op jit(solution)/shard_map/ppermute | solution.py:551
  425.4 26.4 %collective-permute-start.70 = (bf16[576,512]{1,0:T(8,128)(2,1)S(1)}, bf16[576,512]{1,0:T(8,128)(2,1)S(1)}, u32[]{:S(2)}, u32[]{:S(2)}) collective-permute-start(bf16[576,512]{1,0:T(8,128)(2,1)S(1)} %constant_dynamic-update-slice_fusion.9.refs_0_), channel_id=1, source_target_pairs={{0,16},{4,20},{8,24},{12,28},{16,0},{20,4},{24,8},{28,12},{1,17},{... | collective-permute-start | bytes 1769480 | tf_op jit(solution)/shard_map/ppermute | solution.py:551
  425.4 26.4 %collective-permute-start.69 = (bf16[576,512]{1,0:T(8,128)(2,1)S(1)}, bf16[576,512]{1,0:T(8,128)(2,1)S(1)}, u32[]{:S(2)}, u32[]{:S(2)}) collective-permute-start(bf16[576,512]{1,0:T(8,128)(2,1)S(1)} %constant_dynamic-update-slice_fusion.9.refs_0_), channel_id=1, source_target_pairs={{0,8},{4,12},{8,0},{12,4},{16,24},{20,28},{24,16},{28,20},{1,9},{5... | collective-permute-start | bytes 1769480 | tf_op jit(solution)/shard_map/ppermute | solution.py:551
  (77 other events, 663.5 us)
